TPU v7x, 128 devices: a whole 4x4x4 slice. The times are simulated.
128 devices in a mesh: party: 2 (over x_hi), dp: 64 (over y, x_lo, z, core).
Axes of the slice: x: 4 (x_hi: 2, x_lo: 2; x = x_hi * 2 + x_lo), y: 4, z: 4, core: 2. Of those that a mesh axis runs over, the one named last changes fastest.
Arguments:
- x_share: float32 [2, 32768, 1024], P('party', 'dp'), may hold values from -6 to 6
- w_share: float32 [2, 1024, 2048], P('party', 'dp'), may hold values from -0.1875 to 0.1875
- g_share: float32 [2, 32768, 2048], P('party', 'dp'), may hold values from -0.03125 to 0.03125
- fwd_a: float32 [2, 32768, 1024], P('party', 'dp'), may hold values from -4 to 4
- fwd_b: float32 [2, 1024, 2048], P('party', 'dp'), may hold values from -0.125 to 0.125
- fwd_c: float32 [2, 32768, 2048], P('party', 'dp'), may hold values from -2100 to 2100, as said below
- bwd_a: float32 [2, 32768, 1024], P('party', 'dp'), may hold values from -4 to 4
- bwd_b: float32 [2, 32768, 2048], P('party', 'dp'), may hold values from -0.022097087 to 0.022097087
- bwd_c: float32 [2, 1024, 2048], P('party', 'dp'), may hold values from -2100 to 2100, as said below
Outputs:
- y_share: float32 [2, 32768, 2048], P('party', 'dp')
- dw_share: float32 [2, 1024, 2048], P('party', 'dp')
Inputs may be any that keep to these rules, and one draw needn't show every extreme that they name: fwd_c[0] + fwd_c[1] equals (fwd_a[0] + fwd_a[1]) (fwd_b[0] + fwd_b[1]) up to float32 rounding. bwd_c[0] + bwd_c[1] equals (bwd_a[0] + bwd_a[1])^T (bwd_b[0] + bwd_b[1]) up to float32 rounding.
All inputs are finite; a program needn't handle non-finite values.
Results may differ from a plain program's by a relative error of at most 0.0001.
Values sent between devices are 32-bit elements; how exact they have to be, the bound alone decides.
No kernel may reach another device: no remote copies, remote signals or barrier semaphores. Data moves between devices by JAX's collectives and lax.ppermute only.
A program may use at most 128 MiB of HBM per device.

v0:
```python
import jax
import jax.numpy as jnp
from jax import lax
from jax.sharding import Mesh
from jax.sharding import PartitionSpec as P

DP = ("dp_0", "dp_1", "dp_2", "dp_3")


def from_everyone(shard, axis):
    length = lax.axis_size(axis)
    return lax.all_to_all(
        jnp.broadcast_to(shard[None], (length, *shard.shape)), axis, 0, 0, tiled=True
    )


def of_everyone(shard, axis):
    return from_everyone(shard, axis).sum(axis=0)


def in_one_piece(arrays, axis, dim, along):
    ends, at = ([], 0)
    for a in arrays[:-1]:
        at += a.shape[along]
        ends.append(at)
    both = jnp.concatenate(arrays, axis=along)
    return tuple(jnp.split(lax.all_gather(both, axis, axis=dim, tiled=True), ends, axis=along))


def gathered_total(shard, axis):
    return lax.all_gather(shard, axis).sum(0)


def in_blocks(shard, dim, length):
    shape = shard.shape
    pieces = shard.reshape(*shape[:dim], length, shape[dim] // length, *shape[dim + 1 :])
    return jnp.moveaxis(pieces, dim, 0)


def summed_rows(shard, chips, core, dim):
    sizes = (lax.axis_size(chips), lax.axis_size(core))
    pieces = in_blocks(shard, dim, sizes[0] * sizes[1])
    inside = pieces.shape[1:]
    pieces = pieces.reshape(*sizes, *inside).swapaxes(0, 1).reshape(-1, *inside)
    pieces = lax.psum_scatter(pieces, core, scatter_dimension=0, tiled=True)
    return lax.psum_scatter(pieces, chips, scatter_dimension=0, tiled=True)[0]


def matmul(left, right):
    return jnp.dot(left, right, preferred_element_type=jnp.float32, precision=lax.Precision.HIGHEST)


def tmatmul(left, right):
    return lax.dot_general(
        left,
        right,
        (((0,), (0,)), ((), ())),
        precision=lax.Precision.HIGHEST,
        preferred_element_type=jnp.float32,
    )


def body(x_share, w_share, g_share, fwd_a, fwd_b, fwd_c, bwd_a, bwd_b, bwd_c):
    first = (lax.axis_index("party") == 0).astype(jnp.float32)
    inputs = x_share[0]
    left_fwd = fwd_a[0]
    eps_fwd = of_everyone(inputs - left_fwd, "party")
    delta_rows = of_everyone(w_share[0] - fwd_b[0], "party")
    corrected_fwd, delta_fwd = in_one_piece((fwd_b[0] + first * delta_rows, delta_rows), DP, 0, 1)
    outputs = fwd_c[0] + matmul(eps_fwd, corrected_fwd) + matmul(left_fwd, delta_fwd)
    left_bwd = bwd_a[0]
    eps_bwd, delta_bwd = (
        gathered_total(inputs - left_bwd, "party"),
        gathered_total(g_share[0] - bwd_b[0], "party"),
    )
    corrected = bwd_b[0] + first * delta_bwd
    partial_value = tmatmul(eps_bwd, corrected) + tmatmul(left_bwd, delta_bwd)
    summed = summed_rows(partial_value, ("dp_0", "dp_1", "dp_2"), "dp_3", 0)
    return (outputs[None], (bwd_c[0] + summed)[None])


def solution(mesh):
    split = Mesh(
        mesh.devices.reshape(mesh.shape["party"], 4, 2, 4, 2),
        ("party", "dp_0", "dp_1", "dp_2", "dp_3"),
    )
    return jax.shard_map(
        body,
        mesh=split,
        in_specs=(
            P("party", DP, None),
            P("party", DP, None),
            P("party", DP, None),
            P("party", DP, None),
            P("party", DP, None),
            P("party", DP, None),
            P("party", DP, None),
            P("party", DP, None),
            P("party", DP, None),
        ),
        out_specs=(P("party", DP, None), P("party", DP, None)),
        check_vma=False,
    )
```

profile of v0, /device:TPU:0, one launch (start us, length us, event | category | flops | bytes accessed | tf_op | source)
XLA Modules:
  0.0 475.3 jit_solution(8145719380455951791)
XLA Ops:
  8.0 0.0 all-gather.6.cloned.1.call-start
  8.0 5.1 %fusion.12 = (f32[1,512,1024]{2,1,0:T(8,128)}, f32[512,1024]{1,0:T(8,128)S(1)}) fusion(f32[1,512,1024]{2,1,0:T(8,128)} %param.9, f32[1,512,1024]{2,1,0:T(8,128)} %param.15, f32[1,512,1024]{2,1,0:T(8,128)} %param.12), kind=kLoop, calls=%fused_computation.18 | loop fusion | flops 1048576 | bytes 10485760 | tf_op jit(solution)/shard_map/sub | solution.py:73
  13.1 0.0 all-gather.6.cloned.1.call-update
  13.1 0.0 all-gather.8.cloned.1.call-start
  13.2 6.6 %sub.19 = f32[1,512,2048]{2,1,0:T(8,128)} subtract(f32[1,512,2048]{2,1,0:T(8,128)} %param.11, f32[1,512,2048]{2,1,0:T(8,128)} %param.16) | non-fusion elementwise | flops 1048576 | bytes 12582912 | tf_op jit(solution)/shard_map/sub | solution.py:74
  19.8 0.0 all-gather.8.cloned.1.call-update
  19.8 0.0 reduce-scatter.3.cloned.1.call-start
  19.8 56.7 %all-gather.6.cloned.1.call-done = f32[2,512,1024]{2,1,0:T(8,128)} async-done(((f32[1,512,1024]{2,1,0:T(8,128)}), f32[2,512,1024]{2,1,0:T(8,128)}) %all-gather.6.cloned.1.call-update) | async-done | bytes 4194320 | tf_op jit(solution)/shard_map/all_gather | solution.py:31
  76.5 4.1 reduce_sum.38
  80.7 105.6 %all-gather.8.cloned.1.call-done = f32[2,512,2048]{2,1,0:T(8,128)} async-done(((f32[1,512,2048]{2,1,0:T(8,128)}), f32[2,512,2048]{2,1,0:T(8,128)}) %all-gather.8.cloned.1.call-update) | async-done | bytes 8388624 | tf_op jit(solution)/shard_map/all_gather | solution.py:31
  186.3 6.6 %reduce_sum.39 = f32[512,2048]{1,0:T(8,128)} reduce(f32[2,512,2048]{2,1,0:T(8,128)} %all-gather.8.cloned.1.call-done, f32[]{:T(128)} %constant.2.clone.1), dimensions={0}, to_apply=%region_3.0 | reduce | flops 1048576 | bytes 12582916 | tf_op jit(solution)/shard_map/reduce_sum | solution.py:31
  192.9 0.0 copy-start
  192.9 0.0 copy-start.1
  192.9 17.8 %fusion.4 = f32[1024,2048]{1,0:T(8,128)S(1)} fusion(f32[512,1024]{1,0:T(8,128)} %reduce_sum.38, f32[1,512,2048]{2,1,0:T(8,128)} %param.16, f32[512,2048]{1,0:T(8,128)} %reduce_sum.39, f32[]{:T(128)S(6)} %convert_element_type.3), kind=kOutput, calls=%fused_computation.6 | convolution fusion | flops 12886999040 | bytes 18874372 | tf_op jit(solution)/shard_map/dot_general | solution.py:54
  210.7 0.0 copy-done
  210.7 0.0 copy-done.1
  210.7 15.5 %bitcast_add_fusion = f32[1024,2048]{1,0:T(8,128)S(1)} fusion(f32[1024,2048]{1,0:T(8,128)S(1)} %fusion.4, f32[512,2048]{1,0:T(8,128)S(1)} %copy-done, f32[1,512,1024]{2,1,0:T(8,128)S(1)} %copy-done.1), kind=kOutput, calls=%fused_computation.4 | convolution fusion | flops 12886999040 | bytes 23068672 | tf_op jit(solution)/shard_map/dot_general | solution.py:54
  226.3 3.8 copy.16
  230.1 0.0 copy-start.4
  230.1 0.0 copy-start.5
  230.1 0.0 reduce-scatter.3.cloned.1.call-update
  230.1 0.0 all-gather.4.cloned.1.call-start
  230.2 0.8 copy-done.4
  231.0 0.1 copy-done.5
  231.1 9.3 %all_to_all.10 = f32[2,16,2048]{2,1,0:T(8,128)S(1)} all-to-all(f32[2,16,2048]{2,1,0:T(8,128)S(1)} %broadcast_in_dim.23), channel_id=1, replica_groups=mesh['party'=2,'dp_0'=4,'dp_1'=2,'dp_2'=4,'dp_3'=2] {'party'}, dimensions={0} | all-to-all | bytes 524288 | tf_op jit(solution)/shard_map/all_to_all | solution.py:12
  240.5 0.7 pad_maximum_fusion
  241.2 0.0 all-gather.4.cloned.1.call-update
  241.2 0.0 reduce-scatter.5.cloned.1.call-start
  241.3 8.0 %reduce-scatter.3.cloned.1.call-done = f32[32,16,2048]{2,1,0:T(8,128)} async-done(((f32[64,16,2048]{2,1,0:T(8,128)}), f32[32,16,2048]{2,1,0:T(8,128)}) %reduce-scatter.3.cloned.1.call-update) | async-done | bytes 4194320 | tf_op jit(solution)/shard_map/reduce_scatter | solution.py:45
  249.3 0.0 reduce-scatter.5.cloned.1.call-update
  249.3 0.5 broadcast_in_dim.21
  249.8 98.8 %all_to_all.11 = f32[2,512,1024]{2,1,0:T(8,128)} all-to-all(f32[2,512,1024]{2,1,0:T(8,128)S(1)} %broadcast_in_dim.21), channel_id=1, replica_groups=mesh['party'=2,'dp_0'=4,'dp_1'=2,'dp_2'=4,'dp_3'=2] {'party'}, dimensions={0} | all-to-all | bytes 8388608 | tf_op jit(solution)/shard_map/all_to_all | solution.py:12
  348.6 2.8 reduce_sum.36
  351.5 69.9 %all-gather.4.cloned.1.call-done = f32[1024,4096]{1,0:T(8,128)} async-done(((f32[16,4096]{1,0:T(8,128)}), f32[1024,4096]{1,0:T(8,128)}) %all-gather.4.cloned.1.call-update) | async-done | bytes 16777232 | tf_op jit(solution)/shard_map/all_gather | solution.py:27
  421.4 0.0 copy-start.2
  421.4 0.0 copy-start.3
  421.4 16.2 %fusion.2 = f32[512,2048]{1,0:T(8,128)S(1)} fusion(f32[512,1024]{1,0:T(8,128)S(1)} %reduce_sum.36, f32[1024,4096]{1,0:T(8,128)} %all-gather.4.cloned.1.call-done), kind=kOutput, calls=%fused_computation.2 | convolution fusion | flops 12884901888 | bytes 14680064 | tf_op jit(solution)/shard_map/dot_general | solution.py:50
  437.6 0.0 copy-done.2
  437.6 0.0 copy-done.3
  437.6 0.0 copy-start.6
  437.6 18.0 %fusion.5 = f32[1,512,2048]{2,1,0:T(8,128)} fusion(f32[512,2048]{1,0:T(8,128)S(1)} %fusion.2, f32[1,512,2048]{2,1,0:T(8,128)S(1)} %copy-done.3, f32[1024,4096]{1,0:T(8,128)} %all-gather.4.cloned.1.call-done, f32[1,512,1024]{2,1,0:T(8,128)S(1)} %copy-done.2), kind=kOutput, calls=%fused_computation.8 | convolution fusion | flops 12886999040 | bytes 23068672 | tf_op jit(solution)/shard_map/dot_general | solution.py:50
  455.6 10.6 %reduce-scatter.5.cloned.1.call-done = f32[1,16,2048]{2,1,0:T(8,128)} async-done(((f32[32,16,2048]{2,1,0:T(8,128)}), f32[1,16,2048]{2,1,0:T(8,128)}) %reduce-scatter.5.cloned.1.call-update) | async-done | bytes 131088 | tf_op jit(solution)/shard_map/reduce_scatter | solution.py:46
  466.2 0.0 copy-done.6
  466.2 1.6 add.28
  (4 shorter events, 0.1 us)
Async XLA Ops:
  8.0 68.5 %all-gather.6.cloned.1.call-start = ((), (), s32[]{:S(2)}) async-start(), calls=%async_computation.5 | async-start | bytes 6291456 | tf_op jit(solution)/shard_map/all_gather | solution.py:31
  13.1 173.1 %all-gather.8.cloned.1.call-start = ((), (), s32[]{:S(2)}) async-start(), calls=%async_computation.6 | async-start | bytes 12582912 | tf_op jit(solution)/shard_map/all_gather | solution.py:31
  19.8 229.5 %reduce-scatter.3.cloned.1.call-start = ((), (), s32[]{:S(2)}) async-start(), calls=%async_computation.7 | async-start | bytes 12582912 | tf_op jit(solution)/shard_map/reduce_scatter | solution.py:45
  192.9 17.8 %copy-start = (f32[512,2048]{1,0:T(8,128)S(1)}, f32[512,2048]{1,0:T(8,128)}, u32[]{:S(2)}) copy-start(f32[512,2048]{1,0:T(8,128)} %reduce_sum.39) | copy-start | bytes 12582916
  192.9 17.8 %copy-start.1 = (f32[1,512,1024]{2,1,0:T(8,128)S(1)}, f32[1,512,1024]{2,1,0:T(8,128)}, u32[]{:S(2)}) copy-start(f32[1,512,1024]{2,1,0:T(8,128)} %param.15) | copy-start | bytes 6291460
  230.1 0.9 copy-start.4
  230.1 1.0 copy-start.5
  230.1 191.2 %all-gather.4.cloned.1.call-start = ((), (), s32[]{:S(2)}) async-start(), calls=%async_computation.4 | async-start | bytes 17039360 | tf_op jit(solution)/shard_map/all_gather | solution.py:27
  241.2 225.0 %reduce-scatter.5.cloned.1.call-start = ((), (), s32[]{:S(2)}) async-start(), calls=%async_computation.8 | async-start | bytes 4325376 | tf_op jit(solution)/shard_map/reduce_scatter | solution.py:46
  421.4 16.2 %copy-start.2 = (f32[1,512,1024]{2,1,0:T(8,128)S(1)}, f32[1,512,1024]{2,1,0:T(8,128)}, u32[]{:S(2)}) copy-start(f32[1,512,1024]{2,1,0:T(8,128)} %param.12) | copy-start | bytes 6291460
  421.4 16.2 %copy-start.3 = (f32[1,512,2048]{2,1,0:T(8,128)S(1)}, f32[1,512,2048]{2,1,0:T(8,128)}, u32[]{:S(2)}) copy-start(f32[1,512,2048]{2,1,0:T(8,128)} %param.14) | copy-start | bytes 12582916
  437.6 28.6 %copy-start.6 = (f32[1,16,2048]{2,1,0:T(8,128)S(1)}, f32[1,16,2048]{2,1,0:T(8,128)}, u32[]{:S(2)}) copy-start(f32[1,16,2048]{2,1,0:T(8,128)} %param.17) | copy-start | bytes 393220
Sparse Core Ops, SparseCore 0:
  13.3 63.2 all-gather.5
  78.8 107.4 all-gather.7
  230.2 19.0 reduce-scatter.2
  251.6 214.4 reduce-scatter.4
Sparse Core Ops, SparseCore 1:
  241.3 180.0 all-gather.3
where the time goes:
time: 483 us; the launch traced here: 475 us
  waiting for transfers between devices  251 us (52%)
  blocking collectives  108 us (22%)
  matrix products  67.5 us (14%)
  other arithmetic  27.6 us (6%)
  between operations  15.8 us (3%)
  local copies, waits for them, and re-layouts  5.25 us (1%)
    all_gather x2, waiting for transfers between devices, gathered_total(): return lax.all_gather(shard, axis).sum(0)  162 us
    all_to_all x2, blocking collectives, from_everyone(): lax.all_to_all(jnp.broadcast_to(shard[None], (length, *shard.shape)), axi...  108 us
    all_gather x1, waiting for transfers between devices, in_one_piece(): lax.all_gather(both, axis, axis=dim, tiled=True)  69.9 us
    dot_general x2, matrix products, matmul(): jnp.dot(left, right, preferred_element_type=jnp.float32, precision=lax.Pr...  34.2 us
    dot_general x2, matrix products, tmatmul(): lax.dot_general(left, right, (((0,), (0,)), ((), ())), precision=lax.Prec...  33.3 us
    reduce_sum x2, other arithmetic, gathered_total(): return lax.all_gather(shard, axis).sum(0)  10.7 us
    reduce_scatter x1, waiting for transfers between devices, summed_rows(): return lax.psum_scatter(pieces, chips, scatter_dimension=0, tiled=True)[0]  10.6 us
  transfers between devices with their start and end apart: 5, of which 5 were waited for; matrix products, arithmetic and copies ran while one was open for 10% of the time, Pallas kernels for 0%

commit v1 on v0

v1 whole, which is shorter than its diff:
```python
import jax
import jax.numpy as jnp
from jax import lax
from jax.sharding import Mesh
from jax.sharding import PartitionSpec as P

DP = ("y", "xl", "z", "core")
SWAP = [(0, 1), (1, 0)]


def dot(left, right):
    return jnp.dot(left, right, preferred_element_type=jnp.float32, precision=lax.Precision.HIGH)


def after(value, *earlier):
    return lax.optimization_barrier((value, *earlier))[0]


def rows_of(share, core):
    t = share.T.reshape(4, 2, 4, 2, 16, share.shape[0])
    t = lax.dynamic_index_in_dim(t, core, 3, keepdims=False)
    return t.swapaxes(1, 2).reshape(-1, share.shape[0])


def body(x_share, w_share, g_share, fwd_a, fwd_b, fwd_c, bwd_a, bwd_b, bwd_c):
    x, w, g = x_share[0], w_share[0], g_share[0]
    fa, fb, fc = fwd_a[0], fwd_b[0], fwd_c[0]
    ba, bb, bc = bwd_a[0], bwd_b[0], bwd_c[0]
    party0 = lax.axis_index("party") == 0
    first = party0.astype(jnp.float32)
    core = lax.axis_index("core")
    rows = w.shape[0]
    ff = w.shape[1]

    d_rows = w - fb
    delta_rows = d_rows + lax.ppermute(d_rows, "party", SWAP)
    packed = jnp.concatenate([fb + first * delta_rows, delta_rows], axis=1)
    packed_x = lax.ppermute(packed, "xl", SWAP)
    xl0 = lax.axis_index("xl") == 0
    weights = jnp.concatenate(
        [jnp.where(xl0, packed, packed_x), jnp.where(xl0, packed_x, packed)], axis=1
    )
    weights = lax.all_gather(weights, ("y", "z", "core"), axis=0, tiled=True)

    x_mine, x_theirs = rows_of(x, core), rows_of(x, 1 - core)
    a_mine, a_theirs = rows_of(ba, core), rows_of(ba, 1 - core)
    x_other = lax.ppermute(x_theirs, "core", SWAP)
    a_other = lax.ppermute(a_theirs, "core", SWAP)
    r_mine = g - (1.0 - first) * bb
    r_other = lax.ppermute(r_mine, "core", SWAP)
    b_other = lax.ppermute(bb, "core", SWAP)

    xm = lax.ppermute(x_mine, "party", SWAP)
    xo = lax.ppermute(x_other, "party", SWAP)
    am = lax.ppermute(after(a_mine, xm), "party", [(1, 0)])
    ao = lax.ppermute(after(a_other, xo), "party", [(1, 0)])
    half = x.shape[0] // 2
    u = x - fa
    u0 = lax.ppermute(after(u[:half], am), "party", SWAP)
    u1 = lax.ppermute(after(u[half:], ao), "party", SWAP)

    opened = jnp.concatenate([x_mine + xm, x_other + xo], axis=1)
    a_local = jnp.concatenate([a_mine, a_other], axis=1)
    a_second = jnp.where(party0, jnp.concatenate([am, ao], axis=1), a_local)
    left_b = jnp.where(party0, a_local, opened)
    right = jnp.concatenate([r_mine, r_other], axis=0)
    right_b = jnp.concatenate([bb, b_other], axis=0)
    t3 = dot(left_b, right_b)
    part0 = dot(opened - a_second, right) - first * t3
    part1 = dot(a_second, right) + t3
    both = jnp.concatenate(
        [part0.reshape(16, 2 * rows, ff), part1.reshape(16, 2 * rows, ff)], axis=1
    )
    both = after(both, weights)
    both = lax.psum_scatter(both, ("y", "z"), scatter_dimension=0, tiled=True)
    both = both.reshape(2, 2, rows, ff)
    keep = jnp.where(xl0, both[:, 0], both[:, 1])
    give = jnp.where(xl0, both[:, 1], both[:, 0])
    both = keep + lax.ppermute(give, "xl", SWAP)
    give = jnp.where(party0, both[1] - bc, both[0])
    keep = jnp.where(party0, both[0] + bc, both[1])
    grad = keep + lax.ppermute(give, "party", SWAP)

    def columns(share, xl):
        return share.reshape(-1, 4, 2, 128)[:, :, xl].reshape(-1, 512)

    def outputs_of(eps, a, c):
        out = c
        for xl in range(2):
            at = xl * 2 * ff
            out = out + dot(columns(eps, xl), weights[:, at : at + ff])
            out = out + dot(columns(a, xl), weights[:, at + ff : at + 2 * ff])
        return out

    eps0, eps1 = u[:half] + u0, u[half:] + u1
    outputs = outputs_of(jnp.concatenate([eps0, eps1]), fa, fc)
    return (outputs[None], grad[None])


def solution(mesh):
    split = Mesh(
        mesh.devices.reshape(mesh.shape["party"], 4, 2, 4, 2),
        ("party", *DP),
    )
    spec = P("party", DP, None)
    return jax.shard_map(
        body, mesh=split, in_specs=(spec,) * 9, out_specs=(spec, spec), check_vma=False
    )
```

time: 483 us -> 271 us (0.56); the launches traced: 475 us -> 271 us
  waiting for transfers between devices: 251 us -> 129 us
  blocking collectives: 108 us -> 0 us
  local copies, waits for them, and re-layouts: 5.25 us -> 28.1 us
  starting transfers between devices: 0.21 us -> 22.1 us
  matrix products: 67.5 us -> 57.6 us
  other arithmetic: 27.6 us -> 19.9 us
    all_gather x3 -> x1, waiting for transfers between devices: 232 us -> 0.01 us  [body(): weights = lax.all_gather(weights, ('y', 'z', 'core'), axis=0, tiled=True)]
    ppermute x0 -> x14, waiting for transfers between devices: none -> 117 us  [the longest x1 22.1 us: body(): ao = lax.ppermute(after(a_other, xo), 'party', [(1, 0)])]
    all_to_all x2 -> x0, blocking collectives: 108 us -> none  [from_everyone(): lax.all_to_all(jnp.broadcast_to(shard[None], (length, *shard.shape)), axi...]
    ppermute x0 -> x14, starting transfers between devices: none -> 22 us  [the longest x1 3.53 us: body(): u1 = lax.ppermute(after(u[half:], ao), 'party', SWAP)]
    reduce_scatter x2 -> x0, waiting for transfers between devices: 18.6 us -> none  [the longest x1 10.6 us: summed_rows(): return lax.psum_scatter(pieces, chips, scatter_dimension=0, tiled=True)[0]]
    reduce_sum x4 -> x0, other arithmetic: 13.6 us -> none  [the longest x2 10.7 us: gathered_total(): return lax.all_gather(shard, axis).sum(0)]
    unnamed x5 -> x3, waiting for transfers between devices: 0.08 us -> 11.9 us
    slice x0 -> x3, local copies, waits for them, and re-layouts: none -> 11.2 us  [the longest x2 9.72 us: columns(): return share.reshape(-1, 4, 2, 128)[:, :, xl].reshape(-1, 512)]
  transfers between devices with their start and end apart: 5 -> 16, of which waited for: 5 -> 9; matrix products, arithmetic and copies ran while one was open for 10% -> 36% of each run, Pallas kernels for 0% -> 0%
where the time goes in v1:
time: 271 us
  waiting for transfers between devices  129 us (48%)
  matrix products  57.6 us (21%)
  local copies, waits for them, and re-layouts  28.1 us (10%)
  starting transfers between devices  22.1 us (8%)
  other arithmetic  19.9 us (7%)
  between operations  14.3 us (5%)
    dot_general x7, matrix products, dot(): jnp.dot(left, right, preferred_element_type=jnp.float32, precision=lax.Pr...  57.6 us
    ppermute x1, waiting for transfers between devices, body(): ao = lax.ppermute(after(a_other, xo), 'party', [(1, 0)])  22.1 us
    ppermute x1, waiting for transfers between devices, body(): xm = lax.ppermute(x_mine, 'party', SWAP)  21.7 us
    ppermute x1, waiting for transfers between devices, body(): xo = lax.ppermute(x_other, 'party', SWAP)  21.2 us
    ppermute x1, waiting for transfers between devices, body(): u1 = lax.ppermute(after(u[half:], ao), 'party', SWAP)  21.2 us
    unnamed x3, waiting for transfers between devices  11.9 us
    ppermute x1, waiting for transfers between devices, body(): am = lax.ppermute(after(a_mine, xm), 'party', [(1, 0)])  11.1 us
    ppermute x1, waiting for transfers between devices, body(): u0 = lax.ppermute(after(u[:half], am), 'party', SWAP)  10.8 us
  transfers between devices with their start and end apart: 16, of which 9 were waited for; matrix products, arithmetic and copies ran while one was open for 36% of the time, Pallas kernels for 0%

profile of v1, /device:TPU:0, one launch (start us, length us, event | category | flops | bytes accessed | tf_op | source)
XLA Modules:
  0.0 270.8 jit_solution(3667038531877877871)
XLA Ops:
  7.2 1.0 bitcast_subtract_fusion.3
  8.2 3.2 %collective-permute-start.8 = (f32[16,2048]{1,0:T(8,128)S(1)}, f32[16,2048]{1,0:T(8,128)S(1)}, u32[]{:S(2)}, u32[]{:S(2)}) collective-permute-start(f32[16,2048]{1,0:T(8,128)S(1)} %bitcast_subtract_fusion.3), channel_id=1, source_target_pairs={{0,64},{64,0},{1,65},{65,1},{2,66},{66,2},{3,67},{67,3},{4,68},{68... | collective-permute-start | bytes 393224 | tf_op jit(solution)/shard_map/ppermute | solution.py:36
  11.4 3.5 %collective-permute-done.8 = f32[16,2048]{1,0:T(8,128)S(1)} collective-permute-done((f32[16,2048]{1,0:T(8,128)S(1)}, f32[16,2048]{1,0:T(8,128)S(1)}, u32[]{:S(2)}, u32[]{:S(2)}) %collective-permute-start.8) | collective-permute-done | bytes 131104 | tf_op jit(solution)/shard_map/ppermute | solution.py:36
  14.9 0.9 bitcast_add_fusion.4
  15.8 1.8 collective-permute-start.9
  17.6 5.4 %collective-permute-done.9 = f32[16,4096]{1,0:T(8,128)S(1)} collective-permute-done((f32[16,4096]{1,0:T(8,128)S(1)}, f32[16,4096]{1,0:T(8,128)S(1)}, u32[]{:S(2)}, u32[]{:S(2)}) %collective-permute-start.9) | collective-permute-done | bytes 262176 | tf_op jit(solution)/shard_map/ppermute | solution.py:38
  23.1 0.9 pad_maximum_fusion.14
  24.1 6.7 %bitcast_subtract_fusion = f32[512,2048]{1,0:T(8,128)} fusion(f32[1,512,2048]{2,1,0:T(8,128)} %param.11, f32[]{:T(128)S(6)} %sub.29, f32[1,512,2048]{2,1,0:T(8,128)} %param.16), kind=kLoop, calls=%fused_computation.16 | loop fusion | flops 2097152 | bytes 12582916 | tf_op jit(solution)/shard_map/sub | solution.py:49
  30.8 0.5 collective-permute-start.10
  31.3 1.9 copy.35
  33.3 2.9 %copy.37 = f32[1,512,1024]{1,2,0:T(8,128)} copy(f32[1,512,1024]{2,1,0:T(8,128)} %param.15) | data formatting | bytes 4194304 | tf_op args[6]
  36.2 2.3 dynamic-slice_bitcast_fusion.2
  38.9 3.3 %collective-permute-start = (f32[512,512]{1,0:T(8,128)S(1)}, f32[512,512]{1,0:T(8,128)S(1)}, u32[]{:S(2)}, u32[]{:S(2)}) collective-permute-start(f32[512,512]{1,0:T(8,128)S(1)} %bitcast.127), channel_id=1, source_target_pairs={{0,64},{64,0},{1,65},{65,1},{2,66},{66,2},{3,67},{67,3},{4,68},{68... | collective-permute-start | bytes 3145736 | tf_op jit(solution)/shard_map/ppermute | solution.py:53
  42.3 0.3 collective-permute-start.3
  42.6 2.1 collective-permute-start.5
  44.7 21.7 %collective-permute-done = f32[512,512]{1,0:T(8,128)S(1)} collective-permute-done((f32[512,512]{1,0:T(8,128)S(1)}, f32[512,512]{1,0:T(8,128)S(1)}, u32[]{:S(2)}, u32[]{:S(2)}) %collective-permute-start) | collective-permute-done | bytes 1048608 | tf_op jit(solution)/shard_map/ppermute | solution.py:53
  66.4 1.3 collective-permute-start.1
  67.7 21.2 %collective-permute-done.5 = f32[512,512]{1,0:T(8,128)S(1)} collective-permute-done((f32[512,512]{1,0:T(8,128)S(1)}, f32[512,512]{1,0:T(8,128)S(1)}, u32[]{:S(2)}, u32[]{:S(2)}) %collective-permute-start.5) | collective-permute-done | bytes 1048608 | tf_op jit(solution)/shard_map/ppermute | solution.py:54
  88.9 1.5 collective-permute-start.6
  90.4 0.2 bitcast_add_fusion.5
  90.6 0.2 add.65
  90.8 9.4 %fusion = f32[512,2048]{1,0:T(8,128)S(1)} fusion(f32[512,2048]{1,0:T(8,128)} %collective-permute-done.11, f32[512,2048]{1,0:T(8,128)S(1)} %bitcast.129, f32[512,512]{1,0:T(8,128)S(1)} %collective-permute-done.3, f32[512,512]{1,0:T(8,128)S(1)} %bitcast.124, f32[512,512]{1,0:T(8,128)S(1)} %add.65, f32[512,512]{1,0:T(8,128)S(1)} %bitcast_add_fusion.5, pred[]{:T(512)S(6)} %eq.7), kind=kOutput, calls=%fused_computation.1 | convolution fusion | flops 6446120960 | bytes 16777216 | tf_op jit(solution)/shard_map/dot_general | solution.py:12
  100.3 11.1 %collective-permute-done.1 = f32[512,512]{1,0:T(8,128)S(1)} collective-permute-done((f32[512,512]{1,0:T(8,128)S(1)}, f32[512,512]{1,0:T(8,128)S(1)}, u32[]{:S(2)}, u32[]{:S(2)}) %collective-permute-start.1) | collective-permute-done | bytes 1048608 | tf_op jit(solution)/shard_map/ppermute | solution.py:55
  111.4 22.1 %collective-permute-done.6 = f32[512,512]{1,0:T(8,128)S(1)} collective-permute-done((f32[512,512]{1,0:T(8,128)S(1)}, f32[512,512]{1,0:T(8,128)S(1)}, u32[]{:S(2)}, u32[]{:S(2)}) %collective-permute-start.6) | collective-permute-done | bytes 1048608 | tf_op jit(solution)/shard_map/ppermute | solution.py:56
  133.4 1.0 copy-done.8
  134.4 9.5 %fusion.18 = f32[512,2048]{1,0:T(8,128)S(1)} fusion(f32[512,2048]{1,0:T(8,128)S(1)} %fusion, f32[512,2048]{1,0:T(8,128)} %collective-permute-done.10, f32[512,2048]{1,0:T(8,128)} %bitcast_subtract_fusion, f32[512,512]{1,0:T(8,128)S(1)} %collective-permute-done.6, f32[512,512]{1,0:T(8,128)S(1)} %collective-permute-done.1, ...), kind=kOutput, calls=%fused_computation.23 | convolution fusion | flops 6447169536 | bytes 20971520 | tf_op jit(solution)/shard_map/dot_general | solution.py:12
  143.9 10.5 %multiply_subtract_fusion = f32[512,2048]{1,0:T(8,128)S(1)} fusion(f32[512,2048]{1,0:T(8,128)S(1)} %fusion, f32[512,2048]{1,0:T(8,128)} %collective-permute-done.10, f32[512,2048]{1,0:T(8,128)} %bitcast_subtract_fusion, f32[]{:T(128)S(6)} %convert_element_type.3, f32[512,512]{1,0:T(8,128)} %copy-done.10, f32[512,512]{1,0:T(8,128)} %copy-done.9, ...), kind=kOutput, calls=%fused_computation.22 | convolution fusion | flops 6449266688 | bytes 23068676 | tf_op jit(solution)/shard_map/dot_general | solution.py:12
  154.4 3.9 %pad_maximum_fusion.1 = f32[16,64,2048]{2,1,0:T(8,128)} fusion(f32[16,32,2048]{2,1,0:T(8,128)S(1)} %bitcast.119, f32[16,32,2048]{2,1,0:T(8,128)S(1)} %bitcast.134), kind=kLoop, calls=%fused_computation.5 | loop fusion | flops 2097152 | bytes 16777216 | tf_op jit(solution)/shard_map/concatenate | solution.py:71
  158.3 2.9 %copy.36 = f32[1,512,1024]{1,2,0:T(8,128)} copy(f32[1,512,1024]{2,1,0:T(8,128)} %param.12) | data formatting | bytes 4194304 | tf_op args[3]
  161.2 2.1 bitcast_subtract_fusion.1
  163.2 1.3 copy-done
  164.5 1.5 fusion.36
  166.1 3.5 %collective-permute-start.7 = (f32[256,1024]{0,1:T(8,128)}, f32[256,1024]{0,1:T(8,128)}, u32[]{:S(2)}, u32[]{:S(2)}) collective-permute-start(f32[256,1024]{0,1:T(8,128)} %get-tuple-element.10), channel_id=1, source_target_pairs={{0,64},{64,0},{1,65},{65,1},{2,66},{66,2},{3,67},{67,3},{4,68},{68... | collective-permute-start | bytes 3145736 | tf_op jit(solution)/shard_map/ppermute | solution.py:60
  169.6 4.0 %reshape_squeeze.17 = f32[512,4,2,128]{3,2,1,0:T(2,128)} reshape(f32[1,512,1024]{2,1,0:T(8,128)} %param.12) | data formatting | bytes 4194304 | tf_op jit(solution)/shard_map/reshape;squeeze | solution.py:85
  173.6 9.5 %slice_reduce_fusion = (f32[512,4,128]{2,1,0:T(4,128)S(1)}, f32[512,4,128]{2,1,0:T(4,128)}) fusion(f32[512,4,2,128]{3,2,1,0:T(2,128)} %reshape_squeeze.17), kind=kLoop, calls=%fused_computation.35 | loop fusion | bytes 4194304 | tf_op jit(solution)/shard_map/slice | solution.py:85
  183.2 10.8 %collective-permute-done.2 = f32[256,1024]{0,1:T(8,128)} collective-permute-done((f32[256,1024]{0,1:T(8,128)}, f32[256,1024]{0,1:T(8,128)}, u32[]{:S(2)}, u32[]{:S(2)}) %collective-permute-start.2) | collective-permute-done | bytes 1048608 | tf_op jit(solution)/shard_map/ppermute | solution.py:59
  194.0 21.2 %collective-permute-done.7 = f32[256,1024]{0,1:T(8,128)} collective-permute-done((f32[256,1024]{0,1:T(8,128)}, f32[256,1024]{0,1:T(8,128)}, u32[]{:S(2)}, u32[]{:S(2)}) %collective-permute-start.7) | collective-permute-done | bytes 1048608 | tf_op jit(solution)/shard_map/ppermute | solution.py:60
  215.1 1.9 slice_add_fusion.1
  217.0 0.3 pad_maximum_fusion.8
  217.5 7.6 %fusion.12 = f32[512,2048]{1,0:T(8,128)} fusion(f32[512,512]{0,1:T(8,128)S(1)} %bitcast.133, f32[512,8192]{1,0:T(8,128)} %all-gather.2.cloned.1.call-done), kind=kOutput, calls=%fused_computation.14 | convolution fusion | flops 3221225472 | bytes 9437184 | tf_op jit(solution)/shard_map/dot_general | solution.py:12
  225.0 7.6 %fusion.8 = f32[512,2048]{1,0:T(8,128)} fusion(f32[512,512]{0,1:T(8,128)S(1)} %bitcast.132, f32[512,8192]{1,0:T(8,128)} %all-gather.2.cloned.1.call-done), kind=kOutput, calls=%fused_computation.10 | convolution fusion | flops 3221225472 | bytes 9437184 | tf_op jit(solution)/shard_map/dot_general | solution.py:12
  232.6 11.9 %reduce-scatter.4.cloned.1.call-done = f32[1,64,2048]{2,1,0:T(8,128)} async-done(((f32[16,64,2048]{2,1,0:T(8,128)}), f32[1,64,2048]{2,1,0:T(8,128)}) %reduce-scatter.4.cloned.1.call-update) | async-done | bytes 524304
  244.5 1.1 select_bitcast_fusion
  245.6 1.6 collective-permute-start.12
  247.2 5.4 %fusion.10 = f32[2048,512]{0,1:T(8,128)S(1)} fusion(f32[512,8192]{1,0:T(8,128)} %all-gather.2.cloned.1.call-done, f32[64,8,4,128]{3,2,1,0:T(4,128)S(1)} %bitcast.131), kind=kOutput, calls=%fused_computation.12 | convolution fusion | flops 3221225472 | bytes 9437184 | tf_op jit(solution)/shard_map/dot_general | solution.py:12
  252.7 2.8 %collective-permute-start.13 = (f32[16,2048]{1,0:T(8,128)S(1)}, f32[16,2048]{1,0:T(8,128)S(1)}, u32[]{:S(2)}, u32[]{:S(2)}) collective-permute-start(f32[16,2048]{1,0:T(8,128)S(1)} %fusion.31), channel_id=1, source_target_pairs={{0,64},{64,0},{1,65},{65,1},{2,66},{66,2},{3,67},{67,3},{4,68},{68... | collective-permute-start | bytes 393224 | tf_op jit(solution)/shard_map/ppermute | solution.py:82
  255.6 7.7 %fusion.14 = f32[1,512,2048]{2,1,0:T(8,128)} fusion(f32[512,2048]{1,0:T(8,128)S(1)} %copy-done.3, f32[2048,512]{0,1:T(8,128)S(1)} %fusion.10, f32[512,2048]{1,0:T(8,128)S(1)} %copy-done.2, f32[1,512,2048]{2,1,0:T(8,128)S(1)} %copy-done.4, f32[512,8192]{1,0:T(8,128)} %all-gather.2.cloned.1.call-done, f32[64,8,4,128]{3,2,1,0:T(4,128)S(1)} %bitcast.130), kind=kOutput, calls=%fused_computation.18 | convolution fusion | flops 3225419776 | bytes 26214400 | tf_op jit(solution)/shard_map/dot_general | solution.py:12
  263.3 0.7 fusion.30
  (45 shorter events, 1.0 us)
Async XLA Ops:
  7.2 151.1 %all-gather.2.cloned.1.call-start = ((), (), s32[]{:S(2)}) async-start(), calls=%async_computation.1 | async-start | bytes 17301504 | tf_op jit(solution)/shard_map/all_gather | solution.py:43
  8.2 6.7 %collective-permute-start.8 = (f32[16,2048]{1,0:T(8,128)S(1)}, f32[16,2048]{1,0:T(8,128)S(1)}, u32[]{:S(2)}, u32[]{:S(2)}) collective-permute-start(f32[16,2048]{1,0:T(8,128)S(1)} %bitcast_subtract_fusion.3), channel_id=1, source_target_pairs={{0,64},{64,0},{1,65},{65,1},{2,66},{66,2},{3,67},{67,3},{4,68},{68... | collective-permute-start | bytes 393224 | tf_op jit(solution)/shard_map/ppermute | solution.py:36
  15.8 7.2 %collective-permute-start.9 = (f32[16,4096]{1,0:T(8,128)S(1)}, f32[16,4096]{1,0:T(8,128)S(1)}, u32[]{:S(2)}, u32[]{:S(2)}) collective-permute-start(f32[16,4096]{1,0:T(8,128)S(1)} %pad_maximum_fusion.15), channel_id=1, source_target_pairs={{0,8},{8,0},{1,9},{9,1},{2,10},{10,2},{3,11},{11,3},{4,12},{12,4},... | collective-permute-start | bytes 786440 | tf_op jit(solution)/shard_map/ppermute | solution.py:38
  24.0 220.5 %reduce-scatter.4.cloned.1.call-start = ((), (), s32[]{:S(2)}) async-start(), calls=%async_computation.2 | async-start | bytes 8912896
  24.0 66.8 %collective-permute-start.11 = (f32[512,2048]{1,0:T(8,128)}, f32[512,2048]{1,0:T(8,128)}, u32[]{:S(2)}, u32[]{:S(2)}) collective-permute-start(f32[512,2048]{1,0:T(8,128)} %bitcast.128), channel_id=1, source_target_pairs={{0,1},{1,0},{2,3},{3,2},{4,5},{5,4},{6,7},{7,6},{8,9},{9,8},{10,11... | collective-permute-start | bytes 12582920 | tf_op jit(solution)/shard_map/ppermute | solution.py:51
  30.8 102.6 %collective-permute-start.10 = (f32[512,2048]{1,0:T(8,128)}, f32[512,2048]{1,0:T(8,128)}, u32[]{:S(2)}, u32[]{:S(2)}) collective-permute-start(f32[512,2048]{1,0:T(8,128)} %bitcast_subtract_fusion), channel_id=1, source_target_pairs={{0,1},{1,0},{2,3},{3,2},{4,5},{5,4},{6,7},{7,6},{8,9},{9,8},{10,11... | collective-permute-start | bytes 12582920 | tf_op jit(solution)/shard_map/ppermute | solution.py:50
  38.7 3.9 %collective-permute-start.4 = (f32[512,512]{1,0:T(8,128)S(1)}, f32[512,512]{1,0:T(8,128)S(1)}, u32[]{:S(2)}, u32[]{:S(2)}) collective-permute-start(f32[512,512]{1,0:T(8,128)S(1)} %bitcast.138), channel_id=1, source_target_pairs={{0,1},{1,0},{2,3},{3,2},{4,5},{5,4},{6,7},{7,6},{8,9},{9,8},{10,11... | collective-permute-start | bytes 3145736 | tf_op jit(solution)/shard_map/ppermute | solution.py:47
  38.9 27.5 %collective-permute-start = (f32[512,512]{1,0:T(8,128)S(1)}, f32[512,512]{1,0:T(8,128)S(1)}, u32[]{:S(2)}, u32[]{:S(2)}) collective-permute-start(f32[512,512]{1,0:T(8,128)S(1)} %bitcast.127), channel_id=1, source_target_pairs={{0,64},{64,0},{1,65},{65,1},{2,66},{66,2},{3,67},{67,3},{4,68},{68... | collective-permute-start | bytes 3145736 | tf_op jit(solution)/shard_map/ppermute | solution.py:53
  42.3 25.4 %collective-permute-start.3 = (f32[512,512]{1,0:T(8,128)S(1)}, f32[512,512]{1,0:T(8,128)S(1)}, u32[]{:S(2)}, u32[]{:S(2)}) collective-permute-start(f32[512,512]{1,0:T(8,128)S(1)} %bitcast.137), channel_id=1, source_target_pairs={{0,1},{1,0},{2,3},{3,2},{4,5},{5,4},{6,7},{7,6},{8,9},{9,8},{10,11... | collective-permute-start | bytes 3145736 | tf_op jit(solution)/shard_map/ppermute | solution.py:48
  42.6 46.3 %collective-permute-start.5 = (f32[512,512]{1,0:T(8,128)S(1)}, f32[512,512]{1,0:T(8,128)S(1)}, u32[]{:S(2)}, u32[]{:S(2)}) collective-permute-start(f32[512,512]{1,0:T(8,128)S(1)} %collective-permute-done.4), channel_id=1, source_target_pairs={{0,64},{64,0},{1,65},{65,1},{2,66},{66,2},{3,67},{67,3},{4,68},{68... | collective-permute-start | bytes 3145736 | tf_op jit(solution)/shard_map/ppermute | solution.py:54
  44.6 46.2 %copy-start.5 = (f32[1,512,2048]{2,1,0:T(8,128)S(1)}, f32[1,512,2048]{2,1,0:T(8,128)}, u32[]{:S(2)}) copy-start(f32[1,512,2048]{2,1,0:T(8,128)} %param.16) | copy-start | bytes 12582916
  66.4 44.9 %collective-permute-start.1 = (f32[512,512]{1,0:T(8,128)S(1)}, f32[512,512]{1,0:T(8,128)S(1)}, u32[]{:S(2)}, u32[]{:S(2)}) collective-permute-start(f32[512,512]{1,0:T(8,128)S(1)} %bitcast.123), channel_id=1, source_target_pairs={{64,0},{65,1},{66,2},{67,3},{68,4},{69,5},{70,6},{71,7},{72,8},{73... | collective-permute-start | bytes 3145736 | tf_op jit(solution)/shard_map/ppermute | solution.py:55
  88.9 44.5 %collective-permute-start.6 = (f32[512,512]{1,0:T(8,128)S(1)}, f32[512,512]{1,0:T(8,128)S(1)}, u32[]{:S(2)}, u32[]{:S(2)}) collective-permute-start(f32[512,512]{1,0:T(8,128)S(1)} %collective-permute-done.3), channel_id=1, source_target_pairs={{64,0},{65,1},{66,2},{67,3},{68,4},{69,5},{70,6},{71,7},{72,8},{73... | collective-permute-start | bytes 3145736 | tf_op jit(solution)/shard_map/ppermute | solution.py:56
  90.6 9.7 %copy-start.9 = (f32[512,512]{1,0:T(8,128)}, f32[512,512]{1,0:T(8,128)S(1)}, u32[]{:S(2)}) copy-start(f32[512,512]{1,0:T(8,128)S(1)} %bitcast_add_fusion.5) | copy-start | bytes 3145732
  90.8 9.5 %copy-start.10 = (f32[512,512]{1,0:T(8,128)}, f32[512,512]{1,0:T(8,128)S(1)}, u32[]{:S(2)}) copy-start(f32[512,512]{1,0:T(8,128)S(1)} %add.65) | copy-start | bytes 3145732
  133.4 1.0 copy-start.8
  163.2 1.3 copy-start
  166.1 27.9 %collective-permute-start.2 = (f32[256,1024]{0,1:T(8,128)}, f32[256,1024]{0,1:T(8,128)}, u32[]{:S(2)}, u32[]{:S(2)}) collective-permute-start(f32[256,1024]{0,1:T(8,128)} %get-tuple-element.8), channel_id=1, source_target_pairs={{0,64},{64,0},{1,65},{65,1},{2,66},{66,2},{3,67},{67,3},{4,68},{68... | collective-permute-start | bytes 3145736 | tf_op jit(solution)/shard_map/ppermute | solution.py:59
  166.1 49.0 %copy-start.1 = (f32[512,1024]{0,1:T(8,128)S(1)}, f32[512,1024]{0,1:T(8,128)}, u32[]{:S(2)}) copy-start(f32[512,1024]{0,1:T(8,128)} %copy-done) | copy-start | bytes 6291460
  166.1 49.0 %collective-permute-start.7 = (f32[256,1024]{0,1:T(8,128)}, f32[256,1024]{0,1:T(8,128)}, u32[]{:S(2)}, u32[]{:S(2)}) collective-permute-start(f32[256,1024]{0,1:T(8,128)} %get-tuple-element.10), channel_id=1, source_target_pairs={{0,64},{64,0},{1,65},{65,1},{2,66},{66,2},{3,67},{67,3},{4,68},{68... | collective-permute-start | bytes 3145736 | tf_op jit(solution)/shard_map/ppermute | solution.py:60
  225.0 22.1 %copy-start.6 = (f32[512,4,128]{2,1,0:T(4,128)S(1)}, f32[512,4,128]{2,1,0:T(4,128)}, u32[]{:S(2)}) copy-start(f32[512,4,128]{2,1,0:T(4,128)} %get-tuple-element.13) | copy-start | bytes 3145732
  245.6 7.0 %collective-permute-start.12 = (f32[2,16,2048]{2,1,0:T(8,128)S(1)}, f32[2,16,2048]{2,1,0:T(8,128)S(1)}, u32[]{:S(2)}, u32[]{:S(2)}) collective-permute-start(f32[2,16,2048]{2,1,0:T(8,128)S(1)} %select_bitcast_fusion), channel_id=1, source_target_pairs={{0,8},{8,0},{1,9},{9,1},{2,10},{10,2},{3,11},{11,3},{4,12},{12,4},... | collective-permute-start | bytes 786440 | tf_op jit(solution)/shard_map/ppermute | solution.py:79
  247.1 5.5 %copy-start.7 = (f32[1,64,2048]{2,1,0:T(8,128)S(1)}, f32[1,64,2048]{2,1,0:T(8,128)}, u32[]{:S(2)}) copy-start(f32[1,64,2048]{2,1,0:T(8,128)} %reduce-scatter.4.cloned.1.call-done) | copy-start | bytes 1572868
  247.1 5.5 %copy-start.11 = (f32[1,16,2048]{2,1,0:T(8,128)S(1)}, f32[1,16,2048]{2,1,0:T(8,128)}, u32[]{:S(2)}) copy-start(f32[1,16,2048]{2,1,0:T(8,128)} %param.17) | copy-start | bytes 393220
  247.1 8.4 %copy-start.2 = (f32[512,2048]{1,0:T(8,128)S(1)}, f32[512,2048]{1,0:T(8,128)}, u32[]{:S(2)}) copy-start(f32[512,2048]{1,0:T(8,128)} %fusion.12) | copy-start | bytes 12582916
  247.2 8.4 %copy-start.3 = (f32[512,2048]{1,0:T(8,128)S(1)}, f32[512,2048]{1,0:T(8,128)}, u32[]{:S(2)}) copy-start(f32[512,2048]{1,0:T(8,128)} %fusion.8) | copy-start | bytes 12582916
  247.2 8.4 %copy-start.4 = (f32[1,512,2048]{2,1,0:T(8,128)S(1)}, f32[1,512,2048]{2,1,0:T(8,128)}, u32[]{:S(2)}) copy-start(f32[1,512,2048]{2,1,0:T(8,128)} %param.14) | copy-start | bytes 12582916
  252.7 10.5 %collective-permute-start.13 = (f32[16,2048]{1,0:T(8,128)S(1)}, f32[16,2048]{1,0:T(8,128)S(1)}, u32[]{:S(2)}, u32[]{:S(2)}) collective-permute-start(f32[16,2048]{1,0:T(8,128)S(1)} %fusion.31), channel_id=1, source_target_pairs={{0,64},{64,0},{1,65},{65,1},{2,66},{66,2},{3,67},{67,3},{4,68},{68... | collective-permute-start | bytes 393224 | tf_op jit(solution)/shard_map/ppermute | solution.py:82
Sparse Core Ops, SparseCore 0:
  24.1 75.2 all-gather.1
  158.4 86.0 reduce-scatter.3

commit v2 on v1

v2 whole, which is shorter than its diff:
```python
import jax
import jax.numpy as jnp
from jax import lax
from jax.experimental import pallas as pl
from jax.experimental.pallas import tpu as pltpu
from jax.sharding import Mesh
from jax.sharding import PartitionSpec as P

DP = ("y", "xl", "z", "core")
SWAP = [(0, 1), (1, 0)]
F32 = jnp.float32
BF16 = jnp.bfloat16
SMEM = pl.BlockSpec(memory_space=pltpu.SMEM)
TILE = 512
LATE = 8


def cost(flops, *arrays, weight=1):
    moved = sum(4 * a.size for a in arrays)
    return pl.CostEstimate(
        flops=weight * flops, bytes_accessed=weight * moved, transcendentals=0
    )


def params():
    return pltpu.CompilerParams(vmem_limit_bytes=56 * 1024 * 1024)


def after(value, *earlier):
    return lax.optimization_barrier((value, *earlier))[0]


def halves(a):
    high = a.astype(BF16)
    return high, (a - high.astype(F32)).astype(BF16)


def dot(left, right):
    return jnp.dot(left, right, preferred_element_type=F32)


def three_passes(left_high, left_low, right):
    high, low = halves(right)
    return dot(left_high, high) + dot(left_high, low) + dot(left_low, high)


def turn_kernel(core_ref, x_ref, a_ref, x_mine, a_mine, theirs):
    even = core_ref[0] == 0
    for n, (src, mine) in enumerate(((x_ref, x_mine), (a_ref, a_mine))):
        t = src[...].T
        for z in range(4):
            for k in range(2):
                at = z * 32 + k * 8
                e, o = t[at : at + 8], t[at + 16 : at + 24]
                mine[k, 0, z, 0] = jnp.where(even, e, o)
                theirs[n, k, 0, z, 0] = jnp.where(even, o, e)


def turned(core, x, a):
    tokens = x.shape[0]
    mine = jax.ShapeDtypeStruct((2, 4, 4, 2, 8, tokens), F32)
    mine_spec = pl.BlockSpec((2, 1, 4, 1, 8, tokens), lambda i: (0, i // 2, 0, i % 2, 0, 0))
    column = pl.BlockSpec((tokens, 128), lambda i: (0, i))
    x_mine, a_mine, theirs = pl.pallas_call(
        turn_kernel,
        grid=(8,),
        in_specs=[SMEM, column, column],
        out_specs=[
            mine_spec,
            mine_spec,
            pl.BlockSpec((2, 2, 1, 4, 1, 8, tokens), lambda i: (0, 0, i // 2, 0, i % 2, 0, 0)),
        ],
        out_shape=[mine, mine, jax.ShapeDtypeStruct((2, *mine.shape), F32)],
        cost_estimate=cost(0, x, a, x, a),
        compiler_params=params(),
    )(core, x, a)
    return (
        x_mine.reshape(2, 256, tokens),
        a_mine.reshape(2, 256, tokens),
        theirs.reshape(2, 2, 256, tokens),
    )


def grad_kernel(p_ref, x_ref, xr_ref, a_ref, ar_ref, g_ref, b_ref, ro_ref, bo_ref, out, high, low):
    is_first = p_ref[0] == 0

    @pl.when(pl.program_id(0) == 0)
    def _():
        opened = x_ref[...] + xr_ref[...]
        second = jnp.where(is_first, ar_ref[...], a_ref[...])
        last = jnp.where(is_first, a_ref[...], opened)
        for n, v in enumerate((opened - second, second, last)):
            at = slice(n * 256, n * 256 + 256)
            high[at], low[at] = halves(v)

    b = b_ref[...]
    r = g_ref[...] - jnp.where(is_first, 0.0, b)
    right = jnp.concatenate([r, ro_ref[...]], axis=0)
    right_b = jnp.concatenate([b, bo_ref[...]], axis=0)
    both = three_passes(high[:512], low[:512], right)
    shared = three_passes(high[512:], low[512:], right_b)
    part0 = both[:256] - jnp.where(is_first, shared, 0.0)
    part1 = both[256:] + shared
    out[:, 0] = part0.reshape(16, 16, part0.shape[1])
    out[:, 1] = part1.reshape(16, 16, part1.shape[1])


def grad_parts(party, x, x_got, a, a_got, g, b, r_other, b_other, weight):
    tokens, ff = g.shape
    left = pl.BlockSpec((256, 2 * tokens), lambda n: (0, 0))
    right = pl.BlockSpec((tokens, TILE), lambda n: (0, n))
    return pl.pallas_call(
        grad_kernel,
        grid=(ff // TILE,),
        in_specs=[SMEM] + [left] * 4 + [right] * 4,
        out_specs=pl.BlockSpec((16, 2, 16, TILE), lambda n: (0, 0, 0, n)),
        out_shape=jax.ShapeDtypeStruct((16, 2, 16, ff), F32),
        scratch_shapes=[pltpu.VMEM((768, 2 * tokens), BF16)] * 2,
        cost_estimate=cost(3 * 2 * 768 * 2 * tokens * ff, x, x_got, a, a_got, g, b, r_other, b_other, g, g, weight=weight),
        compiler_params=params(),
    )(party, x, x_got, a, a_got, g, b, r_other, b_other)


def store_split(value, high, low):
    for xl in range(2):
        cols = [value[:, (2 * y + xl) * 128 :][:, :128] for y in range(4)]
        high[:, xl * 512 : xl * 512 + 512], low[:, xl * 512 : xl * 512 + 512] = halves(
            jnp.concatenate(cols, axis=1)
        )


def add_product(c_ref, w0_ref, w1_ref, out, high, low):
    w = jnp.concatenate([w0_ref[...], w1_ref[...]], axis=0)
    out[...] = c_ref[...] + three_passes(high[...], low[...], w)


def local_kernel(a_ref, w0_ref, w1_ref, c_ref, out, high, low):
    @pl.when(pl.program_id(0) == 0)
    def _():
        store_split(a_ref[...], high, low)

    add_product(c_ref, w0_ref, w1_ref, out, high, low)


def opened_kernel(x_ref, a_ref, got_ref, w0_ref, w1_ref, c_ref, out, high, low):
    @pl.when(pl.program_id(0) == 0)
    def _():
        store_split((x_ref[...] - a_ref[...]) + got_ref[...], high, low)

    add_product(c_ref, w0_ref, w1_ref, out, high, low)


def forward_call(kernel, lefts, left_rows, weights, at, c, row, rows):
    ff = c.shape[1]
    d = lefts[0].shape[1]
    steps = ff // TILE
    out_spec = pl.BlockSpec((rows, TILE), lambda n: (row, n))
    return pl.pallas_call(
        kernel,
        grid=(steps,),
        in_specs=[pl.BlockSpec((rows, d), lambda n, r=r: (r, 0)) for r in left_rows]
        + [
            pl.BlockSpec((d // 2, TILE), lambda n: (0, at * steps + n)),
            pl.BlockSpec((d // 2, TILE), lambda n: (0, (at + 2) * steps + n)),
            out_spec,
        ],
        out_specs=out_spec,
        out_shape=jax.ShapeDtypeStruct(c.shape, F32),
        scratch_shapes=[pltpu.VMEM((rows, d), BF16)] * 2,
        cost_estimate=cost(3 * 2 * rows * d * ff, weights, c),
        input_output_aliases={len(lefts) + 2: 0} if rows != c.shape[0] else {},
        compiler_params=params(),
    )(*lefts, weights, weights, c)


def scattered(a, axis, dim, *earlier):
    here = lax.axis_index(axis)
    total = lax.dynamic_index_in_dim(a, here, dim, keepdims=False)
    got = []
    for step in (2, 1, 3):
        piece = lax.dynamic_index_in_dim(a, (here + step) % 4, dim, keepdims=False)
        if earlier:
            piece = after(piece, *earlier)
        got.append(lax.ppermute(piece, axis, [(i, (i + step) % 4) for i in range(4)]))
    return total + got[0] + got[1] + got[2]


def body(x_share, w_share, g_share, fwd_a, fwd_b, fwd_c, bwd_a, bwd_b, bwd_c):
    x, w, g = x_share[0], w_share[0], g_share[0]
    fa, fb, fc = fwd_a[0], fwd_b[0], fwd_c[0]
    ba, bb, bc = bwd_a[0], bwd_b[0], bwd_c[0]
    party = lax.axis_index("party")
    party0 = party == 0
    first = party0.astype(F32)
    party_id = party.astype(jnp.int32).reshape(1)
    core_id = lax.axis_index("core").astype(jnp.int32).reshape(1)
    xl0 = lax.axis_index("xl") == 0
    ff = w.shape[1]

    d = w - fb
    d_party = lax.ppermute(d, "party", SWAP)
    near = lax.ppermute(jnp.concatenate([fb, d], axis=1), "xl", SWAP)
    d_across = lax.ppermute(d, ("party", "xl"), [(0, 3), (3, 0), (1, 2), (2, 1)])
    delta = d + d_party
    delta_near = near[:, ff:] + d_across
    packed = jnp.concatenate([fb + first * delta, delta], axis=1)
    packed_near = jnp.concatenate([near[:, :ff] + first * delta_near, delta_near], axis=1)
    weights = jnp.concatenate(
        [jnp.where(xl0, packed, packed_near), jnp.where(xl0, packed_near, packed)], axis=1
    )
    weights = lax.all_gather(weights, ("y", "z", "core"), axis=0, tiled=True)

    x_mine, a_mine, theirs = turned(core_id, x, ba)
    other = lax.ppermute(after(theirs, d_across, d_party, near), "core", SWAP)
    xs = [jnp.concatenate([x_mine[k], other[0, k]], axis=1) for k in range(2)]
    aa = [jnp.concatenate([a_mine[k], other[1, k]], axis=1) for k in range(2)]
    x0 = lax.ppermute(xs[0], "party", SWAP)
    a0 = lax.ppermute(aa[0], "party", [(1, 0)])
    x1 = lax.ppermute(xs[1], "party", SWAP)
    a1 = lax.ppermute(after(aa[1], x0), "party", [(1, 0)])
    u = x - fa
    u0 = lax.ppermute(after(u[:128], a0), "party", SWAP)
    u1 = lax.ppermute(after(u[128:256], x1), "party", SWAP)
    u2 = lax.ppermute(after(u[256:], a1), "party", SWAP)

    r_other = lax.ppermute(after(g - (1.0 - first) * bb, other), "core", SWAP)
    b_other = lax.ppermute(after(bb, other), "core", SWAP)
    rights = (g, bb, r_other, b_other)
    early = grad_parts(party_id, xs[0], x0, aa[0], a0, *rights, 1)
    late = grad_parts(party_id, xs[1], x1, aa[1], a1, *rights, LATE)

    early = lax.psum_scatter(early.reshape(16, 32, ff), ("y", "z"), scatter_dimension=0, tiled=True)
    early = early.reshape(2, 2, 8, ff)
    outputs = forward_call(local_kernel, (fa,), (0,), weights, 1, fc, 0, fc.shape[0])
    late = after(late, outputs, u0).reshape(4, 4, 2, 16, ff)
    part0 = scattered(late[:, :, 0], "z", 1)
    part1 = scattered(late[:, :, 1], "y", 0)
    part0 = scattered(part0, "y", 0, u1)
    part1 = scattered(part1, "z", 0, u1)
    late = jnp.stack([part0, part1]).reshape(2, 2, 8, ff)
    both = jnp.concatenate([early, late], axis=2)
    keep = jnp.where(xl0, both[:, 0], both[:, 1])
    give = jnp.where(xl0, both[:, 1], both[:, 0])
    both = keep + lax.ppermute(after(give, u2), "xl", SWAP)
    give = jnp.where(party0, both[1] - bc, both[0])
    keep = jnp.where(party0, both[0] + bc, both[1])
    grad = keep + lax.ppermute(give, "party", SWAP)

    outputs = forward_call(opened_kernel, (x, fa, u0), (0, 0, 0), weights, 0, outputs, 0, 128)
    outputs = forward_call(opened_kernel, (x, fa, u1), (1, 1, 0), weights, 0, outputs, 1, 128)
    outputs = forward_call(opened_kernel, (x, fa, u2), (1, 1, 0), weights, 0, outputs, 1, 256)
    return (outputs[None], grad[None])


def solution(mesh):
    split = Mesh(
        mesh.devices.reshape(mesh.shape["party"], 4, 2, 4, 2),
        ("party", *DP),
    )
    spec = P("party", DP, None)
    return jax.shard_map(
        body, mesh=split, in_specs=(spec,) * 9, out_specs=(spec, spec), check_vma=False
    )
```

time: 271 us -> 279 us (1.030)
  Pallas kernels: 0 us -> 76.6 us
  matrix products: 57.6 us -> 0 us
  starting transfers between devices: 22.1 us -> 48.8 us
  waiting for transfers between devices: 129 us -> 109 us
  local copies, waits for them, and re-layouts: 28.1 us -> 10 us
    pallas_call x0 -> x7, Pallas kernels: none -> 76.6 us  [the longest x4 35.9 us: forward_call(): pl.pallas_call(kernel, grid=(steps,), in_specs=[pl.BlockSpec((rows, d), l...]
    dot_general x7 -> x0, matrix products: 57.6 us -> none  [dot(): jnp.dot(left, right, preferred_element_type=jnp.float32, precision=lax.Pr...]
    ppermute x13 -> x26, starting transfers between devices: 19.2 us -> 48.6 us  [the longest x12 27.8 us: scattered(): lax.ppermute(piece, axis, [(i, (i + step) % 4) for i in range(4)])]
    unnamed x3, waiting for transfers between devices: 11.9 us -> 0.06 us
    ppermute x13 -> x26, waiting for transfers between devices: 117 us -> 109 us  [the longest x12 38.8 us: scattered(): lax.ppermute(piece, axis, [(i, (i + step) % 4) for i in range(4)])]
    slice x3 -> x4, local copies, waits for them, and re-layouts: 11.2 us -> 3.24 us  [the longest x1 1.07 us: body(): u2 = lax.ppermute(after(u[256:], a1), 'party', SWAP)]
    unnamed x27 -> x32, local copies, waits for them, and re-layouts: 10.1 us -> 2.65 us
    squeeze x0 -> x5, local copies, waits for them, and re-layouts: none -> 4.13 us  [the longest x1 2.68 us: body(): aa = [jnp.concatenate([a_mine[k], other[1, k]], axis=1) for k in range(2)]]
  transfers between devices with their start and end apart: 16 -> 29, of which waited for: 9 -> 10; matrix products, arithmetic and copies ran while one was open for 36% -> 8% of each run, Pallas kernels for 0% -> 28%
where the time goes in v2:
time: 279 us; the launch traced here: 278 us
  waiting for transfers between devices  109 us (39%)
  Pallas kernels  76.6 us (27%)
  starting transfers between devices  48.8 us (17%)
  other arithmetic  18.5 us (7%)
  between operations  15.9 us (6%)
  local copies, waits for them, and re-layouts  10 us (4%)
    ppermute x12, waiting for transfers between devices, scattered(): lax.ppermute(piece, axis, [(i, (i + step) % 4) for i in range(4)])  38.8 us
    pallas_call x4, Pallas kernels, forward_call(): pl.pallas_call(kernel, grid=(steps,), in_specs=[pl.BlockSpec((rows, d), l...  35.9 us
    pallas_call x2, Pallas kernels, grad_parts(): pl.pallas_call(grad_kernel, grid=(ff // TILE,), in_specs=[SMEM] + [left]...  33.4 us
    ppermute x12, starting transfers between devices, scattered(): lax.ppermute(piece, axis, [(i, (i + step) % 4) for i in range(4)])  27.8 us
    ppermute x1, waiting for transfers between devices, body(): a1 = lax.ppermute(after(aa[1], x0), 'party', [(1, 0)])  22.5 us
    ppermute x1, waiting for transfers between devices, body(): a0 = lax.ppermute(aa[0], 'party', [(1, 0)])  20.3 us
    ppermute x1, waiting for transfers between devices, body(): x0 = lax.ppermute(xs[0], 'party', SWAP)  14.8 us
    pallas_call x1, Pallas kernels, turned(): pl.pallas_call(turn_kernel, grid=(8,), in_specs=[SMEM, column, column], o...  7.33 us
  transfers between devices with their start and end apart: 29, of which 10 were waited for; matrix products, arithmetic and copies ran while one was open for 8% of the time, Pallas kernels for 28%

profile of v2, /device:TPU:0, one launch (start us, length us, event | category | flops | bytes accessed | tf_op | source)
XLA Modules:
  0.0 278.4 jit_solution(7348763774856864366)
XLA Ops:
  8.0 1.0 bitcast_subtract_fusion.1
  9.0 2.9 %collective-permute-start = (f32[16,2048]{1,0:T(8,128)S(1)}, f32[16,2048]{1,0:T(8,128)S(1)}, u32[]{:S(2)}, u32[]{:S(2)}) collective-permute-start(f32[16,2048]{1,0:T(8,128)S(1)} %bitcast_subtract_fusion.1), channel_id=1, source_target_pairs={{0,72},{72,0},{8,64},{64,8},{1,73},{73,1},{9,65},{65,9},{2,74},{74... | collective-permute-start | bytes 393224 | tf_op jit(solution)/shard_map/ppermute | solution.py:203
  12.8 0.9 pad_maximum_fusion.5
  14.2 5.5 %collective-permute-done.1 = f32[16,2048]{1,0:T(8,128)S(1)} collective-permute-done((f32[16,2048]{1,0:T(8,128)S(1)}, f32[16,2048]{1,0:T(8,128)S(1)}, u32[]{:S(2)}, u32[]{:S(2)}) %collective-permute-start.1) | collective-permute-done | bytes 131104 | tf_op jit(solution)/shard_map/ppermute | solution.py:201
  19.7 0.9 multiply_add_fusion
  20.6 1.1 collective-permute-done.2
  22.8 7.3 %shard_map.104 = (f32[2,4,4,2,8,512]{5,4,3,2,1,0:T(8,128)}, f32[2,4,4,2,8,512]{5,4,3,2,1,0:T(8,128)}, f32[2,2,4,4,2,8,512]{6,5,4,3,2,1,0:T(8,128)}) custom-call(s32[1]{0:T(128)} %bitcast.2.core_ref, f32[512,1024]{1,0:T(8,128)} %bitcast.135, f32[512,1024]{1,0:T(8,128)} %bitcast.148), custom_call_target="tpu_custom_call" | custom-call | bytes 8388608 | tf_op jit(solution)/shard_map/pallas_call | solution.py:64
  30.1 6.8 %multiply_subtract_fusion = f32[512,2048]{1,0:T(8,128)} fusion(f32[]{:T(128)S(6)} %sub.17, f32[1,512,2048]{2,1,0:T(8,128)} %param.16, f32[1,512,2048]{2,1,0:T(8,128)} %param.11), kind=kLoop, calls=%fused_computation | loop fusion | flops 2097152 | bytes 12582916 | tf_op jit(solution)/shard_map/sub | solution.py:226
  38.3 1.0 fusion.20
  39.3 2.7 slice_bitcast_fusion
  42.0 1.1 pad_maximum_fusion.1.x_ref
  43.1 3.1 %collective-permute-start.4 = (f32[256,1024]{1,0:T(8,128)}, f32[256,1024]{1,0:T(8,128)}, u32[]{:S(2)}, u32[]{:S(2)}) collective-permute-start(f32[256,1024]{1,0:T(8,128)} %pad_maximum_fusion.1.x_ref), channel_id=1, source_target_pairs={{0,64},{64,0},{1,65},{65,1},{2,66},{66,2},{3,67},{67,3},{4,68},{68... | collective-permute-start | bytes 3145736 | tf_op jit(solution)/shard_map/ppermute | solution.py:217
  46.2 1.1 pad_maximum_fusion.3.a_ref
  47.3 1.3 collective-permute-start.9
  48.6 2.1 bitcast_subtract_fusion.2
  50.8 5.1 %collective-permute-start.7 = (f32[256,1024]{1,0:T(8,128)S(1)}, f32[256,1024]{1,0:T(8,128)}, u32[]{:S(2)}, u32[]{:S(2)}) collective-permute-start(f32[256,1024]{1,0:T(8,128)S(1)} %pad_maximum_fusion.2.x_ref), channel_id=1, source_target_pairs={{0,64},{64,0},{1,65},{65,1},{2,66},{66,2},{3,67},{67,3},{4,68},{68... | collective-permute-start | bytes 3145736 | tf_op jit(solution)/shard_map/ppermute | solution.py:219
  56.0 14.8 %collective-permute-done.4.xr_ref = f32[256,1024]{1,0:T(8,128)} collective-permute-done((f32[256,1024]{1,0:T(8,128)}, f32[256,1024]{1,0:T(8,128)}, u32[]{:S(2)}, u32[]{:S(2)}) %collective-permute-start.4) | collective-permute-done | bytes 1048608 | tf_op jit(solution)/shard_map/ppermute | solution.py:217
  70.8 1.3 collective-permute-start.5
  72.1 0.9 fusion.19
  73.0 20.3 %collective-permute-done.9.ar_ref = f32[256,1024]{1,0:T(8,128)} collective-permute-done((f32[256,1024]{1,0:T(8,128)}, f32[256,1024]{1,0:T(8,128)}, u32[]{:S(2)}, u32[]{:S(2)}) %collective-permute-start.9) | collective-permute-done | bytes 1048608 | tf_op jit(solution)/shard_map/ppermute | solution.py:218
  93.3 16.9 %shard_map.109 = f32[16,2,16,2048]{3,2,1,0:T(8,128)} custom-call(s32[1]{0:T(128)} %bitcast.17.p_ref, f32[256,1024]{1,0:T(8,128)} %pad_maximum_fusion.1.x_ref, f32[256,1024]{1,0:T(8,128)} %collective-permute-done.4.xr_ref, f32[256,1024]{1,0:T(8,128)} %pad_maximum_fusion.3.a_ref, f32[256,1024]{1,0:T(8,128)} %collective-permute-done.9.ar_ref, ...), custom_call_target="tpu_custom_call" | custom-call | flops 9663676416 | bytes 29360128 | tf_op jit(solution)/shard_map/pallas_call | solution.py:112
  110.2 5.6 %collective-permute-done.7.xr_ref = f32[256,1024]{1,0:T(8,128)} collective-permute-done((f32[256,1024]{1,0:T(8,128)S(1)}, f32[256,1024]{1,0:T(8,128)}, u32[]{:S(2)}, u32[]{:S(2)}) %collective-permute-start.7) | collective-permute-done | bytes 1048608 | tf_op jit(solution)/shard_map/ppermute | solution.py:219
  115.8 22.5 %collective-permute-done.5.ar_ref = f32[256,1024]{1,0:T(8,128)} collective-permute-done((f32[256,1024]{1,0:T(8,128)S(1)}, f32[256,1024]{1,0:T(8,128)}, u32[]{:S(2)}, u32[]{:S(2)}) %collective-permute-start.5) | collective-permute-done | bytes 1048608 | tf_op jit(solution)/shard_map/ppermute | solution.py:220
  138.2 16.6 %shard_map.110 = f32[16,2,16,2048]{3,2,1,0:T(8,128)} custom-call(s32[1]{0:T(128)} %bitcast.17.p_ref, f32[256,1024]{1,0:T(8,128)} %copy-done.9, f32[256,1024]{1,0:T(8,128)} %collective-permute-done.7.xr_ref, f32[256,1024]{1,0:T(8,128)} %copy-done.10, f32[256,1024]{1,0:T(8,128)} %collective-permute-done.5.ar_ref, f32[512,2048]{1,0:T(8,128)} %bitcast.144, ...), custom_call_target="tpu_custom_call" | custom-call | flops 77309411328 | bytes 234881024 | tf_op jit(solution)/shard_map/pallas_call | solution.py:112
  154.8 12.2 %shard_map.105.c_ref = f32[512,2048]{1,0:T(8,128)} custom-call(f32[512,1024]{1,0:T(8,128)} %bitcast.139, f32[512,8192]{1,0:T(8,128)} %all-gather.2.cloned.1.call-done.w0_ref.w1_ref, f32[512,8192]{1,0:T(8,128)} %all-gather.2.cloned.1.call-done.w0_ref.w1_ref, f32[512,2048]{1,0:T(8,128)} %bitcast.147), custom_call_target="tpu_custom_call" | custom-call | flops 6442450944 | bytes 20971520 | tf_op jit(solution)/shard_map/pallas_call | solution.py:158
  167.9 1.3 copy-done.3
  169.2 1.2 dynamic-slice_bitcast_fusion.2
  170.4 3.1 %collective-permute-start.21 = (f32[4,16,2048]{2,1,0:T(8,128)}, f32[4,16,2048]{2,1,0:T(8,128)}, u32[]{:S(2)}, u32[]{:S(2)}) collective-permute-start(f32[4,16,2048]{2,1,0:T(8,128)} %get-tuple-element.48), channel_id=1, source_target_pairs={{0,48},{16,0},{32,16},{48,32},{1,49},{17,1},{33,17},{49,33},{2,50}... | collective-permute-start | bytes 1572872 | tf_op jit(solution)/shard_map/ppermute | solution.py:184
  173.5 2.2 collective-permute-start.19
  175.8 1.1 slice.84
  176.8 3.5 %collective-permute-start.6 = (f32[256,1024]{1,0:T(8,128)}, f32[256,1024]{1,0:T(8,128)S(1)}, u32[]{:S(2)}, u32[]{:S(2)}) collective-permute-start(f32[256,1024]{1,0:T(8,128)} %slice.84), channel_id=1, source_target_pairs={{0,64},{64,0},{1,65},{65,1},{2,66},{66,2},{3,67},{67,3},{4,68},{68... | collective-permute-start | bytes 3145736 | tf_op jit(solution)/shard_map/ppermute | solution.py:224
  180.5 19.6 %collective-permute-done.21 = f32[4,16,2048]{2,1,0:T(8,128)} collective-permute-done((f32[4,16,2048]{2,1,0:T(8,128)}, f32[4,16,2048]{2,1,0:T(8,128)}, u32[]{:S(2)}, u32[]{:S(2)}) %collective-permute-start.21) | collective-permute-done | bytes 524320 | tf_op jit(solution)/shard_map/ppermute | solution.py:184
  200.1 4.3 %collective-permute-start.15 = (f32[4,16,2048]{2,1,0:T(8,128)S(1)}, f32[4,16,2048]{2,1,0:T(8,128)S(1)}, u32[]{:S(2)}, u32[]{:S(2)}) collective-permute-start(f32[4,16,2048]{2,1,0:T(8,128)S(1)} %get-tuple-element.45), channel_id=1, source_target_pairs={{0,6},{2,0},{4,2},{6,4},{1,7},{3,1},{5,3},{7,5},{8,14},{10,8},{12,... | collective-permute-start | bytes 1572872 | tf_op jit(solution)/shard_map/ppermute | solution.py:184
  204.4 1.0 collective-permute-start.14
  205.4 3.8 %collective-permute-start.13 = (f32[4,16,2048]{2,1,0:T(8,128)S(1)}, f32[4,16,2048]{2,1,0:T(8,128)S(1)}, u32[]{:S(2)}, u32[]{:S(2)}) collective-permute-start(f32[4,16,2048]{2,1,0:T(8,128)S(1)} %get-tuple-element.44), channel_id=1, source_target_pairs={{0,4},{2,6},{4,0},{6,2},{1,5},{3,7},{5,1},{7,3},{8,12},{10,14},{12... | collective-permute-start | bytes 1572872 | tf_op jit(solution)/shard_map/ppermute | solution.py:184
  209.3 1.6 fusion.1
  211.0 1.0 collective-permute-start.24
  211.9 13.2 %collective-permute-done.15 = f32[4,16,2048]{2,1,0:T(8,128)S(1)} collective-permute-done((f32[4,16,2048]{2,1,0:T(8,128)S(1)}, f32[4,16,2048]{2,1,0:T(8,128)S(1)}, u32[]{:S(2)}, u32[]{:S(2)}) %collective-permute-start.15) | collective-permute-done | bytes 524320 | tf_op jit(solution)/shard_map/ppermute | solution.py:184
  225.1 5.2 %collective-permute-start.22 = (f32[16,2048]{1,0:T(8,128)S(1)}, f32[16,2048]{1,0:T(8,128)S(1)}, u32[]{:S(2)}, u32[]{:S(2)}) collective-permute-start(f32[16,2048]{1,0:T(8,128)S(1)} %get-tuple-element.34), channel_id=1, source_target_pairs={{0,4},{2,6},{4,0},{6,2},{1,5},{3,7},{5,1},{7,3},{8,12},{10,14},{12... | collective-permute-start | bytes 393224 | tf_op jit(solution)/shard_map/ppermute | solution.py:184
  230.5 5.6 %collective-permute-start.18 = (f32[16,2048]{1,0:T(8,128)S(1)}, f32[16,2048]{1,0:T(8,128)S(1)}, u32[]{:S(2)}, u32[]{:S(2)}) collective-permute-start(f32[16,2048]{1,0:T(8,128)S(1)} %get-tuple-element.33), channel_id=1, source_target_pairs={{0,48},{16,0},{32,16},{48,32},{1,49},{17,1},{33,17},{49,33},{2,50}... | collective-permute-start | bytes 393224 | tf_op jit(solution)/shard_map/ppermute | solution.py:184
  236.1 1.5 collective-permute-start.16
  237.7 0.9 collective-permute-done.18
  238.6 5.1 %collective-permute-done.17 = f32[16,2048]{1,0:T(8,128)S(1)} collective-permute-done((f32[16,2048]{1,0:T(8,128)S(1)}, f32[16,2048]{1,0:T(8,128)S(1)}, u32[]{:S(2)}, u32[]{:S(2)}) %collective-permute-start.17) | collective-permute-done | bytes 131104 | tf_op jit(solution)/shard_map/ppermute | solution.py:184
  243.7 1.0 maximum_maximum_fusion
  244.8 1.7 collective-permute-start.25
  246.5 7.2 %shard_map.106.c_ref = f32[512,2048]{1,0:T(8,128)} custom-call(f32[512,1024]{1,0:T(8,128)} %bitcast.136, f32[512,1024]{1,0:T(8,128)} %bitcast.140, f32[128,1024]{1,0:T(8,128)} %copy-done.13, f32[512,8192]{1,0:T(8,128)} %all-gather.2.cloned.1.call-done.w0_ref.w1_ref, ...), custom_call_target="tpu_custom_call", output_to_operand_aliasing={{}: (5, {})} | custom-call | flops 1610612736 | bytes 20971520 | tf_op jit(solution)/shard_map/pallas_call | solution.py:158
  253.6 7.2 %shard_map.107.c_ref = f32[512,2048]{1,0:T(8,128)} custom-call(f32[512,1024]{1,0:T(8,128)} %bitcast.137, f32[512,1024]{1,0:T(8,128)} %bitcast.141, f32[128,1024]{1,0:T(8,128)} %copy-done.14, f32[512,8192]{1,0:T(8,128)} %all-gather.2.cloned.1.call-done.w0_ref.w1_ref, ...), custom_call_target="tpu_custom_call", output_to_operand_aliasing={{}: (5, {})} | custom-call | flops 1610612736 | bytes 20971520 | tf_op jit(solution)/shard_map/pallas_call | solution.py:158
  261.1 9.2 %shard_map.108 = f32[512,2048]{1,0:T(8,128)} custom-call(f32[512,1024]{1,0:T(8,128)} %bitcast.138, f32[512,1024]{1,0:T(8,128)} %bitcast.142, f32[256,1024]{1,0:T(8,128)} %copy-done.8, f32[512,8192]{1,0:T(8,128)} %all-gather.2.cloned.1.call-done.w0_ref.w1_ref, f32[512,8192]{1,0:T(8,128)} %all-gather.2.cloned.1.call-done.w0_ref.w1_ref, ...), custom_call_target="tpu_custom_call", output_to_operand_aliasing={{}: (5, {})} | custom-call | flops 3221225472 | bytes 20971520 | tf_op jit(solution)/shard_map/pallas_call | solution.py:158
  (81 shorter events, 6.0 us)
Async XLA Ops:
  8.0 146.8 %all-gather.2.cloned.1.call-start = ((), (), s32[]{:S(2)}) async-start(), calls=%async_computation.1 | async-start | bytes 17301504 | tf_op jit(solution)/shard_map/all_gather | solution.py:211
  9.0 11.6 %collective-permute-start = (f32[16,2048]{1,0:T(8,128)S(1)}, f32[16,2048]{1,0:T(8,128)S(1)}, u32[]{:S(2)}, u32[]{:S(2)}) collective-permute-start(f32[16,2048]{1,0:T(8,128)S(1)} %bitcast_subtract_fusion.1), channel_id=1, source_target_pairs={{0,72},{72,0},{8,64},{64,8},{1,73},{73,1},{9,65},{65,9},{2,74},{74... | collective-permute-start | bytes 393224 | tf_op jit(solution)/shard_map/ppermute | solution.py:203
  11.9 7.7 %collective-permute-start.1 = (f32[16,2048]{1,0:T(8,128)S(1)}, f32[16,2048]{1,0:T(8,128)S(1)}, u32[]{:S(2)}, u32[]{:S(2)}) collective-permute-start(f32[16,2048]{1,0:T(8,128)S(1)} %bitcast_subtract_fusion.1), channel_id=1, source_target_pairs={{0,64},{64,0},{1,65},{65,1},{2,66},{66,2},{3,67},{67,3},{4,68},{68... | collective-permute-start | bytes 393224 | tf_op jit(solution)/shard_map/ppermute | solution.py:201
  13.7 8.1 %collective-permute-start.2 = (f32[16,4096]{1,0:T(8,128)S(1)}, f32[16,4096]{1,0:T(8,128)S(1)}, u32[]{:S(2)}, u32[]{:S(2)}) collective-permute-start(f32[16,4096]{1,0:T(8,128)S(1)} %pad_maximum_fusion.5), channel_id=1, source_target_pairs={{0,8},{8,0},{1,9},{9,1},{2,10},{10,2},{3,11},{11,3},{4,12},{12,4},... | collective-permute-start | bytes 786440 | tf_op jit(solution)/shard_map/ppermute | solution.py:202
  22.7 221.0 %reduce-scatter.4.cloned.1.call-start = ((), (), s32[]{:S(2)}) async-start(), calls=%async_computation.2 | async-start | bytes 4456448
  30.1 6.9 %collective-permute-start.3 = (f32[2,2,256,512]{3,2,1,0:T(8,128)}, f32[2,2,256,512]{3,2,1,0:T(8,128)S(1)}, u32[]{:S(2)}, u32[]{:S(2)}) collective-permute-start(f32[2,2,256,512]{3,2,1,0:T(8,128)} %bitcast.155), channel_id=1, source_target_pairs={{0,1},{1,0},{2,3},{3,2},{4,5},{5,4},{6,7},{7,6},{8,9},{9,8},{10,11... | collective-permute-start | bytes 6291464 | tf_op jit(solution)/shard_map/ppermute | solution.py:214
  30.1 8.2 %copy-start.11 = (f32[2,4,4,2,8,512]{5,4,3,2,1,0:T(8,128)S(1)}, f32[2,4,4,2,8,512]{5,4,3,2,1,0:T(8,128)}, u32[]{:S(2)}) copy-start(f32[2,4,4,2,8,512]{5,4,3,2,1,0:T(8,128)} %get-tuple-element.23) | copy-start | bytes 3145732
  30.1 8.2 %copy-start.12 = (f32[2,4,4,2,8,512]{5,4,3,2,1,0:T(8,128)S(1)}, f32[2,4,4,2,8,512]{5,4,3,2,1,0:T(8,128)}, u32[]{:S(2)}) copy-start(f32[2,4,4,2,8,512]{5,4,3,2,1,0:T(8,128)} %get-tuple-element.20) | copy-start | bytes 3145732
  37.0 1.3 copy-start.5
  37.0 56.4 %collective-permute-start.11 = (f32[512,2048]{1,0:T(8,128)}, f32[512,2048]{1,0:T(8,128)}, u32[]{:S(2)}, u32[]{:S(2)}) collective-permute-start(f32[512,2048]{1,0:T(8,128)} %multiply_subtract_fusion), channel_id=1, source_target_pairs={{0,1},{1,0},{2,3},{3,2},{4,5},{5,4},{6,7},{7,6},{8,9},{9,8},{10,11... | collective-permute-start | bytes 12582920 | tf_op jit(solution)/shard_map/ppermute | solution.py:226
  37.5 55.9 %collective-permute-start.12 = (f32[512,2048]{1,0:T(8,128)}, f32[512,2048]{1,0:T(8,128)}, u32[]{:S(2)}, u32[]{:S(2)}) collective-permute-start(f32[512,2048]{1,0:T(8,128)} %bitcast.19.b_ref), channel_id=1, source_target_pairs={{0,1},{1,0},{2,3},{3,2},{4,5},{5,4},{6,7},{7,6},{8,9},{9,8},{10,11... | collective-permute-start | bytes 12582920 | tf_op jit(solution)/shard_map/ppermute | solution.py:227
  39.3 9.3 %copy-start = (f32[1,512,1024]{2,1,0:T(8,128)S(1)}, f32[1,512,1024]{2,1,0:T(8,128)}, u32[]{:S(2)}) copy-start(f32[1,512,1024]{2,1,0:T(8,128)} %param.9) | copy-start | bytes 6291460
  43.1 27.8 %collective-permute-start.4 = (f32[256,1024]{1,0:T(8,128)}, f32[256,1024]{1,0:T(8,128)}, u32[]{:S(2)}, u32[]{:S(2)}) collective-permute-start(f32[256,1024]{1,0:T(8,128)} %pad_maximum_fusion.1.x_ref), channel_id=1, source_target_pairs={{0,64},{64,0},{1,65},{65,1},{2,66},{66,2},{3,67},{67,3},{4,68},{68... | collective-permute-start | bytes 3145736 | tf_op jit(solution)/shard_map/ppermute | solution.py:217
  47.3 46.0 %collective-permute-start.9 = (f32[256,1024]{1,0:T(8,128)}, f32[256,1024]{1,0:T(8,128)}, u32[]{:S(2)}, u32[]{:S(2)}) collective-permute-start(f32[256,1024]{1,0:T(8,128)} %pad_maximum_fusion.3.a_ref), channel_id=1, source_target_pairs={{64,0},{65,1},{66,2},{67,3},{68,4},{69,5},{70,6},{71,7},{72,8},{73... | collective-permute-start | bytes 3145736 | tf_op jit(solution)/shard_map/ppermute | solution.py:218
  48.6 2.1 copy-start.6
  48.6 2.1 copy-start.7
  50.7 21.4 %copy-start.1 = (f32[512,1024]{1,0:T(8,128)}, f32[512,1024]{1,0:T(8,128)S(1)}, u32[]{:S(2)}) copy-start(f32[512,1024]{1,0:T(8,128)S(1)} %bitcast_subtract_fusion.2) | copy-start | bytes 6291460
  50.8 59.4 %copy-start.9 = (f32[256,1024]{1,0:T(8,128)}, f32[256,1024]{1,0:T(8,128)S(1)}, u32[]{:S(2)}) copy-start(f32[256,1024]{1,0:T(8,128)S(1)} %pad_maximum_fusion.2.x_ref) | copy-start | bytes 3145732
  50.8 64.9 %collective-permute-start.7 = (f32[256,1024]{1,0:T(8,128)S(1)}, f32[256,1024]{1,0:T(8,128)}, u32[]{:S(2)}, u32[]{:S(2)}) collective-permute-start(f32[256,1024]{1,0:T(8,128)S(1)} %pad_maximum_fusion.2.x_ref), channel_id=1, source_target_pairs={{0,64},{64,0},{1,65},{65,1},{2,66},{66,2},{3,67},{67,3},{4,68},{68... | collective-permute-start | bytes 3145736 | tf_op jit(solution)/shard_map/ppermute | solution.py:219
  56.0 54.2 %copy-start.10 = (f32[256,1024]{1,0:T(8,128)}, f32[256,1024]{1,0:T(8,128)S(1)}, u32[]{:S(2)}) copy-start(f32[256,1024]{1,0:T(8,128)S(1)} %pad_maximum_fusion.a_ref) | copy-start | bytes 3145732
  70.8 67.4 %collective-permute-start.5 = (f32[256,1024]{1,0:T(8,128)S(1)}, f32[256,1024]{1,0:T(8,128)}, u32[]{:S(2)}, u32[]{:S(2)}) collective-permute-start(f32[256,1024]{1,0:T(8,128)S(1)} %pad_maximum_fusion.a_ref), channel_id=1, source_target_pairs={{64,0},{65,1},{66,2},{67,3},{68,4},{69,5},{70,6},{71,7},{72,8},{73... | collective-permute-start | bytes 3145736 | tf_op jit(solution)/shard_map/ppermute | solution.py:220
  93.3 73.8 %collective-permute-start.10 = (f32[128,1024]{1,0:T(8,128)S(1)}, f32[128,1024]{1,0:T(8,128)S(1)}, u32[]{:S(2)}, u32[]{:S(2)}) collective-permute-start(f32[128,1024]{1,0:T(8,128)S(1)} %get-tuple-element.27), channel_id=1, source_target_pairs={{0,64},{64,0},{1,65},{65,1},{2,66},{66,2},{3,67},{67,3},{4,68},{68... | collective-permute-start | bytes 1572872 | tf_op jit(solution)/shard_map/ppermute | solution.py:222
  154.8 12.3 %copy-start.4 = (f32[16,2,16,2048]{3,2,1,0:T(8,128)S(1)}, f32[16,2,16,2048]{3,2,1,0:T(8,128)}, u32[]{:S(2)}) copy-start(f32[16,2,16,2048]{3,2,1,0:T(8,128)} %shard_map.110) | copy-start | bytes 12582916
  167.1 0.8 copy-start.13
  167.1 8.7 %copy-start.2 = (f32[512,1024]{1,0:T(8,128)S(1)}, f32[512,1024]{1,0:T(8,128)}, u32[]{:S(2)}) copy-start(f32[512,1024]{1,0:T(8,128)} %copy-done.1) | copy-start | bytes 6291460
  167.9 1.3 copy-start.3
  170.4 29.7 %collective-permute-start.21 = (f32[4,16,2048]{2,1,0:T(8,128)}, f32[4,16,2048]{2,1,0:T(8,128)}, u32[]{:S(2)}, u32[]{:S(2)}) collective-permute-start(f32[4,16,2048]{2,1,0:T(8,128)} %get-tuple-element.48), channel_id=1, source_target_pairs={{0,48},{16,0},{32,16},{48,32},{1,49},{17,1},{33,17},{49,33},{2,50}... | collective-permute-start | bytes 1572872 | tf_op jit(solution)/shard_map/ppermute | solution.py:184
  173.5 30.9 %collective-permute-start.20 = (f32[4,16,2048]{2,1,0:T(8,128)}, f32[4,16,2048]{2,1,0:T(8,128)}, u32[]{:S(2)}, u32[]{:S(2)}) collective-permute-start(f32[4,16,2048]{2,1,0:T(8,128)} %get-tuple-element.49), channel_id=1, source_target_pairs={{0,16},{16,32},{32,48},{48,0},{1,17},{17,33},{33,49},{49,1},{2,18}... | collective-permute-start | bytes 1572872 | tf_op jit(solution)/shard_map/ppermute | solution.py:184
  173.5 31.9 %collective-permute-start.19 = (f32[4,16,2048]{2,1,0:T(8,128)}, f32[4,16,2048]{2,1,0:T(8,128)}, u32[]{:S(2)}, u32[]{:S(2)}) collective-permute-start(f32[4,16,2048]{2,1,0:T(8,128)} %get-tuple-element.47), channel_id=1, source_target_pairs={{0,32},{16,48},{32,0},{48,16},{1,33},{17,49},{33,1},{49,17},{2,34}... | collective-permute-start | bytes 1572872 | tf_op jit(solution)/shard_map/ppermute | solution.py:184
  176.8 34.1 %collective-permute-start.8 = (f32[128,1024]{1,0:T(8,128)}, f32[128,1024]{1,0:T(8,128)S(1)}, u32[]{:S(2)}, u32[]{:S(2)}) collective-permute-start(f32[128,1024]{1,0:T(8,128)} %get-tuple-element.26), channel_id=1, source_target_pairs={{0,64},{64,0},{1,65},{65,1},{2,66},{66,2},{3,67},{67,3},{4,68},{68... | collective-permute-start | bytes 1572872 | tf_op jit(solution)/shard_map/ppermute | solution.py:223
  176.8 67.9 %collective-permute-start.6 = (f32[256,1024]{1,0:T(8,128)}, f32[256,1024]{1,0:T(8,128)S(1)}, u32[]{:S(2)}, u32[]{:S(2)}) collective-permute-start(f32[256,1024]{1,0:T(8,128)} %slice.84), channel_id=1, source_target_pairs={{0,64},{64,0},{1,65},{65,1},{2,66},{66,2},{3,67},{67,3},{4,68},{68... | collective-permute-start | bytes 3145736 | tf_op jit(solution)/shard_map/ppermute | solution.py:224
  200.1 25.0 %collective-permute-start.15 = (f32[4,16,2048]{2,1,0:T(8,128)S(1)}, f32[4,16,2048]{2,1,0:T(8,128)S(1)}, u32[]{:S(2)}, u32[]{:S(2)}) collective-permute-start(f32[4,16,2048]{2,1,0:T(8,128)S(1)} %get-tuple-element.45), channel_id=1, source_target_pairs={{0,6},{2,0},{4,2},{6,4},{1,7},{3,1},{5,3},{7,5},{8,14},{10,8},{12,... | collective-permute-start | bytes 1572872 | tf_op jit(solution)/shard_map/ppermute | solution.py:184
  204.4 20.7 %collective-permute-start.14 = (f32[4,16,2048]{2,1,0:T(8,128)S(1)}, f32[4,16,2048]{2,1,0:T(8,128)S(1)}, u32[]{:S(2)}, u32[]{:S(2)}) collective-permute-start(f32[4,16,2048]{2,1,0:T(8,128)S(1)} %get-tuple-element.46), channel_id=1, source_target_pairs={{0,2},{2,4},{4,6},{6,0},{1,3},{3,5},{5,7},{7,1},{8,10},{10,12},{12... | collective-permute-start | bytes 1572872 | tf_op jit(solution)/shard_map/ppermute | solution.py:184
  205.4 24.9 %collective-permute-start.13 = (f32[4,16,2048]{2,1,0:T(8,128)S(1)}, f32[4,16,2048]{2,1,0:T(8,128)S(1)}, u32[]{:S(2)}, u32[]{:S(2)}) collective-permute-start(f32[4,16,2048]{2,1,0:T(8,128)S(1)} %get-tuple-element.44), channel_id=1, source_target_pairs={{0,4},{2,6},{4,0},{6,2},{1,5},{3,7},{5,1},{7,3},{8,12},{10,14},{12... | collective-permute-start | bytes 1572872 | tf_op jit(solution)/shard_map/ppermute | solution.py:184
  210.9 19.3 %copy-start.14 = (f32[128,1024]{1,0:T(8,128)}, f32[128,1024]{1,0:T(8,128)S(1)}, u32[]{:S(2)}) copy-start(f32[128,1024]{1,0:T(8,128)S(1)} %collective-permute-done.8.got_ref) | copy-start | bytes 1572868
  211.0 25.1 %collective-permute-start.24 = (f32[16,2048]{1,0:T(8,128)S(1)}, f32[16,2048]{1,0:T(8,128)S(1)}, u32[]{:S(2)}, u32[]{:S(2)}) collective-permute-start(f32[16,2048]{1,0:T(8,128)S(1)} %get-tuple-element.36), channel_id=1, source_target_pairs={{0,6},{2,0},{4,2},{6,4},{1,7},{3,1},{5,3},{7,5},{8,14},{10,8},{12,... | collective-permute-start | bytes 393224 | tf_op jit(solution)/shard_map/ppermute | solution.py:184
  225.1 10.9 %collective-permute-start.23 = (f32[16,2048]{1,0:T(8,128)S(1)}, f32[16,2048]{1,0:T(8,128)S(1)}, u32[]{:S(2)}, u32[]{:S(2)}) collective-permute-start(f32[16,2048]{1,0:T(8,128)S(1)} %get-tuple-element.35), channel_id=1, source_target_pairs={{0,2},{2,4},{4,6},{6,0},{1,3},{3,5},{5,7},{7,1},{8,10},{10,12},{12... | collective-permute-start | bytes 393224 | tf_op jit(solution)/shard_map/ppermute | solution.py:184
  225.1 12.5 %collective-permute-start.22 = (f32[16,2048]{1,0:T(8,128)S(1)}, f32[16,2048]{1,0:T(8,128)S(1)}, u32[]{:S(2)}, u32[]{:S(2)}) collective-permute-start(f32[16,2048]{1,0:T(8,128)S(1)} %get-tuple-element.34), channel_id=1, source_target_pairs={{0,4},{2,6},{4,0},{6,2},{1,5},{3,7},{5,1},{7,3},{8,12},{10,14},{12... | collective-permute-start | bytes 393224 | tf_op jit(solution)/shard_map/ppermute | solution.py:184
  230.5 8.1 %collective-permute-start.18 = (f32[16,2048]{1,0:T(8,128)S(1)}, f32[16,2048]{1,0:T(8,128)S(1)}, u32[]{:S(2)}, u32[]{:S(2)}) collective-permute-start(f32[16,2048]{1,0:T(8,128)S(1)} %get-tuple-element.33), channel_id=1, source_target_pairs={{0,48},{16,0},{32,16},{48,32},{1,49},{17,1},{33,17},{49,33},{2,50}... | collective-permute-start | bytes 393224 | tf_op jit(solution)/shard_map/ppermute | solution.py:184
  236.1 7.6 %collective-permute-start.17 = (f32[16,2048]{1,0:T(8,128)S(1)}, f32[16,2048]{1,0:T(8,128)S(1)}, u32[]{:S(2)}, u32[]{:S(2)}) collective-permute-start(f32[16,2048]{1,0:T(8,128)S(1)} %get-tuple-element.32), channel_id=1, source_target_pairs={{0,16},{16,32},{32,48},{48,0},{1,17},{17,33},{33,49},{49,1},{2,18}... | collective-permute-start | bytes 393224 | tf_op jit(solution)/shard_map/ppermute | solution.py:184
  236.1 7.6 %collective-permute-start.16 = (f32[16,2048]{1,0:T(8,128)S(1)}, f32[16,2048]{1,0:T(8,128)S(1)}, u32[]{:S(2)}, u32[]{:S(2)}) collective-permute-start(f32[16,2048]{1,0:T(8,128)S(1)} %get-tuple-element.31), channel_id=1, source_target_pairs={{0,32},{16,48},{32,0},{48,16},{1,33},{17,49},{33,1},{49,17},{2,34}... | collective-permute-start | bytes 393224 | tf_op jit(solution)/shard_map/ppermute | solution.py:184
  244.8 8.9 %copy-start.8 = (f32[256,1024]{1,0:T(8,128)}, f32[256,1024]{1,0:T(8,128)S(1)}, u32[]{:S(2)}) copy-start(f32[256,1024]{1,0:T(8,128)S(1)} %collective-permute-done.6.got_ref) | copy-start | bytes 3145732
  244.8 16.1 %collective-permute-start.25 = (f32[2,16,2048]{2,1,0:T(8,128)S(1)}, f32[2,16,2048]{2,1,0:T(8,128)S(1)}, u32[]{:S(2)}, u32[]{:S(2)}) collective-permute-start(f32[2,16,2048]{2,1,0:T(8,128)S(1)} %select_bitcast_fusion), channel_id=1, source_target_pairs={{0,8},{8,0},{1,9},{9,1},{2,10},{10,2},{3,11},{11,3},{4,12},{12,4},... | collective-permute-start | bytes 786440 | tf_op jit(solution)/shard_map/ppermute | solution.py:244
  253.6 7.3 %copy-start.15 = (f32[1,16,2048]{2,1,0:T(8,128)S(1)}, f32[1,16,2048]{2,1,0:T(8,128)}, u32[]{:S(2)}) copy-start(f32[1,16,2048]{2,1,0:T(8,128)} %param.17) | copy-start | bytes 393220
  261.0 9.3 %collective-permute-start.26 = (f32[16,2048]{1,0:T(8,128)S(1)}, f32[16,2048]{1,0:T(8,128)S(1)}, u32[]{:S(2)}, u32[]{:S(2)}) collective-permute-start(f32[16,2048]{1,0:T(8,128)S(1)} %fusion.11), channel_id=1, source_target_pairs={{0,64},{64,0},{1,65},{65,1},{2,66},{66,2},{3,67},{67,3},{4,68},{68... | collective-permute-start | bytes 393224 | tf_op jit(solution)/shard_map/ppermute | solution.py:247
Sparse Core Ops, SparseCore 0:
  22.8 75.0 all-gather.1
Sparse Core Ops, SparseCore 1:
  110.3 89.9 reduce-scatter.3

commit v3 on v2

v3 whole, which is shorter than its diff:
```python
import jax
import jax.numpy as jnp
from jax import lax
from jax.experimental import pallas as pl
from jax.experimental.pallas import tpu as pltpu
from jax.sharding import Mesh
from jax.sharding import PartitionSpec as P

DP = ("y", "xl", "z", "core")
SWAP = [(0, 1), (1, 0)]
F32 = jnp.float32
BF16 = jnp.bfloat16
SMEM = pl.BlockSpec(memory_space=pltpu.SMEM)
TILE = 512
LATE = 8


def cost(flops, *arrays, weight=1):
    moved = sum(4 * a.size for a in arrays)
    return pl.CostEstimate(
        flops=weight * flops, bytes_accessed=weight * moved, transcendentals=0
    )


def params():
    return pltpu.CompilerParams(vmem_limit_bytes=56 * 1024 * 1024)


def after(value, *earlier):
    return lax.optimization_barrier((value, *earlier))[0]


def halves(a):
    high = a.astype(BF16)
    return high, (a - high.astype(F32)).astype(BF16)


def dot(left, right):
    return jnp.dot(left, right, preferred_element_type=F32)


def three_passes(left_high, left_low, right):
    high, low = halves(right)
    return dot(left_high, high) + dot(left_high, low) + dot(left_low, high)


def turn_kernel(core_ref, src, mine0, mine1, theirs):
    even = core_ref[0] == 0
    t = src[...].T
    for z in range(4):
        for k, mine in enumerate((mine0, mine1)):
            at = z * 32 + k * 8
            e, o = t[at : at + 8], t[at + 16 : at + 24]
            mine[0, z, 0] = jnp.where(even, e, o)
            theirs[k, 0, z, 0] = jnp.where(even, o, e)


def turned(core, share):
    tokens = share.shape[0]
    mine = jax.ShapeDtypeStruct((4, 4, 2, 8, tokens), F32)
    mine_spec = pl.BlockSpec((1, 4, 1, 8, tokens), lambda i: (i // 2, 0, i % 2, 0, 0))
    theirs_spec = pl.BlockSpec((2, 1, 4, 1, 8, tokens), lambda i: (0, i // 2, 0, i % 2, 0, 0))
    mine0, mine1, theirs = pl.pallas_call(
        turn_kernel,
        grid=(8,),
        in_specs=[SMEM, pl.BlockSpec((tokens, 128), lambda i: (0, i))],
        out_specs=[mine_spec, mine_spec, theirs_spec],
        out_shape=[mine, mine, jax.ShapeDtypeStruct((2, *mine.shape), F32)],
        cost_estimate=cost(0, share, share),
        compiler_params=params(),
    )(core, share)
    rows = 128 * 2
    return mine0.reshape(rows, tokens), mine1.reshape(rows, tokens), theirs.reshape(2, rows, tokens)


def right_of(is_first, g_ref, b_ref, go_ref, bo_ref, sent_refs):
    b, bo = b_ref[...], bo_ref[...]
    right = [g_ref[...] - jnp.where(is_first, 0.0, b), go_ref[...] - jnp.where(is_first, 0.0, bo)]
    right += [jnp.where(is_first, 0.0, ref[...]) for ref in sent_refs]
    return jnp.concatenate(right, axis=0), jnp.concatenate([b, bo], axis=0)


def x_kernel(split, p_ref, x_ref, a_ref, *refs):
    out, high, low = refs[-3:]
    got_refs, refs = (refs[:1], refs[1:]) if split else (refs[:2], refs[2:])
    width = x_ref.shape[1]
    is_first = p_ref[0] == 0

    @pl.when(pl.program_id(0) == 0)
    def _():
        x, got = x_ref[...], jnp.concatenate([ref[...] for ref in got_refs], axis=1)
        if split:
            col = lax.broadcasted_iota(jnp.int32, x.shape, 1)
            kept = jnp.logical_or(jnp.logical_not(is_first), col % 512 < 384)
            got = jnp.where(kept, got, 0.0)
        opened = x + got
        high[256:, :width], low[256:, :width] = halves(jnp.where(is_first, a_ref[...], opened))
        if split:
            opened = jnp.concatenate([opened, x[:, 384:512], x[:, 896:]], axis=1)
        high[:256], low[:256] = halves(opened)

    right, right_b = right_of(is_first, *refs[:4], refs[4:-3])
    shared = three_passes(high[256:, :width], low[256:, :width], right_b)
    out[0] = three_passes(high[:256], low[:256], right) - jnp.where(is_first, shared, 0.0)
    out[1] = shared


def a_kernel(split, p_ref, a_ref, early_ref, late_ref, s_ref, *refs):
    out, high, low = refs[-3:]
    is_first = p_ref[0] == 0

    @pl.when(pl.program_id(0) == 0)
    def _():
        a = a_ref[...]
        if split:
            zero = jnp.zeros((256, 128), F32)
            early, late = early_ref[...], late_ref[...]
            got = [early[:, 384:512], late[:, :256], zero, early[:, 896:], late[:, 256:], zero]
            second = jnp.where(is_first, jnp.concatenate(got, axis=1), a)
            second = jnp.concatenate([second, a[:, 384:512], a[:, 896:]], axis=1)
        else:
            second = jnp.where(is_first, late_ref[...], a)
        high[...], low[...] = halves(second)

    right, _ = right_of(is_first, *refs[:4], refs[4:-3])
    product = three_passes(high[...], low[...], right)
    out[:, 0] = (s_ref[0] - product).reshape(16, 16, product.shape[1])
    out[:, 1] = (s_ref[1] + product).reshape(16, 16, product.shape[1])


def right_specs(tokens, sent):
    right = pl.BlockSpec((tokens, TILE), lambda n: (0, n))
    per = sent[0].shape[1] // TILE if sent else 1
    part = pl.BlockSpec((128, TILE), lambda n: (n // per, n % per))
    return [right] * 4 + [part] * len(sent)


def x_parts(party, x, x_got, a, rights, sent, weight):
    tokens, ff = rights[0].shape
    left = pl.BlockSpec((256, 2 * tokens), lambda n: (0, 0))
    depth = 2 * tokens + 128 * len(sent)
    return pl.pallas_call(
        lambda *refs: x_kernel(bool(sent), *refs),
        grid=(ff // TILE,),
        in_specs=[SMEM, left, left]
        + [pl.BlockSpec(v.shape, lambda n: (0, 0)) for v in x_got]
        + right_specs(tokens, sent),
        out_specs=pl.BlockSpec((2, 256, TILE), lambda n: (0, 0, n)),
        out_shape=jax.ShapeDtypeStruct((2, 256, ff), F32),
        scratch_shapes=[pltpu.VMEM((512, depth), BF16)] * 2,
        cost_estimate=cost(3 * 2 * 512 * depth * ff, *rights, x, x, weight=weight),
        compiler_params=params(),
    )(party, x, a, *x_got, *rights, *sent)


def a_parts(party, a, early, late, s, rights, sent, weight):
    tokens, ff = rights[0].shape
    lefts = [pl.BlockSpec(v.shape, lambda n: (0, 0)) for v in (a, early, late)]
    depth = 2 * tokens + 128 * len(sent)
    return pl.pallas_call(
        lambda *refs: a_kernel(bool(sent), *refs),
        grid=(ff // TILE,),
        in_specs=[SMEM, *lefts, pl.BlockSpec((2, 256, TILE), lambda n: (0, 0, n))]
        + right_specs(tokens, sent),
        out_specs=pl.BlockSpec((16, 2, 16, TILE), lambda n: (0, 0, 0, n)),
        out_shape=jax.ShapeDtypeStruct((16, 2, 16, ff), F32),
        scratch_shapes=[pltpu.VMEM((256, depth), BF16)] * 2,
        cost_estimate=cost(3 * 2 * 256 * depth * ff, *rights, s, s, weight=weight),
        compiler_params=params(),
    )(party, a, early, late, s, *rights, *sent)


def store_split(value, high, low):
    for xl in range(2):
        cols = [value[:, (2 * y + xl) * 128 :][:, :128] for y in range(4)]
        high[:, xl * 512 : xl * 512 + 512], low[:, xl * 512 : xl * 512 + 512] = halves(
            jnp.concatenate(cols, axis=1)
        )


def add_product(c_ref, w0_ref, w1_ref, out, high, low):
    w = jnp.concatenate([w0_ref[...], w1_ref[...]], axis=0)
    out[...] = c_ref[...] + three_passes(high[...], low[...], w)


def local_kernel(a_ref, w0_ref, w1_ref, c_ref, out, high, low):
    @pl.when(pl.program_id(0) == 0)
    def _():
        store_split(a_ref[...], high, low)

    add_product(c_ref, w0_ref, w1_ref, out, high, low)


def opened_kernel(x_ref, a_ref, got_ref, w0_ref, w1_ref, c_ref, out, high, low):
    @pl.when(pl.program_id(0) == 0)
    def _():
        store_split((x_ref[...] - a_ref[...]) + got_ref[...], high, low)

    add_product(c_ref, w0_ref, w1_ref, out, high, low)


def forward_call(kernel, lefts, left_rows, weights, at, c, row, rows):
    ff = c.shape[1]
    d = lefts[0].shape[1]
    steps = ff // TILE
    out_spec = pl.BlockSpec((rows, TILE), lambda n: (row, n))
    return pl.pallas_call(
        kernel,
        grid=(steps,),
        in_specs=[pl.BlockSpec((rows, d), lambda n, r=r: (r, 0)) for r in left_rows]
        + [
            pl.BlockSpec((d // 2, TILE), lambda n: (0, at * steps + n)),
            pl.BlockSpec((d // 2, TILE), lambda n: (0, (at + 2) * steps + n)),
            out_spec,
        ],
        out_specs=out_spec,
        out_shape=jax.ShapeDtypeStruct(c.shape, F32),
        scratch_shapes=[pltpu.VMEM((rows, d), BF16)] * 2,
        cost_estimate=cost(3 * 2 * rows * d * ff, weights, c),
        input_output_aliases={len(lefts) + 2: 0} if rows != c.shape[0] else {},
        compiler_params=params(),
    )(*lefts, weights, weights, c)


def scattered_pair(a, a_axis, a_dim, b, b_axis, b_dim, first=(), last=()):
    sums, got = [], [[], []]
    for v, axis, dim in ((a, a_axis, a_dim), (b, b_axis, b_dim)):
        here = lax.axis_index(axis)
        sums.append(lax.dynamic_index_in_dim(v, here, dim, keepdims=False))
    for step in (2, 1, 3):
        for n, (v, axis, dim) in enumerate(((a, a_axis, a_dim), (b, b_axis, b_dim))):
            here = lax.axis_index(axis)
            piece = lax.dynamic_index_in_dim(v, (here + step) % 4, dim, keepdims=False)
            if len(got[n]) < 2:
                piece = after(piece, *first)
            else:
                piece = after(piece, got[n][0], *last)
            got[n].append(lax.ppermute(piece, axis, [(i, (i + step) % 4) for i in range(4)]))
    return [s + r[0] + r[1] + r[2] for s, r in zip(sums, got)]


def body(x_share, w_share, g_share, fwd_a, fwd_b, fwd_c, bwd_a, bwd_b, bwd_c):
    x, w, g = x_share[0], w_share[0], g_share[0]
    fa, fb, fc = fwd_a[0], fwd_b[0], fwd_c[0]
    ba, bb, bc = bwd_a[0], bwd_b[0], bwd_c[0]
    party = lax.axis_index("party")
    party0 = party == 0
    first = party0.astype(F32)
    party_id = party.astype(jnp.int32).reshape(1)
    core_id = lax.axis_index("core").astype(jnp.int32).reshape(1)
    xl0 = lax.axis_index("xl") == 0
    ff = w.shape[1]

    x_mine0, x_mine1, x_theirs = turned(core_id, x)
    x0 = lax.ppermute(x_mine0, "party", SWAP)
    x_other = lax.ppermute(x_theirs, "core", SWAP)
    xs0 = jnp.concatenate([x_mine0, x_other[0]], axis=1)
    xs1 = jnp.concatenate([x_mine1, x_other[1]], axis=1)
    x0_other = lax.ppermute(x_other[0], "party", SWAP)
    a_mine0, a_mine1, a_theirs = turned(core_id, after(ba, x_theirs))
    a_other = lax.ppermute(a_theirs, "core", SWAP)
    aa0 = jnp.concatenate([a_mine0, a_other[0]], axis=1)
    aa1 = jnp.concatenate([a_mine1, a_other[1]], axis=1)
    d = after(w - fb, a_theirs)
    d_party = lax.ppermute(d, "party", SWAP)
    near = lax.ppermute(jnp.concatenate([fb, d], axis=1), "xl", SWAP)
    d_across = lax.ppermute(d, ("party", "xl"), [(0, 3), (3, 0), (1, 2), (2, 1)])
    delta = d + d_party
    delta_near = near[:, ff:] + d_across
    packed = jnp.concatenate([fb + first * delta, delta], axis=1)
    packed_near = jnp.concatenate([near[:, :ff] + first * delta_near, delta_near], axis=1)
    weights = jnp.concatenate(
        [jnp.where(xl0, packed, packed_near), jnp.where(xl0, packed_near, packed)], axis=1
    )
    weights = lax.all_gather(after(weights, x0, x_other, a_other), ("y", "z", "core"), axis=0, tiled=True)

    last = g[3 * g.shape[0] // 4 :]
    last = jnp.concatenate([last[:, : ff // 2], last[:, ff // 2 :]], axis=0)
    a0_sent = jnp.where(party0, last, aa0)
    a0 = lax.ppermute(a0_sent, "party", SWAP)
    x1_sent = jnp.concatenate(
        [
            xs1[:, :384],
            jnp.where(party0, xs1[:, 384:512], aa1[:, :128]),
            xs1[:, 512:896],
            jnp.where(party0, xs1[:, 896:], aa1[:, 512:640]),
        ],
        axis=1,
    )
    x1 = lax.ppermute(x1_sent, "party", SWAP)
    a1 = jnp.concatenate([aa1[:, 128:384], aa1[:, 640:896]], axis=1)
    a1 = lax.ppermute(after(a1, x0_other), "party", [(1, 0)])
    u = x - fa
    half = x.shape[0] // 2
    u0 = lax.ppermute(after(u[: half // 2], a0), "party", SWAP)
    u1 = lax.ppermute(after(u[half // 2 : half], x1), "party", SWAP)
    u2 = lax.ppermute(after(u[half:], x1), "party", SWAP)

    g_other = lax.ppermute(after(g, x0, a0_sent), "core", SWAP)
    b_other = lax.ppermute(after(bb, x0, x1_sent), "core", SWAP)
    rights = (g, bb, g_other, b_other)
    early = x_parts(party_id, xs0, (x0, x0_other), aa0, rights, (), 1)
    sent = (a0, lax.ppermute(after(a0, early), "core", SWAP))
    early = a_parts(party_id, aa0, a0, a0, early, rights, (), 1)
    late = x_parts(party_id, xs1, (x1,), aa1, rights, sent, LATE)
    late = a_parts(party_id, aa1, x1, a1, late, rights, sent, LATE)

    early = lax.psum_scatter(early.reshape(16, 32, ff), ("y", "z"), scatter_dimension=0, tiled=True)
    early = early.reshape(2, 2, 8, ff)
    outputs = forward_call(local_kernel, (fa,), (0,), weights, 1, fc, 0, fc.shape[0])
    late = after(late, outputs).reshape(4, 4, 2, 16, ff)
    part0, part1 = scattered_pair(late[:, :, 0], "z", 1, late[:, :, 1], "y", 0, (), (u0,))
    part0, part1 = scattered_pair(part0, "y", 0, part1, "z", 0, (u1,))
    late = jnp.stack([part0, part1]).reshape(2, 2, 8, ff)
    both = jnp.concatenate([early, late], axis=2)
    keep = jnp.where(xl0, both[:, 0], both[:, 1])
    give = jnp.where(xl0, both[:, 1], both[:, 0])
    both = keep + lax.ppermute(after(give, u2), "xl", SWAP)
    give = jnp.where(party0, both[1] - bc, both[0])
    keep = jnp.where(party0, both[0] + bc, both[1])
    grad = keep + lax.ppermute(give, "party", SWAP)

    outputs = forward_call(opened_kernel, (x, fa, jnp.concatenate([u0, u1])), (0, 0, 0), weights, 0, outputs, 0, half)
    outputs = forward_call(opened_kernel, (x, fa, u2), (1, 1, 0), weights, 0, outputs, 1, half)
    return (outputs[None], grad[None])


def solution(mesh):
    split = Mesh(
        mesh.devices.reshape(mesh.shape["party"], 4, 2, 4, 2),
        ("party", *DP),
    )
    spec = P("party", DP, None)
    return jax.shard_map(
        body, mesh=split, in_specs=(spec,) * 9, out_specs=(spec, spec), check_vma=False
    )
```

time: 279 us -> 260 us (0.932)
  waiting for transfers between devices: 109 us -> 53.5 us
  Pallas kernels: 76.6 us -> 99.6 us
  local copies, waits for them, and re-layouts: 10 us -> 18.5 us
  starting transfers between devices: 48.8 us -> 54.4 us
    ppermute x22 -> x25, waiting for transfers between devices: 102 us -> 38.2 us  [the longest x12 22.3 us: scattered_pair(): lax.ppermute(piece, axis, [(i, (i + step) % 4) for i in range(4)])]
    pallas_call x3 -> x6, Pallas kernels: 40.8 us -> 68.9 us  [the longest x2 29.3 us: x_parts(): pl.pallas_call(lambda *refs: x_kernel(bool(sent), *refs), grid=(ff // TIL...]
    sub x2 -> x1, other arithmetic: 7.83 us -> 0.02 us  [body(): d = after(w - fb, a_theirs)]
    unnamed x32 -> x52, local copies, waits for them, and re-layouts: 2.65 us -> 10.2 us
    ppermute x1, waiting for transfers between devices: 0.01 us -> 7.28 us  [body(): lax.ppermute(d, ('party', 'xl'), [(0, 3), (3, 0), (1, 2), (2, 1)])]
    ppermute x22 -> x25, starting transfers between devices: 42.7 us -> 47.9 us  [the longest x12 28.3 us: scattered_pair(): lax.ppermute(piece, axis, [(i, (i + step) % 4) for i in range(4)])]
    pallas_call x4 -> x3, Pallas kernels: 35.9 us -> 30.7 us  [forward_call(): pl.pallas_call(kernel, grid=(steps,), in_specs=[pl.BlockSpec((rows, d), l...]
    concatenate x4 -> x7, other arithmetic: 2.31 us -> 7.38 us  [the longest x1 1.15 us: body(): aa0 = jnp.concatenate([a_mine0, a_other[0]], axis=1)]
  transfers between devices with their start and end apart: 29 -> 32, of which waited for: 10 -> 12; matrix products, arithmetic and copies ran while one was open for 8% -> 10% of each run, Pallas kernels for 28% -> 36%
where the time goes in v3:
time: 260 us; the launch traced here: 259 us
  Pallas kernels  99.6 us (38%)
  starting transfers between devices  54.4 us (21%)
  waiting for transfers between devices  53.5 us (21%)
  local copies, waits for them, and re-layouts  18.5 us (7%)
  other arithmetic  17.1 us (7%)
  between operations  15.9 us (6%)
    pallas_call x3, Pallas kernels, forward_call(): pl.pallas_call(kernel, grid=(steps,), in_specs=[pl.BlockSpec((rows, d), l...  30.7 us
    pallas_call x2, Pallas kernels, x_parts(): pl.pallas_call(lambda *refs: x_kernel(bool(sent), *refs), grid=(ff // TIL...  29.3 us
    ppermute x12, starting transfers between devices, scattered_pair(): lax.ppermute(piece, axis, [(i, (i + step) % 4) for i in range(4)])  28.3 us
    pallas_call x2, Pallas kernels, a_parts(): pl.pallas_call(lambda *refs: a_kernel(bool(sent), *refs), grid=(ff // TIL...  27.3 us
    ppermute x12, waiting for transfers between devices, scattered_pair(): lax.ppermute(piece, axis, [(i, (i + step) % 4) for i in range(4)])  22.3 us
    pallas_call x2, Pallas kernels, turned(): pl.pallas_call(turn_kernel, grid=(8,), in_specs=[SMEM, pl.BlockSpec((toke...  12.3 us
    unnamed x52, local copies, waits for them, and re-layouts  10.2 us
    ppermute x1, waiting for transfers between devices, body(): x0_other = lax.ppermute(x_other[0], 'party', SWAP)  8.6 us
  transfers between devices with their start and end apart: 32, of which 12 were waited for; matrix products, arithmetic and copies ran while one was open for 10% of the time, Pallas kernels for 36%

profile of v3, /device:TPU:0, one launch (start us, length us, event | category | flops | bytes accessed | tf_op | source)
XLA Modules:
  0.0 259.1 jit_solution(7947594744666666302)
XLA Ops:
  8.1 6.2 %shard_map.104 = (f32[4,4,2,8,512]{4,3,2,1,0:T(8,128)}, f32[4,4,2,8,512]{4,3,2,1,0:T(8,128)}, f32[2,4,4,2,8,512]{5,4,3,2,1,0:T(8,128)}) custom-call(s32[1]{0:T(128)} %bitcast.2.core_ref, f32[512,1024]{1,0:T(8,128)} %bitcast.136), custom_call_target="tpu_custom_call" | custom-call | bytes 4194304 | tf_op jit(solution)/shard_map/pallas_call | solution.py:63
  14.2 6.1 %shard_map.105 = (f32[4,4,2,8,512]{4,3,2,1,0:T(8,128)}, f32[4,4,2,8,512]{4,3,2,1,0:T(8,128)}, f32[2,4,4,2,8,512]{5,4,3,2,1,0:T(8,128)}) custom-call(s32[1]{0:T(128)} %bitcast.2.core_ref, f32[512,1024]{1,0:T(8,128)} %bitcast.155), custom_call_target="tpu_custom_call" | custom-call | bytes 4194304 | tf_op jit(solution)/shard_map/pallas_call | solution.py:63
  20.8 2.9 %collective-permute-start.6 = (f32[16,2048]{1,0:T(8,128)S(1)}, f32[16,2048]{1,0:T(8,128)}, u32[]{:S(2)}, u32[]{:S(2)}) collective-permute-start(f32[16,2048]{1,0:T(8,128)S(1)} %bitcast_subtract_fusion.1), channel_id=1, source_target_pairs={{0,72},{72,0},{8,64},{64,8},{1,73},{73,1},{9,65},{65,9},{2,74},{74... | collective-permute-start | bytes 393224 | tf_op jit(solution)/shard_map/ppermute | solution.py:267
  24.5 2.7 %collective-permute-start.7 = (f32[256,512]{1,0:T(8,128)S(1)}, f32[256,512]{1,0:T(8,128)}, u32[]{:S(2)}, u32[]{:S(2)}) collective-permute-start(f32[256,512]{1,0:T(8,128)S(1)} %bitcast.164), channel_id=1, source_target_pairs={{0,64},{64,0},{1,65},{65,1},{2,66},{66,2},{3,67},{67,3},{4,68},{68... | collective-permute-start | bytes 1572872 | tf_op jit(solution)/shard_map/ppermute | solution.py:255
  28.0 3.6 %collective-permute-done.4 = f32[16,2048]{1,0:T(8,128)S(1)} collective-permute-done((f32[16,2048]{1,0:T(8,128)S(1)}, f32[16,2048]{1,0:T(8,128)S(1)}, u32[]{:S(2)}, u32[]{:S(2)}) %collective-permute-start.4) | collective-permute-done | bytes 131104 | tf_op jit(solution)/shard_map/ppermute | solution.py:265
  33.5 7.3 %collective-permute-done.6 = f32[16,2048]{1,0:T(8,128)} collective-permute-done((f32[16,2048]{1,0:T(8,128)S(1)}, f32[16,2048]{1,0:T(8,128)}, u32[]{:S(2)}, u32[]{:S(2)}) %collective-permute-start.6) | collective-permute-done | bytes 131104 | tf_op jit(solution)/shard_map/ppermute | solution.py:267
  40.7 4.3 %collective-permute-done.5 = f32[16,4096]{1,0:T(8,128)S(1)} collective-permute-done((f32[16,4096]{1,0:T(8,128)}, f32[16,4096]{1,0:T(8,128)S(1)}, u32[]{:S(2)}, u32[]{:S(2)}) %collective-permute-start.5) | collective-permute-done | bytes 262176 | tf_op jit(solution)/shard_map/ppermute | solution.py:266
  48.1 1.3 slice_bitcast_fusion
  51.9 1.4 copy-done.3
  54.4 1.4 copy-done.2
  56.4 3.1 %collective-permute-start.11 = (f32[256,512]{1,0:T(8,128)S(1)}, f32[256,512]{1,0:T(8,128)S(1)}, u32[]{:S(2)}, u32[]{:S(2)}) collective-permute-start(f32[256,512]{1,0:T(8,128)S(1)} %get-tuple-element.70), channel_id=1, source_target_pairs={{0,64},{64,0},{1,65},{65,1},{2,66},{66,2},{3,67},{67,3},{4,68},{68... | collective-permute-start | bytes 1572872 | tf_op jit(solution)/shard_map/ppermute | solution.py:259
  59.9 3.1 %collective-permute-start.2 = (f32[256,1024]{1,0:T(8,128)}, f32[256,1024]{1,0:T(8,128)}, u32[]{:S(2)}, u32[]{:S(2)}) collective-permute-start(f32[256,1024]{1,0:T(8,128)} %pad_maximum_fusion), channel_id=1, source_target_pairs={{0,64},{64,0},{1,65},{65,1},{2,66},{66,2},{3,67},{67,3},{4,68},{68... | collective-permute-start | bytes 3145736 | tf_op jit(solution)/shard_map/ppermute | solution.py:290
  64.1 8.6 %collective-permute-done.11.refs_4_ = f32[256,512]{1,0:T(8,128)S(1)} collective-permute-done((f32[256,512]{1,0:T(8,128)S(1)}, f32[256,512]{1,0:T(8,128)S(1)}, u32[]{:S(2)}, u32[]{:S(2)}) %collective-permute-start.11) | collective-permute-done | bytes 524320 | tf_op jit(solution)/shard_map/ppermute | solution.py:259
  72.7 2.0 copy-done.4
  74.7 1.3 copy-done.5
  76.1 14.5 %shard_map.109.refs_4_ = f32[2,256,2048]{2,1,0:T(8,128)} custom-call(s32[1]{0:T(128)} %bitcast.18.refs_0_, f32[256,1024]{1,0:T(8,128)} %pad_maximum_fusion.3.refs_1_, f32[256,1024]{1,0:T(8,128)} %get-tuple-element.68.refs_2_.refs_1_, f32[256,512]{1,0:T(8,128)} %collective-permute-done.7.refs_3_, f32[256,512]{1,0:T(8,128)} %copy-done.22, ...), custom_call_target="tpu_custom_call" | custom-call | flops 6442450944 | bytes 18874368 | tf_op jit(solution)/shard_map/pallas_call | solution.py:142
  90.6 4.6 %collective-permute-done.8.refs_2_.refs_3_.refs_8_.refs_9_ = f32[256,1024]{1,0:T(8,128)} collective-permute-done((f32[256,1024]{1,0:T(8,128)S(1)}, f32[256,1024]{1,0:T(8,128)}, u32[]{:S(2)}, u32[]{:S(2)}) %collective-permute-start.8) | collective-permute-done | bytes 1048608 | tf_op jit(solution)/shard_map/ppermute | solution.py:280
  99.8 1.3 collective-permute-start.14
  101.1 4.4 %collective-permute-start.9 = (f32[128,1024]{1,0:T(8,128)}, f32[128,1024]{1,0:T(8,128)S(1)}, u32[]{:S(2)}, u32[]{:S(2)}) collective-permute-start(f32[128,1024]{1,0:T(8,128)} %get-tuple-element.38), channel_id=1, source_target_pairs={{0,64},{64,0},{1,65},{65,1},{2,66},{66,2},{3,67},{67,3},{4,68},{68... | collective-permute-start | bytes 1572872 | tf_op jit(solution)/shard_map/ppermute | solution.py:295
  105.5 13.7 %shard_map.110 = f32[16,2,16,2048]{3,2,1,0:T(8,128)} custom-call(s32[1]{0:T(128)} %bitcast.18.refs_0_, f32[256,1024]{1,0:T(8,128)} %get-tuple-element.68.refs_2_.refs_1_, f32[256,1024]{1,0:T(8,128)} %collective-permute-done.8.refs_2_.refs_3_.refs_8_.refs_9_, f32[256,1024]{1,0:T(8,128)} %collective-permute-done.8.refs_2_.refs_3_.refs_8_.refs_9_, ...), custom_call_target="tpu_custom_call" | custom-call | flops 3221225472 | bytes 25165824 | tf_op jit(solution)/shard_map/pallas_call | solution.py:160
  119.3 14.8 %shard_map.111.refs_4_ = f32[2,256,2048]{2,1,0:T(8,128)} custom-call(s32[1]{0:T(128)} %bitcast.18.refs_0_, f32[256,1024]{1,0:T(8,128)} %pad_maximum_fusion.5.refs_1_, f32[256,1024]{1,0:T(8,128)} %pad_maximum_fusion.4.refs_2_.refs_1_, f32[256,1024]{1,0:T(8,128)} %collective-permute-done.2.refs_3_.refs_2_, f32[512,2048]{1,0:T(8,128)} %bitcast.144, ...), custom_call_target="tpu_custom_call" | custom-call | flops 64424509440 | bytes 150994944 | tf_op jit(solution)/shard_map/pallas_call | solution.py:142
  134.9 13.7 %shard_map.112 = f32[16,2,16,2048]{3,2,1,0:T(8,128)} custom-call(s32[1]{0:T(128)} %bitcast.18.refs_0_, f32[256,1024]{1,0:T(8,128)} %pad_maximum_fusion.4.refs_2_.refs_1_, f32[256,1024]{1,0:T(8,128)} %collective-permute-done.2.refs_3_.refs_2_, f32[256,512]{1,0:T(8,128)} %copy-done.25, f32[2,256,2048]{2,1,0:T(8,128)} %shard_map.111.refs_4_, ...), custom_call_target="tpu_custom_call" | custom-call | flops 32212254720 | bytes 201326592 | tf_op jit(solution)/shard_map/pallas_call | solution.py:160
  148.5 12.3 %shard_map.106.c_ref = f32[512,2048]{1,0:T(8,128)} custom-call(f32[512,1024]{1,0:T(8,128)} %bitcast.139, f32[512,8192]{1,0:T(8,128)} %all-gather.2.cloned.1.call-done.w0_ref.w1_ref, f32[512,8192]{1,0:T(8,128)} %all-gather.2.cloned.1.call-done.w0_ref.w1_ref, f32[512,2048]{1,0:T(8,128)} %bitcast.154), custom_call_target="tpu_custom_call" | custom-call | flops 6442450944 | bytes 20971520 | tf_op jit(solution)/shard_map/pallas_call | solution.py:207
  160.8 1.7 fusion.18
  162.5 1.4 copy-done.6
  165.1 3.6 %collective-permute-start.16 = (f32[4,16,2048]{2,1,0:T(8,128)S(1)}, f32[4,16,2048]{2,1,0:T(8,128)}, u32[]{:S(2)}, u32[]{:S(2)}) collective-permute-start(f32[4,16,2048]{2,1,0:T(8,128)S(1)} %get-tuple-element.62), channel_id=1, source_target_pairs={{0,4},{2,6},{4,0},{6,2},{1,5},{3,7},{5,1},{7,3},{8,12},{10,14},{12... | collective-permute-start | bytes 1572872 | tf_op jit(solution)/shard_map/ppermute | solution.py:238
  168.7 2.6 %dynamic-slice_bitcast_fusion.1 = (f32[4,16,2048]{2,1,0:T(8,128)}, f32[4,16,2048]{2,1,0:T(8,128)}, f32[4,16,2048]{2,1,0:T(8,128)}) fusion(f32[4,4,1,16,2048]{4,3,2,1,0:T(8,128)} %get-tuple-element.59, s32[]{:T(128)S(6)} %select_n.157, s32[]{:T(128)S(6)} %select_n.159, s32[]{:T(128)S(6)} %select_n.155), kind=kLoop, calls=%fused_computation.22 | loop fusion | bytes 3145740 | tf_op jit(solution)/shard_map/jit(dynamic_index_in_dim)/squeeze | solution.py:233
  171.3 3.2 %collective-permute-start.22 = (f32[4,16,2048]{2,1,0:T(8,128)}, f32[4,16,2048]{2,1,0:T(8,128)}, u32[]{:S(2)}, u32[]{:S(2)}) collective-permute-start(f32[4,16,2048]{2,1,0:T(8,128)} %get-tuple-element.65), channel_id=1, source_target_pairs={{0,32},{16,48},{32,0},{48,16},{1,33},{17,49},{33,1},{49,17},{2,34}... | collective-permute-start | bytes 1572872 | tf_op jit(solution)/shard_map/ppermute | solution.py:238
  175.3 7.6 %collective-permute-done.16 = f32[4,16,2048]{2,1,0:T(8,128)} collective-permute-done((f32[4,16,2048]{2,1,0:T(8,128)S(1)}, f32[4,16,2048]{2,1,0:T(8,128)}, u32[]{:S(2)}, u32[]{:S(2)}) %collective-permute-start.16) | collective-permute-done | bytes 524320 | tf_op jit(solution)/shard_map/ppermute | solution.py:238
  182.9 2.6 %collective-permute-start.18 = (f32[4,16,2048]{2,1,0:T(8,128)}, f32[4,16,2048]{2,1,0:T(8,128)}, u32[]{:S(2)}, u32[]{:S(2)}) collective-permute-start(f32[4,16,2048]{2,1,0:T(8,128)} %get-tuple-element.45), channel_id=1, source_target_pairs={{0,6},{2,0},{4,2},{6,4},{1,7},{3,1},{5,3},{7,5},{8,14},{10,8},{12,... | collective-permute-start | bytes 1572872 | tf_op jit(solution)/shard_map/ppermute | solution.py:238
  186.8 2.5 collective-permute-start.3
  189.2 1.5 collective-permute-start.23
  190.8 3.1 %collective-permute-done.17 = f32[4,16,2048]{2,1,0:T(8,128)} collective-permute-done((f32[4,16,2048]{2,1,0:T(8,128)}, f32[4,16,2048]{2,1,0:T(8,128)}, u32[]{:S(2)}, u32[]{:S(2)}) %collective-permute-start.17) | collective-permute-done | bytes 524320 | tf_op jit(solution)/shard_map/ppermute | solution.py:238
  193.9 2.7 %collective-permute-start.24 = (f32[4,16,2048]{2,1,0:T(8,128)}, f32[4,16,2048]{2,1,0:T(8,128)S(1)}, u32[]{:S(2)}, u32[]{:S(2)}) collective-permute-start(f32[4,16,2048]{2,1,0:T(8,128)} %get-tuple-element.49), channel_id=1, source_target_pairs={{0,48},{16,0},{32,16},{48,32},{1,49},{17,1},{33,17},{49,33},{2,50}... | collective-permute-start | bytes 1572872 | tf_op jit(solution)/shard_map/ppermute | solution.py:238
  196.6 1.3 collective-permute-done.18
  197.9 1.6 fusion.3
  199.6 2.7 %collective-permute-done.10 = f32[128,1024]{1,0:T(8,128)S(1)} collective-permute-done((f32[128,1024]{1,0:T(8,128)}, f32[128,1024]{1,0:T(8,128)S(1)}, u32[]{:S(2)}, u32[]{:S(2)}) %collective-permute-start.10) | collective-permute-done | bytes 524320 | tf_op jit(solution)/shard_map/ppermute | solution.py:296
  202.3 1.5 collective-permute-start.20
  203.8 2.8 %collective-permute-start.19 = (f32[16,2048]{1,0:T(8,128)S(1)}, f32[16,2048]{1,0:T(8,128)S(1)}, u32[]{:S(2)}, u32[]{:S(2)}) collective-permute-start(f32[16,2048]{1,0:T(8,128)S(1)} %get-tuple-element.46), channel_id=1, source_target_pairs={{0,32},{16,48},{32,0},{48,16},{1,33},{17,49},{33,1},{49,17},{2,34}... | collective-permute-start | bytes 393224 | tf_op jit(solution)/shard_map/ppermute | solution.py:238
  206.6 2.2 collective-permute-done.23
  208.8 5.2 %collective-permute-done.24 = f32[4,16,2048]{2,1,0:T(8,128)S(1)} collective-permute-done((f32[4,16,2048]{2,1,0:T(8,128)}, f32[4,16,2048]{2,1,0:T(8,128)S(1)}, u32[]{:S(2)}, u32[]{:S(2)}) %collective-permute-start.24) | collective-permute-done | bytes 524320 | tf_op jit(solution)/shard_map/ppermute | solution.py:238
  214.0 1.3 fusion.1
  216.3 5.3 %collective-permute-start.21 = (f32[16,2048]{1,0:T(8,128)S(1)}, f32[16,2048]{1,0:T(8,128)S(1)}, u32[]{:S(2)}, u32[]{:S(2)}) collective-permute-start(f32[16,2048]{1,0:T(8,128)S(1)} %get-tuple-element.48), channel_id=1, source_target_pairs={{0,48},{16,0},{32,16},{48,32},{1,49},{17,1},{33,17},{49,33},{2,50}... | collective-permute-start | bytes 393224 | tf_op jit(solution)/shard_map/ppermute | solution.py:238
  222.7 3.2 %collective-permute-start.27 = (f32[16,2048]{1,0:T(8,128)S(1)}, f32[16,2048]{1,0:T(8,128)S(1)}, u32[]{:S(2)}, u32[]{:S(2)}) collective-permute-start(f32[16,2048]{1,0:T(8,128)S(1)} %get-tuple-element.52), channel_id=1, source_target_pairs={{0,6},{2,0},{4,2},{6,4},{1,7},{3,1},{5,3},{7,5},{8,14},{10,8},{12,... | collective-permute-start | bytes 393224 | tf_op jit(solution)/shard_map/ppermute | solution.py:238
  226.0 2.9 %collective-permute-done.26 = f32[16,2048]{1,0:T(8,128)S(1)} collective-permute-done((f32[16,2048]{1,0:T(8,128)S(1)}, f32[16,2048]{1,0:T(8,128)S(1)}, u32[]{:S(2)}, u32[]{:S(2)}) %collective-permute-start.26) | collective-permute-done | bytes 131104 | tf_op jit(solution)/shard_map/ppermute | solution.py:238
  230.0 1.6 collective-permute-start.28
  231.6 9.2 %shard_map.107.c_ref = f32[512,2048]{1,0:T(8,128)} custom-call(f32[512,1024]{1,0:T(8,128)} %bitcast.137, f32[512,1024]{1,0:T(8,128)} %bitcast.140, f32[256,1024]{1,0:T(8,128)} %pad_maximum_fusion.2.got_ref, f32[512,8192]{1,0:T(8,128)} %all-gather.2.cloned.1.call-done.w0_ref.w1_ref, ...), custom_call_target="tpu_custom_call", output_to_operand_aliasing={{}: (5, {})} | custom-call | flops 3221225472 | bytes 20971520 | tf_op jit(solution)/shard_map/pallas_call | solution.py:207
  241.7 9.2 %shard_map.108 = f32[512,2048]{1,0:T(8,128)} custom-call(f32[512,1024]{1,0:T(8,128)} %bitcast.138, f32[512,1024]{1,0:T(8,128)} %bitcast.141, f32[256,1024]{1,0:T(8,128)} %copy-done.13, f32[512,8192]{1,0:T(8,128)} %all-gather.2.cloned.1.call-done.w0_ref.w1_ref, ...), custom_call_target="tpu_custom_call", output_to_operand_aliasing={{}: (5, {})} | custom-call | flops 3221225472 | bytes 20971520 | tf_op jit(solution)/shard_map/pallas_call | solution.py:207
  (119 shorter events, 25.9 us)
Async XLA Ops:
  8.0 140.5 %all-gather.2.cloned.1.call-start = ((), (), s32[]{:S(2)}) async-start(), calls=%async_computation.1 | async-start | bytes 17301504 | tf_op jit(solution)/shard_map/all_gather | solution.py:275
  8.0 12.7 %copy-start.12 = (f32[1,16,2048]{2,1,0:T(8,128)S(1)}, f32[1,16,2048]{2,1,0:T(8,128)}, u32[]{:S(2)}) copy-start(f32[1,16,2048]{2,1,0:T(8,128)} %param.13) | copy-start | bytes 393220
  8.1 12.7 %copy-start.23 = (f32[1,16,2048]{2,1,0:T(8,128)S(1)}, f32[1,16,2048]{2,1,0:T(8,128)}, u32[]{:S(2)}) copy-start(f32[1,16,2048]{2,1,0:T(8,128)} %param.10) | copy-start | bytes 393220
  14.2 10.3 %copy-start.20 = (f32[4,4,2,8,512]{4,3,2,1,0:T(8,128)S(1)}, f32[4,4,2,8,512]{4,3,2,1,0:T(8,128)}, u32[]{:S(2)}) copy-start(f32[4,4,2,8,512]{4,3,2,1,0:T(8,128)} %get-tuple-element.35) | copy-start | bytes 1572868
  14.2 32.6 %collective-permute-start = (f32[2,256,512]{2,1,0:T(8,128)}, f32[2,256,512]{2,1,0:T(8,128)S(1)}, u32[]{:S(2)}, u32[]{:S(2)}) collective-permute-start(f32[2,256,512]{2,1,0:T(8,128)} %bitcast.167), channel_id=1, source_target_pairs={{0,1},{1,0},{2,3},{3,2},{4,5},{5,4},{6,7},{7,6},{8,9},{9,8},{10,11... | collective-permute-start | bytes 3145736 | tf_op jit(solution)/shard_map/ppermute | solution.py:256
  20.3 26.5 %collective-permute-start.1 = (f32[2,256,512]{2,1,0:T(8,128)}, f32[2,256,512]{2,1,0:T(8,128)S(1)}, u32[]{:S(2)}, u32[]{:S(2)}) collective-permute-start(f32[2,256,512]{2,1,0:T(8,128)} %bitcast.168), channel_id=1, source_target_pairs={{0,1},{1,0},{2,3},{3,2},{4,5},{5,4},{6,7},{7,6},{8,9},{9,8},{10,11... | collective-permute-start | bytes 3145736 | tf_op jit(solution)/shard_map/ppermute | solution.py:261
  20.8 20.0 %collective-permute-start.6 = (f32[16,2048]{1,0:T(8,128)S(1)}, f32[16,2048]{1,0:T(8,128)}, u32[]{:S(2)}, u32[]{:S(2)}) collective-permute-start(f32[16,2048]{1,0:T(8,128)S(1)} %bitcast_subtract_fusion.1), channel_id=1, source_target_pairs={{0,72},{72,0},{8,64},{64,8},{1,73},{73,1},{9,65},{65,9},{2,74},{74... | collective-permute-start | bytes 393224 | tf_op jit(solution)/shard_map/ppermute | solution.py:267
  23.7 7.9 %collective-permute-start.4 = (f32[16,2048]{1,0:T(8,128)S(1)}, f32[16,2048]{1,0:T(8,128)S(1)}, u32[]{:S(2)}, u32[]{:S(2)}) collective-permute-start(f32[16,2048]{1,0:T(8,128)S(1)} %bitcast_subtract_fusion.1), channel_id=1, source_target_pairs={{0,64},{64,0},{1,65},{65,1},{2,66},{66,2},{3,67},{67,3},{4,68},{68... | collective-permute-start | bytes 393224 | tf_op jit(solution)/shard_map/ppermute | solution.py:265
  24.5 22.3 %collective-permute-start.7 = (f32[256,512]{1,0:T(8,128)S(1)}, f32[256,512]{1,0:T(8,128)}, u32[]{:S(2)}, u32[]{:S(2)}) collective-permute-start(f32[256,512]{1,0:T(8,128)S(1)} %bitcast.164), channel_id=1, source_target_pairs={{0,64},{64,0},{1,65},{65,1},{2,66},{66,2},{3,67},{67,3},{4,68},{68... | collective-permute-start | bytes 1572872 | tf_op jit(solution)/shard_map/ppermute | solution.py:255
  28.0 19.0 %copy-start.8 = (f32[4,4,2,8,512]{4,3,2,1,0:T(8,128)S(1)}, f32[4,4,2,8,512]{4,3,2,1,0:T(8,128)}, u32[]{:S(2)}) copy-start(f32[4,4,2,8,512]{4,3,2,1,0:T(8,128)} %get-tuple-element.28) | copy-start | bytes 1572868
  32.3 12.8 %collective-permute-start.5 = (f32[16,4096]{1,0:T(8,128)}, f32[16,4096]{1,0:T(8,128)S(1)}, u32[]{:S(2)}, u32[]{:S(2)}) collective-permute-start(f32[16,4096]{1,0:T(8,128)} %pad_maximum_fusion.9), channel_id=1, source_target_pairs={{0,8},{8,0},{1,9},{9,1},{2,10},{10,2},{3,11},{11,3},{4,12},{12,4},... | collective-permute-start | bytes 786440 | tf_op jit(solution)/shard_map/ppermute | solution.py:266
  46.9 182.0 %reduce-scatter.4.cloned.1.call-start = ((), (), s32[]{:S(2)}) async-start(), calls=%async_computation.2 | async-start | bytes 4456448
  49.6 3.7 %copy-start.16 = (f32[4,4,2,8,512]{4,3,2,1,0:T(8,128)S(1)}, f32[4,4,2,8,512]{4,3,2,1,0:T(8,128)}, u32[]{:S(2)}) copy-start(f32[4,4,2,8,512]{4,3,2,1,0:T(8,128)} %get-tuple-element.37) | copy-start | bytes 1572868
  49.6 13.4 %copy-start.21 = (f32[4,4,2,8,512]{4,3,2,1,0:T(8,128)S(1)}, f32[4,4,2,8,512]{4,3,2,1,0:T(8,128)}, u32[]{:S(2)}) copy-start(f32[4,4,2,8,512]{4,3,2,1,0:T(8,128)} %get-tuple-element.35) | copy-start | bytes 1572868
  53.3 19.4 %collective-permute-start.13 = (f32[512,2048]{1,0:T(8,128)S(1)}, f32[512,2048]{1,0:T(8,128)S(1)}, u32[]{:S(2)}, u32[]{:S(2)}) collective-permute-start(f32[512,2048]{1,0:T(8,128)S(1)} %bitcast.152), channel_id=1, source_target_pairs={{0,1},{1,0},{2,3},{3,2},{4,5},{5,4},{6,7},{7,6},{8,9},{9,8},{10,11... | collective-permute-start | bytes 12582920 | tf_op jit(solution)/shard_map/ppermute | solution.py:300
  55.8 16.8 %collective-permute-start.12 = (f32[512,2048]{1,0:T(8,128)S(1)}, f32[512,2048]{1,0:T(8,128)S(1)}, u32[]{:S(2)}, u32[]{:S(2)}) collective-permute-start(f32[512,2048]{1,0:T(8,128)S(1)} %bitcast.146), channel_id=1, source_target_pairs={{0,1},{1,0},{2,3},{3,2},{4,5},{5,4},{6,7},{7,6},{8,9},{9,8},{10,11... | collective-permute-start | bytes 12582920 | tf_op jit(solution)/shard_map/ppermute | solution.py:299
  56.4 16.3 %collective-permute-start.11 = (f32[256,512]{1,0:T(8,128)S(1)}, f32[256,512]{1,0:T(8,128)S(1)}, u32[]{:S(2)}, u32[]{:S(2)}) collective-permute-start(f32[256,512]{1,0:T(8,128)S(1)} %get-tuple-element.70), channel_id=1, source_target_pairs={{0,64},{64,0},{1,65},{65,1},{2,66},{66,2},{3,67},{67,3},{4,68},{68... | collective-permute-start | bytes 1572872 | tf_op jit(solution)/shard_map/ppermute | solution.py:259
  59.5 35.8 %collective-permute-start.8 = (f32[256,1024]{1,0:T(8,128)S(1)}, f32[256,1024]{1,0:T(8,128)}, u32[]{:S(2)}, u32[]{:S(2)}) collective-permute-start(f32[256,1024]{1,0:T(8,128)S(1)} %get-tuple-element.69), channel_id=1, source_target_pairs={{0,64},{64,0},{1,65},{65,1},{2,66},{66,2},{3,67},{67,3},{4,68},{68... | collective-permute-start | bytes 3145736 | tf_op jit(solution)/shard_map/ppermute | solution.py:280
  59.9 59.4 %collective-permute-start.2 = (f32[256,1024]{1,0:T(8,128)}, f32[256,1024]{1,0:T(8,128)}, u32[]{:S(2)}, u32[]{:S(2)}) collective-permute-start(f32[256,1024]{1,0:T(8,128)} %pad_maximum_fusion), channel_id=1, source_target_pairs={{0,64},{64,0},{1,65},{65,1},{2,66},{66,2},{3,67},{67,3},{4,68},{68... | collective-permute-start | bytes 3145736 | tf_op jit(solution)/shard_map/ppermute | solution.py:290
  72.7 3.4 %copy-start.22 = (f32[256,512]{1,0:T(8,128)}, f32[256,512]{1,0:T(8,128)S(1)}, u32[]{:S(2)}) copy-start(f32[256,512]{1,0:T(8,128)S(1)} %collective-permute-done.11.refs_4_) | copy-start | bytes 1572868
  72.7 3.4 %copy-start.5 = (f32[512,2048]{1,0:T(8,128)}, f32[512,2048]{1,0:T(8,128)S(1)}, u32[]{:S(2)}) copy-start(f32[512,2048]{1,0:T(8,128)S(1)} %collective-permute-done.12.refs_7_.refs_6_) | copy-start | bytes 12582916
  76.1 19.1 %copy-start = (f32[1,512,1024]{2,1,0:T(8,128)S(1)}, f32[1,512,1024]{2,1,0:T(8,128)}, u32[]{:S(2)}) copy-start(f32[1,512,1024]{2,1,0:T(8,128)} %param.9) | copy-start | bytes 6291460
  76.1 19.1 %copy-start.1 = (f32[1,512,1024]{2,1,0:T(8,128)S(1)}, f32[1,512,1024]{2,1,0:T(8,128)}, u32[]{:S(2)}) copy-start(f32[1,512,1024]{2,1,0:T(8,128)} %param.12) | copy-start | bytes 6291460
  90.6 5.0 %copy-start.10 = (f32[4,4,2,8,512]{4,3,2,1,0:T(8,128)S(1)}, f32[4,4,2,8,512]{4,3,2,1,0:T(8,128)}, u32[]{:S(2)}) copy-start(f32[4,4,2,8,512]{4,3,2,1,0:T(8,128)} %get-tuple-element.31) | copy-start | bytes 1572868
  95.2 24.0 %collective-permute-start.15 = (f32[256,1024]{1,0:T(8,128)}, f32[256,1024]{1,0:T(8,128)}, u32[]{:S(2)}, u32[]{:S(2)}) collective-permute-start(f32[256,1024]{1,0:T(8,128)} %collective-permute-done.8.refs_2_.refs_3_.refs_8_.refs_9_), channel_id=1, source_target_pairs={{0,1},{1,0},{2,3},{3,2},{4,5},{5,4},{6,7},{7,6},{8,9},{9,8},{10,11... | collective-permute-start | bytes 3145736 | tf_op jit(solution)/shard_map/ppermute | solution.py:303
  99.8 34.3 %collective-permute-start.14 = (f32[256,512]{1,0:T(8,128)}, f32[256,512]{1,0:T(8,128)S(1)}, u32[]{:S(2)}, u32[]{:S(2)}) collective-permute-start(f32[256,512]{1,0:T(8,128)} %pad_maximum_fusion.7), channel_id=1, source_target_pairs={{64,0},{65,1},{66,2},{67,3},{68,4},{69,5},{70,6},{71,7},{72,8},{73... | collective-permute-start | bytes 1572872 | tf_op jit(solution)/shard_map/ppermute | solution.py:292
  101.1 74.2 %collective-permute-start.9 = (f32[128,1024]{1,0:T(8,128)}, f32[128,1024]{1,0:T(8,128)S(1)}, u32[]{:S(2)}, u32[]{:S(2)}) collective-permute-start(f32[128,1024]{1,0:T(8,128)} %get-tuple-element.38), channel_id=1, source_target_pairs={{0,64},{64,0},{1,65},{65,1},{2,66},{66,2},{3,67},{67,3},{4,68},{68... | collective-permute-start | bytes 1572872 | tf_op jit(solution)/shard_map/ppermute | solution.py:295
  148.5 12.3 %copy-start.7 = (f32[16,2,16,2048]{3,2,1,0:T(8,128)S(1)}, f32[16,2,16,2048]{3,2,1,0:T(8,128)}, u32[]{:S(2)}) copy-start(f32[16,2,16,2048]{3,2,1,0:T(8,128)} %shard_map.112) | copy-start | bytes 12582916
  165.1 17.8 %collective-permute-start.16 = (f32[4,16,2048]{2,1,0:T(8,128)S(1)}, f32[4,16,2048]{2,1,0:T(8,128)}, u32[]{:S(2)}, u32[]{:S(2)}) collective-permute-start(f32[4,16,2048]{2,1,0:T(8,128)S(1)} %get-tuple-element.62), channel_id=1, source_target_pairs={{0,4},{2,6},{4,0},{6,2},{1,5},{3,7},{5,1},{7,3},{8,12},{10,14},{12... | collective-permute-start | bytes 1572872 | tf_op jit(solution)/shard_map/ppermute | solution.py:238
  171.3 18.0 %collective-permute-start.22 = (f32[4,16,2048]{2,1,0:T(8,128)}, f32[4,16,2048]{2,1,0:T(8,128)}, u32[]{:S(2)}, u32[]{:S(2)}) collective-permute-start(f32[4,16,2048]{2,1,0:T(8,128)} %get-tuple-element.65), channel_id=1, source_target_pairs={{0,32},{16,48},{32,0},{48,16},{1,33},{17,49},{33,1},{49,17},{2,34}... | collective-permute-start | bytes 1572872 | tf_op jit(solution)/shard_map/ppermute | solution.py:238
  174.4 19.4 %collective-permute-start.17 = (f32[4,16,2048]{2,1,0:T(8,128)}, f32[4,16,2048]{2,1,0:T(8,128)}, u32[]{:S(2)}, u32[]{:S(2)}) collective-permute-start(f32[4,16,2048]{2,1,0:T(8,128)} %get-tuple-element.60), channel_id=1, source_target_pairs={{0,2},{2,4},{4,6},{6,0},{1,3},{3,5},{5,7},{7,1},{8,10},{10,12},{12... | collective-permute-start | bytes 1572872 | tf_op jit(solution)/shard_map/ppermute | solution.py:238
  175.3 10.2 %copy-start.18 = (f32[128,1024]{1,0:T(8,128)}, f32[128,1024]{1,0:T(8,128)S(1)}, u32[]{:S(2)}) copy-start(f32[128,1024]{1,0:T(8,128)S(1)} %collective-permute-done.9) | copy-start | bytes 1572868
  182.9 15.0 %collective-permute-start.18 = (f32[4,16,2048]{2,1,0:T(8,128)}, f32[4,16,2048]{2,1,0:T(8,128)}, u32[]{:S(2)}, u32[]{:S(2)}) collective-permute-start(f32[4,16,2048]{2,1,0:T(8,128)} %get-tuple-element.45), channel_id=1, source_target_pairs={{0,6},{2,0},{4,2},{6,4},{1,7},{3,1},{5,3},{7,5},{8,14},{10,8},{12,... | collective-permute-start | bytes 1572872 | tf_op jit(solution)/shard_map/ppermute | solution.py:238
  185.6 16.7 %collective-permute-start.10 = (f32[128,1024]{1,0:T(8,128)}, f32[128,1024]{1,0:T(8,128)S(1)}, u32[]{:S(2)}, u32[]{:S(2)}) collective-permute-start(f32[128,1024]{1,0:T(8,128)} %get-tuple-element.39), channel_id=1, source_target_pairs={{0,64},{64,0},{1,65},{65,1},{2,66},{66,2},{3,67},{67,3},{4,68},{68... | collective-permute-start | bytes 1572872 | tf_op jit(solution)/shard_map/ppermute | solution.py:296
  186.8 43.2 %collective-permute-start.3 = (f32[256,1024]{1,0:T(8,128)S(1)}, f32[256,1024]{1,0:T(8,128)S(1)}, u32[]{:S(2)}, u32[]{:S(2)}) collective-permute-start(f32[256,1024]{1,0:T(8,128)S(1)} %slice.113), channel_id=1, source_target_pairs={{0,64},{64,0},{1,65},{65,1},{2,66},{66,2},{3,67},{67,3},{4,68},{68... | collective-permute-start | bytes 3145736 | tf_op jit(solution)/shard_map/ppermute | solution.py:297
  189.2 19.5 %collective-permute-start.23 = (f32[4,16,2048]{2,1,0:T(8,128)}, f32[4,16,2048]{2,1,0:T(8,128)S(1)}, u32[]{:S(2)}, u32[]{:S(2)}) collective-permute-start(f32[4,16,2048]{2,1,0:T(8,128)} %get-tuple-element.63), channel_id=1, source_target_pairs={{0,16},{16,32},{32,48},{48,0},{1,17},{17,33},{33,49},{49,1},{2,18}... | collective-permute-start | bytes 1572872 | tf_op jit(solution)/shard_map/ppermute | solution.py:238
  193.9 20.1 %collective-permute-start.24 = (f32[4,16,2048]{2,1,0:T(8,128)}, f32[4,16,2048]{2,1,0:T(8,128)S(1)}, u32[]{:S(2)}, u32[]{:S(2)}) collective-permute-start(f32[4,16,2048]{2,1,0:T(8,128)} %get-tuple-element.49), channel_id=1, source_target_pairs={{0,48},{16,0},{32,16},{48,32},{1,49},{17,1},{33,17},{49,33},{2,50}... | collective-permute-start | bytes 1572872 | tf_op jit(solution)/shard_map/ppermute | solution.py:238
  199.5 22.1 %copy-start.19 = (f32[128,1024]{1,0:T(8,128)S(1)}, f32[128,1024]{1,0:T(8,128)}, u32[]{:S(2)}) copy-start(f32[128,1024]{1,0:T(8,128)} %copy-done.18) | copy-start | bytes 1572868
  202.3 23.6 %collective-permute-start.20 = (f32[16,2048]{1,0:T(8,128)S(1)}, f32[16,2048]{1,0:T(8,128)S(1)}, u32[]{:S(2)}, u32[]{:S(2)}) collective-permute-start(f32[16,2048]{1,0:T(8,128)S(1)} %get-tuple-element.47), channel_id=1, source_target_pairs={{0,16},{16,32},{32,48},{48,0},{1,17},{17,33},{33,49},{49,1},{2,18}... | collective-permute-start | bytes 393224 | tf_op jit(solution)/shard_map/ppermute | solution.py:238
  203.8 12.5 %collective-permute-start.19 = (f32[16,2048]{1,0:T(8,128)S(1)}, f32[16,2048]{1,0:T(8,128)S(1)}, u32[]{:S(2)}, u32[]{:S(2)}) collective-permute-start(f32[16,2048]{1,0:T(8,128)S(1)} %get-tuple-element.46), channel_id=1, source_target_pairs={{0,32},{16,48},{32,0},{48,16},{1,33},{17,49},{33,1},{49,17},{2,34}... | collective-permute-start | bytes 393224 | tf_op jit(solution)/shard_map/ppermute | solution.py:238
  215.3 7.4 %collective-permute-start.25 = (f32[16,2048]{1,0:T(8,128)S(1)}, f32[16,2048]{1,0:T(8,128)S(1)}, u32[]{:S(2)}, u32[]{:S(2)}) collective-permute-start(f32[16,2048]{1,0:T(8,128)S(1)} %get-tuple-element.50), channel_id=1, source_target_pairs={{0,4},{2,6},{4,0},{6,2},{1,5},{3,7},{5,1},{7,3},{8,12},{10,14},{12... | collective-permute-start | bytes 393224 | tf_op jit(solution)/shard_map/ppermute | solution.py:238
  216.3 9.6 %collective-permute-start.21 = (f32[16,2048]{1,0:T(8,128)S(1)}, f32[16,2048]{1,0:T(8,128)S(1)}, u32[]{:S(2)}, u32[]{:S(2)}) collective-permute-start(f32[16,2048]{1,0:T(8,128)S(1)} %get-tuple-element.48), channel_id=1, source_target_pairs={{0,48},{16,0},{32,16},{48,32},{1,49},{17,1},{33,17},{49,33},{2,50}... | collective-permute-start | bytes 393224 | tf_op jit(solution)/shard_map/ppermute | solution.py:238
  222.7 6.2 %collective-permute-start.26 = (f32[16,2048]{1,0:T(8,128)S(1)}, f32[16,2048]{1,0:T(8,128)S(1)}, u32[]{:S(2)}, u32[]{:S(2)}) collective-permute-start(f32[16,2048]{1,0:T(8,128)S(1)} %get-tuple-element.51), channel_id=1, source_target_pairs={{0,2},{2,4},{4,6},{6,0},{1,3},{3,5},{5,7},{7,1},{8,10},{10,12},{12... | collective-permute-start | bytes 393224 | tf_op jit(solution)/shard_map/ppermute | solution.py:238
  222.7 6.2 %collective-permute-start.27 = (f32[16,2048]{1,0:T(8,128)S(1)}, f32[16,2048]{1,0:T(8,128)S(1)}, u32[]{:S(2)}, u32[]{:S(2)}) collective-permute-start(f32[16,2048]{1,0:T(8,128)S(1)} %get-tuple-element.52), channel_id=1, source_target_pairs={{0,6},{2,0},{4,2},{6,4},{1,7},{3,1},{5,3},{7,5},{8,14},{10,8},{12,... | collective-permute-start | bytes 393224 | tf_op jit(solution)/shard_map/ppermute | solution.py:238
  230.0 10.9 %copy-start.17 = (f32[1,16,2048]{2,1,0:T(8,128)S(1)}, f32[1,16,2048]{2,1,0:T(8,128)}, u32[]{:S(2)}) copy-start(f32[1,16,2048]{2,1,0:T(8,128)} %param.17) | copy-start | bytes 393220
  230.0 10.8 %copy-start.13 = (f32[256,1024]{1,0:T(8,128)}, f32[256,1024]{1,0:T(8,128)S(1)}, u32[]{:S(2)}) copy-start(f32[256,1024]{1,0:T(8,128)S(1)} %collective-permute-done.3.got_ref) | copy-start | bytes 3145732
  230.0 10.8 %collective-permute-start.28 = (f32[2,16,2048]{2,1,0:T(8,128)S(1)}, f32[2,16,2048]{2,1,0:T(8,128)S(1)}, u32[]{:S(2)}, u32[]{:S(2)}) collective-permute-start(f32[2,16,2048]{2,1,0:T(8,128)S(1)} %select_bitcast_fusion), channel_id=1, source_target_pairs={{0,8},{8,0},{1,9},{9,1},{2,10},{10,2},{3,11},{11,3},{4,12},{12,4},... | collective-permute-start | bytes 786440 | tf_op jit(solution)/shard_map/ppermute | solution.py:318
  240.9 10.0 %collective-permute-start.29 = (f32[16,2048]{1,0:T(8,128)S(1)}, f32[16,2048]{1,0:T(8,128)S(1)}, u32[]{:S(2)}, u32[]{:S(2)}) collective-permute-start(f32[16,2048]{1,0:T(8,128)S(1)} %fusion.11), channel_id=1, source_target_pairs={{0,64},{64,0},{1,65},{65,1},{2,66},{66,2},{3,67},{67,3},{4,68},{68... | collective-permute-start | bytes 393224 | tf_op jit(solution)/shard_map/ppermute | solution.py:321
  (10 other events, 17.7 us)
Sparse Core Ops, SparseCore 0:
  47.0 75.0 all-gather.1
Sparse Core Ops, SparseCore 1:
  119.3 89.8 reduce-scatter.3

commit v4 on v3

--- a/solution.py
+++ b/solution.py
@@ -73,11 +73,37 @@
     return mine0.reshape(rows, tokens), mine1.reshape(rows, tokens), theirs.reshape(2, rows, tokens)
 
 
-def right_of(is_first, g_ref, b_ref, go_ref, bo_ref, sent_refs):
-    b, bo = b_ref[...], bo_ref[...]
-    right = [g_ref[...] - jnp.where(is_first, 0.0, b), go_ref[...] - jnp.where(is_first, 0.0, bo)]
-    right += [jnp.where(is_first, 0.0, ref[...]) for ref in sent_refs]
-    return jnp.concatenate(right, axis=0), jnp.concatenate([b, bo], axis=0)
+def passes(left_high, left_low, high, low):
+    return dot(left_high, high) + dot(left_high, low) + dot(left_low, high)
+
+
+def split_kernel(p_ref, g_ref, b_ref, go_ref, bo_ref, r_high, r_low, b_high, b_low):
+    own = pl.program_id(0) < pl.num_programs(0) // 2
+    b = jnp.where(own, b_ref[...], bo_ref[...])
+    r = jnp.where(own, g_ref[...], go_ref[...]) - jnp.where(p_ref[0] == 0, 0.0, b)
+    r_high[...], r_low[...] = halves(r)
+    b_high[...], b_low[...] = halves(b)
+
+
+def split_rights(party, g, b, g_other, b_other):
+    tokens, ff = g.shape
+    block, steps = 128, tokens // 128
+    mine = pl.BlockSpec((block, ff), lambda i: (jnp.minimum(i, steps - 1), 0))
+    other = pl.BlockSpec((block, ff), lambda i: (jnp.maximum(i - steps, 0), 0))
+    out = jax.ShapeDtypeStruct((2 * tokens, ff), BF16)
+    return pl.pallas_call(
+        split_kernel,
+        grid=(2 * steps,),
+        in_specs=[SMEM, mine, mine, other, other],
+        out_specs=[pl.BlockSpec((block, ff), lambda i: (i, 0))] * 4,
+        out_shape=[out] * 4,
+        cost_estimate=cost(0, g, g, g, g, g, g, g, g),
+        compiler_params=params(),
+    )(party, g, b, g_other, b_other)
+
+
+def sent_of(is_first, refs):
+    return halves(jnp.where(is_first, 0.0, jnp.concatenate([ref[...] for ref in refs], axis=0)))
 
 
 def x_kernel(split, p_ref, x_ref, a_ref, *refs):
@@ -99,9 +125,12 @@
             opened = jnp.concatenate([opened, x[:, 384:512], x[:, 896:]], axis=1)
         high[:256], low[:256] = halves(opened)
 
-    right, right_b = right_of(is_first, *refs[:4], refs[4:-3])
-    shared = three_passes(high[256:, :width], low[256:, :width], right_b)
-    out[0] = three_passes(high[:256], low[:256], right) - jnp.where(is_first, shared, 0.0)
+    r_high, r_low, b_high, b_low = refs[:4]
+    shared = passes(high[256:, :width], low[256:, :width], b_high[...], b_low[...])
+    product = passes(high[:256, :width], low[:256, :width], r_high[...], r_low[...])
+    if split:
+        product += passes(high[:256, width:], low[:256, width:], *sent_of(is_first, refs[4:-3]))
+    out[0] = product - jnp.where(is_first, shared, 0.0)
     out[1] = shared
 
 
@@ -122,29 +151,30 @@
             second = jnp.where(is_first, late_ref[...], a)
         high[...], low[...] = halves(second)
 
-    right, _ = right_of(is_first, *refs[:4], refs[4:-3])
-    product = three_passes(high[...], low[...], right)
+    width = a_ref.shape[1]
+    product = passes(high[:, :width], low[:, :width], refs[0][...], refs[1][...])
+    if split:
+        product += passes(high[:, width:], low[:, width:], *sent_of(is_first, refs[2:-3]))
     out[:, 0] = (s_ref[0] - product).reshape(16, 16, product.shape[1])
     out[:, 1] = (s_ref[1] + product).reshape(16, 16, product.shape[1])
 
 
-def right_specs(tokens, sent):
-    right = pl.BlockSpec((tokens, TILE), lambda n: (0, n))
+def right_specs(rights, sent):
     per = sent[0].shape[1] // TILE if sent else 1
     part = pl.BlockSpec((128, TILE), lambda n: (n // per, n % per))
-    return [right] * 4 + [part] * len(sent)
+    return [pl.BlockSpec((v.shape[0], TILE), lambda n: (0, n)) for v in rights] + [part] * len(sent)
 
 
 def x_parts(party, x, x_got, a, rights, sent, weight):
     tokens, ff = rights[0].shape
-    left = pl.BlockSpec((256, 2 * tokens), lambda n: (0, 0))
-    depth = 2 * tokens + 128 * len(sent)
+    left = pl.BlockSpec((256, tokens), lambda n: (0, 0))
+    depth = tokens + 128 * len(sent)
     return pl.pallas_call(
         lambda *refs: x_kernel(bool(sent), *refs),
         grid=(ff // TILE,),
         in_specs=[SMEM, left, left]
         + [pl.BlockSpec(v.shape, lambda n: (0, 0)) for v in x_got]
-        + right_specs(tokens, sent),
+        + right_specs(rights, sent),
         out_specs=pl.BlockSpec((2, 256, TILE), lambda n: (0, 0, n)),
         out_shape=jax.ShapeDtypeStruct((2, 256, ff), F32),
         scratch_shapes=[pltpu.VMEM((512, depth), BF16)] * 2,
@@ -156,12 +186,12 @@
 def a_parts(party, a, early, late, s, rights, sent, weight):
     tokens, ff = rights[0].shape
     lefts = [pl.BlockSpec(v.shape, lambda n: (0, 0)) for v in (a, early, late)]
-    depth = 2 * tokens + 128 * len(sent)
+    depth = tokens + 128 * len(sent)
     return pl.pallas_call(
         lambda *refs: a_kernel(bool(sent), *refs),
         grid=(ff // TILE,),
         in_specs=[SMEM, *lefts, pl.BlockSpec((2, 256, TILE), lambda n: (0, 0, n))]
-        + right_specs(tokens, sent),
+        + right_specs(rights, sent),
         out_specs=pl.BlockSpec((16, 2, 16, TILE), lambda n: (0, 0, 0, n)),
         out_shape=jax.ShapeDtypeStruct((16, 2, 16, ff), F32),
         scratch_shapes=[pltpu.VMEM((256, depth), BF16)] * 2,
@@ -257,14 +287,15 @@
     xs0 = jnp.concatenate([x_mine0, x_other[0]], axis=1)
     xs1 = jnp.concatenate([x_mine1, x_other[1]], axis=1)
     x0_other = lax.ppermute(x_other[0], "party", SWAP)
-    a_mine0, a_mine1, a_theirs = turned(core_id, after(ba, x_theirs))
+    a_mine0, a_mine1, a_theirs = turned(core_id, after(ba, x_other))
     a_other = lax.ppermute(a_theirs, "core", SWAP)
     aa0 = jnp.concatenate([a_mine0, a_other[0]], axis=1)
     aa1 = jnp.concatenate([a_mine1, a_other[1]], axis=1)
-    d = after(w - fb, a_theirs)
+    d = w - fb
     d_party = lax.ppermute(d, "party", SWAP)
     near = lax.ppermute(jnp.concatenate([fb, d], axis=1), "xl", SWAP)
     d_across = lax.ppermute(d, ("party", "xl"), [(0, 3), (3, 0), (1, 2), (2, 1)])
+    d_party, near, d_across = lax.optimization_barrier((d_party, near, d_across, x_theirs))[:3]
     delta = d + d_party
     delta_near = near[:, ff:] + d_across
     packed = jnp.concatenate([fb + first * delta, delta], axis=1)
@@ -292,36 +323,35 @@
     a1 = lax.ppermute(after(a1, x0_other), "party", [(1, 0)])
     u = x - fa
     half = x.shape[0] // 2
-    u0 = lax.ppermute(after(u[: half // 2], a0), "party", SWAP)
-    u1 = lax.ppermute(after(u[half // 2 : half], x1), "party", SWAP)
-    u2 = lax.ppermute(after(u[half:], x1), "party", SWAP)
-
-    g_other = lax.ppermute(after(g, x0, a0_sent), "core", SWAP)
-    b_other = lax.ppermute(after(bb, x0, x1_sent), "core", SWAP)
-    rights = (g, bb, g_other, b_other)
+    u0 = lax.ppermute(after(u[:half], a0), "party", SWAP)
+    u1 = lax.ppermute(after(u[half:], x1), "party", SWAP)
+
+    g_other = lax.ppermute(after(g, a_theirs), "core", SWAP)
+    b_other = lax.ppermute(after(bb, a_theirs), "core", SWAP)
+    rights = split_rights(party_id, g, bb, g_other, b_other)
     early = x_parts(party_id, xs0, (x0, x0_other), aa0, rights, (), 1)
     sent = (a0, lax.ppermute(after(a0, early), "core", SWAP))
-    early = a_parts(party_id, aa0, a0, a0, early, rights, (), 1)
+    early = a_parts(party_id, aa0, a0, a0, early, rights[:2], (), 1)
     late = x_parts(party_id, xs1, (x1,), aa1, rights, sent, LATE)
-    late = a_parts(party_id, aa1, x1, a1, late, rights, sent, LATE)
+    late = a_parts(party_id, aa1, x1, a1, late, rights[:2], sent, LATE)
 
     early = lax.psum_scatter(early.reshape(16, 32, ff), ("y", "z"), scatter_dimension=0, tiled=True)
     early = early.reshape(2, 2, 8, ff)
     outputs = forward_call(local_kernel, (fa,), (0,), weights, 1, fc, 0, fc.shape[0])
-    late = after(late, outputs).reshape(4, 4, 2, 16, ff)
+    late = late.reshape(4, 4, 2, 16, ff)
     part0, part1 = scattered_pair(late[:, :, 0], "z", 1, late[:, :, 1], "y", 0, (), (u0,))
-    part0, part1 = scattered_pair(part0, "y", 0, part1, "z", 0, (u1,))
+    part0, part1 = scattered_pair(part0, "y", 0, part1, "z", 0, (outputs,))
     late = jnp.stack([part0, part1]).reshape(2, 2, 8, ff)
     both = jnp.concatenate([early, late], axis=2)
     keep = jnp.where(xl0, both[:, 0], both[:, 1])
     give = jnp.where(xl0, both[:, 1], both[:, 0])
-    both = keep + lax.ppermute(after(give, u2), "xl", SWAP)
+    both = keep + lax.ppermute(after(give, u1), "xl", SWAP)
     give = jnp.where(party0, both[1] - bc, both[0])
     keep = jnp.where(party0, both[0] + bc, both[1])
     grad = keep + lax.ppermute(give, "party", SWAP)
 
-    outputs = forward_call(opened_kernel, (x, fa, jnp.concatenate([u0, u1])), (0, 0, 0), weights, 0, outputs, 0, half)
-    outputs = forward_call(opened_kernel, (x, fa, u2), (1, 1, 0), weights, 0, outputs, 1, half)
+    outputs = forward_call(opened_kernel, (x, fa, u0), (0, 0, 0), weights, 0, outputs, 0, half)
+    outputs = forward_call(opened_kernel, (x, fa, u1), (1, 1, 0), weights, 0, outputs, 1, half)
     return (outputs[None], grad[None])
 
 

time: 260 us -> 254 us (0.977)
  starting transfers between devices: 54.4 us -> 41.6 us
  Pallas kernels: 99.6 us -> 108 us
  local copies, waits for them, and re-layouts: 18.5 us -> 11.8 us
  waiting for transfers between devices: 53.5 us -> 58.9 us
    ppermute x6 -> x5, waiting for transfers between devices: 2.74 us -> 18.8 us  [the longest x1 16.9 us: body(): u1 = lax.ppermute(after(u[half:], x1), 'party', SWAP)]
    pallas_call x0 -> x1, Pallas kernels: none -> 14.9 us  [split_rights(): pl.pallas_call(split_kernel, grid=(2 * steps,), in_specs=[SMEM, mine, min...]
    ppermute x1, waiting for transfers between devices: 8.6 us -> 0.01 us  [body(): x0_other = lax.ppermute(x_other[0], 'party', SWAP)]
    ppermute x1, waiting for transfers between devices: 7.28 us -> 0.01 us  [body(): lax.ppermute(d, ('party', 'xl'), [(0, 3), (3, 0), (1, 2), (2, 1)])]
    ppermute x12, waiting for transfers between devices: 22.3 us -> 29.3 us  [scattered_pair(): lax.ppermute(piece, axis, [(i, (i + step) % 4) for i in range(4)])]
    unnamed x52 -> x32, local copies, waits for them, and re-layouts: 10.2 us -> 3.78 us
    ppermute x12, starting transfers between devices: 28.3 us -> 22.2 us  [scattered_pair(): lax.ppermute(piece, axis, [(i, (i + step) % 4) for i in range(4)])]
    pallas_call x2, Pallas kernels: 27.3 us -> 22.1 us  [a_parts(): pl.pallas_call(lambda *refs: a_kernel(bool(sent), *refs), grid=(ff // TIL...]
  transfers between devices with their start and end apart: 32 -> 31, of which waited for: 12 -> 11; matrix products, arithmetic and copies ran while one was open for 10% -> 9% of each run, Pallas kernels for 36% -> 40%
where the time goes in v4:
time: 254 us; the launch traced here: 252 us
  Pallas kernels  108 us (43%)
  waiting for transfers between devices  58.9 us (23%)
  starting transfers between devices  41.6 us (16%)
  between operations  15.9 us (6%)
  other arithmetic  15.8 us (6%)
  local copies, waits for them, and re-layouts  11.8 us (5%)
    pallas_call x3, Pallas kernels, forward_call(): pl.pallas_call(kernel, grid=(steps,), in_specs=[pl.BlockSpec((rows, d), l...  30.9 us
    ppermute x12, waiting for transfers between devices, scattered_pair(): lax.ppermute(piece, axis, [(i, (i + step) % 4) for i in range(4)])  29.3 us
    pallas_call x2, Pallas kernels, x_parts(): pl.pallas_call(lambda *refs: x_kernel(bool(sent), *refs), grid=(ff // TIL...  28 us
    ppermute x12, starting transfers between devices, scattered_pair(): lax.ppermute(piece, axis, [(i, (i + step) % 4) for i in range(4)])  22.2 us
    pallas_call x2, Pallas kernels, a_parts(): pl.pallas_call(lambda *refs: a_kernel(bool(sent), *refs), grid=(ff // TIL...  22.1 us
    ppermute x1, waiting for transfers between devices, body(): u1 = lax.ppermute(after(u[half:], x1), 'party', SWAP)  16.9 us
    pallas_call x1, Pallas kernels, split_rights(): pl.pallas_call(split_kernel, grid=(2 * steps,), in_specs=[SMEM, mine, min...  14.9 us
    pallas_call x2, Pallas kernels, turned(): pl.pallas_call(turn_kernel, grid=(8,), in_specs=[SMEM, pl.BlockSpec((toke...  12.1 us
  transfers between devices with their start and end apart: 31, of which 11 were waited for; matrix products, arithmetic and copies ran while one was open for 9% of the time, Pallas kernels for 40%

profile of v4, /device:TPU:0, one launch (start us, length us, event | category | flops | bytes accessed | tf_op | source)
XLA Modules:
  0.0 251.9 jit_solution(1147144641644918994)
XLA Ops:
  8.0 6.0 %shard_map.104 = (f32[4,4,2,8,512]{4,3,2,1,0:T(8,128)}, f32[4,4,2,8,512]{4,3,2,1,0:T(8,128)}, f32[2,4,4,2,8,512]{5,4,3,2,1,0:T(8,128)}) custom-call(s32[1]{0:T(128)} %bitcast.2.core_ref, f32[512,1024]{1,0:T(8,128)} %bitcast.136), custom_call_target="tpu_custom_call" | custom-call | bytes 4194304 | tf_op jit(solution)/shard_map/pallas_call | solution.py:63
  16.1 1.7 collective-permute-start.5
  17.7 2.7 %collective-permute-start.4 = (f32[16,2048]{1,0:T(8,128)S(1)}, f32[16,2048]{1,0:T(8,128)S(1)}, u32[]{:S(2)}, u32[]{:S(2)}) collective-permute-start(f32[16,2048]{1,0:T(8,128)S(1)} %bitcast_subtract_fusion.1), channel_id=1, source_target_pairs={{0,64},{64,0},{1,65},{65,1},{2,66},{66,2},{3,67},{67,3},{4,68},{68... | collective-permute-start | bytes 393224 | tf_op jit(solution)/shard_map/ppermute | solution.py:295
  20.8 1.9 collective-permute-start.7
  22.7 7.6 %collective-permute-done.4 = f32[16,2048]{1,0:T(8,128)S(1)} collective-permute-done((f32[16,2048]{1,0:T(8,128)S(1)}, f32[16,2048]{1,0:T(8,128)S(1)}, u32[]{:S(2)}, u32[]{:S(2)}) %collective-permute-start.4) | collective-permute-done | bytes 131104 | tf_op jit(solution)/shard_map/ppermute | solution.py:295
  31.3 6.0 %shard_map.105 = (f32[4,4,2,8,512]{4,3,2,1,0:T(8,128)}, f32[4,4,2,8,512]{4,3,2,1,0:T(8,128)}, f32[2,4,4,2,8,512]{5,4,3,2,1,0:T(8,128)}) custom-call(s32[1]{0:T(128)} %bitcast.2.core_ref, f32[512,1024]{1,0:T(8,128)} %bitcast.149), custom_call_target="tpu_custom_call" | custom-call | bytes 4194304 | tf_op jit(solution)/shard_map/pallas_call | solution.py:63
  38.2 3.0 %collective-permute-done.7.refs_3_ = f32[256,512]{1,0:T(8,128)} collective-permute-done((f32[256,512]{1,0:T(8,128)}, f32[256,512]{1,0:T(8,128)}, u32[]{:S(2)}, u32[]{:S(2)}) %collective-permute-start.7) | collective-permute-done | bytes 524320 | tf_op jit(solution)/shard_map/ppermute | solution.py:285
  42.2 1.3 slice_bitcast_fusion
  45.7 1.6 pad_maximum_fusion.1
  47.2 2.7 %collective-permute-start.8 = (f32[256,1024]{1,0:T(8,128)}, f32[256,1024]{1,0:T(8,128)}, u32[]{:S(2)}, u32[]{:S(2)}) collective-permute-start(f32[256,1024]{1,0:T(8,128)} %get-tuple-element.77), channel_id=1, source_target_pairs={{0,64},{64,0},{1,65},{65,1},{2,66},{66,2},{3,67},{67,3},{4,68},{68... | collective-permute-start | bytes 3145736 | tf_op jit(solution)/shard_map/ppermute | solution.py:311
  50.0 1.1 pad_maximum_fusion.2.refs_1_
  51.1 1.1 pad_maximum_fusion
  53.8 1.1 collective-permute-done.12.bo_ref
  55.8 14.9 %shard_map.109 = (bf16[1024,2048]{1,0:T(8,128)(2,1)}, bf16[1024,2048]{1,0:T(8,128)(2,1)}, bf16[1024,2048]{1,0:T(8,128)(2,1)}, bf16[1024,2048]{1,0:T(8,128)(2,1)}) custom-call(s32[1]{0:T(128)} %bitcast.18.p_ref.refs_0_, f32[512,2048]{1,0:T(8,128)} %bitcast.144, f32[512,2048]{1,0:T(8,128)} %bitcast.146, f32[512,2048]{1,0:T(8,128)} %copy-done.3, ...), custom_call_target="tpu_custom_call" | custom-call | bytes 33554432 | tf_op jit(solution)/shard_map/pallas_call | solution.py:94
  70.7 13.2 %shard_map.110.refs_4_ = f32[2,256,2048]{2,1,0:T(8,128)} custom-call(s32[1]{0:T(128)} %bitcast.18.p_ref.refs_0_, f32[256,1024]{1,0:T(8,128)} %pad_maximum_fusion.2.refs_1_, f32[256,1024]{1,0:T(8,128)} %get-tuple-element.76.refs_2_.refs_1_, f32[256,512]{1,0:T(8,128)} %collective-permute-done.7.refs_3_, f32[256,512]{1,0:T(8,128)} %collective-permute-done.10.refs_4_, ...), custom_call_target="tpu_custom_call" | custom-call | flops 6442450944 | bytes 35651584 | tf_op jit(solution)/shard_map/pallas_call | solution.py:172
  84.7 1.4 fusion.19
  86.5 1.1 pad_maximum_fusion.4.refs_1_
  87.7 1.3 collective-permute-start.13
  90.1 4.2 %collective-permute-start.9 = (f32[256,1024]{1,0:T(8,128)}, f32[256,1024]{1,0:T(8,128)S(1)}, u32[]{:S(2)}, u32[]{:S(2)}) collective-permute-start(f32[256,1024]{1,0:T(8,128)} %get-tuple-element.44), channel_id=1, source_target_pairs={{0,64},{64,0},{1,65},{65,1},{2,66},{66,2},{3,67},{67,3},{4,68},{68... | collective-permute-start | bytes 3145736 | tf_op jit(solution)/shard_map/ppermute | solution.py:326
  94.3 10.8 %shard_map.111 = f32[16,2,16,2048]{3,2,1,0:T(8,128)} custom-call(s32[1]{0:T(128)} %bitcast.18.p_ref.refs_0_, f32[256,1024]{1,0:T(8,128)} %get-tuple-element.76.refs_2_.refs_1_, f32[256,1024]{1,0:T(8,128)} %collective-permute-done.8.refs_2_.refs_3_.refs_8_.refs_7_, f32[256,1024]{1,0:T(8,128)} %collective-permute-done.8.refs_2_.refs_3_.refs_8_.refs_7_, ...), custom_call_target="tpu_custom_call" | custom-call | flops 3221225472 | bytes 25165824 | tf_op jit(solution)/shard_map/pallas_call | solution.py:190
  105.2 14.8 %shard_map.112.refs_4_ = f32[2,256,2048]{2,1,0:T(8,128)} custom-call(s32[1]{0:T(128)} %bitcast.18.p_ref.refs_0_, f32[256,1024]{1,0:T(8,128)} %pad_maximum_fusion.4.refs_1_, f32[256,1024]{1,0:T(8,128)} %pad_maximum_fusion.3.refs_2_.refs_1_, f32[256,1024]{1,0:T(8,128)} %collective-permute-done.2.refs_3_.refs_2_, ...), custom_call_target="tpu_custom_call" | custom-call | flops 64424509440 | bytes 285212672 | tf_op jit(solution)/shard_map/pallas_call | solution.py:172
  120.8 11.2 %shard_map.113 = f32[16,2,16,2048]{3,2,1,0:T(8,128)} custom-call(s32[1]{0:T(128)} %bitcast.18.p_ref.refs_0_, f32[256,1024]{1,0:T(8,128)} %pad_maximum_fusion.3.refs_2_.refs_1_, f32[256,1024]{1,0:T(8,128)} %collective-permute-done.2.refs_3_.refs_2_, f32[256,512]{1,0:T(8,128)} %copy-done.15, f32[2,256,2048]{2,1,0:T(8,128)} %shard_map.112.refs_4_, ...), custom_call_target="tpu_custom_call" | custom-call | flops 32212254720 | bytes 201326592 | tf_op jit(solution)/shard_map/pallas_call | solution.py:190
  132.0 2.6 %fusion.18 = (f32[4,4,1,16,2048]{4,3,2,1,0:T(8,128)S(1)}, f32[4,4,1,16,2048]{4,3,2,1,0:T(8,128)S(1)}) fusion(f32[4,4,2,16,2048]{4,3,2,1,0:T(8,128)} %bitcast.147), kind=kLoop, calls=%fused_computation.64 | loop fusion | bytes 8388608 | tf_op jit(solution)/shard_map/slice | solution.py:342
  134.6 1.3 copy-done.2
  135.9 1.2 dynamic-slice_bitcast_fusion.4
  137.1 3.9 %collective-permute-start.15 = (f32[4,16,2048]{2,1,0:T(8,128)}, f32[4,16,2048]{2,1,0:T(8,128)}, u32[]{:S(2)}, u32[]{:S(2)}) collective-permute-start(f32[4,16,2048]{2,1,0:T(8,128)} %get-tuple-element.70), channel_id=1, source_target_pairs={{0,4},{2,6},{4,0},{6,2},{1,5},{3,7},{5,1},{7,3},{8,12},{10,14},{12... | collective-permute-start | bytes 1572872 | tf_op jit(solution)/shard_map/ppermute | solution.py:268
  140.9 1.1 collective-permute-start.16
  142.0 1.2 dynamic-slice_bitcast_fusion.1
  143.2 3.2 %collective-permute-start.21 = (f32[4,16,2048]{2,1,0:T(8,128)}, f32[4,16,2048]{2,1,0:T(8,128)}, u32[]{:S(2)}, u32[]{:S(2)}) collective-permute-start(f32[4,16,2048]{2,1,0:T(8,128)} %get-tuple-element.73), channel_id=1, source_target_pairs={{0,32},{16,48},{32,0},{48,16},{1,33},{17,49},{33,1},{49,17},{2,34}... | collective-permute-start | bytes 1572872 | tf_op jit(solution)/shard_map/ppermute | solution.py:268
  146.4 10.9 %collective-permute-done.15 = f32[4,16,2048]{2,1,0:T(8,128)} collective-permute-done((f32[4,16,2048]{2,1,0:T(8,128)}, f32[4,16,2048]{2,1,0:T(8,128)}, u32[]{:S(2)}, u32[]{:S(2)}) %collective-permute-start.15) | collective-permute-done | bytes 524320 | tf_op jit(solution)/shard_map/ppermute | solution.py:268
  157.3 2.4 collective-permute-start.17
  159.7 1.6 collective-permute-start.22
  161.3 1.8 collective-permute-start.23
  163.2 7.5 %collective-permute-done.16 = f32[4,16,2048]{2,1,0:T(8,128)} collective-permute-done((f32[4,16,2048]{2,1,0:T(8,128)}, f32[4,16,2048]{2,1,0:T(8,128)}, u32[]{:S(2)}, u32[]{:S(2)}) %collective-permute-start.16) | collective-permute-done | bytes 524320 | tf_op jit(solution)/shard_map/ppermute | solution.py:268
  170.7 2.5 collective-permute-done.17
  173.2 1.6 fusion.3
  174.8 2.0 collective-permute-done.22
  176.8 1.1 fusion.1
  178.0 12.1 %shard_map.106.c_ref = f32[512,2048]{1,0:T(8,128)} custom-call(f32[512,1024]{1,0:T(8,128)} %bitcast.139, f32[512,8192]{1,0:T(8,128)} %all-gather.2.cloned.1.call-done.w0_ref.w1_ref, f32[512,8192]{1,0:T(8,128)} %all-gather.2.cloned.1.call-done.w0_ref.w1_ref, f32[512,2048]{1,0:T(8,128)} %bitcast.148), custom_call_target="tpu_custom_call" | custom-call | flops 6442450944 | bytes 20971520 | tf_op jit(solution)/shard_map/pallas_call | solution.py:237
  190.1 2.4 collective-permute-start.18
  192.5 1.1 collective-permute-start.24
  194.6 3.5 %collective-permute-done.18 = f32[16,2048]{1,0:T(8,128)S(1)} collective-permute-done((f32[16,2048]{1,0:T(8,128)S(1)}, f32[16,2048]{1,0:T(8,128)S(1)}, u32[]{:S(2)}, u32[]{:S(2)}) %collective-permute-start.18) | collective-permute-done | bytes 131104 | tf_op jit(solution)/shard_map/ppermute | solution.py:268
  198.7 1.8 collective-permute-start.3
  201.4 2.4 collective-permute-start.26
  203.8 2.9 %collective-permute-done.25 = f32[16,2048]{1,0:T(8,128)S(1)} collective-permute-done((f32[16,2048]{1,0:T(8,128)S(1)}, f32[16,2048]{1,0:T(8,128)S(1)}, u32[]{:S(2)}, u32[]{:S(2)}) %collective-permute-start.25) | collective-permute-done | bytes 131104 | tf_op jit(solution)/shard_map/ppermute | solution.py:268
  207.8 16.9 %collective-permute-done.3.got_ref = f32[256,1024]{1,0:T(8,128)S(1)} collective-permute-done((f32[256,1024]{1,0:T(8,128)S(1)}, f32[256,1024]{1,0:T(8,128)S(1)}, u32[]{:S(2)}, u32[]{:S(2)}) %collective-permute-start.3) | collective-permute-done | bytes 1048608 | tf_op jit(solution)/shard_map/ppermute | solution.py:327
  224.8 9.6 %shard_map.107.c_ref = f32[512,2048]{1,0:T(8,128)} custom-call(f32[512,1024]{1,0:T(8,128)} %bitcast.137, f32[512,1024]{1,0:T(8,128)} %bitcast.140, f32[256,1024]{1,0:T(8,128)} %copy-done.7, f32[512,8192]{1,0:T(8,128)} %all-gather.2.cloned.1.call-done.w0_ref.w1_ref, ...), custom_call_target="tpu_custom_call", output_to_operand_aliasing={{}: (5, {})} | custom-call | flops 3221225472 | bytes 20971520 | tf_op jit(solution)/shard_map/pallas_call | solution.py:237
  234.6 9.2 %shard_map.108 = f32[512,2048]{1,0:T(8,128)} custom-call(f32[512,1024]{1,0:T(8,128)} %bitcast.138, f32[512,1024]{1,0:T(8,128)} %bitcast.141, f32[256,1024]{1,0:T(8,128)} %copy-done.8, f32[512,8192]{1,0:T(8,128)} %all-gather.2.cloned.1.call-done.w0_ref.w1_ref, f32[512,8192]{1,0:T(8,128)} %all-gather.2.cloned.1.call-done.w0_ref.w1_ref, ...), custom_call_target="tpu_custom_call", output_to_operand_aliasing={{}: (5, {})} | custom-call | flops 3221225472 | bytes 20971520 | tf_op jit(solution)/shard_map/pallas_call | solution.py:237
  (95 shorter events, 17.4 us)
Async XLA Ops:
  8.0 170.0 %all-gather.2.cloned.1.call-start = ((), (), s32[]{:S(2)}) async-start(), calls=%async_computation.1 | async-start | bytes 17301504 | tf_op jit(solution)/shard_map/all_gather | solution.py:306
  14.1 27.8 %copy-start.4 = (f32[4,4,2,8,512]{4,3,2,1,0:T(8,128)S(1)}, f32[4,4,2,8,512]{4,3,2,1,0:T(8,128)}, u32[]{:S(2)}) copy-start(f32[4,4,2,8,512]{4,3,2,1,0:T(8,128)} %get-tuple-element.32) | copy-start | bytes 1572868
  14.1 17.2 %collective-permute-start = (f32[2,256,512]{2,1,0:T(8,128)}, f32[2,256,512]{2,1,0:T(8,128)S(1)}, u32[]{:S(2)}, u32[]{:S(2)}) collective-permute-start(f32[2,256,512]{2,1,0:T(8,128)} %bitcast.161), channel_id=1, source_target_pairs={{0,1},{1,0},{2,3},{3,2},{4,5},{5,4},{6,7},{7,6},{8,9},{9,8},{10,11... | collective-permute-start | bytes 3145736 | tf_op jit(solution)/shard_map/ppermute | solution.py:286
  16.1 14.3 %collective-permute-start.5 = (f32[16,4096]{1,0:T(8,128)S(1)}, f32[16,4096]{1,0:T(8,128)S(1)}, u32[]{:S(2)}, u32[]{:S(2)}) collective-permute-start(f32[16,4096]{1,0:T(8,128)S(1)} %pad_maximum_fusion.7), channel_id=1, source_target_pairs={{0,8},{8,0},{1,9},{9,1},{2,10},{10,2},{3,11},{11,3},{4,12},{12,4},... | collective-permute-start | bytes 786440 | tf_op jit(solution)/shard_map/ppermute | solution.py:296
  17.7 12.6 %collective-permute-start.4 = (f32[16,2048]{1,0:T(8,128)S(1)}, f32[16,2048]{1,0:T(8,128)S(1)}, u32[]{:S(2)}, u32[]{:S(2)}) collective-permute-start(f32[16,2048]{1,0:T(8,128)S(1)} %bitcast_subtract_fusion.1), channel_id=1, source_target_pairs={{0,64},{64,0},{1,65},{65,1},{2,66},{66,2},{3,67},{67,3},{4,68},{68... | collective-permute-start | bytes 393224 | tf_op jit(solution)/shard_map/ppermute | solution.py:295
  20.4 9.9 %collective-permute-start.6 = (f32[16,2048]{1,0:T(8,128)S(1)}, f32[16,2048]{1,0:T(8,128)S(1)}, u32[]{:S(2)}, u32[]{:S(2)}) collective-permute-start(f32[16,2048]{1,0:T(8,128)S(1)} %bitcast_subtract_fusion.1), channel_id=1, source_target_pairs={{0,72},{72,0},{8,64},{64,8},{1,73},{73,1},{9,65},{65,9},{2,74},{74... | collective-permute-start | bytes 393224 | tf_op jit(solution)/shard_map/ppermute | solution.py:297
  20.8 20.4 %collective-permute-start.7 = (f32[256,512]{1,0:T(8,128)}, f32[256,512]{1,0:T(8,128)}, u32[]{:S(2)}, u32[]{:S(2)}) collective-permute-start(f32[256,512]{1,0:T(8,128)} %bitcast.158), channel_id=1, source_target_pairs={{0,64},{64,0},{1,65},{65,1},{2,66},{66,2},{3,67},{67,3},{4,68},{68... | collective-permute-start | bytes 1572872 | tf_op jit(solution)/shard_map/ppermute | solution.py:285
  37.3 3.9 %collective-permute-start.1 = (f32[2,256,512]{2,1,0:T(8,128)}, f32[2,256,512]{2,1,0:T(8,128)S(1)}, u32[]{:S(2)}, u32[]{:S(2)}) collective-permute-start(f32[2,256,512]{2,1,0:T(8,128)} %bitcast.162), channel_id=1, source_target_pairs={{0,1},{1,0},{2,3},{3,2},{4,5},{5,4},{6,7},{7,6},{8,9},{9,8},{10,11... | collective-permute-start | bytes 3145736 | tf_op jit(solution)/shard_map/ppermute | solution.py:291
  41.2 1.0 copy-start.9
  41.3 165.5 %reduce-scatter.4.cloned.1.call-start = ((), (), s32[]{:S(2)}) async-start(), calls=%async_computation.2 | async-start | bytes 4456448
  41.3 12.5 %collective-permute-start.11 = (f32[512,2048]{1,0:T(8,128)}, f32[512,2048]{1,0:T(8,128)S(1)}, u32[]{:S(2)}, u32[]{:S(2)}) collective-permute-start(f32[512,2048]{1,0:T(8,128)} %bitcast.143), channel_id=1, source_target_pairs={{0,1},{1,0},{2,3},{3,2},{4,5},{5,4},{6,7},{7,6},{8,9},{9,8},{10,11... | collective-permute-start | bytes 12582920 | tf_op jit(solution)/shard_map/ppermute | solution.py:329
  41.4 13.5 %collective-permute-start.12 = (f32[512,2048]{1,0:T(8,128)}, f32[512,2048]{1,0:T(8,128)}, u32[]{:S(2)}, u32[]{:S(2)}) collective-permute-start(f32[512,2048]{1,0:T(8,128)} %bitcast.145), channel_id=1, source_target_pairs={{0,1},{1,0},{2,3},{3,2},{4,5},{5,4},{6,7},{7,6},{8,9},{9,8},{10,11... | collective-permute-start | bytes 12582920 | tf_op jit(solution)/shard_map/ppermute | solution.py:330
  43.5 2.1 copy-start.10
  43.5 2.1 copy-start.12
  43.7 6.3 %copy-start.14 = (f32[4,4,2,8,512]{4,3,2,1,0:T(8,128)S(1)}, f32[4,4,2,8,512]{4,3,2,1,0:T(8,128)}, u32[]{:S(2)}) copy-start(f32[4,4,2,8,512]{4,3,2,1,0:T(8,128)} %get-tuple-element.41) | copy-start | bytes 1572868
  43.7 27.0 %collective-permute-start.10 = (f32[256,512]{1,0:T(8,128)S(1)}, f32[256,512]{1,0:T(8,128)}, u32[]{:S(2)}, u32[]{:S(2)}) collective-permute-start(f32[256,512]{1,0:T(8,128)S(1)} %get-tuple-element.78), channel_id=1, source_target_pairs={{0,64},{64,0},{1,65},{65,1},{2,66},{66,2},{3,67},{67,3},{4,68},{68... | collective-permute-start | bytes 1572872 | tf_op jit(solution)/shard_map/ppermute | solution.py:289
  47.2 36.7 %collective-permute-start.8 = (f32[256,1024]{1,0:T(8,128)}, f32[256,1024]{1,0:T(8,128)}, u32[]{:S(2)}, u32[]{:S(2)}) collective-permute-start(f32[256,1024]{1,0:T(8,128)} %get-tuple-element.77), channel_id=1, source_target_pairs={{0,64},{64,0},{1,65},{65,1},{2,66},{66,2},{3,67},{67,3},{4,68},{68... | collective-permute-start | bytes 3145736 | tf_op jit(solution)/shard_map/ppermute | solution.py:311
  52.2 53.0 %collective-permute-start.2 = (f32[256,1024]{1,0:T(8,128)}, f32[256,1024]{1,0:T(8,128)}, u32[]{:S(2)}, u32[]{:S(2)}) collective-permute-start(f32[256,1024]{1,0:T(8,128)} %pad_maximum_fusion), channel_id=1, source_target_pairs={{0,64},{64,0},{1,65},{65,1},{2,66},{66,2},{3,67},{67,3},{4,68},{68... | collective-permute-start | bytes 3145736 | tf_op jit(solution)/shard_map/ppermute | solution.py:321
  53.8 2.0 copy-start.3
  70.7 13.5 %copy-start = (f32[1,512,1024]{2,1,0:T(8,128)S(1)}, f32[1,512,1024]{2,1,0:T(8,128)}, u32[]{:S(2)}) copy-start(f32[1,512,1024]{2,1,0:T(8,128)} %param.9) | copy-start | bytes 6291460
  70.7 13.5 %copy-start.1 = (f32[1,512,1024]{2,1,0:T(8,128)S(1)}, f32[1,512,1024]{2,1,0:T(8,128)}, u32[]{:S(2)}) copy-start(f32[1,512,1024]{2,1,0:T(8,128)} %param.12) | copy-start | bytes 6291460
  83.9 21.3 %collective-permute-start.14 = (f32[256,1024]{1,0:T(8,128)}, f32[256,1024]{1,0:T(8,128)}, u32[]{:S(2)}, u32[]{:S(2)}) collective-permute-start(f32[256,1024]{1,0:T(8,128)} %collective-permute-done.8.refs_2_.refs_3_.refs_8_.refs_7_), channel_id=1, source_target_pairs={{0,1},{1,0},{2,3},{3,2},{4,5},{5,4},{6,7},{7,6},{8,9},{9,8},{10,11... | collective-permute-start | bytes 3145736 | tf_op jit(solution)/shard_map/ppermute | solution.py:333
  84.6 1.5 copy-start.6
  84.6 1.9 copy-start.5
  87.7 32.3 %collective-permute-start.13 = (f32[256,512]{1,0:T(8,128)S(1)}, f32[256,512]{1,0:T(8,128)S(1)}, u32[]{:S(2)}, u32[]{:S(2)}) collective-permute-start(f32[256,512]{1,0:T(8,128)S(1)} %pad_maximum_fusion.6), channel_id=1, source_target_pairs={{64,0},{65,1},{66,2},{67,3},{68,4},{69,5},{70,6},{71,7},{72,8},{73... | collective-permute-start | bytes 1572872 | tf_op jit(solution)/shard_map/ppermute | solution.py:323
  90.1 56.3 %collective-permute-start.9 = (f32[256,1024]{1,0:T(8,128)}, f32[256,1024]{1,0:T(8,128)S(1)}, u32[]{:S(2)}, u32[]{:S(2)}) collective-permute-start(f32[256,1024]{1,0:T(8,128)} %get-tuple-element.44), channel_id=1, source_target_pairs={{0,64},{64,0},{1,65},{65,1},{2,66},{66,2},{3,67},{67,3},{4,68},{68... | collective-permute-start | bytes 3145736 | tf_op jit(solution)/shard_map/ppermute | solution.py:326
  120.0 0.8 copy-start.15
  134.6 1.3 copy-start.2
  137.1 20.2 %collective-permute-start.15 = (f32[4,16,2048]{2,1,0:T(8,128)}, f32[4,16,2048]{2,1,0:T(8,128)}, u32[]{:S(2)}, u32[]{:S(2)}) collective-permute-start(f32[4,16,2048]{2,1,0:T(8,128)} %get-tuple-element.70), channel_id=1, source_target_pairs={{0,4},{2,6},{4,0},{6,2},{1,5},{3,7},{5,1},{7,3},{8,12},{10,14},{12... | collective-permute-start | bytes 1572872 | tf_op jit(solution)/shard_map/ppermute | solution.py:268
  140.9 29.8 %collective-permute-start.16 = (f32[4,16,2048]{2,1,0:T(8,128)}, f32[4,16,2048]{2,1,0:T(8,128)}, u32[]{:S(2)}, u32[]{:S(2)}) collective-permute-start(f32[4,16,2048]{2,1,0:T(8,128)} %get-tuple-element.68), channel_id=1, source_target_pairs={{0,2},{2,4},{4,6},{6,0},{1,3},{3,5},{5,7},{7,1},{8,10},{10,12},{12... | collective-permute-start | bytes 1572872 | tf_op jit(solution)/shard_map/ppermute | solution.py:268
  143.2 18.1 %collective-permute-start.21 = (f32[4,16,2048]{2,1,0:T(8,128)}, f32[4,16,2048]{2,1,0:T(8,128)}, u32[]{:S(2)}, u32[]{:S(2)}) collective-permute-start(f32[4,16,2048]{2,1,0:T(8,128)} %get-tuple-element.73), channel_id=1, source_target_pairs={{0,32},{16,48},{32,0},{48,16},{1,33},{17,49},{33,1},{49,17},{2,34}... | collective-permute-start | bytes 1572872 | tf_op jit(solution)/shard_map/ppermute | solution.py:268
  146.4 24.3 %copy-start.7 = (f32[256,1024]{1,0:T(8,128)}, f32[256,1024]{1,0:T(8,128)S(1)}, u32[]{:S(2)}) copy-start(f32[256,1024]{1,0:T(8,128)S(1)} %collective-permute-done.9.got_ref) | copy-start | bytes 3145732
  157.3 15.9 %collective-permute-start.17 = (f32[4,16,2048]{2,1,0:T(8,128)}, f32[4,16,2048]{2,1,0:T(8,128)}, u32[]{:S(2)}, u32[]{:S(2)}) collective-permute-start(f32[4,16,2048]{2,1,0:T(8,128)} %get-tuple-element.53), channel_id=1, source_target_pairs={{0,6},{2,0},{4,2},{6,4},{1,7},{3,1},{5,3},{7,5},{8,14},{10,8},{12,... | collective-permute-start | bytes 1572872 | tf_op jit(solution)/shard_map/ppermute | solution.py:268
  159.7 17.1 %collective-permute-start.22 = (f32[4,16,2048]{2,1,0:T(8,128)}, f32[4,16,2048]{2,1,0:T(8,128)S(1)}, u32[]{:S(2)}, u32[]{:S(2)}) collective-permute-start(f32[4,16,2048]{2,1,0:T(8,128)} %get-tuple-element.71), channel_id=1, source_target_pairs={{0,16},{16,32},{32,48},{48,0},{1,17},{17,33},{33,49},{49,1},{2,18}... | collective-permute-start | bytes 1572872 | tf_op jit(solution)/shard_map/ppermute | solution.py:268
  161.3 15.5 %collective-permute-start.23 = (f32[4,16,2048]{2,1,0:T(8,128)}, f32[4,16,2048]{2,1,0:T(8,128)S(1)}, u32[]{:S(2)}, u32[]{:S(2)}) collective-permute-start(f32[4,16,2048]{2,1,0:T(8,128)} %get-tuple-element.57), channel_id=1, source_target_pairs={{0,48},{16,0},{32,16},{48,32},{1,49},{17,1},{33,17},{49,33},{2,50}... | collective-permute-start | bytes 1572872 | tf_op jit(solution)/shard_map/ppermute | solution.py:268
  178.0 20.7 %copy-start.11 = (f32[256,1024]{1,0:T(8,128)S(1)}, f32[256,1024]{1,0:T(8,128)}, u32[]{:S(2)}) copy-start(f32[256,1024]{1,0:T(8,128)} %get-tuple-element.37) | copy-start | bytes 3145732
  190.1 8.1 %collective-permute-start.18 = (f32[16,2048]{1,0:T(8,128)S(1)}, f32[16,2048]{1,0:T(8,128)S(1)}, u32[]{:S(2)}, u32[]{:S(2)}) collective-permute-start(f32[16,2048]{1,0:T(8,128)S(1)} %get-tuple-element.54), channel_id=1, source_target_pairs={{0,32},{16,48},{32,0},{48,16},{1,33},{17,49},{33,1},{49,17},{2,34}... | collective-permute-start | bytes 393224 | tf_op jit(solution)/shard_map/ppermute | solution.py:268
  192.5 8.9 %collective-permute-start.24 = (f32[16,2048]{1,0:T(8,128)S(1)}, f32[16,2048]{1,0:T(8,128)S(1)}, u32[]{:S(2)}, u32[]{:S(2)}) collective-permute-start(f32[16,2048]{1,0:T(8,128)S(1)} %get-tuple-element.58), channel_id=1, source_target_pairs={{0,4},{2,6},{4,0},{6,2},{1,5},{3,7},{5,1},{7,3},{8,12},{10,14},{12... | collective-permute-start | bytes 393224 | tf_op jit(solution)/shard_map/ppermute | solution.py:268
  193.7 10.1 %collective-permute-start.19 = (f32[16,2048]{1,0:T(8,128)S(1)}, f32[16,2048]{1,0:T(8,128)S(1)}, u32[]{:S(2)}, u32[]{:S(2)}) collective-permute-start(f32[16,2048]{1,0:T(8,128)S(1)} %get-tuple-element.55), channel_id=1, source_target_pairs={{0,16},{16,32},{32,48},{48,0},{1,17},{17,33},{33,49},{49,1},{2,18}... | collective-permute-start | bytes 393224 | tf_op jit(solution)/shard_map/ppermute | solution.py:268
  198.2 5.6 %collective-permute-start.20 = (f32[16,2048]{1,0:T(8,128)S(1)}, f32[16,2048]{1,0:T(8,128)S(1)}, u32[]{:S(2)}, u32[]{:S(2)}) collective-permute-start(f32[16,2048]{1,0:T(8,128)S(1)} %get-tuple-element.56), channel_id=1, source_target_pairs={{0,48},{16,0},{32,16},{48,32},{1,49},{17,1},{33,17},{49,33},{2,50}... | collective-permute-start | bytes 393224 | tf_op jit(solution)/shard_map/ppermute | solution.py:268
  198.7 26.1 %collective-permute-start.3 = (f32[256,1024]{1,0:T(8,128)S(1)}, f32[256,1024]{1,0:T(8,128)S(1)}, u32[]{:S(2)}, u32[]{:S(2)}) collective-permute-start(f32[256,1024]{1,0:T(8,128)S(1)} %copy-done.11), channel_id=1, source_target_pairs={{0,64},{64,0},{1,65},{65,1},{2,66},{66,2},{3,67},{67,3},{4,68},{68... | collective-permute-start | bytes 3145736 | tf_op jit(solution)/shard_map/ppermute | solution.py:327
  200.5 6.2 %collective-permute-start.25 = (f32[16,2048]{1,0:T(8,128)S(1)}, f32[16,2048]{1,0:T(8,128)S(1)}, u32[]{:S(2)}, u32[]{:S(2)}) collective-permute-start(f32[16,2048]{1,0:T(8,128)S(1)} %get-tuple-element.59), channel_id=1, source_target_pairs={{0,2},{2,4},{4,6},{6,0},{1,3},{3,5},{5,7},{7,1},{8,10},{10,12},{12... | collective-permute-start | bytes 393224 | tf_op jit(solution)/shard_map/ppermute | solution.py:268
  201.4 5.3 %collective-permute-start.26 = (f32[16,2048]{1,0:T(8,128)S(1)}, f32[16,2048]{1,0:T(8,128)S(1)}, u32[]{:S(2)}, u32[]{:S(2)}) collective-permute-start(f32[16,2048]{1,0:T(8,128)S(1)} %get-tuple-element.60), channel_id=1, source_target_pairs={{0,6},{2,0},{4,2},{6,4},{1,7},{3,1},{5,3},{7,5},{8,14},{10,8},{12,... | collective-permute-start | bytes 393224 | tf_op jit(solution)/shard_map/ppermute | solution.py:268
  207.8 26.6 %copy-start.13 = (f32[1,16,2048]{2,1,0:T(8,128)S(1)}, f32[1,16,2048]{2,1,0:T(8,128)}, u32[]{:S(2)}) copy-start(f32[1,16,2048]{2,1,0:T(8,128)} %param.17) | copy-start | bytes 393220
  224.8 9.6 %copy-start.8 = (f32[256,1024]{1,0:T(8,128)}, f32[256,1024]{1,0:T(8,128)S(1)}, u32[]{:S(2)}) copy-start(f32[256,1024]{1,0:T(8,128)S(1)} %collective-permute-done.3.got_ref) | copy-start | bytes 3145732
  224.8 9.6 %collective-permute-start.27 = (f32[2,16,2048]{2,1,0:T(8,128)S(1)}, f32[2,16,2048]{2,1,0:T(8,128)S(1)}, u32[]{:S(2)}, u32[]{:S(2)}) collective-permute-start(f32[2,16,2048]{2,1,0:T(8,128)S(1)} %select_bitcast_fusion), channel_id=1, source_target_pairs={{0,8},{8,0},{1,9},{9,1},{2,10},{10,2},{3,11},{11,3},{4,12},{12,4},... | collective-permute-start | bytes 786440 | tf_op jit(solution)/shard_map/ppermute | solution.py:348
  234.5 9.3 %collective-permute-start.28 = (f32[16,2048]{1,0:T(8,128)S(1)}, f32[16,2048]{1,0:T(8,128)S(1)}, u32[]{:S(2)}, u32[]{:S(2)}) collective-permute-start(f32[16,2048]{1,0:T(8,128)S(1)} %fusion.11), channel_id=1, source_target_pairs={{0,64},{64,0},{1,65},{65,1},{2,66},{66,2},{3,67},{67,3},{4,68},{68... | collective-permute-start | bytes 393224 | tf_op jit(solution)/shard_map/ppermute | solution.py:351
Sparse Core Ops, SparseCore 0:
  41.4 72.7 all-gather.1
Sparse Core Ops, SparseCore 1:
  105.2 90.7 reduce-scatter.3

commit v5 on v3

v5 whole, which is shorter than its diff:
```python
import jax
import jax.numpy as jnp
from jax import lax
from jax.experimental import pallas as pl
from jax.experimental.pallas import tpu as pltpu
from jax.sharding import Mesh
from jax.sharding import PartitionSpec as P

DP = ("y", "xl", "z", "core")
SWAP = [(0, 1), (1, 0)]
F32 = jnp.float32
BF16 = jnp.bfloat16
SMEM = pl.BlockSpec(memory_space=pltpu.SMEM)
TILE = 512
LATE = 8


def cost(flops, *arrays, weight=1):
    moved = sum(4 * a.size for a in arrays)
    return pl.CostEstimate(
        flops=weight * flops, bytes_accessed=weight * moved, transcendentals=0
    )


def params():
    return pltpu.CompilerParams(vmem_limit_bytes=56 * 1024 * 1024)


def after(value, *earlier):
    return lax.optimization_barrier((value, *earlier))[0]


def halves(a):
    high = a.astype(BF16)
    return high, (a - high.astype(F32)).astype(BF16)


def dot(left, right):
    return jnp.dot(left, right, preferred_element_type=F32)


def turn_kernel(core_ref, src, mine0, mine1, theirs):
    even = core_ref[0] == 0
    t = src[...].T
    for y in range(mine0.shape[1]):
        for xl in range(2):
            for z in range(4):
                for k, mine in enumerate((mine0, mine1)):
                    at = (2 * y + xl) * 128 + z * 32 + k * 8
                    e, o = t[at : at + 8], t[at + 16 : at + 24]
                    mine[z, y, xl] = jnp.where(even, e, o)
                    theirs[k, z, y, xl] = jnp.where(even, o, e)


def turned(core, share):
    tokens = share.shape[0]
    mine = jax.ShapeDtypeStruct((4, 4, 2, 8, tokens), F32)
    mine_spec = pl.BlockSpec((4, 2, 2, 8, tokens), lambda i: (0, i, 0, 0, 0))
    theirs_spec = pl.BlockSpec((2, 4, 2, 2, 8, tokens), lambda i: (0, 0, i, 0, 0, 0))
    mine0, mine1, theirs = pl.pallas_call(
        turn_kernel,
        grid=(2,),
        in_specs=[SMEM, pl.BlockSpec((tokens, 512), lambda i: (0, i))],
        out_specs=[mine_spec, mine_spec, theirs_spec],
        out_shape=[mine, mine, jax.ShapeDtypeStruct((2, *mine.shape), F32)],
        cost_estimate=cost(0, share, share),
        compiler_params=params(),
    )(core, share)
    rows = 128 * 2
    return mine0.reshape(rows, tokens), mine1.reshape(rows, tokens), theirs.reshape(2, rows, tokens)


def passes(stack, right):
    rows = stack.shape[0] // 2
    high, low = halves(right)
    both = dot(stack[...], high)
    return both[:rows] + both[rows:] + dot(stack[:rows], low)


def grad_kernel(split, p_ref, x_ref, a_ref, *refs):
    out, pair, pair_sent, single = refs[-4:]
    got_refs, refs = (refs[:1], refs[1:]) if split else (refs[:2], refs[2:])
    g_ref, b_ref, go_ref, bo_ref = refs[:4]
    sent_refs = refs[4:-4]
    is_first = p_ref[0] == 0

    @pl.when(pl.program_id(0) == 0)
    def _():
        x, a = x_ref[...], a_ref[...]
        if split:
            got, late = got_refs[0][:, :1024], got_refs[0][:, 1024:]
            col = lax.broadcasted_iota(jnp.int32, x.shape, 1)
            kept = jnp.logical_or(jnp.logical_not(is_first), col % 512 < 384)
            zero = jnp.zeros((256, 128), F32)
            second = [got[:, 384:512], late[:, :256], zero, got[:, 896:], late[:, 256:], zero]
            second = jnp.where(is_first, jnp.concatenate(second, axis=1), a)
            got = jnp.where(kept, got, 0.0)
            a_sent = jnp.concatenate([a[:, 384:512], a[:, 896:]], axis=1)
            x_sent = jnp.concatenate([x[:, 384:512], x[:, 896:]], axis=1)
            pair_sent[:256], pair_sent[512:768] = halves(x_sent - a_sent)
            pair_sent[256:512], pair_sent[768:] = halves(a_sent)
        else:
            got = jnp.concatenate([got_refs[0][...], got_refs[1][:, :512]], axis=1)
            second = jnp.where(is_first, got_refs[1][:, 512:], a)
        opened = x + got
        pair[:256], pair[512:768] = halves(opened - second)
        pair[256:512], pair[768:] = halves(second)
        single[:256], single[256:] = halves(jnp.where(is_first, a, opened))

    b, bo = b_ref[...], bo_ref[...]
    r = g_ref[...] - jnp.where(is_first, 0.0, b)
    ro = go_ref[...] - jnp.where(is_first, 0.0, bo)
    both = passes(pair, jnp.concatenate([r, ro], axis=0))
    if split:
        sent = jnp.concatenate([ref[...] for ref in sent_refs], axis=0)
        both += passes(pair_sent, jnp.where(is_first, 0.0, sent))
    shared = passes(single, jnp.concatenate([b, bo], axis=0))
    part0 = both[:256] - jnp.where(is_first, shared, 0.0)
    part1 = both[256:] + shared
    out[:, 0] = part0.reshape(16, 16, part0.shape[1])
    out[:, 1] = part1.reshape(16, 16, part1.shape[1])


def grad_parts(party, x, a, got, rights, sent, weight):
    tokens, ff = rights[0].shape
    lefts = (x, a, *got)
    right = pl.BlockSpec((tokens, TILE), lambda n: (0, n))
    skip, per = 512 // TILE, 1024 // TILE
    part = pl.BlockSpec((128, TILE), lambda n: (n // per, skip + n % per))
    return pl.pallas_call(
        lambda *refs: grad_kernel(bool(sent), *refs),
        grid=(ff // TILE,),
        in_specs=[SMEM]
        + [pl.BlockSpec(v.shape, lambda n: (0, 0)) for v in lefts]
        + [right] * 4
        + [part] * len(sent),
        out_specs=pl.BlockSpec((16, 2, 16, TILE), lambda n: (0, 0, 0, n)),
        out_shape=jax.ShapeDtypeStruct((16, 2, 16, ff), F32),
        scratch_shapes=[
            pltpu.VMEM((1024, 2 * tokens), BF16),
            pltpu.VMEM((1024, 256), BF16),
            pltpu.VMEM((512, 2 * tokens), BF16),
        ],
        cost_estimate=cost(3 * 2 * 768 * 2 * tokens * ff, *rights, *lefts, rights[0], weight=weight),
        compiler_params=params(),
    )(party, *lefts, *rights, *sent)


def store_split(value, stack):
    rows = value.shape[0]
    for xl in range(2):
        cols = [value[:, (2 * y + xl) * 128 :][:, :128] for y in range(4)]
        at = slice(xl * 512, xl * 512 + 512)
        stack[:rows, at], stack[rows:, at] = halves(jnp.concatenate(cols, axis=1))


def add_product(c_ref, w0_ref, w1_ref, out, stack):
    w = jnp.concatenate([w0_ref[...], w1_ref[...]], axis=0)
    out[...] = c_ref[...] + passes(stack, w)


def local_kernel(a_ref, w0_ref, w1_ref, c_ref, out, stack):
    @pl.when(pl.program_id(0) == 0)
    def _():
        store_split(a_ref[...], stack)

    add_product(c_ref, w0_ref, w1_ref, out, stack)


def opened_kernel(x_ref, a_ref, got_ref, w0_ref, w1_ref, c_ref, out, stack):
    @pl.when(pl.program_id(0) == 0)
    def _():
        store_split((x_ref[...] - a_ref[...]) + got_ref[...], stack)

    add_product(c_ref, w0_ref, w1_ref, out, stack)


def forward_call(kernel, lefts, weights, at, c):
    rows, ff = c.shape
    d = lefts[0].shape[1]
    steps = ff // TILE
    tile = pl.BlockSpec((rows, TILE), lambda n: (0, n))
    return pl.pallas_call(
        kernel,
        grid=(steps,),
        in_specs=[pl.BlockSpec((rows, d), lambda n: (0, 0))] * len(lefts)
        + [
            pl.BlockSpec((d // 2, TILE), lambda n: (0, at * steps + n)),
            pl.BlockSpec((d // 2, TILE), lambda n: (0, (at + 2) * steps + n)),
            tile,
        ],
        out_specs=tile,
        out_shape=jax.ShapeDtypeStruct(c.shape, F32),
        scratch_shapes=[pltpu.VMEM((2 * rows, d), BF16)],
        cost_estimate=cost(3 * 2 * rows * d * ff, weights, c, weight=LATE),
        compiler_params=params(),
    )(*lefts, weights, weights, c)


def scattered_pair(a, a_axis, a_dim, b, b_axis, b_dim, first=(), last=()):
    sums, got = [], [[], []]
    for v, axis, dim in ((a, a_axis, a_dim), (b, b_axis, b_dim)):
        here = lax.axis_index(axis)
        sums.append(lax.dynamic_index_in_dim(v, here, dim, keepdims=False))
    for step in (2, 1, 3):
        for n, (v, axis, dim) in enumerate(((a, a_axis, a_dim), (b, b_axis, b_dim))):
            here = lax.axis_index(axis)
            piece = lax.dynamic_index_in_dim(v, (here + step) % 4, dim, keepdims=False)
            if len(got[n]) < 2:
                piece = after(piece, *first)
            else:
                piece = after(piece, got[n][0], *last)
            got[n].append(lax.ppermute(piece, axis, [(i, (i + step) % 4) for i in range(4)]))
    return [s + r[0] + r[1] + r[2] for s, r in zip(sums, got)]


def body(x_share, w_share, g_share, fwd_a, fwd_b, fwd_c, bwd_a, bwd_b, bwd_c):
    x, w, g = x_share[0], w_share[0], g_share[0]
    fa, fb, fc = fwd_a[0], fwd_b[0], fwd_c[0]
    ba, bb, bc = bwd_a[0], bwd_b[0], bwd_c[0]
    party = lax.axis_index("party")
    party0 = party == 0
    first = party0.astype(F32)
    party_id = party.astype(jnp.int32).reshape(1)
    core_id = lax.axis_index("core").astype(jnp.int32).reshape(1)
    xl0 = lax.axis_index("xl") == 0
    ff = w.shape[1]

    x_mine0, x_mine1, x_theirs = turned(core_id, x)
    x0 = lax.ppermute(x_mine0, "party", SWAP)
    x_other = lax.ppermute(x_theirs, "core", SWAP)
    xs0 = jnp.concatenate([x_mine0, x_other[0]], axis=1)
    xs1 = jnp.concatenate([x_mine1, x_other[1]], axis=1)
    a_mine0, a_mine1, a_theirs = turned(core_id, after(ba, x_other))
    a_other = lax.ppermute(a_theirs, "core", SWAP)
    aa0 = jnp.concatenate([a_mine0, a_other[0]], axis=1)
    aa1 = jnp.concatenate([a_mine1, a_other[1]], axis=1)
    d = w - fb
    d_party = lax.ppermute(d, "party", SWAP)
    near = lax.ppermute(jnp.concatenate([fb, d], axis=1), "xl", SWAP)
    d_across = lax.ppermute(d, ("party", "xl"), [(0, 3), (3, 0), (1, 2), (2, 1)])
    d_party, near, d_across = lax.optimization_barrier((d_party, near, d_across, x_theirs))[:3]
    delta = d + d_party
    delta_near = near[:, ff:] + d_across
    packed = jnp.concatenate([fb + first * delta, delta], axis=1)
    packed_near = jnp.concatenate([near[:, :ff] + first * delta_near, delta_near], axis=1)
    weights = jnp.concatenate(
        [jnp.where(xl0, packed, packed_near), jnp.where(xl0, packed_near, packed)], axis=1
    )
    weights = lax.all_gather(after(weights, x0, x_other, a_other), ("y", "z", "core"), axis=0, tiled=True)

    last = g[3 * g.shape[0] // 4 :]
    last = jnp.concatenate([last[:, : ff // 2], last[:, ff // 2 :]], axis=0)
    sent0 = jnp.concatenate([x_other[0], jnp.where(party0, last, aa0)], axis=1)
    got0 = lax.ppermute(sent0, "party", SWAP)
    sent1 = jnp.concatenate(
        [
            xs1[:, :384],
            jnp.where(party0, xs1[:, 384:512], aa1[:, :128]),
            xs1[:, 512:896],
            jnp.where(party0, xs1[:, 896:], aa1[:, 512:640]),
            aa1[:, 128:384],
            aa1[:, 640:896],
        ],
        axis=1,
    )
    got1 = lax.ppermute(sent1, "party", SWAP)
    u = x - fa
    u = lax.ppermute(after(u, got0), "party", SWAP)

    g_other = lax.ppermute(after(g, a_theirs), "core", SWAP)
    b_other = lax.ppermute(after(bb, a_theirs), "core", SWAP)
    rights = (g, bb, g_other, b_other)
    early = grad_parts(party_id, xs0, aa0, (x0, got0), rights, (), 1)
    sent = (got0, lax.ppermute(after(got0, early), "core", SWAP))
    late = grad_parts(party_id, xs1, aa1, (got1,), rights, sent, LATE)

    early = lax.psum_scatter(early.reshape(4, 4, 32, ff), "z", scatter_dimension=0, tiled=True)
    early = lax.psum_scatter(early[0], "y", scatter_dimension=0, tiled=True)
    early = early.reshape(2, 2, 8, ff)
    outputs = forward_call(local_kernel, (fa,), weights, 1, fc)
    late = late.reshape(4, 4, 2, 16, ff)
    part0, part1 = scattered_pair(late[:, :, 0], "z", 0, late[:, :, 1], "y", 1, (), (outputs,))
    part0, part1 = scattered_pair(part0, "y", 0, part1, "z", 0, (u,))
    late = jnp.stack([part0, part1]).reshape(2, 2, 8, ff)
    both = jnp.concatenate([early, late], axis=2)
    spot = 2 * party + lax.axis_index("xl")

    def piece(at):
        return lax.dynamic_index_in_dim(both.reshape(4, *bc.shape), at % 4, 0, keepdims=False)

    grad = piece(spot) + first * bc
    for step in (2, 1, 3):
        give = piece(spot + step)
        if step == 2:
            give = give - first * bc
        grad = grad + lax.ppermute(
            give, ("party", "xl"), [(i, (i + step) % 4) for i in range(4)]
        )

    outputs = forward_call(opened_kernel, (x, fa, u), weights, 0, outputs)
    return (outputs[None], grad[None])


def solution(mesh):
    split = Mesh(
        mesh.devices.reshape(mesh.shape["party"], 4, 2, 4, 2),
        ("party", *DP),
    )
    spec = P("party", DP, None)
    return jax.shard_map(
        body, mesh=split, in_specs=(spec,) * 9, out_specs=(spec, spec), check_vma=False
    )
```

time: 260 us -> 242 us (0.931)
  waiting for transfers between devices: 53.5 us -> 88.8 us
  Pallas kernels: 99.6 us -> 66.9 us
  starting transfers between devices: 54.4 us -> 39.1 us
  local copies, waits for them, and re-layouts: 18.5 us -> 15.1 us
    pallas_call x6 -> x4, Pallas kernels: 68.9 us -> 41.5 us  [the longest x2 35.6 us: grad_parts(): pl.pallas_call(lambda *refs: grad_kernel(bool(sent), *refs), grid=(ff //...]
    ppermute x12 -> x9, waiting for transfers between devices: 15.9 us -> 36.9 us  [the longest x1 29.6 us: body(): got0 = lax.ppermute(sent0, 'party', SWAP)]
    reduce_scatter x0 -> x2, waiting for transfers between devices: none -> 9.53 us  [the longest x1 9.5 us: body(): lax.psum_scatter(early.reshape(4, 4, 32, ff), 'z', scatter_dimension=0, t...]
    ppermute x12 -> x9, starting transfers between devices: 18.9 us -> 11.1 us  [the longest x3 6.21 us: body(): lax.ppermute(give, ('party', 'xl'), [(i, (i + step) % 4) for i in range(4)])]
    ppermute x12, starting transfers between devices: 28.3 us -> 20.9 us  [scattered_pair(): lax.ppermute(piece, axis, [(i, (i + step) % 4) for i in range(4)])]
    ppermute x1, waiting for transfers between devices: 7.28 us -> 0.01 us  [body(): lax.ppermute(d, ('party', 'xl'), [(0, 3), (3, 0), (1, 2), (2, 1)])]
    ppermute x1, waiting for transfers between devices: 0.01 us -> 6.97 us  [body(): x0 = lax.ppermute(x_mine0, 'party', SWAP)]
    ppermute x12, waiting for transfers between devices: 22.3 us -> 27.8 us  [scattered_pair(): lax.ppermute(piece, axis, [(i, (i + step) % 4) for i in range(4)])]
  transfers between devices with their start and end apart: 32 -> 30, of which waited for: 12 -> 10; matrix products, arithmetic and copies ran while one was open for 10% -> 10% of each run, Pallas kernels for 36% -> 27%
where the time goes in v5:
time: 242 us; the launch traced here: 241 us
  waiting for transfers between devices  88.8 us (37%)
  Pallas kernels  66.9 us (28%)
  starting transfers between devices  39.1 us (16%)
  between operations  15.9 us (7%)
  other arithmetic  15.2 us (6%)
  local copies, waits for them, and re-layouts  15.1 us (6%)
    pallas_call x2, Pallas kernels, grad_parts(): pl.pallas_call(lambda *refs: grad_kernel(bool(sent), *refs), grid=(ff //...  35.6 us
    ppermute x1, waiting for transfers between devices, body(): got0 = lax.ppermute(sent0, 'party', SWAP)  29.6 us
    ppermute x12, waiting for transfers between devices, scattered_pair(): lax.ppermute(piece, axis, [(i, (i + step) % 4) for i in range(4)])  27.8 us
    pallas_call x2, Pallas kernels, forward_call(): pl.pallas_call(kernel, grid=(steps,), in_specs=[pl.BlockSpec((rows, d), l...  25.4 us
    ppermute x12, starting transfers between devices, scattered_pair(): lax.ppermute(piece, axis, [(i, (i + step) % 4) for i in range(4)])  20.9 us
    reduce_scatter x1, waiting for transfers between devices, body(): lax.psum_scatter(early.reshape(4, 4, 32, ff), 'z', scatter_dimension=0, t...  9.5 us
    unnamed x37, local copies, waits for them, and re-layouts  7.79 us
    ppermute x1, waiting for transfers between devices, body(): d_party = lax.ppermute(d, 'party', SWAP)  7.59 us
  transfers between devices with their start and end apart: 30, of which 10 were waited for; matrix products, arithmetic and copies ran while one was open for 10% of the time, Pallas kernels for 27%

profile of v5, /device:TPU:0, one launch (start us, length us, event | category | flops | bytes accessed | tf_op | source)
XLA Modules:
  0.0 240.9 jit_solution(12916434699143204334)
XLA Ops:
  8.1 3.0 %shard_map.104 = (f32[4,4,2,8,512]{4,3,2,1,0:T(8,128)}, f32[4,4,2,8,512]{4,3,2,1,0:T(8,128)}, f32[2,4,4,2,8,512]{5,4,3,2,1,0:T(8,128)}) custom-call(s32[1]{0:T(128)} %bitcast.2.core_ref, f32[512,1024]{1,0:T(8,128)} %bitcast.111), custom_call_target="tpu_custom_call" | custom-call | bytes 4194304 | tf_op jit(solution)/shard_map/pallas_call | solution.py:60
  11.1 1.7 collective-permute-start.5
  12.7 2.7 %collective-permute-start.4 = (f32[16,2048]{1,0:T(8,128)S(1)}, f32[16,2048]{1,0:T(8,128)S(1)}, u32[]{:S(2)}, u32[]{:S(2)}) collective-permute-start(f32[16,2048]{1,0:T(8,128)S(1)} %bitcast_subtract_fusion), channel_id=1, source_target_pairs={{0,64},{64,0},{1,65},{65,1},{2,66},{66,2},{3,67},{67,3},{4,68},{68... | collective-permute-start | bytes 393224 | tf_op jit(solution)/shard_map/ppermute | solution.py:239
  15.9 1.9 collective-permute-start.7
  17.8 7.6 %collective-permute-done.4 = f32[16,2048]{1,0:T(8,128)S(1)} collective-permute-done((f32[16,2048]{1,0:T(8,128)S(1)}, f32[16,2048]{1,0:T(8,128)S(1)}, u32[]{:S(2)}, u32[]{:S(2)}) %collective-permute-start.4) | collective-permute-done | bytes 131104 | tf_op jit(solution)/shard_map/ppermute | solution.py:239
  25.4 2.9 %shard_map.105 = (f32[4,4,2,8,512]{4,3,2,1,0:T(8,128)}, f32[4,4,2,8,512]{4,3,2,1,0:T(8,128)}, f32[2,4,4,2,8,512]{5,4,3,2,1,0:T(8,128)}) custom-call(s32[1]{0:T(128)} %bitcast.2.core_ref, f32[512,1024]{1,0:T(8,128)} %bitcast.119), custom_call_target="tpu_custom_call" | custom-call | bytes 4194304 | tf_op jit(solution)/shard_map/pallas_call | solution.py:60
  28.4 0.8 pad_maximum_fusion.5
  29.2 7.0 %collective-permute-done.7.refs_3_ = f32[256,512]{1,0:T(8,128)S(1)} collective-permute-done((f32[256,512]{1,0:T(8,128)}, f32[256,512]{1,0:T(8,128)S(1)}, u32[]{:S(2)}, u32[]{:S(2)}) %collective-permute-start.7) | collective-permute-done | bytes 524320 | tf_op jit(solution)/shard_map/ppermute | solution.py:230
  36.9 1.3 slice_bitcast_fusion
  38.4 0.9 copy-done.8
  39.3 1.1 pad_maximum_fusion.1
  40.6 0.9 collective-permute-start.2
  42.3 1.1 pad_maximum_fusion.2.refs_1_
  44.1 0.8 slice_dynamic-update-slice_fusion
  47.1 2.7 %collective-permute-start.10 = (f32[256,1536]{1,0:T(8,128)}, f32[256,1536]{1,0:T(8,128)}, u32[]{:S(2)}, u32[]{:S(2)}) collective-permute-start(f32[256,1536]{1,0:T(8,128)} %slice_dynamic-update-slice_fusion.2), channel_id=1, source_target_pairs={{0,64},{64,0},{1,65},{65,1},{2,66},{66,2},{3,67},{67,3},{4,68},{68... | collective-permute-start | bytes 4718600 | tf_op jit(solution)/shard_map/ppermute | solution.py:267
  49.9 29.6 %collective-permute-done.2.refs_4_.refs_8_ = f32[256,1536]{1,0:T(8,128)S(1)} collective-permute-done((f32[256,1536]{1,0:T(8,128)S(1)}, f32[256,1536]{1,0:T(8,128)S(1)}, u32[]{:S(2)}, u32[]{:S(2)}) %collective-permute-start.2) | collective-permute-done | bytes 1572896 | tf_op jit(solution)/shard_map/ppermute | solution.py:255
  79.5 2.5 %copy-done.15 = f32[256,1536]{1,0:T(8,128)} copy-done((f32[256,1536]{1,0:T(8,128)}, f32[256,1536]{1,0:T(8,128)S(1)}, u32[]{:S(2)}) %copy-start.15) | copy-done | bytes 1572888
  81.9 1.3 copy-done.13
  83.3 16.6 %shard_map.108 = f32[16,2,16,2048]{3,2,1,0:T(8,128)} custom-call(s32[1]{0:T(128)} %bitcast.15.refs_0_, f32[256,1024]{1,0:T(8,128)} %pad_maximum_fusion.2.refs_1_, f32[256,1024]{1,0:T(8,128)} %get-tuple-element.64.refs_2_, f32[256,512]{1,0:T(8,128)} %copy-done.16, f32[256,1536]{1,0:T(8,128)} %copy-done.15, f32[512,2048]{1,0:T(8,128)} %bitcast.134, ...), custom_call_target="tpu_custom_call" | custom-call | flops 9663676416 | bytes 25165824 | tf_op jit(solution)/shard_map/pallas_call | solution.py:130
  100.0 3.4 %bitcast_subtract_fusion.1 = f32[512,1024]{1,0:T(8,128)} fusion(f32[1,512,1024]{2,1,0:T(8,128)} %param.12, f32[1,512,1024]{2,1,0:T(8,128)S(1)} %copy-done), kind=kLoop, calls=%fused_computation.78 | loop fusion | flops 524288 | bytes 6291456 | tf_op jit(solution)/shard_map/sub | solution.py:268
  103.4 1.5 pad_maximum_fusion.3
  106.0 7.3 %collective-permute-done.10.refs_3_ = f32[256,1536]{1,0:T(8,128)} collective-permute-done((f32[256,1536]{1,0:T(8,128)}, f32[256,1536]{1,0:T(8,128)}, u32[]{:S(2)}, u32[]{:S(2)}) %collective-permute-start.10) | collective-permute-done | bytes 1572896 | tf_op jit(solution)/shard_map/ppermute | solution.py:267
  113.2 18.9 %shard_map.109 = f32[16,2,16,2048]{3,2,1,0:T(8,128)} custom-call(s32[1]{0:T(128)} %bitcast.15.refs_0_, f32[256,1024]{1,0:T(8,128)} %get-tuple-element.81.refs_1_, f32[256,1024]{1,0:T(8,128)} %get-tuple-element.82.refs_2_, f32[256,1536]{1,0:T(8,128)} %collective-permute-done.10.refs_3_, f32[512,2048]{1,0:T(8,128)} %bitcast.135, f32[512,2048]{1,0:T(8,128)} %bitcast.138, ...), custom_call_target="tpu_custom_call" | custom-call | flops 77309411328 | bytes 197132288 | tf_op jit(solution)/shard_map/pallas_call | solution.py:130
  132.2 2.6 %fusion.28 = (f32[4,4,1,16,2048]{4,3,2,1,0:T(8,128)S(1)}, f32[4,4,1,16,2048]{4,3,2,1,0:T(8,128)S(1)}) fusion(f32[4,4,2,16,2048]{4,3,2,1,0:T(8,128)} %bitcast.114), kind=kLoop, calls=%fused_computation.79 | loop fusion | bytes 8388608 | tf_op jit(solution)/shard_map/slice | solution.py:283
  134.8 1.2 dynamic-slice_bitcast_fusion.4
  136.0 4.0 %collective-permute-start.12 = (f32[4,16,2048]{2,1,0:T(8,128)}, f32[4,16,2048]{2,1,0:T(8,128)}, u32[]{:S(2)}, u32[]{:S(2)}) collective-permute-start(f32[4,16,2048]{2,1,0:T(8,128)} %get-tuple-element.56), channel_id=1, source_target_pairs={{0,4},{2,6},{4,0},{6,2},{1,5},{3,7},{5,1},{7,3},{8,12},{10,14},{12... | collective-permute-start | bytes 1572872 | tf_op jit(solution)/shard_map/ppermute | solution.py:213
  140.1 1.0 collective-permute-start.13
  141.1 1.1 dynamic-slice_bitcast_fusion.1
  142.2 3.2 %collective-permute-start.18 = (f32[4,16,2048]{2,1,0:T(8,128)}, f32[4,16,2048]{2,1,0:T(8,128)}, u32[]{:S(2)}, u32[]{:S(2)}) collective-permute-start(f32[4,16,2048]{2,1,0:T(8,128)} %get-tuple-element.59), channel_id=1, source_target_pairs={{0,32},{16,48},{32,0},{48,16},{1,33},{17,49},{33,1},{49,17},{2,34}... | collective-permute-start | bytes 1572872 | tf_op jit(solution)/shard_map/ppermute | solution.py:213
  145.4 12.0 %shard_map.106.c_ref = f32[512,2048]{1,0:T(8,128)} custom-call(f32[512,1024]{1,0:T(8,128)} %bitcast.117, f32[512,8192]{1,0:T(8,128)} %all-gather.2.cloned.1.call-done.w0_ref.w1_ref, f32[512,8192]{1,0:T(8,128)} %all-gather.2.cloned.1.call-done.w0_ref.w1_ref, f32[512,2048]{1,0:T(8,128)} %bitcast.139), custom_call_target="tpu_custom_call" | custom-call | flops 51539607552 | bytes 167772160 | tf_op jit(solution)/shard_map/pallas_call | solution.py:183
  157.4 7.1 %collective-permute-done.12 = f32[4,16,2048]{2,1,0:T(8,128)} collective-permute-done((f32[4,16,2048]{2,1,0:T(8,128)}, f32[4,16,2048]{2,1,0:T(8,128)}, u32[]{:S(2)}, u32[]{:S(2)}) %collective-permute-start.12) | collective-permute-done | bytes 524320 | tf_op jit(solution)/shard_map/ppermute | solution.py:213
  164.6 1.8 collective-permute-start.14
  166.4 1.4 collective-permute-start.19
  167.9 9.5 %reduce-scatter.3.cloned.1.call-done = f32[1,4,32,2048]{3,2,1,0:T(8,128)} async-done(((f32[4,4,32,2048]{3,2,1,0:T(8,128)}), f32[1,4,32,2048]{3,2,1,0:T(8,128)}) %reduce-scatter.3.cloned.1.call-update) | async-done | bytes 1048592 | tf_op jit(solution)/shard_map/reduce_scatter | solution.py:278
  177.4 2.8 %collective-permute-start.20 = (f32[4,16,2048]{2,1,0:T(8,128)S(1)}, f32[4,16,2048]{2,1,0:T(8,128)S(1)}, u32[]{:S(2)}, u32[]{:S(2)}) collective-permute-start(f32[4,16,2048]{2,1,0:T(8,128)S(1)} %get-tuple-element.44), channel_id=1, source_target_pairs={{0,48},{16,0},{32,16},{48,32},{1,49},{17,1},{33,17},{49,33},{2,50}... | collective-permute-start | bytes 1572872 | tf_op jit(solution)/shard_map/ppermute | solution.py:213
  180.2 1.6 fusion.3
  181.9 0.9 collective-permute-start.15
  182.8 16.4 %collective-permute-done.20 = f32[4,16,2048]{2,1,0:T(8,128)S(1)} collective-permute-done((f32[4,16,2048]{2,1,0:T(8,128)S(1)}, f32[4,16,2048]{2,1,0:T(8,128)S(1)}, u32[]{:S(2)}, u32[]{:S(2)}) %collective-permute-start.20) | collective-permute-done | bytes 524320 | tf_op jit(solution)/shard_map/ppermute | solution.py:213
  199.2 1.3 fusion.1
  201.4 4.0 %collective-permute-start.17 = (f32[16,2048]{1,0:T(8,128)S(1)}, f32[16,2048]{1,0:T(8,128)S(1)}, u32[]{:S(2)}, u32[]{:S(2)}) collective-permute-start(f32[16,2048]{1,0:T(8,128)S(1)} %get-tuple-element.43), channel_id=1, source_target_pairs={{0,48},{16,0},{32,16},{48,32},{1,49},{17,1},{33,17},{49,33},{2,50}... | collective-permute-start | bytes 393224 | tf_op jit(solution)/shard_map/ppermute | solution.py:213
  205.4 1.7 collective-permute-done.21
  207.1 1.5 collective-permute-start.23
  208.7 0.9 fusion.27
  209.6 2.0 collective-permute-done.22
  212.2 0.9 fusion.17
  213.2 3.0 %collective-permute-start.24 = (f32[16,2048]{1,0:T(8,128)S(1)}, f32[16,2048]{1,0:T(8,128)S(1)}, u32[]{:S(2)}, u32[]{:S(2)}) collective-permute-start(f32[16,2048]{1,0:T(8,128)S(1)} %get-tuple-element.68), channel_id=1, source_target_pairs={{0,64},{8,72},{64,0},{72,8},{1,65},{9,73},{65,1},{73,9},{2,66},{10... | collective-permute-start | bytes 393224 | tf_op jit(solution)/shard_map/ppermute | solution.py:297
  216.7 2.7 %collective-permute-start.26 = (f32[16,2048]{1,0:T(8,128)S(1)}, f32[16,2048]{1,0:T(8,128)S(1)}, u32[]{:S(2)}, u32[]{:S(2)}) collective-permute-start(f32[16,2048]{1,0:T(8,128)S(1)} %get-tuple-element.70), channel_id=1, source_target_pairs={{0,72},{8,0},{64,8},{72,64},{1,73},{9,1},{65,9},{73,65},{2,74},{10... | collective-permute-start | bytes 393224 | tf_op jit(solution)/shard_map/ppermute | solution.py:297
  219.4 13.4 %shard_map.107 = f32[512,2048]{1,0:T(8,128)} custom-call(f32[512,1024]{1,0:T(8,128)} %bitcast.112, f32[512,1024]{1,0:T(8,128)} %bitcast.118, f32[512,1024]{1,0:T(8,128)} %collective-permute-done.3.got_ref, f32[512,8192]{1,0:T(8,128)} %all-gather.2.cloned.1.call-done.w0_ref.w1_ref, f32[512,8192]{1,0:T(8,128)} %all-gather.2.cloned.1.call-done.w0_ref.w1_ref, ...), custom_call_target="tpu_custom_call" | custom-call | flops 51539607552 | bytes 167772160 | tf_op jit(solution)/shard_map/pallas_call | solution.py:183
  (87 shorter events, 9.1 us)
Async XLA Ops:
  8.0 3.0 %copy-start.11 = (f32[1,16,2048]{2,1,0:T(8,128)S(1)}, f32[1,16,2048]{2,1,0:T(8,128)}, u32[]{:S(2)}) copy-start(f32[1,16,2048]{2,1,0:T(8,128)} %param.10) | copy-start | bytes 393220
  8.0 3.0 %copy-start.6 = (f32[1,16,2048]{2,1,0:T(8,128)S(1)}, f32[1,16,2048]{2,1,0:T(8,128)}, u32[]{:S(2)}) copy-start(f32[1,16,2048]{2,1,0:T(8,128)} %param.13) | copy-start | bytes 393220
  8.0 137.4 %all-gather.2.cloned.1.call-start = ((), (), s32[]{:S(2)}) async-start(), calls=%async_computation.2 | async-start | bytes 17301504 | tf_op jit(solution)/shard_map/all_gather | solution.py:250
  11.0 14.4 %collective-permute-start = (f32[2,256,512]{2,1,0:T(8,128)}, f32[2,256,512]{2,1,0:T(8,128)S(1)}, u32[]{:S(2)}, u32[]{:S(2)}) collective-permute-start(f32[2,256,512]{2,1,0:T(8,128)} %bitcast.140), channel_id=1, source_target_pairs={{0,1},{1,0},{2,3},{3,2},{4,5},{5,4},{6,7},{7,6},{8,9},{9,8},{10,11... | collective-permute-start | bytes 3145736 | tf_op jit(solution)/shard_map/ppermute | solution.py:231
  11.1 14.3 %collective-permute-start.5 = (f32[16,4096]{1,0:T(8,128)S(1)}, f32[16,4096]{1,0:T(8,128)S(1)}, u32[]{:S(2)}, u32[]{:S(2)}) collective-permute-start(f32[16,4096]{1,0:T(8,128)S(1)} %pad_maximum_fusion.6), channel_id=1, source_target_pairs={{0,8},{8,0},{1,9},{9,1},{2,10},{10,2},{3,11},{11,3},{4,12},{12,4},... | collective-permute-start | bytes 786440 | tf_op jit(solution)/shard_map/ppermute | solution.py:240
  12.7 12.6 %collective-permute-start.4 = (f32[16,2048]{1,0:T(8,128)S(1)}, f32[16,2048]{1,0:T(8,128)S(1)}, u32[]{:S(2)}, u32[]{:S(2)}) collective-permute-start(f32[16,2048]{1,0:T(8,128)S(1)} %bitcast_subtract_fusion), channel_id=1, source_target_pairs={{0,64},{64,0},{1,65},{65,1},{2,66},{66,2},{3,67},{67,3},{4,68},{68... | collective-permute-start | bytes 393224 | tf_op jit(solution)/shard_map/ppermute | solution.py:239
  15.5 9.9 %collective-permute-start.6 = (f32[16,2048]{1,0:T(8,128)S(1)}, f32[16,2048]{1,0:T(8,128)S(1)}, u32[]{:S(2)}, u32[]{:S(2)}) collective-permute-start(f32[16,2048]{1,0:T(8,128)S(1)} %bitcast_subtract_fusion), channel_id=1, source_target_pairs={{0,72},{72,0},{8,64},{64,8},{1,73},{73,1},{9,65},{65,9},{2,74},{74... | collective-permute-start | bytes 393224 | tf_op jit(solution)/shard_map/ppermute | solution.py:241
  15.9 20.3 %collective-permute-start.7 = (f32[256,512]{1,0:T(8,128)}, f32[256,512]{1,0:T(8,128)S(1)}, u32[]{:S(2)}, u32[]{:S(2)}) collective-permute-start(f32[256,512]{1,0:T(8,128)} %bitcast.131), channel_id=1, source_target_pairs={{0,64},{64,0},{1,65},{65,1},{2,66},{66,2},{3,67},{67,3},{4,68},{68... | collective-permute-start | bytes 1572872 | tf_op jit(solution)/shard_map/ppermute | solution.py:230
  28.3 7.9 %collective-permute-start.1 = (f32[2,256,512]{2,1,0:T(8,128)}, f32[2,256,512]{2,1,0:T(8,128)S(1)}, u32[]{:S(2)}, u32[]{:S(2)}) collective-permute-start(f32[2,256,512]{2,1,0:T(8,128)} %bitcast.141), channel_id=1, source_target_pairs={{0,1},{1,0},{2,3},{3,2},{4,5},{5,4},{6,7},{7,6},{8,9},{9,8},{10,11... | collective-permute-start | bytes 3145736 | tf_op jit(solution)/shard_map/ppermute | solution.py:235
  36.2 2.1 copy-start.16
  36.2 141.1 %reduce-scatter.3.cloned.1.call-start = ((), (), s32[]{:S(2)}) async-start(), calls=%async_computation.3 | async-start | bytes 5242880 | tf_op jit(solution)/shard_map/reduce_scatter | solution.py:278
  36.3 43.2 %collective-permute-start.8 = (f32[512,2048]{1,0:T(8,128)}, f32[512,2048]{1,0:T(8,128)S(1)}, u32[]{:S(2)}, u32[]{:S(2)}) collective-permute-start(f32[512,2048]{1,0:T(8,128)} %bitcast.133), channel_id=1, source_target_pairs={{0,1},{1,0},{2,3},{3,2},{4,5},{5,4},{6,7},{7,6},{8,9},{9,8},{10,11... | collective-permute-start | bytes 12582920 | tf_op jit(solution)/shard_map/ppermute | solution.py:271
  36.4 43.1 %collective-permute-start.9 = (f32[512,2048]{1,0:T(8,128)}, f32[512,2048]{1,0:T(8,128)S(1)}, u32[]{:S(2)}, u32[]{:S(2)}) collective-permute-start(f32[512,2048]{1,0:T(8,128)} %bitcast.136), channel_id=1, source_target_pairs={{0,1},{1,0},{2,3},{3,2},{4,5},{5,4},{6,7},{7,6},{8,9},{9,8},{10,11... | collective-permute-start | bytes 12582920 | tf_op jit(solution)/shard_map/ppermute | solution.py:272
  38.3 1.0 copy-start.8
  40.5 1.0 copy-start.2
  40.5 1.9 copy-start.9
  40.6 2.8 %copy-start.4 = (f32[4,4,2,8,512]{4,3,2,1,0:T(8,128)S(1)}, f32[4,4,2,8,512]{4,3,2,1,0:T(8,128)}, u32[]{:S(2)}) copy-start(f32[4,4,2,8,512]{4,3,2,1,0:T(8,128)} %get-tuple-element.38) | copy-start | bytes 1572868
  40.6 38.8 %collective-permute-start.2 = (f32[256,1536]{1,0:T(8,128)S(1)}, f32[256,1536]{1,0:T(8,128)S(1)}, u32[]{:S(2)}, u32[]{:S(2)}) collective-permute-start(f32[256,1536]{1,0:T(8,128)S(1)} %pad_maximum_fusion), channel_id=1, source_target_pairs={{0,64},{64,0},{1,65},{65,1},{2,66},{66,2},{3,67},{67,3},{4,68},{68... | collective-permute-start | bytes 4718600 | tf_op jit(solution)/shard_map/ppermute | solution.py:255
  47.1 66.1 %collective-permute-start.10 = (f32[256,1536]{1,0:T(8,128)}, f32[256,1536]{1,0:T(8,128)}, u32[]{:S(2)}, u32[]{:S(2)}) collective-permute-start(f32[256,1536]{1,0:T(8,128)} %slice_dynamic-update-slice_fusion.2), channel_id=1, source_target_pairs={{0,64},{64,0},{1,65},{65,1},{2,66},{66,2},{3,67},{67,3},{4,68},{68... | collective-permute-start | bytes 4718600 | tf_op jit(solution)/shard_map/ppermute | solution.py:267
  79.4 2.5 %copy-start.15 = (f32[256,1536]{1,0:T(8,128)}, f32[256,1536]{1,0:T(8,128)S(1)}, u32[]{:S(2)}) copy-start(f32[256,1536]{1,0:T(8,128)S(1)} %collective-permute-done.2.refs_4_.refs_8_) | copy-start | bytes 4718596
  79.4 3.8 %copy-start.13 = (f32[512,2048]{1,0:T(8,128)}, f32[512,2048]{1,0:T(8,128)S(1)}, u32[]{:S(2)}) copy-start(f32[512,2048]{1,0:T(8,128)S(1)} %collective-permute-done.8.refs_7_.refs_6_) | copy-start | bytes 12582916
  79.4 2.5 %copy-start.14 = (f32[512,2048]{1,0:T(8,128)}, f32[512,2048]{1,0:T(8,128)S(1)}, u32[]{:S(2)}) copy-start(f32[512,2048]{1,0:T(8,128)S(1)} %collective-permute-done.9.refs_8_.refs_7_) | copy-start | bytes 12582916
  83.3 16.7 %copy-start = (f32[1,512,1024]{2,1,0:T(8,128)S(1)}, f32[1,512,1024]{2,1,0:T(8,128)}, u32[]{:S(2)}) copy-start(f32[1,512,1024]{2,1,0:T(8,128)} %param.9) | copy-start | bytes 6291460
  99.9 13.3 %collective-permute-start.11 = (f32[256,1536]{1,0:T(8,128)}, f32[256,1536]{1,0:T(8,128)}, u32[]{:S(2)}, u32[]{:S(2)}) collective-permute-start(f32[256,1536]{1,0:T(8,128)} %copy-done.15), channel_id=1, source_target_pairs={{0,1},{1,0},{2,3},{3,2},{4,5},{5,4},{6,7},{7,6},{8,9},{9,8},{10,11... | collective-permute-start | bytes 4718600 | tf_op jit(solution)/shard_map/ppermute | solution.py:275
  100.0 3.4 %copy-start.3 = (f32[4,4,2,8,512]{4,3,2,1,0:T(8,128)S(1)}, f32[4,4,2,8,512]{4,3,2,1,0:T(8,128)}, u32[]{:S(2)}) copy-start(f32[4,4,2,8,512]{4,3,2,1,0:T(8,128)} %get-tuple-element.37) | copy-start | bytes 1572868
  100.0 3.4 %copy-start.5 = (f32[4,4,2,8,512]{4,3,2,1,0:T(8,128)S(1)}, f32[4,4,2,8,512]{4,3,2,1,0:T(8,128)}, u32[]{:S(2)}) copy-start(f32[4,4,2,8,512]{4,3,2,1,0:T(8,128)} %get-tuple-element.38) | copy-start | bytes 1572868
  105.0 76.9 %collective-permute-start.3 = (f32[512,1024]{1,0:T(8,128)}, f32[512,1024]{1,0:T(8,128)}, u32[]{:S(2)}, u32[]{:S(2)}) collective-permute-start(f32[512,1024]{1,0:T(8,128)} %bitcast_subtract_fusion.1), channel_id=1, source_target_pairs={{0,64},{64,0},{1,65},{65,1},{2,66},{66,2},{3,67},{67,3},{4,68},{68... | collective-permute-start | bytes 6291464 | tf_op jit(solution)/shard_map/ppermute | solution.py:269
  105.7 106.5 %reduce-scatter.5.cloned.1.call-start = ((), (), s32[]{:S(2)}) async-start(), calls=%async_computation.4 | async-start | bytes 1310720 | tf_op jit(solution)/shard_map/reduce_scatter | solution.py:279
  134.8 7.5 %copy-start.1 = (f32[4,4,1,16,2048]{4,3,2,1,0:T(8,128)}, f32[4,4,1,16,2048]{4,3,2,1,0:T(8,128)S(1)}, u32[]{:S(2)}) copy-start(f32[4,4,1,16,2048]{4,3,2,1,0:T(8,128)S(1)} %get-tuple-element.52) | copy-start | bytes 6291460
  136.0 28.6 %collective-permute-start.12 = (f32[4,16,2048]{2,1,0:T(8,128)}, f32[4,16,2048]{2,1,0:T(8,128)}, u32[]{:S(2)}, u32[]{:S(2)}) collective-permute-start(f32[4,16,2048]{2,1,0:T(8,128)} %get-tuple-element.56), channel_id=1, source_target_pairs={{0,4},{2,6},{4,0},{6,2},{1,5},{3,7},{5,1},{7,3},{8,12},{10,14},{12... | collective-permute-start | bytes 1572872 | tf_op jit(solution)/shard_map/ppermute | solution.py:213
  140.1 40.1 %collective-permute-start.13 = (f32[4,16,2048]{2,1,0:T(8,128)}, f32[4,16,2048]{2,1,0:T(8,128)}, u32[]{:S(2)}, u32[]{:S(2)}) collective-permute-start(f32[4,16,2048]{2,1,0:T(8,128)} %get-tuple-element.54), channel_id=1, source_target_pairs={{0,2},{2,4},{4,6},{6,0},{1,3},{3,5},{5,7},{7,1},{8,10},{10,12},{12... | collective-permute-start | bytes 1572872 | tf_op jit(solution)/shard_map/ppermute | solution.py:213
  142.2 35.1 %collective-permute-start.18 = (f32[4,16,2048]{2,1,0:T(8,128)}, f32[4,16,2048]{2,1,0:T(8,128)}, u32[]{:S(2)}, u32[]{:S(2)}) collective-permute-start(f32[4,16,2048]{2,1,0:T(8,128)} %get-tuple-element.59), channel_id=1, source_target_pairs={{0,32},{16,48},{32,0},{48,16},{1,33},{17,49},{33,1},{49,17},{2,34}... | collective-permute-start | bytes 1572872 | tf_op jit(solution)/shard_map/ppermute | solution.py:213
  164.6 15.6 %collective-permute-start.14 = (f32[4,16,2048]{2,1,0:T(8,128)S(1)}, f32[4,16,2048]{2,1,0:T(8,128)}, u32[]{:S(2)}, u32[]{:S(2)}) collective-permute-start(f32[4,16,2048]{2,1,0:T(8,128)S(1)} %get-tuple-element.40), channel_id=1, source_target_pairs={{0,6},{2,0},{4,2},{6,4},{1,7},{3,1},{5,3},{7,5},{8,14},{10,8},{12,... | collective-permute-start | bytes 1572872 | tf_op jit(solution)/shard_map/ppermute | solution.py:213
  166.4 16.4 %collective-permute-start.19 = (f32[4,16,2048]{2,1,0:T(8,128)}, f32[4,16,2048]{2,1,0:T(8,128)}, u32[]{:S(2)}, u32[]{:S(2)}) collective-permute-start(f32[4,16,2048]{2,1,0:T(8,128)} %get-tuple-element.57), channel_id=1, source_target_pairs={{0,16},{16,32},{32,48},{48,0},{1,17},{17,33},{33,49},{49,1},{2,18}... | collective-permute-start | bytes 1572872 | tf_op jit(solution)/shard_map/ppermute | solution.py:213
  177.4 21.8 %collective-permute-start.20 = (f32[4,16,2048]{2,1,0:T(8,128)S(1)}, f32[4,16,2048]{2,1,0:T(8,128)S(1)}, u32[]{:S(2)}, u32[]{:S(2)}) collective-permute-start(f32[4,16,2048]{2,1,0:T(8,128)S(1)} %get-tuple-element.44), channel_id=1, source_target_pairs={{0,48},{16,0},{32,16},{48,32},{1,49},{17,1},{33,17},{49,33},{2,50}... | collective-permute-start | bytes 1572872 | tf_op jit(solution)/shard_map/ppermute | solution.py:213
  181.9 30.3 %copy-start.10 = (f32[1,16,2048]{2,1,0:T(8,128)S(1)}, f32[1,16,2048]{2,1,0:T(8,128)}, u32[]{:S(2)}) copy-start(f32[1,16,2048]{2,1,0:T(8,128)} %param.17) | copy-start | bytes 393220
  181.9 18.9 %collective-permute-start.15 = (f32[16,2048]{1,0:T(8,128)S(1)}, f32[16,2048]{1,0:T(8,128)S(1)}, u32[]{:S(2)}, u32[]{:S(2)}) collective-permute-start(f32[16,2048]{1,0:T(8,128)S(1)} %get-tuple-element.41), channel_id=1, source_target_pairs={{0,32},{16,48},{32,0},{48,16},{1,33},{17,49},{33,1},{49,17},{2,34}... | collective-permute-start | bytes 393224 | tf_op jit(solution)/shard_map/ppermute | solution.py:213
  200.6 6.6 %collective-permute-start.21 = (f32[16,2048]{1,0:T(8,128)S(1)}, f32[16,2048]{1,0:T(8,128)S(1)}, u32[]{:S(2)}, u32[]{:S(2)}) collective-permute-start(f32[16,2048]{1,0:T(8,128)S(1)} %get-tuple-element.45), channel_id=1, source_target_pairs={{0,4},{2,6},{4,0},{6,2},{1,5},{3,7},{5,1},{7,3},{8,12},{10,14},{12... | collective-permute-start | bytes 393224 | tf_op jit(solution)/shard_map/ppermute | solution.py:213
  200.7 8.0 %collective-permute-start.16 = (f32[16,2048]{1,0:T(8,128)S(1)}, f32[16,2048]{1,0:T(8,128)S(1)}, u32[]{:S(2)}, u32[]{:S(2)}) collective-permute-start(f32[16,2048]{1,0:T(8,128)S(1)} %get-tuple-element.42), channel_id=1, source_target_pairs={{0,16},{16,32},{32,48},{48,0},{1,17},{17,33},{33,49},{49,1},{2,18}... | collective-permute-start | bytes 393224 | tf_op jit(solution)/shard_map/ppermute | solution.py:213
  200.8 0.7 copy-start.12
  201.4 7.3 %collective-permute-start.17 = (f32[16,2048]{1,0:T(8,128)S(1)}, f32[16,2048]{1,0:T(8,128)S(1)}, u32[]{:S(2)}, u32[]{:S(2)}) collective-permute-start(f32[16,2048]{1,0:T(8,128)S(1)} %get-tuple-element.43), channel_id=1, source_target_pairs={{0,48},{16,0},{32,16},{48,32},{1,49},{17,1},{33,17},{49,33},{2,50}... | collective-permute-start | bytes 393224 | tf_op jit(solution)/shard_map/ppermute | solution.py:213
  205.4 6.2 %collective-permute-start.22 = (f32[16,2048]{1,0:T(8,128)S(1)}, f32[16,2048]{1,0:T(8,128)S(1)}, u32[]{:S(2)}, u32[]{:S(2)}) collective-permute-start(f32[16,2048]{1,0:T(8,128)S(1)} %get-tuple-element.46), channel_id=1, source_target_pairs={{0,2},{2,4},{4,6},{6,0},{1,3},{3,5},{5,7},{7,1},{8,10},{10,12},{12... | collective-permute-start | bytes 393224 | tf_op jit(solution)/shard_map/ppermute | solution.py:213
  207.1 5.0 %collective-permute-start.23 = (f32[16,2048]{1,0:T(8,128)S(1)}, f32[16,2048]{1,0:T(8,128)S(1)}, u32[]{:S(2)}, u32[]{:S(2)}) collective-permute-start(f32[16,2048]{1,0:T(8,128)S(1)} %get-tuple-element.47), channel_id=1, source_target_pairs={{0,6},{2,0},{4,2},{6,4},{1,7},{3,1},{5,3},{7,5},{8,14},{10,8},{12,... | collective-permute-start | bytes 393224 | tf_op jit(solution)/shard_map/ppermute | solution.py:213
  213.2 19.6 %collective-permute-start.24 = (f32[16,2048]{1,0:T(8,128)S(1)}, f32[16,2048]{1,0:T(8,128)S(1)}, u32[]{:S(2)}, u32[]{:S(2)}) collective-permute-start(f32[16,2048]{1,0:T(8,128)S(1)} %get-tuple-element.68), channel_id=1, source_target_pairs={{0,64},{8,72},{64,0},{72,8},{1,65},{9,73},{65,1},{73,9},{2,66},{10... | collective-permute-start | bytes 393224 | tf_op jit(solution)/shard_map/ppermute | solution.py:297
  216.1 16.7 %collective-permute-start.25 = (f32[16,2048]{1,0:T(8,128)S(1)}, f32[16,2048]{1,0:T(8,128)S(1)}, u32[]{:S(2)}, u32[]{:S(2)}) collective-permute-start(f32[16,2048]{1,0:T(8,128)S(1)} %get-tuple-element.69), channel_id=1, source_target_pairs={{0,8},{8,64},{64,72},{72,0},{1,9},{9,65},{65,73},{73,1},{2,10},{10... | collective-permute-start | bytes 393224 | tf_op jit(solution)/shard_map/ppermute | solution.py:297
  216.7 16.1 %copy-start.7 = (f32[1,32,2048]{2,1,0:T(8,128)S(1)}, f32[1,32,2048]{2,1,0:T(8,128)}, u32[]{:S(2)}) copy-start(f32[1,32,2048]{2,1,0:T(8,128)} %reduce-scatter.5.cloned.1.call-done) | copy-start | bytes 786436
  216.7 16.1 %collective-permute-start.26 = (f32[16,2048]{1,0:T(8,128)S(1)}, f32[16,2048]{1,0:T(8,128)S(1)}, u32[]{:S(2)}, u32[]{:S(2)}) collective-permute-start(f32[16,2048]{1,0:T(8,128)S(1)} %get-tuple-element.70), channel_id=1, source_target_pairs={{0,72},{8,0},{64,8},{72,64},{1,73},{9,1},{65,9},{73,65},{2,74},{10... | collective-permute-start | bytes 393224 | tf_op jit(solution)/shard_map/ppermute | solution.py:297
Sparse Core Ops, SparseCore 0:
  36.3 72.7 all-gather.1
Sparse Core Ops, SparseCore 1:
  105.8 71.5 reduce-scatter.2
  179.8 26.4 reduce-scatter.4

commit v6 on v5

--- a/solution.py
+++ b/solution.py
@@ -12,7 +12,7 @@
 BF16 = jnp.bfloat16
 SMEM = pl.BlockSpec(memory_space=pltpu.SMEM)
 TILE = 512
-LATE = 8
+LATE, BESIDE = 8, 1
 
 
 def cost(flops, *arrays, weight=1):
@@ -79,7 +79,7 @@
 
 def grad_kernel(split, p_ref, x_ref, a_ref, *refs):
     out, pair, pair_sent, single = refs[-4:]
-    got_refs, refs = (refs[:1], refs[1:]) if split else (refs[:2], refs[2:])
+    got_refs, refs = (refs[:1], refs[1:]) if split else (refs[:3], refs[3:])
     g_ref, b_ref, go_ref, bo_ref = refs[:4]
     sent_refs = refs[4:-4]
     is_first = p_ref[0] == 0
@@ -100,8 +100,8 @@
             pair_sent[:256], pair_sent[512:768] = halves(x_sent - a_sent)
             pair_sent[256:512], pair_sent[768:] = halves(a_sent)
         else:
-            got = jnp.concatenate([got_refs[0][...], got_refs[1][:, :512]], axis=1)
-            second = jnp.where(is_first, got_refs[1][:, 512:], a)
+            got = jnp.concatenate([got_refs[0][...], got_refs[1][...]], axis=1)
+            second = jnp.where(is_first, got_refs[2][...], a)
         opened = x + got
         pair[:256], pair[512:768] = halves(opened - second)
         pair[256:512], pair[768:] = halves(second)
@@ -125,8 +125,8 @@
     tokens, ff = rights[0].shape
     lefts = (x, a, *got)
     right = pl.BlockSpec((tokens, TILE), lambda n: (0, n))
-    skip, per = 512 // TILE, 1024 // TILE
-    part = pl.BlockSpec((128, TILE), lambda n: (n // per, skip + n % per))
+    per = 1024 // TILE
+    part = pl.BlockSpec((128, TILE), lambda n: (n // per, n % per))
     return pl.pallas_call(
         lambda *refs: grad_kernel(bool(sent), *refs),
         grid=(ff // TILE,),
@@ -192,24 +192,23 @@
         out_specs=tile,
         out_shape=jax.ShapeDtypeStruct(c.shape, F32),
         scratch_shapes=[pltpu.VMEM((2 * rows, d), BF16)],
-        cost_estimate=cost(3 * 2 * rows * d * ff, weights, c, weight=LATE),
+        cost_estimate=cost(3 * 2 * rows * d * ff, weights, c, weight=BESIDE),
         compiler_params=params(),
     )(*lefts, weights, weights, c)
 
 
-def scattered_pair(a, a_axis, a_dim, b, b_axis, b_dim, first=(), last=()):
+def scattered_pair(a, a_axis, a_dim, b, b_axis, b_dim, beside):
     sums, got = [], [[], []]
     for v, axis, dim in ((a, a_axis, a_dim), (b, b_axis, b_dim)):
         here = lax.axis_index(axis)
-        sums.append(lax.dynamic_index_in_dim(v, here, dim, keepdims=False))
+        own = lax.dynamic_index_in_dim(v, here, dim, keepdims=False)
+        sums.append(after(own, *beside))
     for step in (2, 1, 3):
         for n, (v, axis, dim) in enumerate(((a, a_axis, a_dim), (b, b_axis, b_dim))):
             here = lax.axis_index(axis)
             piece = lax.dynamic_index_in_dim(v, (here + step) % 4, dim, keepdims=False)
-            if len(got[n]) < 2:
-                piece = after(piece, *first)
-            else:
-                piece = after(piece, got[n][0], *last)
+            if len(got[n]) == 2:
+                piece = after(piece, got[n][0])
             got[n].append(lax.ppermute(piece, axis, [(i, (i + step) % 4) for i in range(4)]))
     return [s + r[0] + r[1] + r[2] for s, r in zip(sums, got)]
 
@@ -231,6 +230,7 @@
     x_other = lax.ppermute(x_theirs, "core", SWAP)
     xs0 = jnp.concatenate([x_mine0, x_other[0]], axis=1)
     xs1 = jnp.concatenate([x_mine1, x_other[1]], axis=1)
+    x0_other = lax.ppermute(x_other[0], "party", SWAP)
     a_mine0, a_mine1, a_theirs = turned(core_id, after(ba, x_other))
     a_other = lax.ppermute(a_theirs, "core", SWAP)
     aa0 = jnp.concatenate([a_mine0, a_other[0]], axis=1)
@@ -247,12 +247,11 @@
     weights = jnp.concatenate(
         [jnp.where(xl0, packed, packed_near), jnp.where(xl0, packed_near, packed)], axis=1
     )
-    weights = lax.all_gather(after(weights, x0, x_other, a_other), ("y", "z", "core"), axis=0, tiled=True)
+    weights = lax.all_gather(after(weights, x0, x0_other), ("y", "z", "core"), axis=0, tiled=True)
 
     last = g[3 * g.shape[0] // 4 :]
     last = jnp.concatenate([last[:, : ff // 2], last[:, ff // 2 :]], axis=0)
-    sent0 = jnp.concatenate([x_other[0], jnp.where(party0, last, aa0)], axis=1)
-    got0 = lax.ppermute(sent0, "party", SWAP)
+    got0 = lax.ppermute(jnp.where(party0, last, aa0), "party", SWAP)
     sent1 = jnp.concatenate(
         [
             xs1[:, :384],
@@ -265,23 +264,23 @@
         axis=1,
     )
     got1 = lax.ppermute(sent1, "party", SWAP)
-    u = x - fa
-    u = lax.ppermute(after(u, got0), "party", SWAP)
+    u_local = x - fa
+    u = lax.ppermute(after(u_local, got0), "party", SWAP)
 
     g_other = lax.ppermute(after(g, a_theirs), "core", SWAP)
     b_other = lax.ppermute(after(bb, a_theirs), "core", SWAP)
     rights = (g, bb, g_other, b_other)
-    early = grad_parts(party_id, xs0, aa0, (x0, got0), rights, (), 1)
+    early = grad_parts(party_id, after(xs0, u_local), aa0, (x0, x0_other, got0), rights, (), 1)
     sent = (got0, lax.ppermute(after(got0, early), "core", SWAP))
     late = grad_parts(party_id, xs1, aa1, (got1,), rights, sent, LATE)
 
-    early = lax.psum_scatter(early.reshape(4, 4, 32, ff), "z", scatter_dimension=0, tiled=True)
-    early = lax.psum_scatter(early[0], "y", scatter_dimension=0, tiled=True)
+    early = lax.psum_scatter(early.reshape(16, 32, ff), ("z", "y"), scatter_dimension=0, tiled=True)
     early = early.reshape(2, 2, 8, ff)
     outputs = forward_call(local_kernel, (fa,), weights, 1, fc)
     late = late.reshape(4, 4, 2, 16, ff)
-    part0, part1 = scattered_pair(late[:, :, 0], "z", 0, late[:, :, 1], "y", 1, (), (outputs,))
-    part0, part1 = scattered_pair(part0, "y", 0, part1, "z", 0, (u,))
+    part0, part1 = scattered_pair(late[:, :, 0], "z", 0, late[:, :, 1], "y", 1, (outputs, u))
+    outputs = forward_call(opened_kernel, (x, fa, u), weights, 0, after(outputs, part0, part1))
+    part0, part1 = scattered_pair(part0, "y", 0, part1, "z", 0, (outputs,))
     late = jnp.stack([part0, part1]).reshape(2, 2, 8, ff)
     both = jnp.concatenate([early, late], axis=2)
     spot = 2 * party + lax.axis_index("xl")
@@ -298,7 +297,6 @@
             give, ("party", "xl"), [(i, (i + step) % 4) for i in range(4)]
         )
 
-    outputs = forward_call(opened_kernel, (x, fa, u), weights, 0, outputs)
     return (outputs[None], grad[None])
 
 

time: 242 us -> 245 us (1.012)
  waiting for transfers between devices: 88.8 us -> 94.7 us
    ppermute x1, waiting for transfers between devices: 0.01 us -> 16.3 us  [body(): lax.ppermute(d, ('party', 'xl'), [(0, 3), (3, 0), (1, 2), (2, 1)])]
    ppermute x12, waiting for transfers between devices: 27.8 us -> 18.2 us  [scattered_pair(): lax.ppermute(piece, axis, [(i, (i + step) % 4) for i in range(4)])]
    reduce_scatter x2 -> x0, waiting for transfers between devices: 9.53 us -> none  [the longest x1 9.5 us: body(): lax.psum_scatter(early.reshape(4, 4, 32, ff), 'z', scatter_dimension=0, t...]
    ppermute x1, waiting for transfers between devices: 0.01 us -> 9.31 us  [body(): a_other = lax.ppermute(a_theirs, 'core', SWAP)]
    ppermute x1, waiting for transfers between devices: 6.97 us -> 0.01 us  [body(): x0 = lax.ppermute(x_mine0, 'party', SWAP)]
    ppermute x1, waiting for transfers between devices: 7.28 us -> 12.4 us  [body(): got1 = lax.ppermute(sent1, 'party', SWAP)]
    ppermute x3, waiting for transfers between devices: 0.01 us -> 4.35 us  [body(): lax.ppermute(give, ('party', 'xl'), [(i, (i + step) % 4) for i in range(4)])]
    ppermute x1, waiting for transfers between devices: 7.59 us -> 4.38 us  [body(): d_party = lax.ppermute(d, 'party', SWAP)]
  transfers between devices with their start and end apart: 30 -> 30, of which waited for: 10 -> 12; matrix products, arithmetic and copies ran while one was open for 10% -> 9% of each run, Pallas kernels for 27% -> 27%
where the time goes in v6:
time: 245 us; the launch traced here: 244 us
  waiting for transfers between devices  94.7 us (39%)
  Pallas kernels  66.6 us (27%)
  starting transfers between devices  36.9 us (15%)
  other arithmetic  16.6 us (7%)
  between operations  15.9 us (6%)
  local copies, waits for them, and re-layouts  13.7 us (6%)
    pallas_call x2, Pallas kernels, grad_parts(): pl.pallas_call(lambda *refs: grad_kernel(bool(sent), *refs), grid=(ff //...  35 us
    pallas_call x2, Pallas kernels, forward_call(): pl.pallas_call(kernel, grid=(steps,), in_specs=[pl.BlockSpec((rows, d), l...  25.6 us
    ppermute x12, starting transfers between devices, scattered_pair(): lax.ppermute(piece, axis, [(i, (i + step) % 4) for i in range(4)])  22.9 us
    ppermute x1, waiting for transfers between devices, body(): got0 = lax.ppermute(jnp.where(party0, last, aa0), 'party', SWAP)  19.9 us
    ppermute x12, waiting for transfers between devices, scattered_pair(): lax.ppermute(piece, axis, [(i, (i + step) % 4) for i in range(4)])  18.2 us
    ppermute x1, waiting for transfers between devices, body(): lax.ppermute(d, ('party', 'xl'), [(0, 3), (3, 0), (1, 2), (2, 1)])  16.3 us
    ppermute x1, waiting for transfers between devices, body(): got1 = lax.ppermute(sent1, 'party', SWAP)  12.4 us
    ppermute x1, waiting for transfers between devices, body(): x0_other = lax.ppermute(x_other[0], 'party', SWAP)  9.76 us
  transfers between devices with their start and end apart: 30, of which 12 were waited for; matrix products, arithmetic and copies ran while one was open for 9% of the time, Pallas kernels for 27%

profile of v6, /device:TPU:0, one launch (start us, length us, event | category | flops | bytes accessed | tf_op | source)
XLA Modules:
  0.0 244.3 jit_solution(50950298321207044)
XLA Ops:
  8.1 1.0 bitcast_subtract_fusion
  10.0 1.7 collective-permute-start.5
  11.7 2.7 %collective-permute-start.4 = (f32[16,2048]{1,0:T(8,128)S(1)}, f32[16,2048]{1,0:T(8,128)S(1)}, u32[]{:S(2)}, u32[]{:S(2)}) collective-permute-start(f32[16,2048]{1,0:T(8,128)S(1)} %bitcast_subtract_fusion), channel_id=1, source_target_pairs={{0,64},{64,0},{1,65},{65,1},{2,66},{66,2},{3,67},{67,3},{4,68},{68... | collective-permute-start | bytes 393224 | tf_op jit(solution)/shard_map/ppermute | solution.py:239
  14.8 2.9 %shard_map.104 = (f32[4,4,2,8,512]{4,3,2,1,0:T(8,128)}, f32[4,4,2,8,512]{4,3,2,1,0:T(8,128)}, f32[2,4,4,2,8,512]{5,4,3,2,1,0:T(8,128)}) custom-call(s32[1]{0:T(128)} %bitcast.3.core_ref, f32[512,1024]{1,0:T(8,128)} %bitcast.91), custom_call_target="tpu_custom_call" | custom-call | bytes 4194304 | tf_op jit(solution)/shard_map/pallas_call | solution.py:60
  17.7 1.9 collective-permute-start.7
  19.6 4.4 %collective-permute-done.4 = f32[16,2048]{1,0:T(8,128)S(1)} collective-permute-done((f32[16,2048]{1,0:T(8,128)S(1)}, f32[16,2048]{1,0:T(8,128)S(1)}, u32[]{:S(2)}, u32[]{:S(2)}) %collective-permute-start.4) | collective-permute-done | bytes 131104 | tf_op jit(solution)/shard_map/ppermute | solution.py:239
  24.0 16.3 %collective-permute-done.6 = f32[16,2048]{1,0:T(8,128)S(1)} collective-permute-done((f32[16,2048]{1,0:T(8,128)S(1)}, f32[16,2048]{1,0:T(8,128)S(1)}, u32[]{:S(2)}, u32[]{:S(2)}) %collective-permute-start.6) | collective-permute-done | bytes 131104 | tf_op jit(solution)/shard_map/ppermute | solution.py:241
  41.4 9.8 %collective-permute-done.8.refs_4_ = f32[256,512]{1,0:T(8,128)S(1)} collective-permute-done((f32[256,512]{1,0:T(8,128)S(1)}, f32[256,512]{1,0:T(8,128)S(1)}, u32[]{:S(2)}, u32[]{:S(2)}) %collective-permute-start.8) | collective-permute-done | bytes 524320 | tf_op jit(solution)/shard_map/ppermute | solution.py:233
  51.3 3.1 %shard_map.105 = (f32[4,4,2,8,512]{4,3,2,1,0:T(8,128)}, f32[4,4,2,8,512]{4,3,2,1,0:T(8,128)}, f32[2,4,4,2,8,512]{5,4,3,2,1,0:T(8,128)}) custom-call(s32[1]{0:T(128)} %bitcast.3.core_ref, f32[512,1024]{1,0:T(8,128)} %bitcast.101), custom_call_target="tpu_custom_call" | custom-call | bytes 4194304 | tf_op jit(solution)/shard_map/pallas_call | solution.py:60
  54.9 1.6 slice_bitcast_fusion
  57.5 1.7 bitcast_subtract_fusion.1
  59.9 9.3 %collective-permute-done.1 = f32[2,256,512]{2,1,0:T(8,128)S(1)} collective-permute-done((f32[2,256,512]{2,1,0:T(8,128)}, f32[2,256,512]{2,1,0:T(8,128)S(1)}, u32[]{:S(2)}, u32[]{:S(2)}) %collective-permute-start.1) | collective-permute-done | bytes 1048608 | tf_op jit(solution)/shard_map/ppermute | solution.py:235
  69.3 1.1 pad_maximum_fusion
  70.8 1.1 pad_maximum_fusion.3.refs_1_
  74.9 3.2 %collective-permute-start.9 = (f32[256,1536]{1,0:T(8,128)}, f32[256,1536]{1,0:T(8,128)}, u32[]{:S(2)}, u32[]{:S(2)}) collective-permute-start(f32[256,1536]{1,0:T(8,128)} %slice_dynamic-update-slice_fusion.2), channel_id=1, source_target_pairs={{0,64},{64,0},{1,65},{65,1},{2,66},{66,2},{3,67},{67,3},{4,68},{68... | collective-permute-start | bytes 4718600 | tf_op jit(solution)/shard_map/ppermute | solution.py:266
  78.1 19.9 %collective-permute-done.2.refs_5_.refs_8_ = f32[256,1024]{1,0:T(8,128)S(1)} collective-permute-done((f32[256,1024]{1,0:T(8,128)S(1)}, f32[256,1024]{1,0:T(8,128)S(1)}, u32[]{:S(2)}, u32[]{:S(2)}) %collective-permute-start.2) | collective-permute-done | bytes 1048608 | tf_op jit(solution)/shard_map/ppermute | solution.py:254
  98.9 1.4 copy-done.12
  100.3 16.7 %shard_map.107 = f32[16,2,16,2048]{3,2,1,0:T(8,128)} custom-call(s32[1]{0:T(128)} %bitcast.14.refs_0_, f32[256,1024]{1,0:T(8,128)} %pad_maximum_fusion.3.refs_1_, f32[256,1024]{1,0:T(8,128)} %get-tuple-element.66.refs_2_, f32[256,512]{1,0:T(8,128)} %copy-done.15, f32[256,512]{1,0:T(8,128)} %copy-done.16, f32[256,1024]{1,0:T(8,128)} %copy-done.13, ...), custom_call_target="tpu_custom_call" | custom-call | flops 9663676416 | bytes 25165824 | tf_op jit(solution)/shard_map/pallas_call | solution.py:130
  117.1 1.1 pad_maximum_fusion.1.refs_1_
  118.2 1.1 pad_maximum_fusion.2.refs_2_
  119.3 12.4 %collective-permute-done.9.refs_3_ = f32[256,1536]{1,0:T(8,128)} collective-permute-done((f32[256,1536]{1,0:T(8,128)}, f32[256,1536]{1,0:T(8,128)}, u32[]{:S(2)}, u32[]{:S(2)}) %collective-permute-start.9) | collective-permute-done | bytes 1572896 | tf_op jit(solution)/shard_map/ppermute | solution.py:266
  131.8 1.0 copy-done.14
  132.8 18.3 %shard_map.108 = f32[16,2,16,2048]{3,2,1,0:T(8,128)} custom-call(s32[1]{0:T(128)} %bitcast.14.refs_0_, f32[256,1024]{1,0:T(8,128)} %pad_maximum_fusion.1.refs_1_, f32[256,1024]{1,0:T(8,128)} %pad_maximum_fusion.2.refs_2_, f32[256,1536]{1,0:T(8,128)} %collective-permute-done.9.refs_3_, f32[512,2048]{1,0:T(8,128)} %bitcast.116, f32[512,2048]{1,0:T(8,128)} %bitcast.119, ...), custom_call_target="tpu_custom_call" | custom-call | flops 77309411328 | bytes 197132288 | tf_op jit(solution)/shard_map/pallas_call | solution.py:130
  151.0 2.5 %fusion.18 = (f32[4,4,1,16,2048]{4,3,2,1,0:T(8,128)S(1)}, f32[4,4,1,16,2048]{4,3,2,1,0:T(8,128)S(1)}) fusion(f32[4,4,2,16,2048]{4,3,2,1,0:T(8,128)} %bitcast.97), kind=kLoop, calls=%fused_computation.72 | loop fusion | bytes 8388608 | tf_op jit(solution)/shard_map/slice | solution.py:281
  153.6 1.2 dynamic-slice_bitcast_fusion.3
  154.8 3.2 %collective-permute-start.16 = (f32[4,16,2048]{2,1,0:T(8,128)}, f32[4,16,2048]{2,1,0:T(8,128)}, u32[]{:S(2)}, u32[]{:S(2)}) collective-permute-start(f32[4,16,2048]{2,1,0:T(8,128)} %get-tuple-element.61), channel_id=1, source_target_pairs={{0,32},{16,48},{32,0},{48,16},{1,33},{17,49},{33,1},{49,17},{2,34}... | collective-permute-start | bytes 1572872 | tf_op jit(solution)/shard_map/ppermute | solution.py:212
  158.0 1.2 dynamic-slice_bitcast_fusion.7
  159.2 4.1 %collective-permute-start.13 = (f32[4,16,2048]{2,1,0:T(8,128)}, f32[4,16,2048]{2,1,0:T(8,128)}, u32[]{:S(2)}, u32[]{:S(2)}) collective-permute-start(f32[4,16,2048]{2,1,0:T(8,128)} %get-tuple-element.65), channel_id=1, source_target_pairs={{0,4},{2,6},{4,0},{6,2},{1,5},{3,7},{5,1},{7,3},{8,12},{10,14},{12... | collective-permute-start | bytes 1572872 | tf_op jit(solution)/shard_map/ppermute | solution.py:212
  163.9 1.0 collective-permute-start.14
  164.9 10.2 %collective-permute-done.16 = f32[4,16,2048]{2,1,0:T(8,128)} collective-permute-done((f32[4,16,2048]{2,1,0:T(8,128)}, f32[4,16,2048]{2,1,0:T(8,128)}, u32[]{:S(2)}, u32[]{:S(2)}) %collective-permute-start.16) | collective-permute-done | bytes 524320 | tf_op jit(solution)/shard_map/ppermute | solution.py:212
  175.1 1.5 collective-permute-start.18
  176.6 2.1 collective-permute-done.13
  178.7 1.5 collective-permute-start.15
  180.2 12.1 %shard_map.106.c_ref = f32[512,2048]{1,0:T(8,128)} custom-call(f32[512,1024]{1,0:T(8,128)} %bitcast.93, f32[512,8192]{1,0:T(8,128)} %all-gather.2.cloned.1.call-done.w0_ref.w1_ref, f32[512,8192]{1,0:T(8,128)} %all-gather.2.cloned.1.call-done.w0_ref.w1_ref, f32[512,2048]{1,0:T(8,128)} %bitcast.98), custom_call_target="tpu_custom_call" | custom-call | flops 6442450944 | bytes 20971520 | tf_op jit(solution)/shard_map/pallas_call | solution.py:183
  192.3 2.2 add_add_fusion
  194.5 1.5 add_add_fusion.1
  196.1 1.2 collective-permute-start.19
  197.3 1.4 collective-permute-start.20
  198.8 2.3 collective-permute-start.22
  201.0 3.0 %collective-permute-done.19 = f32[16,2048]{1,0:T(8,128)S(1)} collective-permute-done((f32[16,2048]{1,0:T(8,128)S(1)}, f32[16,2048]{1,0:T(8,128)S(1)}, u32[]{:S(2)}, u32[]{:S(2)}) %collective-permute-start.19) | collective-permute-done | bytes 131104 | tf_op jit(solution)/shard_map/ppermute | solution.py:212
  204.1 1.9 collective-permute-start.21
  206.0 13.5 %shard_map.109 = f32[512,2048]{1,0:T(8,128)} custom-call(f32[512,1024]{1,0:T(8,128)} %bitcast.92, f32[512,1024]{1,0:T(8,128)} %bitcast.94, f32[512,1024]{1,0:T(8,128)} %copy-done.2, f32[512,8192]{1,0:T(8,128)} %all-gather.2.cloned.1.call-done.w0_ref.w1_ref, f32[512,8192]{1,0:T(8,128)} %all-gather.2.cloned.1.call-done.w0_ref.w1_ref, f32[512,2048]{1,0:T(8,128)} %shard_map.106.c_ref), custom_call_target="tpu_custom_call" | custom-call | flops 6442450944 | bytes 20971520 | tf_op jit(solution)/shard_map/pallas_call | solution.py:183
  220.2 3.4 %collective-permute-start.24 = (f32[16,2048]{1,0:T(8,128)S(1)}, f32[16,2048]{1,0:T(8,128)S(1)}, u32[]{:S(2)}, u32[]{:S(2)}) collective-permute-start(f32[16,2048]{1,0:T(8,128)S(1)} %get-tuple-element.51), channel_id=1, source_target_pairs={{0,6},{2,0},{4,2},{6,4},{1,7},{3,1},{5,3},{7,5},{8,14},{10,8},{12,... | collective-permute-start | bytes 393224 | tf_op jit(solution)/shard_map/ppermute | solution.py:212
  223.7 2.8 %collective-permute-done.23 = f32[16,2048]{1,0:T(8,128)S(1)} collective-permute-done((f32[16,2048]{1,0:T(8,128)S(1)}, f32[16,2048]{1,0:T(8,128)S(1)}, u32[]{:S(2)}, u32[]{:S(2)}) %collective-permute-start.23) | collective-permute-done | bytes 131104 | tf_op jit(solution)/shard_map/ppermute | solution.py:212
  227.8 3.2 %collective-permute-start.27 = (f32[16,2048]{1,0:T(8,128)S(1)}, f32[16,2048]{1,0:T(8,128)S(1)}, u32[]{:S(2)}, u32[]{:S(2)}) collective-permute-start(f32[16,2048]{1,0:T(8,128)S(1)} %get-tuple-element.76), channel_id=1, source_target_pairs={{0,72},{8,0},{64,8},{72,64},{1,73},{9,1},{65,9},{73,65},{2,74},{10... | collective-permute-start | bytes 393224 | tf_op jit(solution)/shard_map/ppermute | solution.py:296
  231.0 3.3 %collective-permute-done.25 = f32[16,2048]{1,0:T(8,128)S(1)} collective-permute-done((f32[16,2048]{1,0:T(8,128)S(1)}, f32[16,2048]{1,0:T(8,128)S(1)}, u32[]{:S(2)}, u32[]{:S(2)}) %collective-permute-start.25) | collective-permute-done | bytes 131104 | tf_op jit(solution)/shard_map/ppermute | solution.py:296
  234.2 1.1 collective-permute-done.26
  235.3 1.5 fusion.10
  (86 shorter events, 12.0 us)
Async XLA Ops:
  8.0 32.2 %copy-start.8 = (f32[1,16,2048]{2,1,0:T(8,128)S(1)}, f32[1,16,2048]{2,1,0:T(8,128)}, u32[]{:S(2)}) copy-start(f32[1,16,2048]{2,1,0:T(8,128)} %param.13) | copy-start | bytes 393220
  8.0 172.1 %all-gather.2.cloned.1.call-start = ((), (), s32[]{:S(2)}) async-start(), calls=%async_computation.1 | async-start | bytes 17301504 | tf_op jit(solution)/shard_map/all_gather | solution.py:250
  10.0 30.2 %collective-permute-start.5 = (f32[16,4096]{1,0:T(8,128)S(1)}, f32[16,4096]{1,0:T(8,128)S(1)}, u32[]{:S(2)}, u32[]{:S(2)}) collective-permute-start(f32[16,4096]{1,0:T(8,128)S(1)} %pad_maximum_fusion.5), channel_id=1, source_target_pairs={{0,8},{8,0},{1,9},{9,1},{2,10},{10,2},{3,11},{11,3},{4,12},{12,4},... | collective-permute-start | bytes 786440 | tf_op jit(solution)/shard_map/ppermute | solution.py:240
  11.7 12.3 %collective-permute-start.4 = (f32[16,2048]{1,0:T(8,128)S(1)}, f32[16,2048]{1,0:T(8,128)S(1)}, u32[]{:S(2)}, u32[]{:S(2)}) collective-permute-start(f32[16,2048]{1,0:T(8,128)S(1)} %bitcast_subtract_fusion), channel_id=1, source_target_pairs={{0,64},{64,0},{1,65},{65,1},{2,66},{66,2},{3,67},{67,3},{4,68},{68... | collective-permute-start | bytes 393224 | tf_op jit(solution)/shard_map/ppermute | solution.py:239
  14.4 25.8 %collective-permute-start.6 = (f32[16,2048]{1,0:T(8,128)S(1)}, f32[16,2048]{1,0:T(8,128)S(1)}, u32[]{:S(2)}, u32[]{:S(2)}) collective-permute-start(f32[16,2048]{1,0:T(8,128)S(1)} %bitcast_subtract_fusion), channel_id=1, source_target_pairs={{0,72},{72,0},{8,64},{64,8},{1,73},{73,1},{9,65},{65,9},{2,74},{74... | collective-permute-start | bytes 393224 | tf_op jit(solution)/shard_map/ppermute | solution.py:241
  17.7 22.7 %collective-permute-start = (f32[2,256,512]{2,1,0:T(8,128)}, f32[2,256,512]{2,1,0:T(8,128)S(1)}, u32[]{:S(2)}, u32[]{:S(2)}) collective-permute-start(f32[2,256,512]{2,1,0:T(8,128)} %bitcast.120), channel_id=1, source_target_pairs={{0,1},{1,0},{2,3},{3,2},{4,5},{5,4},{6,7},{7,6},{8,9},{9,8},{10,11... | collective-permute-start | bytes 3145736 | tf_op jit(solution)/shard_map/ppermute | solution.py:230
  17.7 23.8 %collective-permute-start.7 = (f32[256,512]{1,0:T(8,128)}, f32[256,512]{1,0:T(8,128)S(1)}, u32[]{:S(2)}, u32[]{:S(2)}) collective-permute-start(f32[256,512]{1,0:T(8,128)} %bitcast.112), channel_id=1, source_target_pairs={{0,64},{64,0},{1,65},{65,1},{2,66},{66,2},{3,67},{67,3},{4,68},{68... | collective-permute-start | bytes 1572872 | tf_op jit(solution)/shard_map/ppermute | solution.py:229
  40.4 13.9 %copy-start.4 = (f32[256,512]{1,0:T(8,128)}, f32[256,512]{1,0:T(8,128)S(1)}, u32[]{:S(2)}) copy-start(f32[256,512]{1,0:T(8,128)S(1)} %get-tuple-element.71) | copy-start | bytes 1572868
  40.4 10.8 %collective-permute-start.8 = (f32[256,512]{1,0:T(8,128)S(1)}, f32[256,512]{1,0:T(8,128)S(1)}, u32[]{:S(2)}, u32[]{:S(2)}) collective-permute-start(f32[256,512]{1,0:T(8,128)S(1)} %get-tuple-element.71), channel_id=1, source_target_pairs={{0,64},{64,0},{1,65},{65,1},{2,66},{66,2},{3,67},{67,3},{4,68},{68... | collective-permute-start | bytes 1572872 | tf_op jit(solution)/shard_map/ppermute | solution.py:233
  41.4 15.0 %copy-start.15 = (f32[256,512]{1,0:T(8,128)}, f32[256,512]{1,0:T(8,128)S(1)}, u32[]{:S(2)}) copy-start(f32[256,512]{1,0:T(8,128)S(1)} %collective-permute-done.7.refs_3_) | copy-start | bytes 1572868
  51.2 5.2 %copy-start.16 = (f32[256,512]{1,0:T(8,128)}, f32[256,512]{1,0:T(8,128)S(1)}, u32[]{:S(2)}) copy-start(f32[256,512]{1,0:T(8,128)S(1)} %collective-permute-done.8.refs_4_) | copy-start | bytes 1572868
  51.2 175.4 %reduce-scatter.4.cloned.1.call-start = ((), (), s32[]{:S(2)}) async-start(), calls=%async_computation.2 | async-start | bytes 4456448
  51.3 5.3 %copy-start.3 = (f32[4,4,2,8,512]{4,3,2,1,0:T(8,128)S(1)}, f32[4,4,2,8,512]{4,3,2,1,0:T(8,128)}, u32[]{:S(2)}) copy-start(f32[4,4,2,8,512]{4,3,2,1,0:T(8,128)} %get-tuple-element.37) | copy-start | bytes 1572868
  54.3 43.6 %collective-permute-start.10 = (f32[512,2048]{1,0:T(8,128)}, f32[512,2048]{1,0:T(8,128)S(1)}, u32[]{:S(2)}, u32[]{:S(2)}) collective-permute-start(f32[512,2048]{1,0:T(8,128)} %bitcast.114), channel_id=1, source_target_pairs={{0,1},{1,0},{2,3},{3,2},{4,5},{5,4},{6,7},{7,6},{8,9},{9,8},{10,11... | collective-permute-start | bytes 12582920 | tf_op jit(solution)/shard_map/ppermute | solution.py:270
  54.3 3.1 %copy-start = (f32[1,512,1024]{2,1,0:T(8,128)S(1)}, f32[1,512,1024]{2,1,0:T(8,128)}, u32[]{:S(2)}) copy-start(f32[1,512,1024]{2,1,0:T(8,128)} %param.9) | copy-start | bytes 6291460
  54.4 3.1 %copy-start.1 = (f32[1,512,1024]{2,1,0:T(8,128)S(1)}, f32[1,512,1024]{2,1,0:T(8,128)}, u32[]{:S(2)}) copy-start(f32[1,512,1024]{2,1,0:T(8,128)} %param.12) | copy-start | bytes 6291460
  54.4 43.6 %collective-permute-start.11 = (f32[512,2048]{1,0:T(8,128)}, f32[512,2048]{1,0:T(8,128)}, u32[]{:S(2)}, u32[]{:S(2)}) collective-permute-start(f32[512,2048]{1,0:T(8,128)} %bitcast.117), channel_id=1, source_target_pairs={{0,1},{1,0},{2,3},{3,2},{4,5},{5,4},{6,7},{7,6},{8,9},{9,8},{10,11... | collective-permute-start | bytes 12582920 | tf_op jit(solution)/shard_map/ppermute | solution.py:271
  56.4 12.8 %collective-permute-start.1 = (f32[2,256,512]{2,1,0:T(8,128)}, f32[2,256,512]{2,1,0:T(8,128)S(1)}, u32[]{:S(2)}, u32[]{:S(2)}) collective-permute-start(f32[2,256,512]{2,1,0:T(8,128)} %bitcast.121), channel_id=1, source_target_pairs={{0,1},{1,0},{2,3},{3,2},{4,5},{5,4},{6,7},{7,6},{8,9},{9,8},{10,11... | collective-permute-start | bytes 3145736 | tf_op jit(solution)/shard_map/ppermute | solution.py:235
  57.5 1.7 copy-start.6
  59.2 10.1 %copy-start.9 = (f32[4,4,2,8,512]{4,3,2,1,0:T(8,128)S(1)}, f32[4,4,2,8,512]{4,3,2,1,0:T(8,128)}, u32[]{:S(2)}) copy-start(f32[4,4,2,8,512]{4,3,2,1,0:T(8,128)} %get-tuple-element.29) | copy-start | bytes 1572868
  69.3 1.2 copy-start.5
  69.3 1.5 copy-start.10
  70.4 27.5 %collective-permute-start.2 = (f32[256,1024]{1,0:T(8,128)S(1)}, f32[256,1024]{1,0:T(8,128)S(1)}, u32[]{:S(2)}, u32[]{:S(2)}) collective-permute-start(f32[256,1024]{1,0:T(8,128)S(1)} %get-tuple-element.67), channel_id=1, source_target_pairs={{0,64},{64,0},{1,65},{65,1},{2,66},{66,2},{3,67},{67,3},{4,68},{68... | collective-permute-start | bytes 3145736 | tf_op jit(solution)/shard_map/ppermute | solution.py:254
  74.9 56.8 %collective-permute-start.9 = (f32[256,1536]{1,0:T(8,128)}, f32[256,1536]{1,0:T(8,128)}, u32[]{:S(2)}, u32[]{:S(2)}) collective-permute-start(f32[256,1536]{1,0:T(8,128)} %slice_dynamic-update-slice_fusion.2), channel_id=1, source_target_pairs={{0,64},{64,0},{1,65},{65,1},{2,66},{66,2},{3,67},{67,3},{4,68},{68... | collective-permute-start | bytes 4718600 | tf_op jit(solution)/shard_map/ppermute | solution.py:266
  98.0 1.0 copy-start.13
  98.0 2.4 copy-start.12
  117.0 1.2 copy-start.7
  117.1 14.7 %collective-permute-start.12 = (f32[256,1024]{1,0:T(8,128)}, f32[256,1024]{1,0:T(8,128)S(1)}, u32[]{:S(2)}, u32[]{:S(2)}) collective-permute-start(f32[256,1024]{1,0:T(8,128)} %copy-done.13), channel_id=1, source_target_pairs={{0,1},{1,0},{2,3},{3,2},{4,5},{5,4},{6,7},{7,6},{8,9},{9,8},{10,11... | collective-permute-start | bytes 3145736 | tf_op jit(solution)/shard_map/ppermute | solution.py:274
  119.3 73.0 %collective-permute-start.3 = (f32[512,1024]{1,0:T(8,128)}, f32[512,1024]{1,0:T(8,128)S(1)}, u32[]{:S(2)}, u32[]{:S(2)}) collective-permute-start(f32[512,1024]{1,0:T(8,128)} %bitcast_subtract_fusion.1), channel_id=1, source_target_pairs={{0,64},{64,0},{1,65},{65,1},{2,66},{66,2},{3,67},{67,3},{4,68},{68... | collective-permute-start | bytes 6291464 | tf_op jit(solution)/shard_map/ppermute | solution.py:268
  131.8 1.0 copy-start.14
  154.8 20.3 %collective-permute-start.16 = (f32[4,16,2048]{2,1,0:T(8,128)}, f32[4,16,2048]{2,1,0:T(8,128)}, u32[]{:S(2)}, u32[]{:S(2)}) collective-permute-start(f32[4,16,2048]{2,1,0:T(8,128)} %get-tuple-element.61), channel_id=1, source_target_pairs={{0,32},{16,48},{32,0},{48,16},{1,33},{17,49},{33,1},{49,17},{2,34}... | collective-permute-start | bytes 1572872 | tf_op jit(solution)/shard_map/ppermute | solution.py:212
  159.2 19.5 %collective-permute-start.13 = (f32[4,16,2048]{2,1,0:T(8,128)}, f32[4,16,2048]{2,1,0:T(8,128)}, u32[]{:S(2)}, u32[]{:S(2)}) collective-permute-start(f32[4,16,2048]{2,1,0:T(8,128)} %get-tuple-element.65), channel_id=1, source_target_pairs={{0,4},{2,6},{4,0},{6,2},{1,5},{3,7},{5,1},{7,3},{8,12},{10,14},{12... | collective-permute-start | bytes 1572872 | tf_op jit(solution)/shard_map/ppermute | solution.py:212
  163.3 29.0 %collective-permute-start.17 = (f32[4,16,2048]{2,1,0:T(8,128)}, f32[4,16,2048]{2,1,0:T(8,128)}, u32[]{:S(2)}, u32[]{:S(2)}) collective-permute-start(f32[4,16,2048]{2,1,0:T(8,128)} %get-tuple-element.60), channel_id=1, source_target_pairs={{0,16},{16,32},{32,48},{48,0},{1,17},{17,33},{33,49},{49,1},{2,18}... | collective-permute-start | bytes 1572872 | tf_op jit(solution)/shard_map/ppermute | solution.py:212
  163.9 30.6 %collective-permute-start.14 = (f32[4,16,2048]{2,1,0:T(8,128)}, f32[4,16,2048]{2,1,0:T(8,128)}, u32[]{:S(2)}, u32[]{:S(2)}) collective-permute-start(f32[4,16,2048]{2,1,0:T(8,128)} %get-tuple-element.64), channel_id=1, source_target_pairs={{0,2},{2,4},{4,6},{6,0},{1,3},{3,5},{5,7},{7,1},{8,10},{10,12},{12... | collective-permute-start | bytes 1572872 | tf_op jit(solution)/shard_map/ppermute | solution.py:212
  175.1 17.2 %collective-permute-start.18 = (f32[4,16,2048]{2,1,0:T(8,128)}, f32[4,16,2048]{2,1,0:T(8,128)}, u32[]{:S(2)}, u32[]{:S(2)}) collective-permute-start(f32[4,16,2048]{2,1,0:T(8,128)} %get-tuple-element.46), channel_id=1, source_target_pairs={{0,48},{16,0},{32,16},{48,32},{1,49},{17,1},{33,17},{49,33},{2,50}... | collective-permute-start | bytes 1572872 | tf_op jit(solution)/shard_map/ppermute | solution.py:212
  178.7 15.8 %collective-permute-start.15 = (f32[4,16,2048]{2,1,0:T(8,128)}, f32[4,16,2048]{2,1,0:T(8,128)}, u32[]{:S(2)}, u32[]{:S(2)}) collective-permute-start(f32[4,16,2048]{2,1,0:T(8,128)} %get-tuple-element.44), channel_id=1, source_target_pairs={{0,6},{2,0},{4,2},{6,4},{1,7},{3,1},{5,3},{7,5},{8,14},{10,8},{12,... | collective-permute-start | bytes 1572872 | tf_op jit(solution)/shard_map/ppermute | solution.py:212
  192.3 3.7 %copy-start.2 = (f32[512,1024]{1,0:T(8,128)}, f32[512,1024]{1,0:T(8,128)S(1)}, u32[]{:S(2)}) copy-start(f32[512,1024]{1,0:T(8,128)S(1)} %collective-permute-done.3.got_ref) | copy-start | bytes 6291460
  196.1 8.0 %collective-permute-start.19 = (f32[16,2048]{1,0:T(8,128)S(1)}, f32[16,2048]{1,0:T(8,128)S(1)}, u32[]{:S(2)}, u32[]{:S(2)}) collective-permute-start(f32[16,2048]{1,0:T(8,128)S(1)} %get-tuple-element.80), channel_id=1, source_target_pairs={{0,32},{16,48},{32,0},{48,16},{1,33},{17,49},{33,1},{49,17},{2,34}... | collective-permute-start | bytes 393224 | tf_op jit(solution)/shard_map/ppermute | solution.py:212
  197.3 26.4 %collective-permute-start.20 = (f32[16,2048]{1,0:T(8,128)S(1)}, f32[16,2048]{1,0:T(8,128)S(1)}, u32[]{:S(2)}, u32[]{:S(2)}) collective-permute-start(f32[16,2048]{1,0:T(8,128)S(1)} %get-tuple-element.79), channel_id=1, source_target_pairs={{0,16},{16,32},{32,48},{48,0},{1,17},{17,33},{33,49},{49,1},{2,18}... | collective-permute-start | bytes 393224 | tf_op jit(solution)/shard_map/ppermute | solution.py:212
  198.8 21.5 %collective-permute-start.22 = (f32[16,2048]{1,0:T(8,128)S(1)}, f32[16,2048]{1,0:T(8,128)S(1)}, u32[]{:S(2)}, u32[]{:S(2)}) collective-permute-start(f32[16,2048]{1,0:T(8,128)S(1)} %get-tuple-element.84), channel_id=1, source_target_pairs={{0,4},{2,6},{4,0},{6,2},{1,5},{3,7},{5,1},{7,3},{8,12},{10,14},{12... | collective-permute-start | bytes 393224 | tf_op jit(solution)/shard_map/ppermute | solution.py:212
  204.1 22.6 %copy-start.11 = (f32[1,16,2048]{2,1,0:T(8,128)S(1)}, f32[1,16,2048]{2,1,0:T(8,128)}, u32[]{:S(2)}) copy-start(f32[1,16,2048]{2,1,0:T(8,128)} %param.17) | copy-start | bytes 393220
  204.1 19.6 %collective-permute-start.21 = (f32[16,2048]{1,0:T(8,128)S(1)}, f32[16,2048]{1,0:T(8,128)S(1)}, u32[]{:S(2)}, u32[]{:S(2)}) collective-permute-start(f32[16,2048]{1,0:T(8,128)S(1)} %get-tuple-element.49), channel_id=1, source_target_pairs={{0,48},{16,0},{32,16},{48,32},{1,49},{17,1},{33,17},{49,33},{2,50}... | collective-permute-start | bytes 393224 | tf_op jit(solution)/shard_map/ppermute | solution.py:212
  219.4 7.1 %collective-permute-start.23 = (f32[16,2048]{1,0:T(8,128)S(1)}, f32[16,2048]{1,0:T(8,128)S(1)}, u32[]{:S(2)}, u32[]{:S(2)}) collective-permute-start(f32[16,2048]{1,0:T(8,128)S(1)} %get-tuple-element.83), channel_id=1, source_target_pairs={{0,2},{2,4},{4,6},{6,0},{1,3},{3,5},{5,7},{7,1},{8,10},{10,12},{12... | collective-permute-start | bytes 393224 | tf_op jit(solution)/shard_map/ppermute | solution.py:212
  220.2 6.3 %collective-permute-start.24 = (f32[16,2048]{1,0:T(8,128)S(1)}, f32[16,2048]{1,0:T(8,128)S(1)}, u32[]{:S(2)}, u32[]{:S(2)}) collective-permute-start(f32[16,2048]{1,0:T(8,128)S(1)} %get-tuple-element.51), channel_id=1, source_target_pairs={{0,6},{2,0},{4,2},{6,4},{1,7},{3,1},{5,3},{7,5},{8,14},{10,8},{12,... | collective-permute-start | bytes 393224 | tf_op jit(solution)/shard_map/ppermute | solution.py:212
  227.6 6.7 %collective-permute-start.25 = (f32[16,2048]{1,0:T(8,128)S(1)}, f32[16,2048]{1,0:T(8,128)S(1)}, u32[]{:S(2)}, u32[]{:S(2)}) collective-permute-start(f32[16,2048]{1,0:T(8,128)S(1)} %get-tuple-element.74), channel_id=1, source_target_pairs={{0,64},{8,72},{64,0},{72,8},{1,65},{9,73},{65,1},{73,9},{2,66},{10... | collective-permute-start | bytes 393224 | tf_op jit(solution)/shard_map/ppermute | solution.py:296
  227.7 7.7 %collective-permute-start.26 = (f32[16,2048]{1,0:T(8,128)S(1)}, f32[16,2048]{1,0:T(8,128)S(1)}, u32[]{:S(2)}, u32[]{:S(2)}) collective-permute-start(f32[16,2048]{1,0:T(8,128)S(1)} %get-tuple-element.75), channel_id=1, source_target_pairs={{0,8},{8,64},{64,72},{72,0},{1,9},{9,65},{65,73},{73,1},{2,10},{10... | collective-permute-start | bytes 393224 | tf_op jit(solution)/shard_map/ppermute | solution.py:296
  227.8 7.6 %collective-permute-start.27 = (f32[16,2048]{1,0:T(8,128)S(1)}, f32[16,2048]{1,0:T(8,128)S(1)}, u32[]{:S(2)}, u32[]{:S(2)}) collective-permute-start(f32[16,2048]{1,0:T(8,128)S(1)} %get-tuple-element.76), channel_id=1, source_target_pairs={{0,72},{8,0},{64,8},{72,64},{1,73},{9,1},{65,9},{73,65},{2,74},{10... | collective-permute-start | bytes 393224 | tf_op jit(solution)/shard_map/ppermute | solution.py:296
Sparse Core Ops, SparseCore 0:
  51.3 72.5 all-gather.1
Sparse Core Ops, SparseCore 1:
  119.4 93.1 reduce-scatter.3

commit v7 on v6

--- a/solution.py
+++ b/solution.py
@@ -78,10 +78,11 @@
 
 
 def grad_kernel(split, p_ref, x_ref, a_ref, *refs):
-    out, pair, pair_sent, single = refs[-4:]
-    got_refs, refs = (refs[:1], refs[1:]) if split else (refs[:3], refs[3:])
+    pair, pair_sent, single = refs[-3:]
+    outs, refs = (refs[-5:-3], refs[:-5]) if split else (refs[-4:-3], refs[:-4])
+    got_refs, refs = (refs[:1], refs[1:]) if split else (refs[:2], refs[2:])
     g_ref, b_ref, go_ref, bo_ref = refs[:4]
-    sent_refs = refs[4:-4]
+    sent_refs = refs[4:]
     is_first = p_ref[0] == 0
 
     @pl.when(pl.program_id(0) == 0)
@@ -100,8 +101,8 @@
             pair_sent[:256], pair_sent[512:768] = halves(x_sent - a_sent)
             pair_sent[256:512], pair_sent[768:] = halves(a_sent)
         else:
-            got = jnp.concatenate([got_refs[0][...], got_refs[1][...]], axis=1)
-            second = jnp.where(is_first, got_refs[2][...], a)
+            got = got_refs[0][...]
+            second = jnp.where(is_first, got_refs[1][...], a)
         opened = x + got
         pair[:256], pair[512:768] = halves(opened - second)
         pair[256:512], pair[768:] = halves(second)
@@ -117,8 +118,12 @@
     shared = passes(single, jnp.concatenate([b, bo], axis=0))
     part0 = both[:256] - jnp.where(is_first, shared, 0.0)
     part1 = both[256:] + shared
-    out[:, 0] = part0.reshape(16, 16, part0.shape[1])
-    out[:, 1] = part1.reshape(16, 16, part1.shape[1])
+    for n, part in enumerate((part0, part1)):
+        part = part.reshape(16, 16, part.shape[1])
+        if split:
+            outs[n][...] = part
+        else:
+            outs[0][:, n] = part
 
 
 def grad_parts(party, x, a, got, rights, sent, weight):
@@ -134,8 +139,12 @@
         + [pl.BlockSpec(v.shape, lambda n: (0, 0)) for v in lefts]
         + [right] * 4
         + [part] * len(sent),
-        out_specs=pl.BlockSpec((16, 2, 16, TILE), lambda n: (0, 0, 0, n)),
-        out_shape=jax.ShapeDtypeStruct((16, 2, 16, ff), F32),
+        out_specs=[pl.BlockSpec((16, 16, TILE), lambda n: (0, 0, n))] * 2
+        if sent
+        else pl.BlockSpec((16, 2, 16, TILE), lambda n: (0, 0, 0, n)),
+        out_shape=[jax.ShapeDtypeStruct((16, 16, ff), F32)] * 2
+        if sent
+        else jax.ShapeDtypeStruct((16, 2, 16, ff), F32),
         scratch_shapes=[
             pltpu.VMEM((1024, 2 * tokens), BF16),
             pltpu.VMEM((1024, 256), BF16),
@@ -202,7 +211,7 @@
     for v, axis, dim in ((a, a_axis, a_dim), (b, b_axis, b_dim)):
         here = lax.axis_index(axis)
         own = lax.dynamic_index_in_dim(v, here, dim, keepdims=False)
-        sums.append(after(own, *beside))
+        sums.append(after(own, *beside) if beside else own)
     for step in (2, 1, 3):
         for n, (v, axis, dim) in enumerate(((a, a_axis, a_dim), (b, b_axis, b_dim))):
             here = lax.axis_index(axis)
@@ -226,32 +235,18 @@
     ff = w.shape[1]
 
     x_mine0, x_mine1, x_theirs = turned(core_id, x)
-    x0 = lax.ppermute(x_mine0, "party", SWAP)
     x_other = lax.ppermute(x_theirs, "core", SWAP)
     xs0 = jnp.concatenate([x_mine0, x_other[0]], axis=1)
     xs1 = jnp.concatenate([x_mine1, x_other[1]], axis=1)
-    x0_other = lax.ppermute(x_other[0], "party", SWAP)
-    a_mine0, a_mine1, a_theirs = turned(core_id, after(ba, x_other))
+    x0 = lax.ppermute(xs0, "party", SWAP)
+    a_mine0, a_mine1, a_theirs = turned(core_id, after(ba, x_theirs))
     a_other = lax.ppermute(a_theirs, "core", SWAP)
     aa0 = jnp.concatenate([a_mine0, a_other[0]], axis=1)
     aa1 = jnp.concatenate([a_mine1, a_other[1]], axis=1)
-    d = w - fb
-    d_party = lax.ppermute(d, "party", SWAP)
-    near = lax.ppermute(jnp.concatenate([fb, d], axis=1), "xl", SWAP)
-    d_across = lax.ppermute(d, ("party", "xl"), [(0, 3), (3, 0), (1, 2), (2, 1)])
-    d_party, near, d_across = lax.optimization_barrier((d_party, near, d_across, x_theirs))[:3]
-    delta = d + d_party
-    delta_near = near[:, ff:] + d_across
-    packed = jnp.concatenate([fb + first * delta, delta], axis=1)
-    packed_near = jnp.concatenate([near[:, :ff] + first * delta_near, delta_near], axis=1)
-    weights = jnp.concatenate(
-        [jnp.where(xl0, packed, packed_near), jnp.where(xl0, packed_near, packed)], axis=1
-    )
-    weights = lax.all_gather(after(weights, x0, x0_other), ("y", "z", "core"), axis=0, tiled=True)
-
     last = g[3 * g.shape[0] // 4 :]
     last = jnp.concatenate([last[:, : ff // 2], last[:, ff // 2 :]], axis=0)
-    got0 = lax.ppermute(jnp.where(party0, last, aa0), "party", SWAP)
+    sent0 = jnp.where(party0, last, aa0)
+    got0 = lax.ppermute(sent0, "party", SWAP)
     sent1 = jnp.concatenate(
         [
             xs1[:, :384],
@@ -263,26 +258,40 @@
         ],
         axis=1,
     )
+    d = w - fb
+    d_party = lax.ppermute(d, "party", SWAP)
+    near = lax.ppermute(jnp.concatenate([fb, d], axis=1), "xl", SWAP)
+    d_across = lax.ppermute(d, ("party", "xl"), [(0, 3), (3, 0), (1, 2), (2, 1)])
+    d_party, near, d_across = lax.optimization_barrier((d_party, near, d_across, sent0, sent1))[:3]
+    delta = d + d_party
+    delta_near = near[:, ff:] + d_across
+    packed = jnp.concatenate([fb + first * delta, delta], axis=1)
+    packed_near = jnp.concatenate([near[:, :ff] + first * delta_near, delta_near], axis=1)
+    weights = jnp.concatenate(
+        [jnp.where(xl0, packed, packed_near), jnp.where(xl0, packed_near, packed)], axis=1
+    )
+    weights = lax.all_gather(after(weights, x0), ("y", "z", "core"), axis=0, tiled=True)
+
     got1 = lax.ppermute(sent1, "party", SWAP)
     u_local = x - fa
     u = lax.ppermute(after(u_local, got0), "party", SWAP)
 
-    g_other = lax.ppermute(after(g, a_theirs), "core", SWAP)
-    b_other = lax.ppermute(after(bb, a_theirs), "core", SWAP)
+    g_other = lax.ppermute(after(g, a_other), "core", SWAP)
+    b_other = lax.ppermute(after(bb, a_other), "core", SWAP)
     rights = (g, bb, g_other, b_other)
-    early = grad_parts(party_id, after(xs0, u_local), aa0, (x0, x0_other, got0), rights, (), 1)
+    early = grad_parts(party_id, after(xs0, u_local), aa0, (x0, got0), rights, (), 1)
     sent = (got0, lax.ppermute(after(got0, early), "core", SWAP))
     late = grad_parts(party_id, xs1, aa1, (got1,), rights, sent, LATE)
 
     early = lax.psum_scatter(early.reshape(16, 32, ff), ("z", "y"), scatter_dimension=0, tiled=True)
     early = early.reshape(2, 2, 8, ff)
     outputs = forward_call(local_kernel, (fa,), weights, 1, fc)
-    late = late.reshape(4, 4, 2, 16, ff)
-    part0, part1 = scattered_pair(late[:, :, 0], "z", 0, late[:, :, 1], "y", 1, (outputs, u))
-    outputs = forward_call(opened_kernel, (x, fa, u), weights, 0, after(outputs, part0, part1))
-    part0, part1 = scattered_pair(part0, "y", 0, part1, "z", 0, (outputs,))
+    part0, part1 = (part.reshape(4, 4, 16, ff) for part in late)
+    part0, part1 = scattered_pair(part0, "z", 0, part1, "y", 1, (outputs, u))
+    part0, part1 = scattered_pair(part0, "y", 0, part1, "z", 0, ())
     late = jnp.stack([part0, part1]).reshape(2, 2, 8, ff)
     both = jnp.concatenate([early, late], axis=2)
+    outputs = forward_call(opened_kernel, (x, fa, u), weights, 0, after(outputs, both))
     spot = 2 * party + lax.axis_index("xl")
 
     def piece(at):

time: 245 us -> 232 us (0.947)
  waiting for transfers between devices: 94.7 us -> 69.8 us
  starting transfers between devices: 36.9 us -> 45 us
    ppermute x1, waiting for transfers between devices: 16.3 us -> 0.01 us  [body(): lax.ppermute(d, ('party', 'xl'), [(0, 3), (3, 0), (1, 2), (2, 1)])]
    ppermute x1, waiting for transfers between devices: 9.31 us -> 0.01 us  [body(): a_other = lax.ppermute(a_theirs, 'core', SWAP)]
    ppermute x5 -> x4, waiting for transfers between devices: 29.6 us -> 37.9 us  [the longest x1 21 us: body(): got0 = lax.ppermute(sent0, 'party', SWAP)]
    unnamed x3, waiting for transfers between devices: 0.06 us -> 6.04 us
    ppermute x5 -> x4, starting transfers between devices: 2.47 us -> 7.13 us  [the longest x1 3.56 us: body(): x0 = lax.ppermute(xs0, 'party', SWAP)]
    ppermute x1, waiting for transfers between devices: 4.38 us -> 0.01 us  [body(): d_party = lax.ppermute(d, 'party', SWAP)]
    ppermute x3, waiting for transfers between devices: 4.35 us -> 0.01 us  [body(): lax.ppermute(give, ('party', 'xl'), [(i, (i + step) % 4) for i in range(4)])]
    ppermute x1, waiting for transfers between devices: 12.4 us -> 8.8 us  [body(): got1 = lax.ppermute(sent1, 'party', SWAP)]
  transfers between devices with their start and end apart: 30 -> 29, of which waited for: 12 -> 10; matrix products, arithmetic and copies ran while one was open for 9% -> 12% of each run, Pallas kernels for 27% -> 29%
where the time goes in v7:
time: 232 us; the launch traced here: 231 us
  waiting for transfers between devices  69.8 us (30%)
  Pallas kernels  66.9 us (29%)
  starting transfers between devices  45 us (19%)
  other arithmetic  18.2 us (8%)
  between operations  15.8 us (7%)
  local copies, waits for them, and re-layouts  15.6 us (7%)
    pallas_call x2, Pallas kernels, grad_parts(): pl.pallas_call(lambda *refs: grad_kernel(bool(sent), *refs), grid=(ff //...  35.4 us
    pallas_call x2, Pallas kernels, forward_call(): pl.pallas_call(kernel, grid=(steps,), in_specs=[pl.BlockSpec((rows, d), l...  25.6 us
    ppermute x12, starting transfers between devices, scattered_pair(): lax.ppermute(piece, axis, [(i, (i + step) % 4) for i in range(4)])  23.1 us
    ppermute x1, waiting for transfers between devices, body(): got0 = lax.ppermute(sent0, 'party', SWAP)  21 us
    ppermute x12, waiting for transfers between devices, scattered_pair(): lax.ppermute(piece, axis, [(i, (i + step) % 4) for i in range(4)])  17 us
    ppermute x1, waiting for transfers between devices, body(): x0 = lax.ppermute(xs0, 'party', SWAP)  16.9 us
    ppermute x1, waiting for transfers between devices, body(): got1 = lax.ppermute(sent1, 'party', SWAP)  8.8 us
    unnamed x35, local copies, waits for them, and re-layouts  6.54 us
  transfers between devices with their start and end apart: 29, of which 10 were waited for; matrix products, arithmetic and copies ran while one was open for 12% of the time, Pallas kernels for 29%

profile of v7, /device:TPU:0, one launch (start us, length us, event | category | flops | bytes accessed | tf_op | source)
XLA Modules:
  0.0 231.3 jit_solution(8279180425431334619)
XLA Ops:
  8.0 1.0 bitcast_subtract_fusion
  9.0 3.2 %collective-permute-start.3 = (f32[16,2048]{1,0:T(8,128)S(1)}, f32[16,2048]{1,0:T(8,128)S(1)}, u32[]{:S(2)}, u32[]{:S(2)}) collective-permute-start(f32[16,2048]{1,0:T(8,128)S(1)} %bitcast_subtract_fusion), channel_id=1, source_target_pairs={{0,64},{64,0},{1,65},{65,1},{2,66},{66,2},{3,67},{67,3},{4,68},{68... | collective-permute-start | bytes 393224 | tf_op jit(solution)/shard_map/ppermute | solution.py:262
  12.2 1.1 collective-permute-start.5
  13.4 2.9 %shard_map.104 = (f32[4,4,2,8,512]{4,3,2,1,0:T(8,128)}, f32[4,4,2,8,512]{4,3,2,1,0:T(8,128)}, f32[2,4,4,2,8,512]{5,4,3,2,1,0:T(8,128)}) custom-call(s32[1]{0:T(128)} %bitcast.3.core_ref, f32[512,1024]{1,0:T(8,128)} %bitcast.104), custom_call_target="tpu_custom_call" | custom-call | bytes 4194304 | tf_op jit(solution)/shard_map/pallas_call | solution.py:60
  16.3 3.0 %shard_map.105 = (f32[4,4,2,8,512]{4,3,2,1,0:T(8,128)}, f32[4,4,2,8,512]{4,3,2,1,0:T(8,128)}, f32[2,4,4,2,8,512]{5,4,3,2,1,0:T(8,128)}) custom-call(s32[1]{0:T(128)} %bitcast.3.core_ref, f32[512,1024]{1,0:T(8,128)} %bitcast.113), custom_call_target="tpu_custom_call" | custom-call | bytes 4194304 | tf_op jit(solution)/shard_map/pallas_call | solution.py:60
  21.3 1.3 slice_bitcast_fusion
  23.4 1.3 slice_bitcast_fusion.1
  24.7 1.1 pad_maximum_fusion.1.refs_1_
  25.8 3.6 %collective-permute-start.7 = (f32[256,1024]{1,0:T(8,128)}, f32[256,1024]{1,0:T(8,128)}, u32[]{:S(2)}, u32[]{:S(2)}) collective-permute-start(f32[256,1024]{1,0:T(8,128)} %pad_maximum_fusion.1.refs_1_), channel_id=1, source_target_pairs={{0,64},{64,0},{1,65},{65,1},{2,66},{66,2},{3,67},{67,3},{4,68},{68... | collective-permute-start | bytes 3145736 | tf_op jit(solution)/shard_map/ppermute | solution.py:241
  29.4 0.9 slice_dynamic-update-slice_fusion
  32.5 1.5 pad_maximum_fusion
  34.0 1.2 multiply_add_fusion
  35.3 0.8 pad_maximum_fusion.4
  36.1 16.9 %collective-permute-done.7.refs_3_ = f32[256,1024]{1,0:T(8,128)} collective-permute-done((f32[256,1024]{1,0:T(8,128)}, f32[256,1024]{1,0:T(8,128)}, u32[]{:S(2)}, u32[]{:S(2)}) %collective-permute-start.7) | collective-permute-done | bytes 1048608 | tf_op jit(solution)/shard_map/ppermute | solution.py:241
  53.7 3.0 %collective-permute-start.1 = (f32[256,1024]{1,0:T(8,128)}, f32[256,1024]{1,0:T(8,128)}, u32[]{:S(2)}, u32[]{:S(2)}) collective-permute-start(f32[256,1024]{1,0:T(8,128)} %get-tuple-element.63), channel_id=1, source_target_pairs={{0,64},{64,0},{1,65},{65,1},{2,66},{66,2},{3,67},{67,3},{4,68},{68... | collective-permute-start | bytes 3145736 | tf_op jit(solution)/shard_map/ppermute | solution.py:249
  56.7 3.3 %bitcast_subtract_fusion.1 = f32[512,1024]{1,0:T(8,128)} fusion(f32[1,512,1024]{2,1,0:T(8,128)} %param.12, f32[1,512,1024]{2,1,0:T(8,128)S(1)} %copy-done), kind=kLoop, calls=%fused_computation.75 | loop fusion | flops 524288 | bytes 6291456 | tf_op jit(solution)/shard_map/sub | solution.py:276
  60.6 21.0 %collective-permute-done.1.refs_4_.refs_8_ = f32[256,1024]{1,0:T(8,128)} collective-permute-done((f32[256,1024]{1,0:T(8,128)}, f32[256,1024]{1,0:T(8,128)}, u32[]{:S(2)}, u32[]{:S(2)}) %collective-permute-start.1) | collective-permute-done | bytes 1048608 | tf_op jit(solution)/shard_map/ppermute | solution.py:249
  81.6 2.0 copy-done.15
  83.6 1.3 copy-done.14
  84.9 16.3 %shard_map.108 = f32[16,2,16,2048]{3,2,1,0:T(8,128)} custom-call(s32[1]{0:T(128)} %bitcast.19.refs_0_, f32[256,1024]{1,0:T(8,128)} %pad_maximum_fusion.1.refs_1_, f32[256,1024]{1,0:T(8,128)} %get-tuple-element.62.refs_2_, f32[256,1024]{1,0:T(8,128)} %collective-permute-done.7.refs_3_, f32[256,1024]{1,0:T(8,128)} %collective-permute-done.1.refs_4_.refs_8_, ...), custom_call_target="tpu_custom_call" | custom-call | flops 9663676416 | bytes 25165824 | tf_op jit(solution)/shard_map/pallas_call | solution.py:135
  101.3 1.1 pad_maximum_fusion.3.refs_2_
  102.4 1.1 pad_maximum_fusion.2.refs_1_
  103.5 3.0 %collective-permute-start.2 = (f32[512,1024]{1,0:T(8,128)}, f32[512,1024]{1,0:T(8,128)S(1)}, u32[]{:S(2)}, u32[]{:S(2)}) collective-permute-start(f32[512,1024]{1,0:T(8,128)} %bitcast_subtract_fusion.1), channel_id=1, source_target_pairs={{0,64},{64,0},{1,65},{65,1},{2,66},{66,2},{3,67},{67,3},{4,68},{68... | collective-permute-start | bytes 6291464 | tf_op jit(solution)/shard_map/ppermute | solution.py:277
  106.5 8.8 %collective-permute-done.10.refs_3_ = f32[256,1536]{1,0:T(8,128)} collective-permute-done((f32[256,1536]{1,0:T(8,128)}, f32[256,1536]{1,0:T(8,128)}, u32[]{:S(2)}, u32[]{:S(2)}) %collective-permute-start.10) | collective-permute-done | bytes 1572896 | tf_op jit(solution)/shard_map/ppermute | solution.py:275
  115.3 19.1 %shard_map.109 = (f32[16,16,2048]{2,1,0:T(8,128)}, f32[16,16,2048]{2,1,0:T(8,128)}) custom-call(s32[1]{0:T(128)} %bitcast.19.refs_0_, f32[256,1024]{1,0:T(8,128)} %pad_maximum_fusion.2.refs_1_, f32[256,1024]{1,0:T(8,128)} %pad_maximum_fusion.3.refs_2_, f32[256,1536]{1,0:T(8,128)} %collective-permute-done.10.refs_3_, f32[512,2048]{1,0:T(8,128)} %bitcast.129, ...), custom_call_target="tpu_custom_call" | custom-call | flops 77309411328 | bytes 197132288 | tf_op jit(solution)/shard_map/pallas_call | solution.py:135
  134.4 3.0 %dynamic-slice_bitcast_fusion.7 = (f32[4,16,2048]{2,1,0:T(8,128)S(1)}, f32[4,16,2048]{2,1,0:T(8,128)}, f32[4,16,2048]{2,1,0:T(8,128)}, f32[4,16,2048]{2,1,0:T(8,128)S(1)}) fusion(f32[4,4,16,2048]{3,2,1,0:T(8,128)} %bitcast.115, s32[]{:T(128)S(6)} %select_n.142, s32[]{:T(128)S(6)} %select_n.148, s32[]{:T(128)S(6)} %select_n.146, s32[]{:T(128)S(6)} %select_n.144), kind=kLoop, calls=%fused_computation.28 | loop fusion | bytes 4194320 | tf_op jit(solution)/shard_map/jit(dynamic_index_in_dim)/squeeze | solution.py:213
  137.3 3.7 %collective-permute-start.12 = (f32[4,16,2048]{2,1,0:T(8,128)S(1)}, f32[4,16,2048]{2,1,0:T(8,128)}, u32[]{:S(2)}, u32[]{:S(2)}) collective-permute-start(f32[4,16,2048]{2,1,0:T(8,128)S(1)} %get-tuple-element.57), channel_id=1, source_target_pairs={{0,4},{2,6},{4,0},{6,2},{1,5},{3,7},{5,1},{7,3},{8,12},{10,14},{12... | collective-permute-start | bytes 1572872 | tf_op jit(solution)/shard_map/ppermute | solution.py:221
  141.0 1.2 dynamic-slice_bitcast_fusion.3
  142.2 3.1 %collective-permute-start.18 = (f32[4,16,2048]{2,1,0:T(8,128)S(1)}, f32[4,16,2048]{2,1,0:T(8,128)}, u32[]{:S(2)}, u32[]{:S(2)}) collective-permute-start(f32[4,16,2048]{2,1,0:T(8,128)S(1)} %get-tuple-element.61), channel_id=1, source_target_pairs={{0,32},{16,48},{32,0},{48,16},{1,33},{17,49},{33,1},{49,17},{2,34}... | collective-permute-start | bytes 1572872 | tf_op jit(solution)/shard_map/ppermute | solution.py:221
  146.7 10.9 %collective-permute-done.12 = f32[4,16,2048]{2,1,0:T(8,128)} collective-permute-done((f32[4,16,2048]{2,1,0:T(8,128)S(1)}, f32[4,16,2048]{2,1,0:T(8,128)}, u32[]{:S(2)}, u32[]{:S(2)}) %collective-permute-start.12) | collective-permute-done | bytes 524320 | tf_op jit(solution)/shard_map/ppermute | solution.py:221
  157.7 1.6 collective-permute-start.14
  159.3 1.3 collective-permute-done.18
  160.6 1.3 collective-permute-start.20
  161.9 12.2 %shard_map.106.c_ref = f32[512,2048]{1,0:T(8,128)} custom-call(f32[512,1024]{1,0:T(8,128)} %bitcast.106, f32[512,8192]{1,0:T(8,128)} %all-gather.2.cloned.1.call-done.w0_ref.w1_ref, f32[512,8192]{1,0:T(8,128)} %all-gather.2.cloned.1.call-done.w0_ref.w1_ref, f32[512,2048]{1,0:T(8,128)} %bitcast.110), custom_call_target="tpu_custom_call" | custom-call | flops 6442450944 | bytes 20971520 | tf_op jit(solution)/shard_map/pallas_call | solution.py:192
  175.0 1.7 add_add_fusion.1
  177.4 2.1 collective-permute-start.15
  179.5 1.5 add_add_fusion
  181.8 1.3 collective-permute-start.21
  183.8 2.6 %collective-permute-start.17 = (f32[16,2048]{1,0:T(8,128)S(1)}, f32[16,2048]{1,0:T(8,128)S(1)}, u32[]{:S(2)}, u32[]{:S(2)}) collective-permute-start(f32[16,2048]{1,0:T(8,128)S(1)} %get-tuple-element.45), channel_id=1, source_target_pairs={{0,48},{16,0},{32,16},{48,32},{1,49},{17,1},{33,17},{49,33},{2,50}... | collective-permute-start | bytes 393224 | tf_op jit(solution)/shard_map/ppermute | solution.py:221
  186.4 2.5 %collective-permute-start.22 = (f32[16,2048]{1,0:T(8,128)}, f32[16,2048]{1,0:T(8,128)S(1)}, u32[]{:S(2)}, u32[]{:S(2)}) collective-permute-start(f32[16,2048]{1,0:T(8,128)} %get-tuple-element.76), channel_id=1, source_target_pairs={{0,2},{2,4},{4,6},{6,0},{1,3},{3,5},{5,7},{7,1},{8,10},{10,12},{12... | collective-permute-start | bytes 393224 | tf_op jit(solution)/shard_map/ppermute | solution.py:221
  189.5 3.0 %collective-permute-start.23 = (f32[16,2048]{1,0:T(8,128)}, f32[16,2048]{1,0:T(8,128)S(1)}, u32[]{:S(2)}, u32[]{:S(2)}) collective-permute-start(f32[16,2048]{1,0:T(8,128)} %get-tuple-element.49), channel_id=1, source_target_pairs={{0,6},{2,0},{4,2},{6,4},{1,7},{3,1},{5,3},{7,5},{8,14},{10,8},{12,... | collective-permute-start | bytes 393224 | tf_op jit(solution)/shard_map/ppermute | solution.py:221
  192.6 1.6 collective-permute-done.22
  194.2 2.2 collective-permute-done.23
  196.5 6.0 %reduce-scatter.4.cloned.1.call-done = f32[1,32,2048]{2,1,0:T(8,128)} async-done(((f32[16,32,2048]{2,1,0:T(8,128)}), f32[1,32,2048]{2,1,0:T(8,128)}) %reduce-scatter.4.cloned.1.call-update) | async-done | bytes 262160
  202.5 0.9 fusion.13
  203.4 3.1 %collective-permute-start.24 = (f32[16,2048]{1,0:T(8,128)S(1)}, f32[16,2048]{1,0:T(8,128)S(1)}, u32[]{:S(2)}, u32[]{:S(2)}) collective-permute-start(f32[16,2048]{1,0:T(8,128)S(1)} %get-tuple-element.70), channel_id=1, source_target_pairs={{0,64},{8,72},{64,0},{72,8},{1,65},{9,73},{65,1},{73,9},{2,66},{10... | collective-permute-start | bytes 393224 | tf_op jit(solution)/shard_map/ppermute | solution.py:305
  207.0 2.7 %collective-permute-start.26 = (f32[16,2048]{1,0:T(8,128)S(1)}, f32[16,2048]{1,0:T(8,128)S(1)}, u32[]{:S(2)}, u32[]{:S(2)}) collective-permute-start(f32[16,2048]{1,0:T(8,128)S(1)} %get-tuple-element.72), channel_id=1, source_target_pairs={{0,72},{8,0},{64,8},{72,64},{1,73},{9,1},{65,9},{73,65},{2,74},{10... | collective-permute-start | bytes 393224 | tf_op jit(solution)/shard_map/ppermute | solution.py:305
  209.7 13.4 %shard_map.107 = f32[512,2048]{1,0:T(8,128)} custom-call(f32[512,1024]{1,0:T(8,128)} %bitcast.105, f32[512,1024]{1,0:T(8,128)} %bitcast.107, f32[512,1024]{1,0:T(8,128)} %copy-done.1, f32[512,8192]{1,0:T(8,128)} %all-gather.2.cloned.1.call-done.w0_ref.w1_ref, f32[512,8192]{1,0:T(8,128)} %all-gather.2.cloned.1.call-done.w0_ref.w1_ref, ...), custom_call_target="tpu_custom_call" | custom-call | flops 6442450944 | bytes 20971520 | tf_op jit(solution)/shard_map/pallas_call | solution.py:192
  (81 shorter events, 12.8 us)
Async XLA Ops:
  8.0 153.9 %all-gather.2.cloned.1.call-start = ((), (), s32[]{:S(2)}) async-start(), calls=%async_computation.1 | async-start | bytes 17301504 | tf_op jit(solution)/shard_map/all_gather | solution.py:273
  9.0 25.0 %collective-permute-start.3 = (f32[16,2048]{1,0:T(8,128)S(1)}, f32[16,2048]{1,0:T(8,128)S(1)}, u32[]{:S(2)}, u32[]{:S(2)}) collective-permute-start(f32[16,2048]{1,0:T(8,128)S(1)} %bitcast_subtract_fusion), channel_id=1, source_target_pairs={{0,64},{64,0},{1,65},{65,1},{2,66},{66,2},{3,67},{67,3},{4,68},{68... | collective-permute-start | bytes 393224 | tf_op jit(solution)/shard_map/ppermute | solution.py:262
  12.2 21.8 %collective-permute-start.5 = (f32[16,2048]{1,0:T(8,128)S(1)}, f32[16,2048]{1,0:T(8,128)}, u32[]{:S(2)}, u32[]{:S(2)}) collective-permute-start(f32[16,2048]{1,0:T(8,128)S(1)} %bitcast_subtract_fusion), channel_id=1, source_target_pairs={{0,72},{72,0},{8,64},{64,8},{1,73},{73,1},{9,65},{65,9},{2,74},{74... | collective-permute-start | bytes 393224 | tf_op jit(solution)/shard_map/ppermute | solution.py:264
  13.4 6.4 %copy-start.8 = (f32[1,16,2048]{2,1,0:T(8,128)S(1)}, f32[1,16,2048]{2,1,0:T(8,128)}, u32[]{:S(2)}) copy-start(f32[1,16,2048]{2,1,0:T(8,128)} %param.13) | copy-start | bytes 393220
  16.3 4.2 %copy-start.3 = (f32[4,4,2,8,512]{4,3,2,1,0:T(8,128)S(1)}, f32[4,4,2,8,512]{4,3,2,1,0:T(8,128)}, u32[]{:S(2)}) copy-start(f32[4,4,2,8,512]{4,3,2,1,0:T(8,128)} %get-tuple-element.31) | copy-start | bytes 1572868
  16.3 7.1 %collective-permute-start.6 = (f32[2,256,512]{2,1,0:T(8,128)}, f32[2,256,512]{2,1,0:T(8,128)}, u32[]{:S(2)}, u32[]{:S(2)}) collective-permute-start(f32[2,256,512]{2,1,0:T(8,128)} %bitcast.134), channel_id=1, source_target_pairs={{0,1},{1,0},{2,3},{3,2},{4,5},{5,4},{6,7},{7,6},{8,9},{9,8},{10,11... | collective-permute-start | bytes 3145736 | tf_op jit(solution)/shard_map/ppermute | solution.py:238
  19.3 3.3 %copy-start.6 = (f32[4,4,2,8,512]{4,3,2,1,0:T(8,128)S(1)}, f32[4,4,2,8,512]{4,3,2,1,0:T(8,128)}, u32[]{:S(2)}) copy-start(f32[4,4,2,8,512]{4,3,2,1,0:T(8,128)} %get-tuple-element.32) | copy-start | bytes 1572868
  19.3 11.0 %collective-permute-start = (f32[2,256,512]{2,1,0:T(8,128)}, f32[2,256,512]{2,1,0:T(8,128)S(1)}, u32[]{:S(2)}, u32[]{:S(2)}) collective-permute-start(f32[2,256,512]{2,1,0:T(8,128)} %bitcast.133), channel_id=1, source_target_pairs={{0,1},{1,0},{2,3},{3,2},{4,5},{5,4},{6,7},{7,6},{8,9},{9,8},{10,11... | collective-permute-start | bytes 3145736 | tf_op jit(solution)/shard_map/ppermute | solution.py:243
  20.5 13.5 %collective-permute-start.4 = (f32[16,4096]{1,0:T(8,128)}, f32[16,4096]{1,0:T(8,128)}, u32[]{:S(2)}, u32[]{:S(2)}) collective-permute-start(f32[16,4096]{1,0:T(8,128)} %pad_maximum_fusion.5), channel_id=1, source_target_pairs={{0,8},{8,0},{1,9},{9,1},{2,10},{10,2},{3,11},{11,3},{4,12},{12,4},... | collective-permute-start | bytes 786440 | tf_op jit(solution)/shard_map/ppermute | solution.py:263
  23.3 1.4 copy-start.12
  25.8 27.2 %collective-permute-start.7 = (f32[256,1024]{1,0:T(8,128)}, f32[256,1024]{1,0:T(8,128)}, u32[]{:S(2)}, u32[]{:S(2)}) collective-permute-start(f32[256,1024]{1,0:T(8,128)} %pad_maximum_fusion.1.refs_1_), channel_id=1, source_target_pairs={{0,64},{64,0},{1,65},{65,1},{2,66},{66,2},{3,67},{67,3},{4,68},{68... | collective-permute-start | bytes 3145736 | tf_op jit(solution)/shard_map/ppermute | solution.py:241
  29.4 3.1 %copy-start.10 = (f32[4,4,2,8,512]{4,3,2,1,0:T(8,128)S(1)}, f32[4,4,2,8,512]{4,3,2,1,0:T(8,128)}, u32[]{:S(2)}) copy-start(f32[4,4,2,8,512]{4,3,2,1,0:T(8,128)} %get-tuple-element.28) | copy-start | bytes 1572868
  34.0 22.7 %copy-start = (f32[1,512,1024]{2,1,0:T(8,128)S(1)}, f32[1,512,1024]{2,1,0:T(8,128)}, u32[]{:S(2)}) copy-start(f32[1,512,1024]{2,1,0:T(8,128)} %param.9) | copy-start | bytes 6291460
  53.1 149.4 %reduce-scatter.4.cloned.1.call-start = ((), (), s32[]{:S(2)}) async-start(), calls=%async_computation.2 | async-start | bytes 4456448
  53.2 28.4 %collective-permute-start.8 = (f32[512,2048]{1,0:T(8,128)}, f32[512,2048]{1,0:T(8,128)S(1)}, u32[]{:S(2)}, u32[]{:S(2)}) collective-permute-start(f32[512,2048]{1,0:T(8,128)} %bitcast.127), channel_id=1, source_target_pairs={{0,1},{1,0},{2,3},{3,2},{4,5},{5,4},{6,7},{7,6},{8,9},{9,8},{10,11... | collective-permute-start | bytes 12582920 | tf_op jit(solution)/shard_map/ppermute | solution.py:279
  53.2 28.3 %collective-permute-start.9 = (f32[512,2048]{1,0:T(8,128)}, f32[512,2048]{1,0:T(8,128)S(1)}, u32[]{:S(2)}, u32[]{:S(2)}) collective-permute-start(f32[512,2048]{1,0:T(8,128)} %bitcast.130), channel_id=1, source_target_pairs={{0,1},{1,0},{2,3},{3,2},{4,5},{5,4},{6,7},{7,6},{8,9},{9,8},{10,11... | collective-permute-start | bytes 12582920 | tf_op jit(solution)/shard_map/ppermute | solution.py:280
  53.7 27.8 %collective-permute-start.1 = (f32[256,1024]{1,0:T(8,128)}, f32[256,1024]{1,0:T(8,128)}, u32[]{:S(2)}, u32[]{:S(2)}) collective-permute-start(f32[256,1024]{1,0:T(8,128)} %get-tuple-element.63), channel_id=1, source_target_pairs={{0,64},{64,0},{1,65},{65,1},{2,66},{66,2},{3,67},{67,3},{4,68},{68... | collective-permute-start | bytes 3145736 | tf_op jit(solution)/shard_map/ppermute | solution.py:249
  60.0 55.2 %collective-permute-start.10 = (f32[256,1536]{1,0:T(8,128)}, f32[256,1536]{1,0:T(8,128)}, u32[]{:S(2)}, u32[]{:S(2)}) collective-permute-start(f32[256,1536]{1,0:T(8,128)} %slice_dynamic-update-slice_fusion.2), channel_id=1, source_target_pairs={{0,64},{64,0},{1,65},{65,1},{2,66},{66,2},{3,67},{67,3},{4,68},{68... | collective-permute-start | bytes 4718600 | tf_op jit(solution)/shard_map/ppermute | solution.py:275
  81.6 3.3 %copy-start.14 = (f32[512,2048]{1,0:T(8,128)}, f32[512,2048]{1,0:T(8,128)S(1)}, u32[]{:S(2)}) copy-start(f32[512,2048]{1,0:T(8,128)S(1)} %collective-permute-done.8.refs_7_.refs_6_) | copy-start | bytes 12582916
  81.6 2.0 copy-start.15
  84.9 16.4 %copy-start.7 = (f32[4,4,2,8,512]{4,3,2,1,0:T(8,128)S(1)}, f32[4,4,2,8,512]{4,3,2,1,0:T(8,128)}, u32[]{:S(2)}) copy-start(f32[4,4,2,8,512]{4,3,2,1,0:T(8,128)} %get-tuple-element.32) | copy-start | bytes 1572868
  101.2 1.2 copy-start.4
  101.2 14.1 %collective-permute-start.11 = (f32[256,1024]{1,0:T(8,128)}, f32[256,1024]{1,0:T(8,128)}, u32[]{:S(2)}, u32[]{:S(2)}) collective-permute-start(f32[256,1024]{1,0:T(8,128)} %collective-permute-done.1.refs_4_.refs_8_), channel_id=1, source_target_pairs={{0,1},{1,0},{2,3},{3,2},{4,5},{5,4},{6,7},{7,6},{8,9},{9,8},{10,11... | collective-permute-start | bytes 3145736 | tf_op jit(solution)/shard_map/ppermute | solution.py:283
  103.5 70.7 %collective-permute-start.2 = (f32[512,1024]{1,0:T(8,128)}, f32[512,1024]{1,0:T(8,128)S(1)}, u32[]{:S(2)}, u32[]{:S(2)}) collective-permute-start(f32[512,1024]{1,0:T(8,128)} %bitcast_subtract_fusion.1), channel_id=1, source_target_pairs={{0,64},{64,0},{1,65},{65,1},{2,66},{66,2},{3,67},{67,3},{4,68},{68... | collective-permute-start | bytes 6291464 | tf_op jit(solution)/shard_map/ppermute | solution.py:277
  134.4 6.6 %copy-start.2 = (f32[16,16,2048]{2,1,0:T(8,128)S(1)}, f32[16,16,2048]{2,1,0:T(8,128)}, u32[]{:S(2)}) copy-start(f32[16,16,2048]{2,1,0:T(8,128)} %get-tuple-element.46) | copy-start | bytes 6291460
  137.3 20.3 %collective-permute-start.12 = (f32[4,16,2048]{2,1,0:T(8,128)S(1)}, f32[4,16,2048]{2,1,0:T(8,128)}, u32[]{:S(2)}, u32[]{:S(2)}) collective-permute-start(f32[4,16,2048]{2,1,0:T(8,128)S(1)} %get-tuple-element.57), channel_id=1, source_target_pairs={{0,4},{2,6},{4,0},{6,2},{1,5},{3,7},{5,1},{7,3},{8,12},{10,14},{12... | collective-permute-start | bytes 1572872 | tf_op jit(solution)/shard_map/ppermute | solution.py:221
  142.2 18.4 %collective-permute-start.18 = (f32[4,16,2048]{2,1,0:T(8,128)S(1)}, f32[4,16,2048]{2,1,0:T(8,128)}, u32[]{:S(2)}, u32[]{:S(2)}) collective-permute-start(f32[4,16,2048]{2,1,0:T(8,128)S(1)} %get-tuple-element.61), channel_id=1, source_target_pairs={{0,32},{16,48},{32,0},{48,16},{1,33},{17,49},{33,1},{49,17},{2,34}... | collective-permute-start | bytes 1572872 | tf_op jit(solution)/shard_map/ppermute | solution.py:221
  145.3 28.9 %collective-permute-start.13 = (f32[4,16,2048]{2,1,0:T(8,128)}, f32[4,16,2048]{2,1,0:T(8,128)S(1)}, u32[]{:S(2)}, u32[]{:S(2)}) collective-permute-start(f32[4,16,2048]{2,1,0:T(8,128)} %get-tuple-element.56), channel_id=1, source_target_pairs={{0,2},{2,4},{4,6},{6,0},{1,3},{3,5},{5,7},{7,1},{8,10},{10,12},{12... | collective-permute-start | bytes 1572872 | tf_op jit(solution)/shard_map/ppermute | solution.py:221
  146.1 33.4 %collective-permute-start.19 = (f32[4,16,2048]{2,1,0:T(8,128)}, f32[4,16,2048]{2,1,0:T(8,128)}, u32[]{:S(2)}, u32[]{:S(2)}) collective-permute-start(f32[4,16,2048]{2,1,0:T(8,128)} %get-tuple-element.60), channel_id=1, source_target_pairs={{0,16},{16,32},{32,48},{48,0},{1,17},{17,33},{33,49},{49,1},{2,18}... | collective-permute-start | bytes 1572872 | tf_op jit(solution)/shard_map/ppermute | solution.py:221
  157.7 17.3 %collective-permute-start.14 = (f32[4,16,2048]{2,1,0:T(8,128)}, f32[4,16,2048]{2,1,0:T(8,128)}, u32[]{:S(2)}, u32[]{:S(2)}) collective-permute-start(f32[4,16,2048]{2,1,0:T(8,128)} %get-tuple-element.44), channel_id=1, source_target_pairs={{0,6},{2,0},{4,2},{6,4},{1,7},{3,1},{5,3},{7,5},{8,14},{10,8},{12,... | collective-permute-start | bytes 1572872 | tf_op jit(solution)/shard_map/ppermute | solution.py:221
  160.6 18.9 %collective-permute-start.20 = (f32[4,16,2048]{2,1,0:T(8,128)}, f32[4,16,2048]{2,1,0:T(8,128)}, u32[]{:S(2)}, u32[]{:S(2)}) collective-permute-start(f32[4,16,2048]{2,1,0:T(8,128)} %get-tuple-element.48), channel_id=1, source_target_pairs={{0,48},{16,0},{32,16},{48,32},{1,49},{17,1},{33,17},{49,33},{2,50}... | collective-permute-start | bytes 1572872 | tf_op jit(solution)/shard_map/ppermute | solution.py:221
  174.1 5.4 %copy-start.5 = (f32[4,16,2048]{2,1,0:T(8,128)S(1)}, f32[4,16,2048]{2,1,0:T(8,128)}, u32[]{:S(2)}) copy-start(f32[4,16,2048]{2,1,0:T(8,128)} %get-tuple-element.47) | copy-start | bytes 1572868
  174.1 6.9 %copy-start.1 = (f32[512,1024]{1,0:T(8,128)}, f32[512,1024]{1,0:T(8,128)S(1)}, u32[]{:S(2)}) copy-start(f32[512,1024]{1,0:T(8,128)S(1)} %collective-permute-done.2.got_ref) | copy-start | bytes 6291460
  174.2 0.8 copy-start.11
  177.4 6.5 %collective-permute-start.15 = (f32[16,2048]{1,0:T(8,128)S(1)}, f32[16,2048]{1,0:T(8,128)S(1)}, u32[]{:S(2)}, u32[]{:S(2)}) collective-permute-start(f32[16,2048]{1,0:T(8,128)S(1)} %get-tuple-element.75), channel_id=1, source_target_pairs={{0,32},{16,48},{32,0},{48,16},{1,33},{17,49},{33,1},{49,17},{2,34}... | collective-permute-start | bytes 393224 | tf_op jit(solution)/shard_map/ppermute | solution.py:221
  179.5 23.0 %copy-start.13 = (f32[1,16,2048]{2,1,0:T(8,128)S(1)}, f32[1,16,2048]{2,1,0:T(8,128)}, u32[]{:S(2)}) copy-start(f32[1,16,2048]{2,1,0:T(8,128)} %param.17) | copy-start | bytes 393220
  181.8 7.7 %collective-permute-start.21 = (f32[16,2048]{1,0:T(8,128)}, f32[16,2048]{1,0:T(8,128)S(1)}, u32[]{:S(2)}, u32[]{:S(2)}) collective-permute-start(f32[16,2048]{1,0:T(8,128)} %get-tuple-element.78), channel_id=1, source_target_pairs={{0,4},{2,6},{4,0},{6,2},{1,5},{3,7},{5,1},{7,3},{8,12},{10,14},{12... | collective-permute-start | bytes 393224 | tf_op jit(solution)/shard_map/ppermute | solution.py:221
  183.1 9.5 %collective-permute-start.16 = (f32[16,2048]{1,0:T(8,128)}, f32[16,2048]{1,0:T(8,128)S(1)}, u32[]{:S(2)}, u32[]{:S(2)}) collective-permute-start(f32[16,2048]{1,0:T(8,128)} %get-tuple-element.73), channel_id=1, source_target_pairs={{0,16},{16,32},{32,48},{48,0},{1,17},{17,33},{33,49},{49,1},{2,18}... | collective-permute-start | bytes 393224 | tf_op jit(solution)/shard_map/ppermute | solution.py:221
  183.8 8.7 %collective-permute-start.17 = (f32[16,2048]{1,0:T(8,128)S(1)}, f32[16,2048]{1,0:T(8,128)S(1)}, u32[]{:S(2)}, u32[]{:S(2)}) collective-permute-start(f32[16,2048]{1,0:T(8,128)S(1)} %get-tuple-element.45), channel_id=1, source_target_pairs={{0,48},{16,0},{32,16},{48,32},{1,49},{17,1},{33,17},{49,33},{2,50}... | collective-permute-start | bytes 393224 | tf_op jit(solution)/shard_map/ppermute | solution.py:221
  186.4 7.8 %collective-permute-start.22 = (f32[16,2048]{1,0:T(8,128)}, f32[16,2048]{1,0:T(8,128)S(1)}, u32[]{:S(2)}, u32[]{:S(2)}) collective-permute-start(f32[16,2048]{1,0:T(8,128)} %get-tuple-element.76), channel_id=1, source_target_pairs={{0,2},{2,4},{4,6},{6,0},{1,3},{3,5},{5,7},{7,1},{8,10},{10,12},{12... | collective-permute-start | bytes 393224 | tf_op jit(solution)/shard_map/ppermute | solution.py:221
  189.5 6.9 %collective-permute-start.23 = (f32[16,2048]{1,0:T(8,128)}, f32[16,2048]{1,0:T(8,128)S(1)}, u32[]{:S(2)}, u32[]{:S(2)}) collective-permute-start(f32[16,2048]{1,0:T(8,128)} %get-tuple-element.49), channel_id=1, source_target_pairs={{0,6},{2,0},{4,2},{6,4},{1,7},{3,1},{5,3},{7,5},{8,14},{10,8},{12,... | collective-permute-start | bytes 393224 | tf_op jit(solution)/shard_map/ppermute | solution.py:221
  203.4 19.7 %collective-permute-start.24 = (f32[16,2048]{1,0:T(8,128)S(1)}, f32[16,2048]{1,0:T(8,128)S(1)}, u32[]{:S(2)}, u32[]{:S(2)}) collective-permute-start(f32[16,2048]{1,0:T(8,128)S(1)} %get-tuple-element.70), channel_id=1, source_target_pairs={{0,64},{8,72},{64,0},{72,8},{1,65},{9,73},{65,1},{73,9},{2,66},{10... | collective-permute-start | bytes 393224 | tf_op jit(solution)/shard_map/ppermute | solution.py:305
  206.5 16.7 %collective-permute-start.25 = (f32[16,2048]{1,0:T(8,128)S(1)}, f32[16,2048]{1,0:T(8,128)S(1)}, u32[]{:S(2)}, u32[]{:S(2)}) collective-permute-start(f32[16,2048]{1,0:T(8,128)S(1)} %get-tuple-element.71), channel_id=1, source_target_pairs={{0,8},{8,64},{64,72},{72,0},{1,9},{9,65},{65,73},{73,1},{2,10},{10... | collective-permute-start | bytes 393224 | tf_op jit(solution)/shard_map/ppermute | solution.py:305
  207.0 16.1 %copy-start.9 = (f32[1,32,2048]{2,1,0:T(8,128)S(1)}, f32[1,32,2048]{2,1,0:T(8,128)}, u32[]{:S(2)}) copy-start(f32[1,32,2048]{2,1,0:T(8,128)} %reduce-scatter.4.cloned.1.call-done) | copy-start | bytes 786436
  207.0 16.1 %collective-permute-start.26 = (f32[16,2048]{1,0:T(8,128)S(1)}, f32[16,2048]{1,0:T(8,128)S(1)}, u32[]{:S(2)}, u32[]{:S(2)}) collective-permute-start(f32[16,2048]{1,0:T(8,128)S(1)} %get-tuple-element.72), channel_id=1, source_target_pairs={{0,72},{8,0},{64,8},{72,64},{1,73},{9,1},{65,9},{73,65},{2,74},{10... | collective-permute-start | bytes 393224 | tf_op jit(solution)/shard_map/ppermute | solution.py:305
Sparse Core Ops, SparseCore 0:
  53.2 75.1 all-gather.1
Sparse Core Ops, SparseCore 1:
  106.6 95.8 reduce-scatter.3

commit v8 on v7

--- a/solution.py
+++ b/solution.py
@@ -206,20 +206,23 @@
     )(*lefts, weights, weights, c)
 
 
-def scattered_pair(a, a_axis, a_dim, b, b_axis, b_dim, beside):
+def scattered_pair(a, a_axis, a_dim, b, b_axis, b_dim, between=(), beside=None):
     sums, got = [], [[], []]
     for v, axis, dim in ((a, a_axis, a_dim), (b, b_axis, b_dim)):
         here = lax.axis_index(axis)
-        own = lax.dynamic_index_in_dim(v, here, dim, keepdims=False)
-        sums.append(after(own, *beside) if beside else own)
+        sums.append(lax.dynamic_index_in_dim(v, here, dim, keepdims=False))
     for step in (2, 1, 3):
         for n, (v, axis, dim) in enumerate(((a, a_axis, a_dim), (b, b_axis, b_dim))):
             here = lax.axis_index(axis)
             piece = lax.dynamic_index_in_dim(v, (here + step) % 4, dim, keepdims=False)
             if len(got[n]) == 2:
-                piece = after(piece, got[n][0])
+                piece = after(piece, got[n][0], *between)
             got[n].append(lax.ppermute(piece, axis, [(i, (i + step) % 4) for i in range(4)]))
-    return [s + r[0] + r[1] + r[2] for s, r in zip(sums, got)]
+    made = None
+    if beside:
+        made = beside(got[0][0], got[1][0])
+        sums = [after(s, made) for s in sums]
+    return [s + r[0] + r[1] + r[2] for s, r in zip(sums, got)], made
 
 
 def body(x_share, w_share, g_share, fwd_a, fwd_b, fwd_c, bwd_a, bwd_b, bwd_c):
@@ -279,7 +282,7 @@
     g_other = lax.ppermute(after(g, a_other), "core", SWAP)
     b_other = lax.ppermute(after(bb, a_other), "core", SWAP)
     rights = (g, bb, g_other, b_other)
-    early = grad_parts(party_id, after(xs0, u_local), aa0, (x0, got0), rights, (), 1)
+    early = grad_parts(party_id, after(xs0, u_local, xs1, aa1), aa0, (x0, got0), rights, (), 1)
     sent = (got0, lax.ppermute(after(got0, early), "core", SWAP))
     late = grad_parts(party_id, xs1, aa1, (got1,), rights, sent, LATE)
 
@@ -287,11 +290,14 @@
     early = early.reshape(2, 2, 8, ff)
     outputs = forward_call(local_kernel, (fa,), weights, 1, fc)
     part0, part1 = (part.reshape(4, 4, 16, ff) for part in late)
-    part0, part1 = scattered_pair(part0, "z", 0, part1, "y", 1, (outputs, u))
-    part0, part1 = scattered_pair(part0, "y", 0, part1, "z", 0, ())
+
+    def opened(*earlier):
+        return forward_call(opened_kernel, (x, fa, u), weights, 0, after(outputs, *earlier))
+
+    (part0, part1), y = scattered_pair(part0, "z", 0, part1, "y", 1, (outputs,), opened)
+    (part0, part1), _ = scattered_pair(part0, "y", 0, part1, "z", 0)
     late = jnp.stack([part0, part1]).reshape(2, 2, 8, ff)
     both = jnp.concatenate([early, late], axis=2)
-    outputs = forward_call(opened_kernel, (x, fa, u), weights, 0, after(outputs, both))
     spot = 2 * party + lax.axis_index("xl")
 
     def piece(at):
@@ -306,7 +312,7 @@
             give, ("party", "xl"), [(i, (i + step) % 4) for i in range(4)]
         )
 
-    return (outputs[None], grad[None])
+    return (y[None], grad[None])
 
 
 def solution(mesh):

time: 232 us -> 228 us (0.983)
  waiting for transfers between devices: 69.8 us -> 64.7 us
    unnamed x3, waiting for transfers between devices: 6.04 us -> 0.06 us
    ppermute x3, waiting for transfers between devices: 0.01 us -> 2.94 us  [body(): lax.ppermute(give, ('party', 'xl'), [(i, (i + step) % 4) for i in range(4)])]
    unnamed x35 -> x37, local copies, waits for them, and re-layouts: 6.54 us -> 6.11 us
  transfers between devices with their start and end apart: 29 -> 29, of which waited for: 10 -> 10; matrix products, arithmetic and copies ran while one was open for 12% -> 11% of each run, Pallas kernels for 29% -> 30%
where the time goes in v8:
time: 228 us; the launch traced here: 227 us
  Pallas kernels  67.1 us (29%)
  waiting for transfers between devices  64.7 us (28%)
  starting transfers between devices  46.9 us (21%)
  other arithmetic  18.4 us (8%)
  between operations  15.8 us (7%)
  local copies, waits for them, and re-layouts  13.8 us (6%)
    pallas_call x2, Pallas kernels, grad_parts(): pl.pallas_call(lambda *refs: grad_kernel(bool(sent), *refs), grid=(ff //...  35.5 us
    pallas_call x2, Pallas kernels, forward_call(): pl.pallas_call(kernel, grid=(steps,), in_specs=[pl.BlockSpec((rows, d), l...  25.7 us
    ppermute x12, starting transfers between devices, scattered_pair(): lax.ppermute(piece, axis, [(i, (i + step) % 4) for i in range(4)])  24.7 us
    ppermute x1, waiting for transfers between devices, body(): got0 = lax.ppermute(sent0, 'party', SWAP)  18.8 us
    ppermute x1, waiting for transfers between devices, body(): x0 = lax.ppermute(xs0, 'party', SWAP)  16.9 us
    ppermute x12, waiting for transfers between devices, scattered_pair(): lax.ppermute(piece, axis, [(i, (i + step) % 4) for i in range(4)])  15.9 us
    ppermute x1, waiting for transfers between devices, body(): got1 = lax.ppermute(sent1, 'party', SWAP)  10.1 us
    ppermute x3, starting transfers between devices, body(): lax.ppermute(give, ('party', 'xl'), [(i, (i + step) % 4) for i in range(4)])  6.26 us
  transfers between devices with their start and end apart: 29, of which 10 were waited for; matrix products, arithmetic and copies ran while one was open for 11% of the time, Pallas kernels for 30%

profile of v8, /device:TPU:0, one launch (start us, length us, event | category | flops | bytes accessed | tf_op | source)
XLA Modules:
  0.0 226.7 jit_solution(8939800631932151613)
XLA Ops:
  8.0 1.0 bitcast_subtract_fusion
  9.0 3.2 %collective-permute-start.3 = (f32[16,2048]{1,0:T(8,128)S(1)}, f32[16,2048]{1,0:T(8,128)S(1)}, u32[]{:S(2)}, u32[]{:S(2)}) collective-permute-start(f32[16,2048]{1,0:T(8,128)S(1)} %bitcast_subtract_fusion), channel_id=1, source_target_pairs={{0,64},{64,0},{1,65},{65,1},{2,66},{66,2},{3,67},{67,3},{4,68},{68... | collective-permute-start | bytes 393224 | tf_op jit(solution)/shard_map/ppermute | solution.py:265
  12.2 1.1 collective-permute-start.5
  13.4 2.9 %shard_map.104 = (f32[4,4,2,8,512]{4,3,2,1,0:T(8,128)}, f32[4,4,2,8,512]{4,3,2,1,0:T(8,128)}, f32[2,4,4,2,8,512]{5,4,3,2,1,0:T(8,128)}) custom-call(s32[1]{0:T(128)} %bitcast.3.core_ref, f32[512,1024]{1,0:T(8,128)} %bitcast.104), custom_call_target="tpu_custom_call" | custom-call | bytes 4194304 | tf_op jit(solution)/shard_map/pallas_call | solution.py:60
  16.3 3.0 %shard_map.105 = (f32[4,4,2,8,512]{4,3,2,1,0:T(8,128)}, f32[4,4,2,8,512]{4,3,2,1,0:T(8,128)}, f32[2,4,4,2,8,512]{5,4,3,2,1,0:T(8,128)}) custom-call(s32[1]{0:T(128)} %bitcast.3.core_ref, f32[512,1024]{1,0:T(8,128)} %bitcast.113), custom_call_target="tpu_custom_call" | custom-call | bytes 4194304 | tf_op jit(solution)/shard_map/pallas_call | solution.py:60
  21.3 1.3 slice_bitcast_fusion
  23.4 1.3 slice_bitcast_fusion.1
  24.8 1.1 pad_maximum_fusion.1.refs_1_
  25.9 3.6 %collective-permute-start.7 = (f32[256,1024]{1,0:T(8,128)}, f32[256,1024]{1,0:T(8,128)}, u32[]{:S(2)}, u32[]{:S(2)}) collective-permute-start(f32[256,1024]{1,0:T(8,128)} %pad_maximum_fusion.1.refs_1_), channel_id=1, source_target_pairs={{0,64},{64,0},{1,65},{65,1},{2,66},{66,2},{3,67},{67,3},{4,68},{68... | collective-permute-start | bytes 3145736 | tf_op jit(solution)/shard_map/ppermute | solution.py:244
  32.5 1.5 pad_maximum_fusion
  34.0 1.2 multiply_add_fusion
  36.1 16.9 %collective-permute-done.7.refs_3_ = f32[256,1024]{1,0:T(8,128)} collective-permute-done((f32[256,1024]{1,0:T(8,128)}, f32[256,1024]{1,0:T(8,128)}, u32[]{:S(2)}, u32[]{:S(2)}) %collective-permute-start.7) | collective-permute-done | bytes 1048608 | tf_op jit(solution)/shard_map/ppermute | solution.py:244
  53.7 3.1 %collective-permute-start.1 = (f32[256,1024]{1,0:T(8,128)}, f32[256,1024]{1,0:T(8,128)S(1)}, u32[]{:S(2)}, u32[]{:S(2)}) collective-permute-start(f32[256,1024]{1,0:T(8,128)} %get-tuple-element.65), channel_id=1, source_target_pairs={{0,64},{64,0},{1,65},{65,1},{2,66},{66,2},{3,67},{67,3},{4,68},{68... | collective-permute-start | bytes 3145736 | tf_op jit(solution)/shard_map/ppermute | solution.py:252
  56.8 3.3 %bitcast_subtract_fusion.1 = f32[512,1024]{1,0:T(8,128)} fusion(f32[1,512,1024]{2,1,0:T(8,128)} %param.12, f32[1,512,1024]{2,1,0:T(8,128)S(1)} %copy-done), kind=kLoop, calls=%fused_computation.75 | loop fusion | flops 524288 | bytes 6291456 | tf_op jit(solution)/shard_map/sub | solution.py:279
  60.5 1.1 pad_maximum_fusion.3.refs_2_
  61.6 1.1 pad_maximum_fusion.2.refs_1_
  62.7 18.8 %collective-permute-done.1.refs_4_.refs_8_ = f32[256,1024]{1,0:T(8,128)S(1)} collective-permute-done((f32[256,1024]{1,0:T(8,128)}, f32[256,1024]{1,0:T(8,128)S(1)}, u32[]{:S(2)}, u32[]{:S(2)}) %collective-permute-start.1) | collective-permute-done | bytes 1048608 | tf_op jit(solution)/shard_map/ppermute | solution.py:252
  81.5 2.4 %copy-done.15 = f32[256,1024]{1,0:T(8,128)} copy-done((f32[256,1024]{1,0:T(8,128)}, f32[256,1024]{1,0:T(8,128)S(1)}, u32[]{:S(2)}) %copy-start.15) | copy-done | bytes 1048600
  83.8 1.2 copy-done.13
  85.1 16.5 %shard_map.107 = f32[16,2,16,2048]{3,2,1,0:T(8,128)} custom-call(s32[1]{0:T(128)} %bitcast.18.refs_0_, f32[256,1024]{1,0:T(8,128)} %pad_maximum_fusion.1.refs_1_, f32[256,1024]{1,0:T(8,128)} %get-tuple-element.64.refs_2_, f32[256,1024]{1,0:T(8,128)} %collective-permute-done.7.refs_3_, f32[256,1024]{1,0:T(8,128)} %copy-done.15, f32[512,2048]{1,0:T(8,128)} %bitcast.128, ...), custom_call_target="tpu_custom_call" | custom-call | flops 9663676416 | bytes 25165824 | tf_op jit(solution)/shard_map/pallas_call | solution.py:135
  101.8 3.3 %collective-permute-start.2 = (f32[512,1024]{1,0:T(8,128)S(1)}, f32[512,1024]{1,0:T(8,128)}, u32[]{:S(2)}, u32[]{:S(2)}) collective-permute-start(f32[512,1024]{1,0:T(8,128)S(1)} %copy-done.1), channel_id=1, source_target_pairs={{0,64},{64,0},{1,65},{65,1},{2,66},{66,2},{3,67},{67,3},{4,68},{68... | collective-permute-start | bytes 6291464 | tf_op jit(solution)/shard_map/ppermute | solution.py:280
  105.1 10.1 %collective-permute-done.8.refs_3_ = f32[256,1536]{1,0:T(8,128)} collective-permute-done((f32[256,1536]{1,0:T(8,128)}, f32[256,1536]{1,0:T(8,128)}, u32[]{:S(2)}, u32[]{:S(2)}) %collective-permute-start.8) | collective-permute-done | bytes 1572896 | tf_op jit(solution)/shard_map/ppermute | solution.py:278
  115.2 19.0 %shard_map.108 = (f32[16,16,2048]{2,1,0:T(8,128)}, f32[16,16,2048]{2,1,0:T(8,128)}) custom-call(s32[1]{0:T(128)} %bitcast.18.refs_0_, f32[256,1024]{1,0:T(8,128)} %pad_maximum_fusion.2.refs_1_, f32[256,1024]{1,0:T(8,128)} %pad_maximum_fusion.3.refs_2_, f32[256,1536]{1,0:T(8,128)} %collective-permute-done.8.refs_3_, f32[512,2048]{1,0:T(8,128)} %bitcast.129, ...), custom_call_target="tpu_custom_call" | custom-call | flops 77309411328 | bytes 197132288 | tf_op jit(solution)/shard_map/pallas_call | solution.py:135
  134.2 2.9 %dynamic-slice_bitcast_fusion.2 = (f32[4,16,2048]{2,1,0:T(8,128)S(1)}, f32[4,16,2048]{2,1,0:T(8,128)}, f32[4,16,2048]{2,1,0:T(8,128)}, f32[4,16,2048]{2,1,0:T(8,128)}) fusion(f32[4,4,16,2048]{3,2,1,0:T(8,128)} %bitcast.115, s32[]{:T(128)S(6)} %select_n.151, s32[]{:T(128)S(6)} %select_n.155, s32[]{:T(128)S(6)} %select_n.153, s32[]{:T(128)S(6)} %select_n.145), kind=kLoop, calls=%fused_computation.22 | loop fusion | bytes 4194320 | tf_op jit(solution)/shard_map/jit(dynamic_index_in_dim)/squeeze | solution.py:213
  137.2 3.2 %collective-permute-start.13 = (f32[4,16,2048]{2,1,0:T(8,128)}, f32[4,16,2048]{2,1,0:T(8,128)}, u32[]{:S(2)}, u32[]{:S(2)}) collective-permute-start(f32[4,16,2048]{2,1,0:T(8,128)} %get-tuple-element.63), channel_id=1, source_target_pairs={{0,32},{16,48},{32,0},{48,16},{1,33},{17,49},{33,1},{49,17},{2,34}... | collective-permute-start | bytes 1572872 | tf_op jit(solution)/shard_map/ppermute | solution.py:220
  140.3 1.2 dynamic-slice_bitcast_fusion.5
  141.6 3.5 %collective-permute-start.12 = (f32[4,16,2048]{2,1,0:T(8,128)}, f32[4,16,2048]{2,1,0:T(8,128)}, u32[]{:S(2)}, u32[]{:S(2)}) collective-permute-start(f32[4,16,2048]{2,1,0:T(8,128)} %get-tuple-element.59), channel_id=1, source_target_pairs={{0,4},{2,6},{4,0},{6,2},{1,5},{3,7},{5,1},{7,3},{8,12},{10,14},{12... | collective-permute-start | bytes 1572872 | tf_op jit(solution)/shard_map/ppermute | solution.py:220
  145.0 0.9 collective-permute-start.14
  146.6 12.2 %shard_map.106.c_ref = f32[512,2048]{1,0:T(8,128)} custom-call(f32[512,1024]{1,0:T(8,128)} %bitcast.106, f32[512,8192]{1,0:T(8,128)} %all-gather.2.cloned.1.call-done.w0_ref.w1_ref, f32[512,8192]{1,0:T(8,128)} %all-gather.2.cloned.1.call-done.w0_ref.w1_ref, f32[512,2048]{1,0:T(8,128)} %bitcast.110), custom_call_target="tpu_custom_call" | custom-call | flops 6442450944 | bytes 20971520 | tf_op jit(solution)/shard_map/pallas_call | solution.py:192
  158.9 1.6 collective-permute-done.12
  160.5 1.8 collective-permute-start.15
  162.3 13.5 %shard_map.109 = f32[512,2048]{1,0:T(8,128)} custom-call(f32[512,1024]{1,0:T(8,128)} %bitcast.105, f32[512,1024]{1,0:T(8,128)} %bitcast.107, f32[512,1024]{1,0:T(8,128)} %collective-permute-done.2.got_ref, f32[512,8192]{1,0:T(8,128)} %all-gather.2.cloned.1.call-done.w0_ref.w1_ref, f32[512,8192]{1,0:T(8,128)} %all-gather.2.cloned.1.call-done.w0_ref.w1_ref, ...), custom_call_target="tpu_custom_call" | custom-call | flops 6442450944 | bytes 20971520 | tf_op jit(solution)/shard_map/pallas_call | solution.py:192
  175.8 1.5 collective-permute-start.20
  177.3 1.3 add_add_fusion.1
  178.7 1.5 collective-permute-start.16
  180.2 11.4 %collective-permute-done.20 = f32[4,16,2048]{2,1,0:T(8,128)S(1)} collective-permute-done((f32[4,16,2048]{2,1,0:T(8,128)S(1)}, f32[4,16,2048]{2,1,0:T(8,128)S(1)}, u32[]{:S(2)}, u32[]{:S(2)}) %collective-permute-start.20) | collective-permute-done | bytes 524320 | tf_op jit(solution)/shard_map/ppermute | solution.py:220
  191.6 1.3 add_add_fusion
  193.0 3.6 %collective-permute-start.21 = (f32[16,2048]{1,0:T(8,128)S(1)}, f32[16,2048]{1,0:T(8,128)S(1)}, u32[]{:S(2)}, u32[]{:S(2)}) collective-permute-start(f32[16,2048]{1,0:T(8,128)S(1)} %get-tuple-element.80), channel_id=1, source_target_pairs={{0,4},{2,6},{4,0},{6,2},{1,5},{3,7},{5,1},{7,3},{8,12},{10,14},{12... | collective-permute-start | bytes 393224 | tf_op jit(solution)/shard_map/ppermute | solution.py:220
  196.5 3.7 %collective-permute-start.18 = (f32[16,2048]{1,0:T(8,128)S(1)}, f32[16,2048]{1,0:T(8,128)S(1)}, u32[]{:S(2)}, u32[]{:S(2)}) collective-permute-start(f32[16,2048]{1,0:T(8,128)S(1)} %get-tuple-element.48), channel_id=1, source_target_pairs={{0,48},{16,0},{32,16},{48,32},{1,49},{17,1},{33,17},{49,33},{2,50}... | collective-permute-start | bytes 393224 | tf_op jit(solution)/shard_map/ppermute | solution.py:220
  200.2 0.9 collective-permute-start.22
  201.5 3.4 %collective-permute-start.23 = (f32[16,2048]{1,0:T(8,128)S(1)}, f32[16,2048]{1,0:T(8,128)S(1)}, u32[]{:S(2)}, u32[]{:S(2)}) collective-permute-start(f32[16,2048]{1,0:T(8,128)S(1)} %get-tuple-element.51), channel_id=1, source_target_pairs={{0,6},{2,0},{4,2},{6,4},{1,7},{3,1},{5,3},{7,5},{8,14},{10,8},{12,... | collective-permute-start | bytes 393224 | tf_op jit(solution)/shard_map/ppermute | solution.py:220
  205.0 1.4 collective-permute-done.22
  206.4 1.1 collective-permute-done.23
  207.6 0.9 fusion.13
  208.5 3.0 %collective-permute-start.24 = (f32[16,2048]{1,0:T(8,128)S(1)}, f32[16,2048]{1,0:T(8,128)S(1)}, u32[]{:S(2)}, u32[]{:S(2)}) collective-permute-start(f32[16,2048]{1,0:T(8,128)S(1)} %get-tuple-element.72), channel_id=1, source_target_pairs={{0,64},{8,72},{64,0},{72,8},{1,65},{9,73},{65,1},{73,9},{2,66},{10... | collective-permute-start | bytes 393224 | tf_op jit(solution)/shard_map/ppermute | solution.py:311
  211.6 3.2 %collective-permute-start.26 = (f32[16,2048]{1,0:T(8,128)S(1)}, f32[16,2048]{1,0:T(8,128)S(1)}, u32[]{:S(2)}, u32[]{:S(2)}) collective-permute-start(f32[16,2048]{1,0:T(8,128)S(1)} %get-tuple-element.74), channel_id=1, source_target_pairs={{0,72},{8,0},{64,8},{72,64},{1,73},{9,1},{65,9},{73,65},{2,74},{10... | collective-permute-start | bytes 393224 | tf_op jit(solution)/shard_map/ppermute | solution.py:311
  215.1 2.7 %collective-permute-done.25 = f32[16,2048]{1,0:T(8,128)S(1)} collective-permute-done((f32[16,2048]{1,0:T(8,128)S(1)}, f32[16,2048]{1,0:T(8,128)S(1)}, u32[]{:S(2)}, u32[]{:S(2)}) %collective-permute-start.25) | collective-permute-done | bytes 131104 | tf_op jit(solution)/shard_map/ppermute | solution.py:311
  217.8 1.5 fusion.10
  (83 shorter events, 9.6 us)
Async XLA Ops:
  8.0 138.6 %all-gather.2.cloned.1.call-start = ((), (), s32[]{:S(2)}) async-start(), calls=%async_computation.1 | async-start | bytes 17301504 | tf_op jit(solution)/shard_map/all_gather | solution.py:276
  9.0 25.0 %collective-permute-start.3 = (f32[16,2048]{1,0:T(8,128)S(1)}, f32[16,2048]{1,0:T(8,128)S(1)}, u32[]{:S(2)}, u32[]{:S(2)}) collective-permute-start(f32[16,2048]{1,0:T(8,128)S(1)} %bitcast_subtract_fusion), channel_id=1, source_target_pairs={{0,64},{64,0},{1,65},{65,1},{2,66},{66,2},{3,67},{67,3},{4,68},{68... | collective-permute-start | bytes 393224 | tf_op jit(solution)/shard_map/ppermute | solution.py:265
  12.2 21.8 %collective-permute-start.5 = (f32[16,2048]{1,0:T(8,128)S(1)}, f32[16,2048]{1,0:T(8,128)}, u32[]{:S(2)}, u32[]{:S(2)}) collective-permute-start(f32[16,2048]{1,0:T(8,128)S(1)} %bitcast_subtract_fusion), channel_id=1, source_target_pairs={{0,72},{72,0},{8,64},{64,8},{1,73},{73,1},{9,65},{65,9},{2,74},{74... | collective-permute-start | bytes 393224 | tf_op jit(solution)/shard_map/ppermute | solution.py:267
  13.4 6.4 %copy-start.7 = (f32[1,16,2048]{2,1,0:T(8,128)S(1)}, f32[1,16,2048]{2,1,0:T(8,128)}, u32[]{:S(2)}) copy-start(f32[1,16,2048]{2,1,0:T(8,128)} %param.13) | copy-start | bytes 393220
  16.3 4.2 %copy-start.3 = (f32[4,4,2,8,512]{4,3,2,1,0:T(8,128)S(1)}, f32[4,4,2,8,512]{4,3,2,1,0:T(8,128)}, u32[]{:S(2)}) copy-start(f32[4,4,2,8,512]{4,3,2,1,0:T(8,128)} %get-tuple-element.32) | copy-start | bytes 1572868
  16.3 7.1 %collective-permute-start.6 = (f32[2,256,512]{2,1,0:T(8,128)}, f32[2,256,512]{2,1,0:T(8,128)}, u32[]{:S(2)}, u32[]{:S(2)}) collective-permute-start(f32[2,256,512]{2,1,0:T(8,128)} %bitcast.134), channel_id=1, source_target_pairs={{0,1},{1,0},{2,3},{3,2},{4,5},{5,4},{6,7},{7,6},{8,9},{9,8},{10,11... | collective-permute-start | bytes 3145736 | tf_op jit(solution)/shard_map/ppermute | solution.py:241
  19.3 3.4 %copy-start.5 = (f32[4,4,2,8,512]{4,3,2,1,0:T(8,128)S(1)}, f32[4,4,2,8,512]{4,3,2,1,0:T(8,128)}, u32[]{:S(2)}) copy-start(f32[4,4,2,8,512]{4,3,2,1,0:T(8,128)} %get-tuple-element.33) | copy-start | bytes 1572868
  19.3 11.0 %collective-permute-start = (f32[2,256,512]{2,1,0:T(8,128)}, f32[2,256,512]{2,1,0:T(8,128)S(1)}, u32[]{:S(2)}, u32[]{:S(2)}) collective-permute-start(f32[2,256,512]{2,1,0:T(8,128)} %bitcast.133), channel_id=1, source_target_pairs={{0,1},{1,0},{2,3},{3,2},{4,5},{5,4},{6,7},{7,6},{8,9},{9,8},{10,11... | collective-permute-start | bytes 3145736 | tf_op jit(solution)/shard_map/ppermute | solution.py:246
  20.4 13.6 %collective-permute-start.4 = (f32[16,4096]{1,0:T(8,128)}, f32[16,4096]{1,0:T(8,128)}, u32[]{:S(2)}, u32[]{:S(2)}) collective-permute-start(f32[16,4096]{1,0:T(8,128)} %pad_maximum_fusion.5), channel_id=1, source_target_pairs={{0,8},{8,0},{1,9},{9,1},{2,10},{10,2},{3,11},{11,3},{4,12},{12,4},... | collective-permute-start | bytes 786440 | tf_op jit(solution)/shard_map/ppermute | solution.py:266
  23.4 1.4 copy-start.9
  25.9 27.2 %collective-permute-start.7 = (f32[256,1024]{1,0:T(8,128)}, f32[256,1024]{1,0:T(8,128)}, u32[]{:S(2)}, u32[]{:S(2)}) collective-permute-start(f32[256,1024]{1,0:T(8,128)} %pad_maximum_fusion.1.refs_1_), channel_id=1, source_target_pairs={{0,64},{64,0},{1,65},{65,1},{2,66},{66,2},{3,67},{67,3},{4,68},{68... | collective-permute-start | bytes 3145736 | tf_op jit(solution)/shard_map/ppermute | solution.py:244
  29.4 3.1 %copy-start.8 = (f32[4,4,2,8,512]{4,3,2,1,0:T(8,128)S(1)}, f32[4,4,2,8,512]{4,3,2,1,0:T(8,128)}, u32[]{:S(2)}) copy-start(f32[4,4,2,8,512]{4,3,2,1,0:T(8,128)} %get-tuple-element.29) | copy-start | bytes 1572868
  34.0 22.8 %copy-start = (f32[1,512,1024]{2,1,0:T(8,128)S(1)}, f32[1,512,1024]{2,1,0:T(8,128)}, u32[]{:S(2)}) copy-start(f32[1,512,1024]{2,1,0:T(8,128)} %param.9) | copy-start | bytes 6291460
  53.1 154.5 %reduce-scatter.4.cloned.1.call-start = ((), (), s32[]{:S(2)}) async-start(), calls=%async_computation.2 | async-start | bytes 4456448
  53.1 28.3 %collective-permute-start.10 = (f32[512,2048]{1,0:T(8,128)}, f32[512,2048]{1,0:T(8,128)S(1)}, u32[]{:S(2)}, u32[]{:S(2)}) collective-permute-start(f32[512,2048]{1,0:T(8,128)} %bitcast.130), channel_id=1, source_target_pairs={{0,1},{1,0},{2,3},{3,2},{4,5},{5,4},{6,7},{7,6},{8,9},{9,8},{10,11... | collective-permute-start | bytes 12582920 | tf_op jit(solution)/shard_map/ppermute | solution.py:283
  53.2 7.3 %copy-start.6 = (f32[4,4,2,8,512]{4,3,2,1,0:T(8,128)S(1)}, f32[4,4,2,8,512]{4,3,2,1,0:T(8,128)}, u32[]{:S(2)}) copy-start(f32[4,4,2,8,512]{4,3,2,1,0:T(8,128)} %get-tuple-element.33) | copy-start | bytes 1572868
  53.2 28.2 %collective-permute-start.9 = (f32[512,2048]{1,0:T(8,128)}, f32[512,2048]{1,0:T(8,128)S(1)}, u32[]{:S(2)}, u32[]{:S(2)}) collective-permute-start(f32[512,2048]{1,0:T(8,128)} %bitcast.127), channel_id=1, source_target_pairs={{0,1},{1,0},{2,3},{3,2},{4,5},{5,4},{6,7},{7,6},{8,9},{9,8},{10,11... | collective-permute-start | bytes 12582920 | tf_op jit(solution)/shard_map/ppermute | solution.py:282
  53.7 27.7 %collective-permute-start.1 = (f32[256,1024]{1,0:T(8,128)}, f32[256,1024]{1,0:T(8,128)S(1)}, u32[]{:S(2)}, u32[]{:S(2)}) collective-permute-start(f32[256,1024]{1,0:T(8,128)} %get-tuple-element.65), channel_id=1, source_target_pairs={{0,64},{64,0},{1,65},{65,1},{2,66},{66,2},{3,67},{67,3},{4,68},{68... | collective-permute-start | bytes 3145736 | tf_op jit(solution)/shard_map/ppermute | solution.py:252
  60.1 1.5 copy-start.4
  60.1 55.2 %collective-permute-start.8 = (f32[256,1536]{1,0:T(8,128)}, f32[256,1536]{1,0:T(8,128)}, u32[]{:S(2)}, u32[]{:S(2)}) collective-permute-start(f32[256,1536]{1,0:T(8,128)} %slice_dynamic-update-slice_fusion.2), channel_id=1, source_target_pairs={{0,64},{64,0},{1,65},{65,1},{2,66},{66,2},{3,67},{67,3},{4,68},{68... | collective-permute-start | bytes 4718600 | tf_op jit(solution)/shard_map/ppermute | solution.py:278
  81.4 2.4 %copy-start.15 = (f32[256,1024]{1,0:T(8,128)}, f32[256,1024]{1,0:T(8,128)S(1)}, u32[]{:S(2)}) copy-start(f32[256,1024]{1,0:T(8,128)S(1)} %collective-permute-done.1.refs_4_.refs_8_) | copy-start | bytes 3145732
  81.4 3.6 %copy-start.13 = (f32[512,2048]{1,0:T(8,128)}, f32[512,2048]{1,0:T(8,128)S(1)}, u32[]{:S(2)}) copy-start(f32[512,2048]{1,0:T(8,128)S(1)} %collective-permute-done.10.refs_8_.refs_7_) | copy-start | bytes 12582916
  81.4 2.4 %copy-start.14 = (f32[512,2048]{1,0:T(8,128)}, f32[512,2048]{1,0:T(8,128)S(1)}, u32[]{:S(2)}) copy-start(f32[512,2048]{1,0:T(8,128)S(1)} %collective-permute-done.9.refs_7_.refs_6_) | copy-start | bytes 12582916
  85.1 16.5 %copy-start.16 = (f32[256,1024]{1,0:T(8,128)S(1)}, f32[256,1024]{1,0:T(8,128)}, u32[]{:S(2)}) copy-start(f32[256,1024]{1,0:T(8,128)} %copy-done.15) | copy-start | bytes 3145732
  85.1 16.7 %copy-start.1 = (f32[512,1024]{1,0:T(8,128)S(1)}, f32[512,1024]{1,0:T(8,128)}, u32[]{:S(2)}) copy-start(f32[512,1024]{1,0:T(8,128)} %bitcast_subtract_fusion.1) | copy-start | bytes 6291460
  101.6 13.7 %collective-permute-start.11 = (f32[256,1024]{1,0:T(8,128)S(1)}, f32[256,1024]{1,0:T(8,128)}, u32[]{:S(2)}, u32[]{:S(2)}) collective-permute-start(f32[256,1024]{1,0:T(8,128)S(1)} %copy-done.16), channel_id=1, source_target_pairs={{0,1},{1,0},{2,3},{3,2},{4,5},{5,4},{6,7},{7,6},{8,9},{9,8},{10,11... | collective-permute-start | bytes 3145736 | tf_op jit(solution)/shard_map/ppermute | solution.py:286
  101.8 60.5 %collective-permute-start.2 = (f32[512,1024]{1,0:T(8,128)S(1)}, f32[512,1024]{1,0:T(8,128)}, u32[]{:S(2)}, u32[]{:S(2)}) collective-permute-start(f32[512,1024]{1,0:T(8,128)S(1)} %copy-done.1), channel_id=1, source_target_pairs={{0,64},{64,0},{1,65},{65,1},{2,66},{66,2},{3,67},{67,3},{4,68},{68... | collective-permute-start | bytes 6291464 | tf_op jit(solution)/shard_map/ppermute | solution.py:280
  134.2 6.1 %copy-start.2 = (f32[16,16,2048]{2,1,0:T(8,128)S(1)}, f32[16,16,2048]{2,1,0:T(8,128)}, u32[]{:S(2)}) copy-start(f32[16,16,2048]{2,1,0:T(8,128)} %get-tuple-element.43) | copy-start | bytes 6291460
  137.2 21.7 %collective-permute-start.13 = (f32[4,16,2048]{2,1,0:T(8,128)}, f32[4,16,2048]{2,1,0:T(8,128)}, u32[]{:S(2)}, u32[]{:S(2)}) collective-permute-start(f32[4,16,2048]{2,1,0:T(8,128)} %get-tuple-element.63), channel_id=1, source_target_pairs={{0,32},{16,48},{32,0},{48,16},{1,33},{17,49},{33,1},{49,17},{2,34}... | collective-permute-start | bytes 1572872 | tf_op jit(solution)/shard_map/ppermute | solution.py:220
  141.6 18.9 %collective-permute-start.12 = (f32[4,16,2048]{2,1,0:T(8,128)}, f32[4,16,2048]{2,1,0:T(8,128)}, u32[]{:S(2)}, u32[]{:S(2)}) collective-permute-start(f32[4,16,2048]{2,1,0:T(8,128)} %get-tuple-element.59), channel_id=1, source_target_pairs={{0,4},{2,6},{4,0},{6,2},{1,5},{3,7},{5,1},{7,3},{8,12},{10,14},{12... | collective-permute-start | bytes 1572872 | tf_op jit(solution)/shard_map/ppermute | solution.py:220
  145.0 32.3 %collective-permute-start.14 = (f32[4,16,2048]{2,1,0:T(8,128)}, f32[4,16,2048]{2,1,0:T(8,128)}, u32[]{:S(2)}, u32[]{:S(2)}) collective-permute-start(f32[4,16,2048]{2,1,0:T(8,128)} %get-tuple-element.58), channel_id=1, source_target_pairs={{0,2},{2,4},{4,6},{6,0},{1,3},{3,5},{5,7},{7,1},{8,10},{10,12},{12... | collective-permute-start | bytes 1572872 | tf_op jit(solution)/shard_map/ppermute | solution.py:220
  146.0 34.3 %collective-permute-start.19 = (f32[4,16,2048]{2,1,0:T(8,128)}, f32[4,16,2048]{2,1,0:T(8,128)}, u32[]{:S(2)}, u32[]{:S(2)}) collective-permute-start(f32[4,16,2048]{2,1,0:T(8,128)} %get-tuple-element.62), channel_id=1, source_target_pairs={{0,16},{16,32},{32,48},{48,0},{1,17},{17,33},{33,49},{49,1},{2,18}... | collective-permute-start | bytes 1572872 | tf_op jit(solution)/shard_map/ppermute | solution.py:220
  146.6 13.9 %copy-start.11 = (f32[4,16,2048]{2,1,0:T(8,128)S(1)}, f32[4,16,2048]{2,1,0:T(8,128)}, u32[]{:S(2)}) copy-start(f32[4,16,2048]{2,1,0:T(8,128)} %get-tuple-element.47) | copy-start | bytes 1572868
  160.5 15.3 %copy-start.10 = (f32[4,16,2048]{2,1,0:T(8,128)S(1)}, f32[4,16,2048]{2,1,0:T(8,128)}, u32[]{:S(2)}) copy-start(f32[4,16,2048]{2,1,0:T(8,128)} %get-tuple-element.50) | copy-start | bytes 1572868
  160.5 16.8 %collective-permute-start.15 = (f32[4,16,2048]{2,1,0:T(8,128)S(1)}, f32[4,16,2048]{2,1,0:T(8,128)S(1)}, u32[]{:S(2)}, u32[]{:S(2)}) collective-permute-start(f32[4,16,2048]{2,1,0:T(8,128)S(1)} %copy-done.11), channel_id=1, source_target_pairs={{0,6},{2,0},{4,2},{6,4},{1,7},{3,1},{5,3},{7,5},{8,14},{10,8},{12,... | collective-permute-start | bytes 1572872 | tf_op jit(solution)/shard_map/ppermute | solution.py:220
  175.8 15.8 %collective-permute-start.20 = (f32[4,16,2048]{2,1,0:T(8,128)S(1)}, f32[4,16,2048]{2,1,0:T(8,128)S(1)}, u32[]{:S(2)}, u32[]{:S(2)}) collective-permute-start(f32[4,16,2048]{2,1,0:T(8,128)S(1)} %copy-done.10), channel_id=1, source_target_pairs={{0,48},{16,0},{32,16},{48,32},{1,49},{17,1},{33,17},{49,33},{2,50}... | collective-permute-start | bytes 1572872 | tf_op jit(solution)/shard_map/ppermute | solution.py:220
  178.7 28.9 %copy-start.12 = (f32[1,16,2048]{2,1,0:T(8,128)S(1)}, f32[1,16,2048]{2,1,0:T(8,128)}, u32[]{:S(2)}) copy-start(f32[1,16,2048]{2,1,0:T(8,128)} %param.17) | copy-start | bytes 393220
  178.7 17.9 %collective-permute-start.16 = (f32[16,2048]{1,0:T(8,128)S(1)}, f32[16,2048]{1,0:T(8,128)S(1)}, u32[]{:S(2)}, u32[]{:S(2)}) collective-permute-start(f32[16,2048]{1,0:T(8,128)S(1)} %get-tuple-element.77), channel_id=1, source_target_pairs={{0,32},{16,48},{32,0},{48,16},{1,33},{17,49},{33,1},{49,17},{2,34}... | collective-permute-start | bytes 393224 | tf_op jit(solution)/shard_map/ppermute | solution.py:220
  193.0 8.5 %collective-permute-start.21 = (f32[16,2048]{1,0:T(8,128)S(1)}, f32[16,2048]{1,0:T(8,128)S(1)}, u32[]{:S(2)}, u32[]{:S(2)}) collective-permute-start(f32[16,2048]{1,0:T(8,128)S(1)} %get-tuple-element.80), channel_id=1, source_target_pairs={{0,4},{2,6},{4,0},{6,2},{1,5},{3,7},{5,1},{7,3},{8,12},{10,14},{12... | collective-permute-start | bytes 393224 | tf_op jit(solution)/shard_map/ppermute | solution.py:220
  196.5 8.4 %collective-permute-start.17 = (f32[16,2048]{1,0:T(8,128)S(1)}, f32[16,2048]{1,0:T(8,128)S(1)}, u32[]{:S(2)}, u32[]{:S(2)}) collective-permute-start(f32[16,2048]{1,0:T(8,128)S(1)} %get-tuple-element.75), channel_id=1, source_target_pairs={{0,16},{16,32},{32,48},{48,0},{1,17},{17,33},{33,49},{49,1},{2,18}... | collective-permute-start | bytes 393224 | tf_op jit(solution)/shard_map/ppermute | solution.py:220
  196.5 8.4 %collective-permute-start.18 = (f32[16,2048]{1,0:T(8,128)S(1)}, f32[16,2048]{1,0:T(8,128)S(1)}, u32[]{:S(2)}, u32[]{:S(2)}) collective-permute-start(f32[16,2048]{1,0:T(8,128)S(1)} %get-tuple-element.48), channel_id=1, source_target_pairs={{0,48},{16,0},{32,16},{48,32},{1,49},{17,1},{33,17},{49,33},{2,50}... | collective-permute-start | bytes 393224 | tf_op jit(solution)/shard_map/ppermute | solution.py:220
  200.2 6.2 %collective-permute-start.22 = (f32[16,2048]{1,0:T(8,128)S(1)}, f32[16,2048]{1,0:T(8,128)S(1)}, u32[]{:S(2)}, u32[]{:S(2)}) collective-permute-start(f32[16,2048]{1,0:T(8,128)S(1)} %get-tuple-element.78), channel_id=1, source_target_pairs={{0,2},{2,4},{4,6},{6,0},{1,3},{3,5},{5,7},{7,1},{8,10},{10,12},{12... | collective-permute-start | bytes 393224 | tf_op jit(solution)/shard_map/ppermute | solution.py:220
  201.5 6.0 %collective-permute-start.23 = (f32[16,2048]{1,0:T(8,128)S(1)}, f32[16,2048]{1,0:T(8,128)S(1)}, u32[]{:S(2)}, u32[]{:S(2)}) collective-permute-start(f32[16,2048]{1,0:T(8,128)S(1)} %get-tuple-element.51), channel_id=1, source_target_pairs={{0,6},{2,0},{4,2},{6,4},{1,7},{3,1},{5,3},{7,5},{8,14},{10,8},{12,... | collective-permute-start | bytes 393224 | tf_op jit(solution)/shard_map/ppermute | solution.py:220
  208.5 6.6 %collective-permute-start.24 = (f32[16,2048]{1,0:T(8,128)S(1)}, f32[16,2048]{1,0:T(8,128)S(1)}, u32[]{:S(2)}, u32[]{:S(2)}) collective-permute-start(f32[16,2048]{1,0:T(8,128)S(1)} %get-tuple-element.72), channel_id=1, source_target_pairs={{0,64},{8,72},{64,0},{72,8},{1,65},{9,73},{65,1},{73,9},{2,66},{10... | collective-permute-start | bytes 393224 | tf_op jit(solution)/shard_map/ppermute | solution.py:311
  211.6 6.2 %collective-permute-start.25 = (f32[16,2048]{1,0:T(8,128)S(1)}, f32[16,2048]{1,0:T(8,128)S(1)}, u32[]{:S(2)}, u32[]{:S(2)}) collective-permute-start(f32[16,2048]{1,0:T(8,128)S(1)} %get-tuple-element.73), channel_id=1, source_target_pairs={{0,8},{8,64},{64,72},{72,0},{1,9},{9,65},{65,73},{73,1},{2,10},{10... | collective-permute-start | bytes 393224 | tf_op jit(solution)/shard_map/ppermute | solution.py:311
  211.6 6.2 %collective-permute-start.26 = (f32[16,2048]{1,0:T(8,128)S(1)}, f32[16,2048]{1,0:T(8,128)S(1)}, u32[]{:S(2)}, u32[]{:S(2)}) collective-permute-start(f32[16,2048]{1,0:T(8,128)S(1)} %get-tuple-element.74), channel_id=1, source_target_pairs={{0,72},{8,0},{64,8},{72,64},{1,73},{9,1},{65,9},{73,65},{2,74},{10... | collective-permute-start | bytes 393224 | tf_op jit(solution)/shard_map/ppermute | solution.py:311
Sparse Core Ops, SparseCore 0:
  53.2 75.8 all-gather.1
Sparse Core Ops, SparseCore 1:
  105.2 98.1 reduce-scatter.3

commit v9 on v8

--- a/solution.py
+++ b/solution.py
@@ -221,7 +221,8 @@
     made = None
     if beside:
         made = beside(got[0][0], got[1][0])
-        sums = [after(s, made) for s in sums]
+        ready = lax.optimization_barrier((*sums, *got[0], *got[1], made))
+        sums, got = ready[:2], (ready[2:5], ready[5:8])
     return [s + r[0] + r[1] + r[2] for s, r in zip(sums, got)], made
 
 
@@ -238,10 +239,12 @@
     ff = w.shape[1]
 
     x_mine0, x_mine1, x_theirs = turned(core_id, x)
+    x0_mine = lax.ppermute(x_mine0, "party", SWAP)
     x_other = lax.ppermute(x_theirs, "core", SWAP)
     xs0 = jnp.concatenate([x_mine0, x_other[0]], axis=1)
     xs1 = jnp.concatenate([x_mine1, x_other[1]], axis=1)
-    x0 = lax.ppermute(xs0, "party", SWAP)
+    x0_other = lax.ppermute(x_other[0], "party", SWAP)
+    x0 = jnp.concatenate([x0_mine, x0_other], axis=1)
     a_mine0, a_mine1, a_theirs = turned(core_id, after(ba, x_theirs))
     a_other = lax.ppermute(a_theirs, "core", SWAP)
     aa0 = jnp.concatenate([a_mine0, a_other[0]], axis=1)
@@ -273,7 +276,7 @@
     weights = jnp.concatenate(
         [jnp.where(xl0, packed, packed_near), jnp.where(xl0, packed_near, packed)], axis=1
     )
-    weights = lax.all_gather(after(weights, x0), ("y", "z", "core"), axis=0, tiled=True)
+    weights = lax.all_gather(after(weights, x0_mine), ("y", "z", "core"), axis=0, tiled=True)
 
     got1 = lax.ppermute(sent1, "party", SWAP)
     u_local = x - fa

time: 228 us -> 217 us (0.952)
  waiting for transfers between devices: 64.7 us -> 55.4 us
  starting transfers between devices: 46.9 us -> 40.7 us
  other arithmetic: 18.4 us -> 21.4 us
    ppermute x1, waiting for transfers between devices: 18.8 us -> 0.01 us  [body(): got0 = lax.ppermute(sent0, 'party', SWAP)]
    ppermute x1 -> x2, waiting for transfers between devices: 16.9 us -> 27 us  [the longest x1 27 us: body(): x0_other = lax.ppermute(x_other[0], 'party', SWAP)]
    ppermute x12, waiting for transfers between devices: 15.9 us -> 7.18 us  [scattered_pair(): lax.ppermute(piece, axis, [(i, (i + step) % 4) for i in range(4)])]
    ppermute x1, waiting for transfers between devices: 0.01 us -> 5.83 us  [body(): near = lax.ppermute(jnp.concatenate([fb, d], axis=1), 'xl', SWAP)]
    ppermute x12, starting transfers between devices: 24.7 us -> 20.3 us  [scattered_pair(): lax.ppermute(piece, axis, [(i, (i + step) % 4) for i in range(4)])]
    squeeze x2 -> x0, local copies, waits for them, and re-layouts: 4.15 us -> none  [scattered_pair(): sums.append(lax.dynamic_index_in_dim(v, here, dim, keepdims=False))]
    squeeze x2 -> x4, local copies, waits for them, and re-layouts: 0.07 us -> 4.19 us  [scattered_pair(): piece = lax.dynamic_index_in_dim(v, (here + step) % 4, dim, keepdims=False)]
    unnamed x3, waiting for transfers between devices: 0.06 us -> 2.61 us
  transfers between devices with their start and end apart: 29 -> 30, of which waited for: 10 -> 10; matrix products, arithmetic and copies ran while one was open for 11% -> 14% of each run, Pallas kernels for 30% -> 31%
where the time goes in v9:
time: 217 us; the launch traced here: 216 us
  Pallas kernels  66.7 us (31%)
  waiting for transfers between devices  55.4 us (26%)
  starting transfers between devices  40.7 us (19%)
  other arithmetic  21.4 us (10%)
  between operations  15.8 us (7%)
  local copies, waits for them, and re-layouts  15.7 us (7%)
    pallas_call x2, Pallas kernels, grad_parts(): pl.pallas_call(lambda *refs: grad_kernel(bool(sent), *refs), grid=(ff //...  35.1 us
    ppermute x1, waiting for transfers between devices, body(): x0_other = lax.ppermute(x_other[0], 'party', SWAP)  27 us
    pallas_call x2, Pallas kernels, forward_call(): pl.pallas_call(kernel, grid=(steps,), in_specs=[pl.BlockSpec((rows, d), l...  25.7 us
    ppermute x12, starting transfers between devices, scattered_pair(): lax.ppermute(piece, axis, [(i, (i + step) % 4) for i in range(4)])  20.3 us
    ppermute x1, waiting for transfers between devices, body(): got1 = lax.ppermute(sent1, 'party', SWAP)  9.71 us
    ppermute x12, waiting for transfers between devices, scattered_pair(): lax.ppermute(piece, axis, [(i, (i + step) % 4) for i in range(4)])  7.18 us
    unnamed x37, local copies, waits for them, and re-layouts  6.08 us
    pallas_call x2, Pallas kernels, turned(): pl.pallas_call(turn_kernel, grid=(2,), in_specs=[SMEM, pl.BlockSpec((toke...  5.9 us
  transfers between devices with their start and end apart: 30, of which 10 were waited for; matrix products, arithmetic and copies ran while one was open for 14% of the time, Pallas kernels for 31%

profile of v9, /device:TPU:0, one launch (start us, length us, event | category | flops | bytes accessed | tf_op | source)
XLA Modules:
  0.0 215.7 jit_solution(9732115832860835705)
XLA Ops:
  9.0 3.2 %collective-permute-start.3 = (f32[16,2048]{1,0:T(8,128)S(1)}, f32[16,2048]{1,0:T(8,128)S(1)}, u32[]{:S(2)}, u32[]{:S(2)}) collective-permute-start(f32[16,2048]{1,0:T(8,128)S(1)} %bitcast_subtract_fusion), channel_id=1, source_target_pairs={{0,64},{64,0},{1,65},{65,1},{2,66},{66,2},{3,67},{67,3},{4,68},{68... | collective-permute-start | bytes 393224 | tf_op jit(solution)/shard_map/ppermute | solution.py:268
  12.2 1.1 collective-permute-start.5
  13.4 2.9 %shard_map.104 = (f32[4,4,2,8,512]{4,3,2,1,0:T(8,128)}, f32[4,4,2,8,512]{4,3,2,1,0:T(8,128)}, f32[2,4,4,2,8,512]{5,4,3,2,1,0:T(8,128)}) custom-call(s32[1]{0:T(128)} %bitcast.3.core_ref, f32[512,1024]{1,0:T(8,128)} %bitcast.104), custom_call_target="tpu_custom_call" | custom-call | bytes 4194304 | tf_op jit(solution)/shard_map/pallas_call | solution.py:60
  16.3 3.0 %shard_map.105 = (f32[4,4,2,8,512]{4,3,2,1,0:T(8,128)}, f32[4,4,2,8,512]{4,3,2,1,0:T(8,128)}, f32[2,4,4,2,8,512]{5,4,3,2,1,0:T(8,128)}) custom-call(s32[1]{0:T(128)} %bitcast.3.core_ref, f32[512,1024]{1,0:T(8,128)} %bitcast.113), custom_call_target="tpu_custom_call" | custom-call | bytes 4194304 | tf_op jit(solution)/shard_map/pallas_call | solution.py:60
  19.8 1.5 collective-permute-start.7
  21.3 1.3 slice_bitcast_fusion
  23.5 1.6 fusion.17
  25.2 1.5 collective-permute-start.4
  26.7 2.1 slice_bitcast_fusion.1
  29.6 1.3 slice_bitcast_fusion.2
  33.0 1.5 pad_maximum_fusion
  34.5 5.8 %collective-permute-done.4 = f32[16,4096]{1,0:T(8,128)S(1)} collective-permute-done((f32[16,4096]{1,0:T(8,128)S(1)}, f32[16,4096]{1,0:T(8,128)S(1)}, u32[]{:S(2)}, u32[]{:S(2)}) %collective-permute-start.4) | collective-permute-done | bytes 262176 | tf_op jit(solution)/shard_map/ppermute | solution.py:269
  43.8 2.6 %collective-permute-start.11 = (f32[256,512]{1,0:T(8,128)}, f32[256,512]{1,0:T(8,128)S(1)}, u32[]{:S(2)}, u32[]{:S(2)}) collective-permute-start(f32[256,512]{1,0:T(8,128)} %get-tuple-element.78), channel_id=1, source_target_pairs={{0,64},{64,0},{1,65},{65,1},{2,66},{66,2},{3,67},{67,3},{4,68},{68... | collective-permute-start | bytes 1572872 | tf_op jit(solution)/shard_map/ppermute | solution.py:246
  46.4 3.3 %bitcast_subtract_fusion.1 = f32[512,1024]{1,0:T(8,128)} fusion(f32[1,512,1024]{2,1,0:T(8,128)} %param.12, f32[1,512,1024]{2,1,0:T(8,128)S(1)} %copy-done), kind=kLoop, calls=%fused_computation.76 | loop fusion | flops 524288 | bytes 6291456 | tf_op jit(solution)/shard_map/sub | solution.py:282
  50.6 1.1 pad_maximum_fusion.2.refs_2_
  51.7 1.1 pad_maximum_fusion.1.refs_1_
  52.7 2.1 pad_maximum_fusion.3.refs_1_
  54.9 27.0 %collective-permute-done.11 = f32[256,512]{1,0:T(8,128)S(1)} collective-permute-done((f32[256,512]{1,0:T(8,128)}, f32[256,512]{1,0:T(8,128)S(1)}, u32[]{:S(2)}, u32[]{:S(2)}) %collective-permute-start.11) | collective-permute-done | bytes 524320 | tf_op jit(solution)/shard_map/ppermute | solution.py:246
  81.8 2.1 pad_maximum_fusion.4.refs_3_
  84.0 2.4 %copy-done.15 = f32[256,1024]{1,0:T(8,128)} copy-done((f32[256,1024]{1,0:T(8,128)}, f32[256,1024]{1,0:T(8,128)S(1)}, u32[]{:S(2)}) %copy-start.15) | copy-done | bytes 1048600
  86.3 1.2 copy-done.13
  87.6 16.6 %shard_map.107 = f32[16,2,16,2048]{3,2,1,0:T(8,128)} custom-call(s32[1]{0:T(128)} %bitcast.17.refs_0_, f32[256,1024]{1,0:T(8,128)} %pad_maximum_fusion.3.refs_1_, f32[256,1024]{1,0:T(8,128)} %get-tuple-element.76.refs_2_, f32[256,1024]{1,0:T(8,128)} %pad_maximum_fusion.4.refs_3_, f32[256,1024]{1,0:T(8,128)} %copy-done.15, f32[512,2048]{1,0:T(8,128)} %bitcast.127, ...), custom_call_target="tpu_custom_call" | custom-call | flops 9663676416 | bytes 25165824 | tf_op jit(solution)/shard_map/pallas_call | solution.py:135
  104.4 1.5 collective-permute-start.2
  105.9 9.7 %collective-permute-done.8.refs_3_ = f32[256,1536]{1,0:T(8,128)} collective-permute-done((f32[256,1536]{1,0:T(8,128)}, f32[256,1536]{1,0:T(8,128)}, u32[]{:S(2)}, u32[]{:S(2)}) %collective-permute-start.8) | collective-permute-done | bytes 1572896 | tf_op jit(solution)/shard_map/ppermute | solution.py:281
  115.6 18.5 %shard_map.108 = (f32[16,16,2048]{2,1,0:T(8,128)}, f32[16,16,2048]{2,1,0:T(8,128)}) custom-call(s32[1]{0:T(128)} %bitcast.17.refs_0_, f32[256,1024]{1,0:T(8,128)} %pad_maximum_fusion.1.refs_1_, f32[256,1024]{1,0:T(8,128)} %pad_maximum_fusion.2.refs_2_, f32[256,1536]{1,0:T(8,128)} %collective-permute-done.8.refs_3_, f32[512,2048]{1,0:T(8,128)} %bitcast.128, ...), custom_call_target="tpu_custom_call" | custom-call | flops 77309411328 | bytes 197132288 | tf_op jit(solution)/shard_map/pallas_call | solution.py:135
  134.1 2.9 %dynamic-slice_bitcast_fusion = (f32[4,16,2048]{2,1,0:T(8,128)}, f32[4,16,2048]{2,1,0:T(8,128)}, f32[4,16,2048]{2,1,0:T(8,128)S(1)}, f32[4,16,2048]{2,1,0:T(8,128)}) fusion(f32[4,4,16,2048]{3,2,1,0:T(8,128)} %bitcast.115, s32[]{:T(128)S(6)} %select_n.155, s32[]{:T(128)S(6)} %select_n.153, s32[]{:T(128)S(6)} %select_n.147, s32[]{:T(128)S(6)} %select_n.145), kind=kLoop, calls=%fused_computation.22 | loop fusion | bytes 4194320 | tf_op jit(solution)/shard_map/jit(dynamic_index_in_dim)/squeeze | solution.py:217
  137.0 3.2 %collective-permute-start.14 = (f32[4,16,2048]{2,1,0:T(8,128)}, f32[4,16,2048]{2,1,0:T(8,128)}, u32[]{:S(2)}, u32[]{:S(2)}) collective-permute-start(f32[4,16,2048]{2,1,0:T(8,128)} %get-tuple-element.71), channel_id=1, source_target_pairs={{0,32},{16,48},{32,0},{48,16},{1,33},{17,49},{33,1},{49,17},{2,34}... | collective-permute-start | bytes 1572872 | tf_op jit(solution)/shard_map/ppermute | solution.py:220
  140.2 1.2 dynamic-slice_bitcast_fusion.2
  141.4 3.9 %collective-permute-start.13 = (f32[4,16,2048]{2,1,0:T(8,128)}, f32[4,16,2048]{2,1,0:T(8,128)}, u32[]{:S(2)}, u32[]{:S(2)}) collective-permute-start(f32[4,16,2048]{2,1,0:T(8,128)} %get-tuple-element.75), channel_id=1, source_target_pairs={{0,4},{2,6},{4,0},{6,2},{1,5},{3,7},{5,1},{7,3},{8,12},{10,14},{12... | collective-permute-start | bytes 1572872 | tf_op jit(solution)/shard_map/ppermute | solution.py:220
  146.9 12.1 %shard_map.106.c_ref = f32[512,2048]{1,0:T(8,128)} custom-call(f32[512,1024]{1,0:T(8,128)} %bitcast.106, f32[512,8192]{1,0:T(8,128)} %all-gather.2.cloned.1.call-done.w0_ref.w1_ref, f32[512,8192]{1,0:T(8,128)} %all-gather.2.cloned.1.call-done.w0_ref.w1_ref, f32[512,2048]{1,0:T(8,128)} %bitcast.110), custom_call_target="tpu_custom_call" | custom-call | flops 6442450944 | bytes 20971520 | tf_op jit(solution)/shard_map/pallas_call | solution.py:192
  159.1 2.6 %collective-permute-start.18 = (f32[4,16,2048]{2,1,0:T(8,128)S(1)}, f32[4,16,2048]{2,1,0:T(8,128)S(1)}, u32[]{:S(2)}, u32[]{:S(2)}) collective-permute-start(f32[4,16,2048]{2,1,0:T(8,128)S(1)} %copy-done.10), channel_id=1, source_target_pairs={{0,48},{16,0},{32,16},{48,32},{1,49},{17,1},{33,17},{49,33},{2,50}... | collective-permute-start | bytes 1572872 | tf_op jit(solution)/shard_map/ppermute | solution.py:220
  161.7 2.4 %collective-permute-start.16 = (f32[4,16,2048]{2,1,0:T(8,128)S(1)}, f32[4,16,2048]{2,1,0:T(8,128)S(1)}, u32[]{:S(2)}, u32[]{:S(2)}) collective-permute-start(f32[4,16,2048]{2,1,0:T(8,128)S(1)} %copy-done.11), channel_id=1, source_target_pairs={{0,6},{2,0},{4,2},{6,4},{1,7},{3,1},{5,3},{7,5},{8,14},{10,8},{12,... | collective-permute-start | bytes 1572872 | tf_op jit(solution)/shard_map/ppermute | solution.py:220
  164.0 13.5 %shard_map.109 = f32[512,2048]{1,0:T(8,128)} custom-call(f32[512,1024]{1,0:T(8,128)} %bitcast.105, f32[512,1024]{1,0:T(8,128)} %bitcast.107, f32[512,1024]{1,0:T(8,128)} %collective-permute-done.2.got_ref, f32[512,8192]{1,0:T(8,128)} %all-gather.2.cloned.1.call-done.w0_ref.w1_ref, f32[512,8192]{1,0:T(8,128)} %all-gather.2.cloned.1.call-done.w0_ref.w1_ref, ...), custom_call_target="tpu_custom_call" | custom-call | flops 6442450944 | bytes 20971520 | tf_op jit(solution)/shard_map/pallas_call | solution.py:192
  177.6 1.3 add_add_fusion.1
  179.0 1.3 add_add_fusion
  180.4 2.8 %collective-permute-start.22 = (f32[16,2048]{1,0:T(8,128)S(1)}, f32[16,2048]{1,0:T(8,128)S(1)}, u32[]{:S(2)}, u32[]{:S(2)}) collective-permute-start(f32[16,2048]{1,0:T(8,128)S(1)} %get-tuple-element.92), channel_id=1, source_target_pairs={{0,4},{2,6},{4,0},{6,2},{1,5},{3,7},{5,1},{7,3},{8,12},{10,14},{12... | collective-permute-start | bytes 393224 | tf_op jit(solution)/shard_map/ppermute | solution.py:220
  183.9 2.6 %collective-permute-done.19 = f32[16,2048]{1,0:T(8,128)S(1)} collective-permute-done((f32[16,2048]{1,0:T(8,128)S(1)}, f32[16,2048]{1,0:T(8,128)S(1)}, u32[]{:S(2)}, u32[]{:S(2)}) %collective-permute-start.19) | collective-permute-done | bytes 131104 | tf_op jit(solution)/shard_map/ppermute | solution.py:220
  186.5 1.0 collective-permute-start.23
  187.5 1.1 collective-permute-done.22
  188.5 2.1 collective-permute-start.24
  190.7 1.8 collective-permute-done.21
  192.5 1.7 collective-permute-done.23
  194.3 2.6 %reduce-scatter.4.cloned.1.call-done = f32[1,32,2048]{2,1,0:T(8,128)} async-done(((f32[16,32,2048]{2,1,0:T(8,128)}), f32[1,32,2048]{2,1,0:T(8,128)}) %reduce-scatter.4.cloned.1.call-update) | async-done | bytes 262160
  197.8 2.6 %collective-permute-start.25 = (f32[16,2048]{1,0:T(8,128)S(1)}, f32[16,2048]{1,0:T(8,128)S(1)}, u32[]{:S(2)}, u32[]{:S(2)}) collective-permute-start(f32[16,2048]{1,0:T(8,128)S(1)} %get-tuple-element.84), channel_id=1, source_target_pairs={{0,64},{8,72},{64,0},{72,8},{1,65},{9,73},{65,1},{73,9},{2,66},{10... | collective-permute-start | bytes 393224 | tf_op jit(solution)/shard_map/ppermute | solution.py:314
  200.9 2.7 %collective-permute-start.27 = (f32[16,2048]{1,0:T(8,128)S(1)}, f32[16,2048]{1,0:T(8,128)S(1)}, u32[]{:S(2)}, u32[]{:S(2)}) collective-permute-start(f32[16,2048]{1,0:T(8,128)S(1)} %get-tuple-element.86), channel_id=1, source_target_pairs={{0,72},{8,0},{64,8},{72,64},{1,73},{9,1},{65,9},{73,65},{2,74},{10... | collective-permute-start | bytes 393224 | tf_op jit(solution)/shard_map/ppermute | solution.py:314
  203.6 1.7 collective-permute-done.25
  205.3 1.4 collective-permute-done.26
  206.7 1.5 fusion.10
  (86 shorter events, 14.0 us)
Async XLA Ops:
  8.0 138.9 %all-gather.2.cloned.1.call-start = ((), (), s32[]{:S(2)}) async-start(), calls=%async_computation.1 | async-start | bytes 17301504 | tf_op jit(solution)/shard_map/all_gather | solution.py:279
  9.0 25.5 %collective-permute-start.3 = (f32[16,2048]{1,0:T(8,128)S(1)}, f32[16,2048]{1,0:T(8,128)S(1)}, u32[]{:S(2)}, u32[]{:S(2)}) collective-permute-start(f32[16,2048]{1,0:T(8,128)S(1)} %bitcast_subtract_fusion), channel_id=1, source_target_pairs={{0,64},{64,0},{1,65},{65,1},{2,66},{66,2},{3,67},{67,3},{4,68},{68... | collective-permute-start | bytes 393224 | tf_op jit(solution)/shard_map/ppermute | solution.py:268
  12.2 22.3 %collective-permute-start.5 = (f32[16,2048]{1,0:T(8,128)S(1)}, f32[16,2048]{1,0:T(8,128)}, u32[]{:S(2)}, u32[]{:S(2)}) collective-permute-start(f32[16,2048]{1,0:T(8,128)S(1)} %bitcast_subtract_fusion), channel_id=1, source_target_pairs={{0,72},{72,0},{8,64},{64,8},{1,73},{73,1},{9,65},{65,9},{2,74},{74... | collective-permute-start | bytes 393224 | tf_op jit(solution)/shard_map/ppermute | solution.py:270
  16.3 8.9 %collective-permute-start.6 = (f32[2,256,512]{2,1,0:T(8,128)}, f32[2,256,512]{2,1,0:T(8,128)}, u32[]{:S(2)}, u32[]{:S(2)}) collective-permute-start(f32[2,256,512]{2,1,0:T(8,128)} %bitcast.133), channel_id=1, source_target_pairs={{0,1},{1,0},{2,3},{3,2},{4,5},{5,4},{6,7},{7,6},{8,9},{9,8},{10,11... | collective-permute-start | bytes 3145736 | tf_op jit(solution)/shard_map/ppermute | solution.py:243
  16.3 6.3 %copy-start.3 = (f32[4,4,2,8,512]{4,3,2,1,0:T(8,128)S(1)}, f32[4,4,2,8,512]{4,3,2,1,0:T(8,128)}, u32[]{:S(2)}) copy-start(f32[4,4,2,8,512]{4,3,2,1,0:T(8,128)} %get-tuple-element.38) | copy-start | bytes 1572868
  19.3 10.3 %collective-permute-start = (f32[2,256,512]{2,1,0:T(8,128)}, f32[2,256,512]{2,1,0:T(8,128)}, u32[]{:S(2)}, u32[]{:S(2)}) collective-permute-start(f32[2,256,512]{2,1,0:T(8,128)} %bitcast.132), channel_id=1, source_target_pairs={{0,1},{1,0},{2,3},{3,2},{4,5},{5,4},{6,7},{7,6},{8,9},{9,8},{10,11... | collective-permute-start | bytes 3145736 | tf_op jit(solution)/shard_map/ppermute | solution.py:249
  19.8 22.4 %collective-permute-start.7 = (f32[256,512]{1,0:T(8,128)}, f32[256,512]{1,0:T(8,128)}, u32[]{:S(2)}, u32[]{:S(2)}) collective-permute-start(f32[256,512]{1,0:T(8,128)} %bitcast.15), channel_id=1, source_target_pairs={{0,64},{64,0},{1,65},{65,1},{2,66},{66,2},{3,67},{67,3},{4,68},{68... | collective-permute-start | bytes 1572872 | tf_op jit(solution)/shard_map/ppermute | solution.py:242
  22.6 2.6 %copy-start.8 = (f32[1,16,2048]{2,1,0:T(8,128)S(1)}, f32[1,16,2048]{2,1,0:T(8,128)}, u32[]{:S(2)}) copy-start(f32[1,16,2048]{2,1,0:T(8,128)} %param.13) | copy-start | bytes 393220
  25.2 15.2 %collective-permute-start.4 = (f32[16,4096]{1,0:T(8,128)S(1)}, f32[16,4096]{1,0:T(8,128)S(1)}, u32[]{:S(2)}, u32[]{:S(2)}) collective-permute-start(f32[16,4096]{1,0:T(8,128)S(1)} %pad_maximum_fusion.6), channel_id=1, source_target_pairs={{0,8},{8,0},{1,9},{9,1},{2,10},{10,2},{3,11},{11,3},{4,12},{12,4},... | collective-permute-start | bytes 786440 | tf_op jit(solution)/shard_map/ppermute | solution.py:269
  28.7 2.8 %copy-start.6 = (f32[4,4,2,8,512]{4,3,2,1,0:T(8,128)S(1)}, f32[4,4,2,8,512]{4,3,2,1,0:T(8,128)}, u32[]{:S(2)}) copy-start(f32[4,4,2,8,512]{4,3,2,1,0:T(8,128)} %get-tuple-element.39) | copy-start | bytes 1572868
  28.7 4.3 %copy-start.9 = (f32[4,4,2,8,512]{4,3,2,1,0:T(8,128)S(1)}, f32[4,4,2,8,512]{4,3,2,1,0:T(8,128)}, u32[]{:S(2)}) copy-start(f32[4,4,2,8,512]{4,3,2,1,0:T(8,128)} %get-tuple-element.35) | copy-start | bytes 1572868
  34.5 11.9 %copy-start = (f32[1,512,1024]{2,1,0:T(8,128)S(1)}, f32[1,512,1024]{2,1,0:T(8,128)}, u32[]{:S(2)}) copy-start(f32[1,512,1024]{2,1,0:T(8,128)} %param.9) | copy-start | bytes 6291460
  42.2 154.6 %reduce-scatter.4.cloned.1.call-start = ((), (), s32[]{:S(2)}) async-start(), calls=%async_computation.2 | async-start | bytes 4456448
  42.3 41.7 %collective-permute-start.10 = (f32[512,2048]{1,0:T(8,128)}, f32[512,2048]{1,0:T(8,128)S(1)}, u32[]{:S(2)}, u32[]{:S(2)}) collective-permute-start(f32[512,2048]{1,0:T(8,128)} %bitcast.129), channel_id=1, source_target_pairs={{0,1},{1,0},{2,3},{3,2},{4,5},{5,4},{6,7},{7,6},{8,9},{9,8},{10,11... | collective-permute-start | bytes 12582920 | tf_op jit(solution)/shard_map/ppermute | solution.py:286
  42.4 41.6 %collective-permute-start.9 = (f32[512,2048]{1,0:T(8,128)}, f32[512,2048]{1,0:T(8,128)S(1)}, u32[]{:S(2)}, u32[]{:S(2)}) collective-permute-start(f32[512,2048]{1,0:T(8,128)} %bitcast.126), channel_id=1, source_target_pairs={{0,1},{1,0},{2,3},{3,2},{4,5},{5,4},{6,7},{7,6},{8,9},{9,8},{10,11... | collective-permute-start | bytes 12582920 | tf_op jit(solution)/shard_map/ppermute | solution.py:285
  42.9 41.1 %collective-permute-start.1 = (f32[256,1024]{1,0:T(8,128)}, f32[256,1024]{1,0:T(8,128)S(1)}, u32[]{:S(2)}, u32[]{:S(2)}) collective-permute-start(f32[256,1024]{1,0:T(8,128)} %get-tuple-element.77), channel_id=1, source_target_pairs={{0,64},{64,0},{1,65},{65,1},{2,66},{66,2},{3,67},{67,3},{4,68},{68... | collective-permute-start | bytes 3145736 | tf_op jit(solution)/shard_map/ppermute | solution.py:255
  43.7 6.8 %copy-start.7 = (f32[4,4,2,8,512]{4,3,2,1,0:T(8,128)S(1)}, f32[4,4,2,8,512]{4,3,2,1,0:T(8,128)}, u32[]{:S(2)}) copy-start(f32[4,4,2,8,512]{4,3,2,1,0:T(8,128)} %get-tuple-element.39) | copy-start | bytes 1572868
  43.8 38.1 %collective-permute-start.11 = (f32[256,512]{1,0:T(8,128)}, f32[256,512]{1,0:T(8,128)S(1)}, u32[]{:S(2)}, u32[]{:S(2)}) collective-permute-start(f32[256,512]{1,0:T(8,128)} %get-tuple-element.78), channel_id=1, source_target_pairs={{0,64},{64,0},{1,65},{65,1},{2,66},{66,2},{3,67},{67,3},{4,68},{68... | collective-permute-start | bytes 1572872 | tf_op jit(solution)/shard_map/ppermute | solution.py:246
  49.7 2.0 copy-start.4
  49.7 3.0 %copy-start.5 = (f32[256,512]{1,0:T(8,128)S(1)}, f32[256,512]{1,0:T(8,128)}, u32[]{:S(2)}) copy-start(f32[256,512]{1,0:T(8,128)} %get-tuple-element.78) | copy-start | bytes 1572868
  49.7 65.9 %collective-permute-start.8 = (f32[256,1536]{1,0:T(8,128)}, f32[256,1536]{1,0:T(8,128)}, u32[]{:S(2)}, u32[]{:S(2)}) collective-permute-start(f32[256,1536]{1,0:T(8,128)} %slice_dynamic-update-slice_fusion.2), channel_id=1, source_target_pairs={{0,64},{64,0},{1,65},{65,1},{2,66},{66,2},{3,67},{67,3},{4,68},{68... | collective-permute-start | bytes 4718600 | tf_op jit(solution)/shard_map/ppermute | solution.py:281
  83.9 2.4 %copy-start.15 = (f32[256,1024]{1,0:T(8,128)}, f32[256,1024]{1,0:T(8,128)S(1)}, u32[]{:S(2)}) copy-start(f32[256,1024]{1,0:T(8,128)S(1)} %collective-permute-done.1.refs_4_.refs_8_) | copy-start | bytes 3145732
  83.9 3.6 %copy-start.13 = (f32[512,2048]{1,0:T(8,128)}, f32[512,2048]{1,0:T(8,128)S(1)}, u32[]{:S(2)}) copy-start(f32[512,2048]{1,0:T(8,128)S(1)} %collective-permute-done.10.refs_8_.refs_7_) | copy-start | bytes 12582916
  84.0 2.4 %copy-start.14 = (f32[512,2048]{1,0:T(8,128)}, f32[512,2048]{1,0:T(8,128)S(1)}, u32[]{:S(2)}) copy-start(f32[512,2048]{1,0:T(8,128)S(1)} %collective-permute-done.9.refs_7_.refs_6_) | copy-start | bytes 12582916
  87.6 16.6 %copy-start.16 = (f32[256,1024]{1,0:T(8,128)S(1)}, f32[256,1024]{1,0:T(8,128)}, u32[]{:S(2)}) copy-start(f32[256,1024]{1,0:T(8,128)} %copy-done.15) | copy-start | bytes 3145732
  87.6 16.8 %copy-start.1 = (f32[512,1024]{1,0:T(8,128)S(1)}, f32[512,1024]{1,0:T(8,128)}, u32[]{:S(2)}) copy-start(f32[512,1024]{1,0:T(8,128)} %bitcast_subtract_fusion.1) | copy-start | bytes 6291460
  104.2 11.4 %collective-permute-start.12 = (f32[256,1024]{1,0:T(8,128)S(1)}, f32[256,1024]{1,0:T(8,128)}, u32[]{:S(2)}, u32[]{:S(2)}) collective-permute-start(f32[256,1024]{1,0:T(8,128)S(1)} %copy-done.16), channel_id=1, source_target_pairs={{0,1},{1,0},{2,3},{3,2},{4,5},{5,4},{6,7},{7,6},{8,9},{9,8},{10,11... | collective-permute-start | bytes 3145736 | tf_op jit(solution)/shard_map/ppermute | solution.py:289
  104.4 59.6 %collective-permute-start.2 = (f32[512,1024]{1,0:T(8,128)S(1)}, f32[512,1024]{1,0:T(8,128)}, u32[]{:S(2)}, u32[]{:S(2)}) collective-permute-start(f32[512,1024]{1,0:T(8,128)S(1)} %copy-done.1), channel_id=1, source_target_pairs={{0,64},{64,0},{1,65},{65,1},{2,66},{66,2},{3,67},{67,3},{4,68},{68... | collective-permute-start | bytes 6291464 | tf_op jit(solution)/shard_map/ppermute | solution.py:283
  134.1 6.1 %copy-start.2 = (f32[16,16,2048]{2,1,0:T(8,128)S(1)}, f32[16,16,2048]{2,1,0:T(8,128)}, u32[]{:S(2)}) copy-start(f32[16,16,2048]{2,1,0:T(8,128)} %get-tuple-element.49) | copy-start | bytes 6291460
  137.0 22.0 %collective-permute-start.14 = (f32[4,16,2048]{2,1,0:T(8,128)}, f32[4,16,2048]{2,1,0:T(8,128)}, u32[]{:S(2)}, u32[]{:S(2)}) collective-permute-start(f32[4,16,2048]{2,1,0:T(8,128)} %get-tuple-element.71), channel_id=1, source_target_pairs={{0,32},{16,48},{32,0},{48,16},{1,33},{17,49},{33,1},{49,17},{2,34}... | collective-permute-start | bytes 1572872 | tf_op jit(solution)/shard_map/ppermute | solution.py:220
  141.4 20.2 %collective-permute-start.13 = (f32[4,16,2048]{2,1,0:T(8,128)}, f32[4,16,2048]{2,1,0:T(8,128)}, u32[]{:S(2)}, u32[]{:S(2)}) collective-permute-start(f32[4,16,2048]{2,1,0:T(8,128)} %get-tuple-element.75), channel_id=1, source_target_pairs={{0,4},{2,6},{4,0},{6,2},{1,5},{3,7},{5,1},{7,3},{8,12},{10,14},{12... | collective-permute-start | bytes 1572872 | tf_op jit(solution)/shard_map/ppermute | solution.py:220
  145.3 32.3 %collective-permute-start.17 = (f32[4,16,2048]{2,1,0:T(8,128)}, f32[4,16,2048]{2,1,0:T(8,128)}, u32[]{:S(2)}, u32[]{:S(2)}) collective-permute-start(f32[4,16,2048]{2,1,0:T(8,128)} %get-tuple-element.69), channel_id=1, source_target_pairs={{0,16},{16,32},{32,48},{48,0},{1,17},{17,33},{33,49},{49,1},{2,18}... | collective-permute-start | bytes 1572872 | tf_op jit(solution)/shard_map/ppermute | solution.py:220
  145.9 31.6 %collective-permute-start.15 = (f32[4,16,2048]{2,1,0:T(8,128)}, f32[4,16,2048]{2,1,0:T(8,128)}, u32[]{:S(2)}, u32[]{:S(2)}) collective-permute-start(f32[4,16,2048]{2,1,0:T(8,128)} %get-tuple-element.73), channel_id=1, source_target_pairs={{0,2},{2,4},{4,6},{6,0},{1,3},{3,5},{5,7},{7,1},{8,10},{10,12},{12... | collective-permute-start | bytes 1572872 | tf_op jit(solution)/shard_map/ppermute | solution.py:220
  146.9 12.2 %copy-start.10 = (f32[4,16,2048]{2,1,0:T(8,128)S(1)}, f32[4,16,2048]{2,1,0:T(8,128)}, u32[]{:S(2)}) copy-start(f32[4,16,2048]{2,1,0:T(8,128)} %get-tuple-element.53) | copy-start | bytes 1572868
  146.9 14.8 %copy-start.11 = (f32[4,16,2048]{2,1,0:T(8,128)S(1)}, f32[4,16,2048]{2,1,0:T(8,128)}, u32[]{:S(2)}) copy-start(f32[4,16,2048]{2,1,0:T(8,128)} %get-tuple-element.52) | copy-start | bytes 1572868
  159.1 18.5 %collective-permute-start.18 = (f32[4,16,2048]{2,1,0:T(8,128)S(1)}, f32[4,16,2048]{2,1,0:T(8,128)S(1)}, u32[]{:S(2)}, u32[]{:S(2)}) collective-permute-start(f32[4,16,2048]{2,1,0:T(8,128)S(1)} %copy-done.10), channel_id=1, source_target_pairs={{0,48},{16,0},{32,16},{48,32},{1,49},{17,1},{33,17},{49,33},{2,50}... | collective-permute-start | bytes 1572872 | tf_op jit(solution)/shard_map/ppermute | solution.py:220
  161.7 15.9 %collective-permute-start.16 = (f32[4,16,2048]{2,1,0:T(8,128)S(1)}, f32[4,16,2048]{2,1,0:T(8,128)S(1)}, u32[]{:S(2)}, u32[]{:S(2)}) collective-permute-start(f32[4,16,2048]{2,1,0:T(8,128)S(1)} %copy-done.11), channel_id=1, source_target_pairs={{0,6},{2,0},{4,2},{6,4},{1,7},{3,1},{5,3},{7,5},{8,14},{10,8},{12,... | collective-permute-start | bytes 1572872 | tf_op jit(solution)/shard_map/ppermute | solution.py:220
  178.9 17.9 %copy-start.12 = (f32[1,16,2048]{2,1,0:T(8,128)S(1)}, f32[1,16,2048]{2,1,0:T(8,128)}, u32[]{:S(2)}) copy-start(f32[1,16,2048]{2,1,0:T(8,128)} %param.17) | copy-start | bytes 393220
  178.9 7.5 %collective-permute-start.19 = (f32[16,2048]{1,0:T(8,128)S(1)}, f32[16,2048]{1,0:T(8,128)S(1)}, u32[]{:S(2)}, u32[]{:S(2)}) collective-permute-start(f32[16,2048]{1,0:T(8,128)S(1)} %get-tuple-element.89), channel_id=1, source_target_pairs={{0,32},{16,48},{32,0},{48,16},{1,33},{17,49},{33,1},{49,17},{2,34}... | collective-permute-start | bytes 393224 | tf_op jit(solution)/shard_map/ppermute | solution.py:220
  180.4 8.2 %collective-permute-start.22 = (f32[16,2048]{1,0:T(8,128)S(1)}, f32[16,2048]{1,0:T(8,128)S(1)}, u32[]{:S(2)}, u32[]{:S(2)}) collective-permute-start(f32[16,2048]{1,0:T(8,128)S(1)} %get-tuple-element.92), channel_id=1, source_target_pairs={{0,4},{2,6},{4,0},{6,2},{1,5},{3,7},{5,1},{7,3},{8,12},{10,14},{12... | collective-permute-start | bytes 393224 | tf_op jit(solution)/shard_map/ppermute | solution.py:220
  183.2 7.5 %collective-permute-start.20 = (f32[16,2048]{1,0:T(8,128)S(1)}, f32[16,2048]{1,0:T(8,128)S(1)}, u32[]{:S(2)}, u32[]{:S(2)}) collective-permute-start(f32[16,2048]{1,0:T(8,128)S(1)} %get-tuple-element.87), channel_id=1, source_target_pairs={{0,16},{16,32},{32,48},{48,0},{1,17},{17,33},{33,49},{49,1},{2,18}... | collective-permute-start | bytes 393224 | tf_op jit(solution)/shard_map/ppermute | solution.py:220
  186.5 6.0 %collective-permute-start.21 = (f32[16,2048]{1,0:T(8,128)S(1)}, f32[16,2048]{1,0:T(8,128)S(1)}, u32[]{:S(2)}, u32[]{:S(2)}) collective-permute-start(f32[16,2048]{1,0:T(8,128)S(1)} %get-tuple-element.58), channel_id=1, source_target_pairs={{0,48},{16,0},{32,16},{48,32},{1,49},{17,1},{33,17},{49,33},{2,50}... | collective-permute-start | bytes 393224 | tf_op jit(solution)/shard_map/ppermute | solution.py:220
  186.5 7.8 %collective-permute-start.23 = (f32[16,2048]{1,0:T(8,128)S(1)}, f32[16,2048]{1,0:T(8,128)S(1)}, u32[]{:S(2)}, u32[]{:S(2)}) collective-permute-start(f32[16,2048]{1,0:T(8,128)S(1)} %get-tuple-element.90), channel_id=1, source_target_pairs={{0,2},{2,4},{4,6},{6,0},{1,3},{3,5},{5,7},{7,1},{8,10},{10,12},{12... | collective-permute-start | bytes 393224 | tf_op jit(solution)/shard_map/ppermute | solution.py:220
  188.5 5.7 %collective-permute-start.24 = (f32[16,2048]{1,0:T(8,128)S(1)}, f32[16,2048]{1,0:T(8,128)S(1)}, u32[]{:S(2)}, u32[]{:S(2)}) collective-permute-start(f32[16,2048]{1,0:T(8,128)S(1)} %get-tuple-element.63), channel_id=1, source_target_pairs={{0,6},{2,0},{4,2},{6,4},{1,7},{3,1},{5,3},{7,5},{8,14},{10,8},{12,... | collective-permute-start | bytes 393224 | tf_op jit(solution)/shard_map/ppermute | solution.py:220
  197.8 7.5 %collective-permute-start.25 = (f32[16,2048]{1,0:T(8,128)S(1)}, f32[16,2048]{1,0:T(8,128)S(1)}, u32[]{:S(2)}, u32[]{:S(2)}) collective-permute-start(f32[16,2048]{1,0:T(8,128)S(1)} %get-tuple-element.84), channel_id=1, source_target_pairs={{0,64},{8,72},{64,0},{72,8},{1,65},{9,73},{65,1},{73,9},{2,66},{10... | collective-permute-start | bytes 393224 | tf_op jit(solution)/shard_map/ppermute | solution.py:314
  200.4 6.3 %collective-permute-start.26 = (f32[16,2048]{1,0:T(8,128)S(1)}, f32[16,2048]{1,0:T(8,128)S(1)}, u32[]{:S(2)}, u32[]{:S(2)}) collective-permute-start(f32[16,2048]{1,0:T(8,128)S(1)} %get-tuple-element.85), channel_id=1, source_target_pairs={{0,8},{8,64},{64,72},{72,0},{1,9},{9,65},{65,73},{73,1},{2,10},{10... | collective-permute-start | bytes 393224 | tf_op jit(solution)/shard_map/ppermute | solution.py:314
  200.9 5.8 %collective-permute-start.27 = (f32[16,2048]{1,0:T(8,128)S(1)}, f32[16,2048]{1,0:T(8,128)S(1)}, u32[]{:S(2)}, u32[]{:S(2)}) collective-permute-start(f32[16,2048]{1,0:T(8,128)S(1)} %get-tuple-element.86), channel_id=1, source_target_pairs={{0,72},{8,0},{64,8},{72,64},{1,73},{9,1},{65,9},{73,65},{2,74},{10... | collective-permute-start | bytes 393224 | tf_op jit(solution)/shard_map/ppermute | solution.py:314
Sparse Core Ops, SparseCore 0:
  42.3 73.0 all-gather.1
Sparse Core Ops, SparseCore 1:
  106.0 90.8 reduce-scatter.3

commit v10 on v9

--- a/solution.py
+++ b/solution.py
@@ -39,35 +39,37 @@
     return jnp.dot(left, right, preferred_element_type=F32)
 
 
-def turn_kernel(core_ref, src, mine0, mine1, theirs):
+def turn_kernel(core_ref, x_ref, a_ref, x_mine0, x_mine1, a_mine0, a_mine1, theirs):
     even = core_ref[0] == 0
-    t = src[...].T
-    for y in range(mine0.shape[1]):
-        for xl in range(2):
-            for z in range(4):
-                for k, mine in enumerate((mine0, mine1)):
-                    at = (2 * y + xl) * 128 + z * 32 + k * 8
-                    e, o = t[at : at + 8], t[at + 16 : at + 24]
-                    mine[z, y, xl] = jnp.where(even, e, o)
-                    theirs[k, z, y, xl] = jnp.where(even, o, e)
-
-
-def turned(core, share):
-    tokens = share.shape[0]
+    for n, (src, mines) in enumerate(((x_ref, (x_mine0, x_mine1)), (a_ref, (a_mine0, a_mine1)))):
+        t = src[...].T
+        for y in range(x_mine0.shape[1]):
+            for xl in range(2):
+                for z in range(4):
+                    for k, mine in enumerate(mines):
+                        at = (2 * y + xl) * 128 + z * 32 + k * 8
+                        e, o = t[at : at + 8], t[at + 16 : at + 24]
+                        mine[z, y, xl] = jnp.where(even, e, o)
+                        theirs[n, k, z, y, xl] = jnp.where(even, o, e)
+
+
+def turned(core, x, a):
+    tokens = x.shape[0]
     mine = jax.ShapeDtypeStruct((4, 4, 2, 8, tokens), F32)
     mine_spec = pl.BlockSpec((4, 2, 2, 8, tokens), lambda i: (0, i, 0, 0, 0))
-    theirs_spec = pl.BlockSpec((2, 4, 2, 2, 8, tokens), lambda i: (0, 0, i, 0, 0, 0))
-    mine0, mine1, theirs = pl.pallas_call(
+    theirs_spec = pl.BlockSpec((2, 2, 4, 2, 2, 8, tokens), lambda i: (0, 0, 0, i, 0, 0, 0))
+    source = pl.BlockSpec((tokens, 512), lambda i: (0, i))
+    *mines, theirs = pl.pallas_call(
         turn_kernel,
         grid=(2,),
-        in_specs=[SMEM, pl.BlockSpec((tokens, 512), lambda i: (0, i))],
-        out_specs=[mine_spec, mine_spec, theirs_spec],
-        out_shape=[mine, mine, jax.ShapeDtypeStruct((2, *mine.shape), F32)],
-        cost_estimate=cost(0, share, share),
+        in_specs=[SMEM, source, source],
+        out_specs=[mine_spec] * 4 + [theirs_spec],
+        out_shape=[mine] * 4 + [jax.ShapeDtypeStruct((2, 2, *mine.shape), F32)],
+        cost_estimate=cost(0, x, x, a, a),
         compiler_params=params(),
-    )(core, share)
+    )(core, x, a)
     rows = 128 * 2
-    return mine0.reshape(rows, tokens), mine1.reshape(rows, tokens), theirs.reshape(2, rows, tokens)
+    return [m.reshape(rows, tokens) for m in mines], theirs.reshape(2, 2, rows, tokens)
 
 
 def passes(stack, right):
@@ -80,7 +82,7 @@
 def grad_kernel(split, p_ref, x_ref, a_ref, *refs):
     pair, pair_sent, single = refs[-3:]
     outs, refs = (refs[-5:-3], refs[:-5]) if split else (refs[-4:-3], refs[:-4])
-    got_refs, refs = (refs[:1], refs[1:]) if split else (refs[:2], refs[2:])
+    got_refs, refs = (refs[:1], refs[1:]) if split else (refs[:3], refs[3:])
     g_ref, b_ref, go_ref, bo_ref = refs[:4]
     sent_refs = refs[4:]
     is_first = p_ref[0] == 0
@@ -101,8 +103,8 @@
             pair_sent[:256], pair_sent[512:768] = halves(x_sent - a_sent)
             pair_sent[256:512], pair_sent[768:] = halves(a_sent)
         else:
-            got = got_refs[0][...]
-            second = jnp.where(is_first, got_refs[1][...], a)
+            got = jnp.concatenate([got_refs[0][...], got_refs[1][...]], axis=1)
+            second = jnp.where(is_first, got_refs[2][...], a)
         opened = x + got
         pair[:256], pair[512:768] = halves(opened - second)
         pair[256:512], pair[768:] = halves(second)
@@ -238,15 +240,13 @@
     xl0 = lax.axis_index("xl") == 0
     ff = w.shape[1]
 
-    x_mine0, x_mine1, x_theirs = turned(core_id, x)
+    (x_mine0, x_mine1, a_mine0, a_mine1), theirs = turned(core_id, x, ba)
     x0_mine = lax.ppermute(x_mine0, "party", SWAP)
-    x_other = lax.ppermute(x_theirs, "core", SWAP)
+    other = lax.ppermute(theirs, "core", SWAP)
+    x_other, a_other = other[0], other[1]
     xs0 = jnp.concatenate([x_mine0, x_other[0]], axis=1)
     xs1 = jnp.concatenate([x_mine1, x_other[1]], axis=1)
     x0_other = lax.ppermute(x_other[0], "party", SWAP)
-    x0 = jnp.concatenate([x0_mine, x0_other], axis=1)
-    a_mine0, a_mine1, a_theirs = turned(core_id, after(ba, x_theirs))
-    a_other = lax.ppermute(a_theirs, "core", SWAP)
     aa0 = jnp.concatenate([a_mine0, a_other[0]], axis=1)
     aa1 = jnp.concatenate([a_mine1, a_other[1]], axis=1)
     last = g[3 * g.shape[0] // 4 :]
@@ -282,10 +282,10 @@
     u_local = x - fa
     u = lax.ppermute(after(u_local, got0), "party", SWAP)
 
-    g_other = lax.ppermute(after(g, a_other), "core", SWAP)
-    b_other = lax.ppermute(after(bb, a_other), "core", SWAP)
+    g_other = lax.ppermute(after(g, other), "core", SWAP)
+    b_other = lax.ppermute(after(bb, other), "core", SWAP)
     rights = (g, bb, g_other, b_other)
-    early = grad_parts(party_id, after(xs0, u_local, xs1, aa1), aa0, (x0, got0), rights, (), 1)
+    early = grad_parts(party_id, after(xs0, u_local, xs1, aa1), aa0, (x0_mine, x0_other, got0), rights, (), 1)
     sent = (got0, lax.ppermute(after(got0, early), "core", SWAP))
     late = grad_parts(party_id, xs1, aa1, (got1,), rights, sent, LATE)
 

time: 217 us -> 213 us (0.982)
  other arithmetic: 21.4 us -> 17.5 us
  waiting for transfers between devices: 55.4 us -> 57.6 us
    ppermute x1, waiting for transfers between devices: 0.01 us -> 3.3 us  [body(): lax.ppermute(d, ('party', 'xl'), [(0, 3), (3, 0), (1, 2), (2, 1)])]
    concatenate x2 -> x0, other arithmetic: 3.16 us -> none  [the longest x1 2.1 us: body(): x0 = jnp.concatenate([x0_mine, x0_other], axis=1)]
    ppermute x1, waiting for transfers between devices: 5.83 us -> 3.32 us  [body(): near = lax.ppermute(jnp.concatenate([fb, d], axis=1), 'xl', SWAP)]
    pallas_call x2 -> x1, Pallas kernels: 5.9 us -> 4.26 us  [turned(): pl.pallas_call(turn_kernel, grid=(2,), in_specs=[SMEM, source, source], o...]
    unnamed x37 -> x41, local copies, waits for them, and re-layouts: 6.08 us -> 7.2 us
  transfers between devices with their start and end apart: 30 -> 29, of which waited for: 10 -> 10; matrix products, arithmetic and copies ran while one was open for 14% -> 12% of each run, Pallas kernels for 31% -> 29%
where the time goes in v10:
time: 213 us; the launch traced here: 212 us
  Pallas kernels  64.8 us (30%)
  waiting for transfers between devices  57.6 us (27%)
  starting transfers between devices  42.1 us (20%)
  other arithmetic  17.5 us (8%)
  between operations  15.8 us (7%)
  local copies, waits for them, and re-layouts  14.5 us (7%)
    pallas_call x2, Pallas kernels, grad_parts(): pl.pallas_call(lambda *refs: grad_kernel(bool(sent), *refs), grid=(ff //...  34.9 us
    ppermute x1, waiting for transfers between devices, body(): x0_other = lax.ppermute(x_other[0], 'party', SWAP)  27.8 us
    pallas_call x2, Pallas kernels, forward_call(): pl.pallas_call(kernel, grid=(steps,), in_specs=[pl.BlockSpec((rows, d), l...  25.7 us
    ppermute x12, starting transfers between devices, scattered_pair(): lax.ppermute(piece, axis, [(i, (i + step) % 4) for i in range(4)])  20.6 us
    ppermute x1, waiting for transfers between devices, body(): got1 = lax.ppermute(sent1, 'party', SWAP)  11.2 us
    ppermute x12, waiting for transfers between devices, scattered_pair(): lax.ppermute(piece, axis, [(i, (i + step) % 4) for i in range(4)])  7.93 us
    unnamed x41, local copies, waits for them, and re-layouts  7.2 us
    ppermute x3, starting transfers between devices, body(): lax.ppermute(give, ('party', 'xl'), [(i, (i + step) % 4) for i in range(4)])  6.22 us
  transfers between devices with their start and end apart: 29, of which 10 were waited for; matrix products, arithmetic and copies ran while one was open for 12% of the time, Pallas kernels for 29%

profile of v10, /device:TPU:0, one launch (start us, length us, event | category | flops | bytes accessed | tf_op | source)
XLA Modules:
  0.0 212.4 jit_solution(8842245686157921680)
XLA Ops:
  8.1 4.3 %shard_map.104 = (f32[4,4,2,8,512]{4,3,2,1,0:T(8,128)}, f32[4,4,2,8,512]{4,3,2,1,0:T(8,128)}, f32[4,4,2,8,512]{4,3,2,1,0:T(8,128)}, f32[4,4,2,8,512]{4,3,2,1,0:T(8,128)}, f32[2,2,4,4,2,8,512]{6,5,4,3,2,1,0:T(8,128)}) custom-call(s32[1]{0:T(128)} %bitcast.3.core_ref, f32[512,1024]{1,0:T(8,128)} %bitcast.103, f32[512,1024]{1,0:T(8,128)} %bitcast.112), custom_call_target="tpu_custom_call" | custom-call | bytes 8388608 | tf_op jit(solution)/shard_map/pallas_call | solution.py:62
  12.4 3.2 %collective-permute-start.3 = (f32[16,2048]{1,0:T(8,128)S(1)}, f32[16,2048]{1,0:T(8,128)S(1)}, u32[]{:S(2)}, u32[]{:S(2)}) collective-permute-start(f32[16,2048]{1,0:T(8,128)S(1)} %bitcast_subtract_fusion), channel_id=1, source_target_pairs={{0,64},{64,0},{1,65},{65,1},{2,66},{66,2},{3,67},{67,3},{4,68},{68... | collective-permute-start | bytes 393224 | tf_op jit(solution)/shard_map/ppermute | solution.py:268
  15.6 1.1 collective-permute-start.5
  16.7 1.5 collective-permute-start.6
  18.9 1.4 collective-permute-start.4
  20.4 1.8 slice_dynamic-update-slice_fusion.1
  22.2 1.6 fusion.17
  23.8 1.3 slice_bitcast_fusion
  25.2 1.0 slice_bitcast_fusion.1
  29.2 1.5 pad_maximum_fusion
  30.7 3.3 %collective-permute-done.5 = f32[16,2048]{1,0:T(8,128)} collective-permute-done((f32[16,2048]{1,0:T(8,128)S(1)}, f32[16,2048]{1,0:T(8,128)}, u32[]{:S(2)}, u32[]{:S(2)}) %collective-permute-start.5) | collective-permute-done | bytes 131104 | tf_op jit(solution)/shard_map/ppermute | solution.py:270
  34.0 3.3 %collective-permute-done.4 = f32[16,4096]{1,0:T(8,128)} collective-permute-done((f32[16,4096]{1,0:T(8,128)}, f32[16,4096]{1,0:T(8,128)}, u32[]{:S(2)}, u32[]{:S(2)}) %collective-permute-start.4) | collective-permute-done | bytes 262176 | tf_op jit(solution)/shard_map/ppermute | solution.py:269
  37.3 1.1 multiply_add_fusion
  39.9 1.7 collective-permute-start.1
  41.7 1.8 collective-permute-start.10
  43.5 3.3 %bitcast_subtract_fusion.1 = f32[512,1024]{1,0:T(8,128)} fusion(f32[1,512,1024]{2,1,0:T(8,128)} %param.12, f32[1,512,1024]{2,1,0:T(8,128)S(1)} %copy-done), kind=kLoop, calls=%fused_computation.75 | loop fusion | flops 524288 | bytes 6291456 | tf_op jit(solution)/shard_map/sub | solution.py:282
  46.8 1.7 collective-permute-start.7
  48.5 1.1 pad_maximum_fusion.3.refs_1_
  49.6 1.5 pad_maximum_fusion.1
  51.1 27.8 %collective-permute-done.10.refs_4_ = f32[256,512]{1,0:T(8,128)S(1)} collective-permute-done((f32[256,512]{1,0:T(8,128)}, f32[256,512]{1,0:T(8,128)S(1)}, u32[]{:S(2)}, u32[]{:S(2)}) %collective-permute-start.10) | collective-permute-done | bytes 524320 | tf_op jit(solution)/shard_map/ppermute | solution.py:249
  79.0 1.0 copy-done.16
  79.9 1.3 copy-done.15
  81.4 1.2 copy-done.14
  82.7 16.6 %shard_map.106 = f32[16,2,16,2048]{3,2,1,0:T(8,128)} custom-call(s32[1]{0:T(128)} %bitcast.16.refs_0_, f32[256,1024]{1,0:T(8,128)} %pad_maximum_fusion.3.refs_1_, f32[256,1024]{1,0:T(8,128)} %get-tuple-element.76.refs_2_, f32[256,512]{1,0:T(8,128)} %collective-permute-done.6.refs_3_, f32[256,512]{1,0:T(8,128)} %copy-done.18, f32[256,1024]{1,0:T(8,128)} %copy-done.16, ...), custom_call_target="tpu_custom_call" | custom-call | flops 9663676416 | bytes 25165824 | tf_op jit(solution)/shard_map/pallas_call | solution.py:137
  99.5 2.0 collective-permute-start.2
  101.6 11.2 %collective-permute-done.7.refs_3_ = f32[256,1536]{1,0:T(8,128)} collective-permute-done((f32[256,1536]{1,0:T(8,128)}, f32[256,1536]{1,0:T(8,128)}, u32[]{:S(2)}, u32[]{:S(2)}) %collective-permute-start.7) | collective-permute-done | bytes 1572896 | tf_op jit(solution)/shard_map/ppermute | solution.py:281
  112.7 18.3 %shard_map.107 = (f32[16,16,2048]{2,1,0:T(8,128)}, f32[16,16,2048]{2,1,0:T(8,128)}) custom-call(s32[1]{0:T(128)} %bitcast.16.refs_0_, f32[256,1024]{1,0:T(8,128)} %get-tuple-element.91.refs_1_, f32[256,1024]{1,0:T(8,128)} %get-tuple-element.92.refs_2_, f32[256,1536]{1,0:T(8,128)} %collective-permute-done.7.refs_3_, f32[512,2048]{1,0:T(8,128)} %bitcast.129, ...), custom_call_target="tpu_custom_call" | custom-call | flops 77309411328 | bytes 197132288 | tf_op jit(solution)/shard_map/pallas_call | solution.py:137
  131.0 2.9 %dynamic-slice_bitcast_fusion = (f32[4,16,2048]{2,1,0:T(8,128)}, f32[4,16,2048]{2,1,0:T(8,128)}, f32[4,16,2048]{2,1,0:T(8,128)S(1)}, f32[4,16,2048]{2,1,0:T(8,128)}) fusion(f32[4,4,16,2048]{3,2,1,0:T(8,128)} %bitcast.114, s32[]{:T(128)S(6)} %select_n.155, s32[]{:T(128)S(6)} %select_n.153, s32[]{:T(128)S(6)} %select_n.147, s32[]{:T(128)S(6)} %select_n.145), kind=kLoop, calls=%fused_computation.21 | loop fusion | bytes 4194320 | tf_op jit(solution)/shard_map/jit(dynamic_index_in_dim)/squeeze | solution.py:219
  133.9 3.2 %collective-permute-start.13 = (f32[4,16,2048]{2,1,0:T(8,128)}, f32[4,16,2048]{2,1,0:T(8,128)}, u32[]{:S(2)}, u32[]{:S(2)}) collective-permute-start(f32[4,16,2048]{2,1,0:T(8,128)} %get-tuple-element.67), channel_id=1, source_target_pairs={{0,32},{16,48},{32,0},{48,16},{1,33},{17,49},{33,1},{49,17},{2,34}... | collective-permute-start | bytes 1572872 | tf_op jit(solution)/shard_map/ppermute | solution.py:222
  137.1 1.2 dynamic-slice_bitcast_fusion.2
  138.3 3.9 %collective-permute-start.12 = (f32[4,16,2048]{2,1,0:T(8,128)}, f32[4,16,2048]{2,1,0:T(8,128)}, u32[]{:S(2)}, u32[]{:S(2)}) collective-permute-start(f32[4,16,2048]{2,1,0:T(8,128)} %get-tuple-element.71), channel_id=1, source_target_pairs={{0,4},{2,6},{4,0},{6,2},{1,5},{3,7},{5,1},{7,3},{8,12},{10,14},{12... | collective-permute-start | bytes 1572872 | tf_op jit(solution)/shard_map/ppermute | solution.py:222
  143.0 1.0 collective-permute-start.14
  144.0 12.1 %shard_map.105.c_ref = f32[512,2048]{1,0:T(8,128)} custom-call(f32[512,1024]{1,0:T(8,128)} %bitcast.105, f32[512,8192]{1,0:T(8,128)} %all-gather.2.cloned.1.call-done.w0_ref.w1_ref, f32[512,8192]{1,0:T(8,128)} %all-gather.2.cloned.1.call-done.w0_ref.w1_ref, f32[512,2048]{1,0:T(8,128)} %bitcast.109), custom_call_target="tpu_custom_call" | custom-call | flops 6442450944 | bytes 20971520 | tf_op jit(solution)/shard_map/pallas_call | solution.py:194
  156.1 2.6 %collective-permute-start.17 = (f32[4,16,2048]{2,1,0:T(8,128)S(1)}, f32[4,16,2048]{2,1,0:T(8,128)S(1)}, u32[]{:S(2)}, u32[]{:S(2)}) collective-permute-start(f32[4,16,2048]{2,1,0:T(8,128)S(1)} %copy-done.10), channel_id=1, source_target_pairs={{0,48},{16,0},{32,16},{48,32},{1,49},{17,1},{33,17},{49,33},{2,50}... | collective-permute-start | bytes 1572872 | tf_op jit(solution)/shard_map/ppermute | solution.py:222
  158.8 2.2 %collective-permute-start.15 = (f32[4,16,2048]{2,1,0:T(8,128)S(1)}, f32[4,16,2048]{2,1,0:T(8,128)S(1)}, u32[]{:S(2)}, u32[]{:S(2)}) collective-permute-start(f32[4,16,2048]{2,1,0:T(8,128)S(1)} %copy-done.11), channel_id=1, source_target_pairs={{0,6},{2,0},{4,2},{6,4},{1,7},{3,1},{5,3},{7,5},{8,14},{10,8},{12,... | collective-permute-start | bytes 1572872 | tf_op jit(solution)/shard_map/ppermute | solution.py:222
  161.0 13.5 %shard_map.108 = f32[512,2048]{1,0:T(8,128)} custom-call(f32[512,1024]{1,0:T(8,128)} %bitcast.104, f32[512,1024]{1,0:T(8,128)} %bitcast.106, f32[512,1024]{1,0:T(8,128)} %collective-permute-done.2.got_ref, f32[512,8192]{1,0:T(8,128)} %all-gather.2.cloned.1.call-done.w0_ref.w1_ref, f32[512,8192]{1,0:T(8,128)} %all-gather.2.cloned.1.call-done.w0_ref.w1_ref, ...), custom_call_target="tpu_custom_call" | custom-call | flops 6442450944 | bytes 20971520 | tf_op jit(solution)/shard_map/pallas_call | solution.py:194
  174.6 1.3 add_add_fusion.1
  176.0 1.3 add_add_fusion
  177.4 3.0 %collective-permute-start.21 = (f32[16,2048]{1,0:T(8,128)S(1)}, f32[16,2048]{1,0:T(8,128)S(1)}, u32[]{:S(2)}, u32[]{:S(2)}) collective-permute-start(f32[16,2048]{1,0:T(8,128)S(1)} %get-tuple-element.88), channel_id=1, source_target_pairs={{0,4},{2,6},{4,0},{6,2},{1,5},{3,7},{5,1},{7,3},{8,12},{10,14},{12... | collective-permute-start | bytes 393224 | tf_op jit(solution)/shard_map/ppermute | solution.py:222
  180.9 3.8 %collective-permute-done.18 = f32[16,2048]{1,0:T(8,128)S(1)} collective-permute-done((f32[16,2048]{1,0:T(8,128)S(1)}, f32[16,2048]{1,0:T(8,128)S(1)}, u32[]{:S(2)}, u32[]{:S(2)}) %collective-permute-start.18) | collective-permute-done | bytes 131104 | tf_op jit(solution)/shard_map/ppermute | solution.py:222
  184.8 3.2 %collective-permute-start.23 = (f32[16,2048]{1,0:T(8,128)S(1)}, f32[16,2048]{1,0:T(8,128)S(1)}, u32[]{:S(2)}, u32[]{:S(2)}) collective-permute-start(f32[16,2048]{1,0:T(8,128)S(1)} %get-tuple-element.59), channel_id=1, source_target_pairs={{0,6},{2,0},{4,2},{6,4},{1,7},{3,1},{5,3},{7,5},{8,14},{10,8},{12,... | collective-permute-start | bytes 393224 | tf_op jit(solution)/shard_map/ppermute | solution.py:222
  188.0 2.8 %collective-permute-done.20 = f32[16,2048]{1,0:T(8,128)S(1)} collective-permute-done((f32[16,2048]{1,0:T(8,128)S(1)}, f32[16,2048]{1,0:T(8,128)S(1)}, u32[]{:S(2)}, u32[]{:S(2)}) %collective-permute-start.20) | collective-permute-done | bytes 131104 | tf_op jit(solution)/shard_map/ppermute | solution.py:222
  190.8 1.3 collective-permute-done.22
  193.9 3.0 %collective-permute-start.24 = (f32[16,2048]{1,0:T(8,128)S(1)}, f32[16,2048]{1,0:T(8,128)S(1)}, u32[]{:S(2)}, u32[]{:S(2)}) collective-permute-start(f32[16,2048]{1,0:T(8,128)S(1)} %get-tuple-element.80), channel_id=1, source_target_pairs={{0,64},{8,72},{64,0},{72,8},{1,65},{9,73},{65,1},{73,9},{2,66},{10... | collective-permute-start | bytes 393224 | tf_op jit(solution)/shard_map/ppermute | solution.py:314
  197.3 2.8 %collective-permute-start.26 = (f32[16,2048]{1,0:T(8,128)S(1)}, f32[16,2048]{1,0:T(8,128)S(1)}, u32[]{:S(2)}, u32[]{:S(2)}) collective-permute-start(f32[16,2048]{1,0:T(8,128)S(1)} %get-tuple-element.82), channel_id=1, source_target_pairs={{0,72},{8,0},{64,8},{72,64},{1,73},{9,1},{65,9},{73,65},{2,74},{10... | collective-permute-start | bytes 393224 | tf_op jit(solution)/shard_map/ppermute | solution.py:314
  200.1 1.8 collective-permute-done.24
  201.9 1.5 collective-permute-done.25
  203.4 1.5 fusion.10
  (84 shorter events, 9.4 us)
Async XLA Ops:
  8.0 136.0 %all-gather.2.cloned.1.call-start = ((), (), s32[]{:S(2)}) async-start(), calls=%async_computation.1 | async-start | bytes 17301504 | tf_op jit(solution)/shard_map/all_gather | solution.py:279
  8.0 4.3 %copy-start.7 = (f32[1,16,2048]{2,1,0:T(8,128)S(1)}, f32[1,16,2048]{2,1,0:T(8,128)}, u32[]{:S(2)}) copy-start(f32[1,16,2048]{2,1,0:T(8,128)} %param.13) | copy-start | bytes 393220
  8.1 4.3 %copy-start.13 = (f32[1,16,2048]{2,1,0:T(8,128)S(1)}, f32[1,16,2048]{2,1,0:T(8,128)}, u32[]{:S(2)}) copy-start(f32[1,16,2048]{2,1,0:T(8,128)} %param.10) | copy-start | bytes 393220
  12.3 12.9 %collective-permute-start = (f32[2,2,256,512]{3,2,1,0:T(8,128)}, f32[2,2,256,512]{3,2,1,0:T(8,128)S(1)}, u32[]{:S(2)}, u32[]{:S(2)}) collective-permute-start(f32[2,2,256,512]{3,2,1,0:T(8,128)} %bitcast.133), channel_id=1, source_target_pairs={{0,1},{1,0},{2,3},{3,2},{4,5},{5,4},{6,7},{7,6},{8,9},{9,8},{10,11... | collective-permute-start | bytes 6291464 | tf_op jit(solution)/shard_map/ppermute | solution.py:245
  12.4 18.3 %collective-permute-start.3 = (f32[16,2048]{1,0:T(8,128)S(1)}, f32[16,2048]{1,0:T(8,128)S(1)}, u32[]{:S(2)}, u32[]{:S(2)}) collective-permute-start(f32[16,2048]{1,0:T(8,128)S(1)} %bitcast_subtract_fusion), channel_id=1, source_target_pairs={{0,64},{64,0},{1,65},{65,1},{2,66},{66,2},{3,67},{67,3},{4,68},{68... | collective-permute-start | bytes 393224 | tf_op jit(solution)/shard_map/ppermute | solution.py:268
  15.6 18.4 %collective-permute-start.5 = (f32[16,2048]{1,0:T(8,128)S(1)}, f32[16,2048]{1,0:T(8,128)}, u32[]{:S(2)}, u32[]{:S(2)}) collective-permute-start(f32[16,2048]{1,0:T(8,128)S(1)} %bitcast_subtract_fusion), channel_id=1, source_target_pairs={{0,72},{72,0},{8,64},{64,8},{1,73},{73,1},{9,65},{65,9},{2,74},{74... | collective-permute-start | bytes 393224 | tf_op jit(solution)/shard_map/ppermute | solution.py:270
  16.7 22.6 %collective-permute-start.6 = (f32[256,512]{1,0:T(8,128)}, f32[256,512]{1,0:T(8,128)}, u32[]{:S(2)}, u32[]{:S(2)}) collective-permute-start(f32[256,512]{1,0:T(8,128)} %bitcast.125), channel_id=1, source_target_pairs={{0,64},{64,0},{1,65},{65,1},{2,66},{66,2},{3,67},{67,3},{4,68},{68... | collective-permute-start | bytes 1572872 | tf_op jit(solution)/shard_map/ppermute | solution.py:244
  18.9 18.4 %collective-permute-start.4 = (f32[16,4096]{1,0:T(8,128)}, f32[16,4096]{1,0:T(8,128)}, u32[]{:S(2)}, u32[]{:S(2)}) collective-permute-start(f32[16,4096]{1,0:T(8,128)} %pad_maximum_fusion.5), channel_id=1, source_target_pairs={{0,8},{8,0},{1,9},{9,1},{2,10},{10,2},{3,11},{11,3},{4,12},{12,4},... | collective-permute-start | bytes 786440 | tf_op jit(solution)/shard_map/ppermute | solution.py:269
  25.2 2.5 %copy-start.5 = (f32[4,4,2,8,512]{4,3,2,1,0:T(8,128)S(1)}, f32[4,4,2,8,512]{4,3,2,1,0:T(8,128)}, u32[]{:S(2)}) copy-start(f32[4,4,2,8,512]{4,3,2,1,0:T(8,128)} %get-tuple-element.35) | copy-start | bytes 1572868
  26.2 3.0 %copy-start.8 = (f32[4,4,2,8,512]{4,3,2,1,0:T(8,128)S(1)}, f32[4,4,2,8,512]{4,3,2,1,0:T(8,128)}, u32[]{:S(2)}) copy-start(f32[4,4,2,8,512]{4,3,2,1,0:T(8,128)} %get-tuple-element.31) | copy-start | bytes 1572868
  30.7 12.8 %copy-start = (f32[1,512,1024]{2,1,0:T(8,128)S(1)}, f32[1,512,1024]{2,1,0:T(8,128)}, u32[]{:S(2)}) copy-start(f32[1,512,1024]{2,1,0:T(8,128)} %param.9) | copy-start | bytes 6291460
  39.3 153.6 %reduce-scatter.4.cloned.1.call-start = ((), (), s32[]{:S(2)}) async-start(), calls=%async_computation.2 | async-start | bytes 4456448
  39.4 39.6 %collective-permute-start.8 = (f32[512,2048]{1,0:T(8,128)}, f32[512,2048]{1,0:T(8,128)S(1)}, u32[]{:S(2)}, u32[]{:S(2)}) collective-permute-start(f32[512,2048]{1,0:T(8,128)} %bitcast.127), channel_id=1, source_target_pairs={{0,1},{1,0},{2,3},{3,2},{4,5},{5,4},{6,7},{7,6},{8,9},{9,8},{10,11... | collective-permute-start | bytes 12582920 | tf_op jit(solution)/shard_map/ppermute | solution.py:285
  39.4 39.5 %collective-permute-start.9 = (f32[512,2048]{1,0:T(8,128)}, f32[512,2048]{1,0:T(8,128)S(1)}, u32[]{:S(2)}, u32[]{:S(2)}) collective-permute-start(f32[512,2048]{1,0:T(8,128)} %bitcast.130), channel_id=1, source_target_pairs={{0,1},{1,0},{2,3},{3,2},{4,5},{5,4},{6,7},{7,6},{8,9},{9,8},{10,11... | collective-permute-start | bytes 12582920 | tf_op jit(solution)/shard_map/ppermute | solution.py:286
  39.9 39.0 %collective-permute-start.1 = (f32[256,1024]{1,0:T(8,128)}, f32[256,1024]{1,0:T(8,128)S(1)}, u32[]{:S(2)}, u32[]{:S(2)}) collective-permute-start(f32[256,1024]{1,0:T(8,128)} %get-tuple-element.77), channel_id=1, source_target_pairs={{0,64},{64,0},{1,65},{65,1},{2,66},{66,2},{3,67},{67,3},{4,68},{68... | collective-permute-start | bytes 3145736 | tf_op jit(solution)/shard_map/ppermute | solution.py:255
  41.7 6.8 %copy-start.4 = (f32[256,512]{1,0:T(8,128)S(1)}, f32[256,512]{1,0:T(8,128)}, u32[]{:S(2)}) copy-start(f32[256,512]{1,0:T(8,128)} %get-tuple-element.72) | copy-start | bytes 1572868
  41.7 6.8 %copy-start.9 = (f32[4,4,2,8,512]{4,3,2,1,0:T(8,128)S(1)}, f32[4,4,2,8,512]{4,3,2,1,0:T(8,128)}, u32[]{:S(2)}) copy-start(f32[4,4,2,8,512]{4,3,2,1,0:T(8,128)} %get-tuple-element.39) | copy-start | bytes 1572868
  41.7 37.2 %collective-permute-start.10 = (f32[256,512]{1,0:T(8,128)}, f32[256,512]{1,0:T(8,128)S(1)}, u32[]{:S(2)}, u32[]{:S(2)}) collective-permute-start(f32[256,512]{1,0:T(8,128)} %get-tuple-element.72), channel_id=1, source_target_pairs={{0,64},{64,0},{1,65},{65,1},{2,66},{66,2},{3,67},{67,3},{4,68},{68... | collective-permute-start | bytes 1572872 | tf_op jit(solution)/shard_map/ppermute | solution.py:249
  46.8 2.8 %copy-start.3 = (f32[4,4,2,8,512]{4,3,2,1,0:T(8,128)S(1)}, f32[4,4,2,8,512]{4,3,2,1,0:T(8,128)}, u32[]{:S(2)}) copy-start(f32[4,4,2,8,512]{4,3,2,1,0:T(8,128)} %get-tuple-element.34) | copy-start | bytes 1572868
  46.8 2.8 %copy-start.6 = (f32[4,4,2,8,512]{4,3,2,1,0:T(8,128)S(1)}, f32[4,4,2,8,512]{4,3,2,1,0:T(8,128)}, u32[]{:S(2)}) copy-start(f32[4,4,2,8,512]{4,3,2,1,0:T(8,128)} %get-tuple-element.35) | copy-start | bytes 1572868
  46.8 65.9 %collective-permute-start.7 = (f32[256,1536]{1,0:T(8,128)}, f32[256,1536]{1,0:T(8,128)}, u32[]{:S(2)}, u32[]{:S(2)}) collective-permute-start(f32[256,1536]{1,0:T(8,128)} %slice_dynamic-update-slice_fusion.2), channel_id=1, source_target_pairs={{0,64},{64,0},{1,65},{65,1},{2,66},{66,2},{3,67},{67,3},{4,68},{68... | collective-permute-start | bytes 4718600 | tf_op jit(solution)/shard_map/ppermute | solution.py:281
  78.9 2.5 %copy-start.18 = (f32[256,512]{1,0:T(8,128)}, f32[256,512]{1,0:T(8,128)S(1)}, u32[]{:S(2)}) copy-start(f32[256,512]{1,0:T(8,128)S(1)} %collective-permute-done.10.refs_4_) | copy-start | bytes 1572868
  78.9 1.0 copy-start.16
  78.9 3.8 %copy-start.14 = (f32[512,2048]{1,0:T(8,128)}, f32[512,2048]{1,0:T(8,128)S(1)}, u32[]{:S(2)}) copy-start(f32[512,2048]{1,0:T(8,128)S(1)} %collective-permute-done.8.refs_8_.refs_6_) | copy-start | bytes 12582916
  78.9 2.3 %copy-start.15 = (f32[512,2048]{1,0:T(8,128)}, f32[512,2048]{1,0:T(8,128)S(1)}, u32[]{:S(2)}) copy-start(f32[512,2048]{1,0:T(8,128)S(1)} %collective-permute-done.9.refs_9_.refs_7_) | copy-start | bytes 12582916
  82.7 16.6 %copy-start.17 = (f32[256,1024]{1,0:T(8,128)S(1)}, f32[256,1024]{1,0:T(8,128)}, u32[]{:S(2)}) copy-start(f32[256,1024]{1,0:T(8,128)} %copy-done.16) | copy-start | bytes 3145732
  82.7 16.8 %copy-start.1 = (f32[512,1024]{1,0:T(8,128)S(1)}, f32[512,1024]{1,0:T(8,128)}, u32[]{:S(2)}) copy-start(f32[512,1024]{1,0:T(8,128)} %bitcast_subtract_fusion.1) | copy-start | bytes 6291460
  99.3 13.4 %collective-permute-start.11 = (f32[256,1024]{1,0:T(8,128)S(1)}, f32[256,1024]{1,0:T(8,128)}, u32[]{:S(2)}, u32[]{:S(2)}) collective-permute-start(f32[256,1024]{1,0:T(8,128)S(1)} %copy-done.17), channel_id=1, source_target_pairs={{0,1},{1,0},{2,3},{3,2},{4,5},{5,4},{6,7},{7,6},{8,9},{9,8},{10,11... | collective-permute-start | bytes 3145736 | tf_op jit(solution)/shard_map/ppermute | solution.py:289
  99.5 61.5 %collective-permute-start.2 = (f32[512,1024]{1,0:T(8,128)S(1)}, f32[512,1024]{1,0:T(8,128)}, u32[]{:S(2)}, u32[]{:S(2)}) collective-permute-start(f32[512,1024]{1,0:T(8,128)S(1)} %copy-done.1), channel_id=1, source_target_pairs={{0,64},{64,0},{1,65},{65,1},{2,66},{66,2},{3,67},{67,3},{4,68},{68... | collective-permute-start | bytes 6291464 | tf_op jit(solution)/shard_map/ppermute | solution.py:283
  131.0 6.1 %copy-start.2 = (f32[16,16,2048]{2,1,0:T(8,128)S(1)}, f32[16,16,2048]{2,1,0:T(8,128)}, u32[]{:S(2)}) copy-start(f32[16,16,2048]{2,1,0:T(8,128)} %get-tuple-element.45) | copy-start | bytes 6291460
  133.9 22.2 %collective-permute-start.13 = (f32[4,16,2048]{2,1,0:T(8,128)}, f32[4,16,2048]{2,1,0:T(8,128)}, u32[]{:S(2)}, u32[]{:S(2)}) collective-permute-start(f32[4,16,2048]{2,1,0:T(8,128)} %get-tuple-element.67), channel_id=1, source_target_pairs={{0,32},{16,48},{32,0},{48,16},{1,33},{17,49},{33,1},{49,17},{2,34}... | collective-permute-start | bytes 1572872 | tf_op jit(solution)/shard_map/ppermute | solution.py:222
  138.3 20.5 %collective-permute-start.12 = (f32[4,16,2048]{2,1,0:T(8,128)}, f32[4,16,2048]{2,1,0:T(8,128)}, u32[]{:S(2)}, u32[]{:S(2)}) collective-permute-start(f32[4,16,2048]{2,1,0:T(8,128)} %get-tuple-element.71), channel_id=1, source_target_pairs={{0,4},{2,6},{4,0},{6,2},{1,5},{3,7},{5,1},{7,3},{8,12},{10,14},{12... | collective-permute-start | bytes 1572872 | tf_op jit(solution)/shard_map/ppermute | solution.py:222
  142.3 32.3 %collective-permute-start.16 = (f32[4,16,2048]{2,1,0:T(8,128)}, f32[4,16,2048]{2,1,0:T(8,128)}, u32[]{:S(2)}, u32[]{:S(2)}) collective-permute-start(f32[4,16,2048]{2,1,0:T(8,128)} %get-tuple-element.65), channel_id=1, source_target_pairs={{0,16},{16,32},{32,48},{48,0},{1,17},{17,33},{33,49},{49,1},{2,18}... | collective-permute-start | bytes 1572872 | tf_op jit(solution)/shard_map/ppermute | solution.py:222
  143.0 31.6 %collective-permute-start.14 = (f32[4,16,2048]{2,1,0:T(8,128)}, f32[4,16,2048]{2,1,0:T(8,128)}, u32[]{:S(2)}, u32[]{:S(2)}) collective-permute-start(f32[4,16,2048]{2,1,0:T(8,128)} %get-tuple-element.69), channel_id=1, source_target_pairs={{0,2},{2,4},{4,6},{6,0},{1,3},{3,5},{5,7},{7,1},{8,10},{10,12},{12... | collective-permute-start | bytes 1572872 | tf_op jit(solution)/shard_map/ppermute | solution.py:222
  144.0 12.1 %copy-start.10 = (f32[4,16,2048]{2,1,0:T(8,128)S(1)}, f32[4,16,2048]{2,1,0:T(8,128)}, u32[]{:S(2)}) copy-start(f32[4,16,2048]{2,1,0:T(8,128)} %get-tuple-element.49) | copy-start | bytes 1572868
  144.0 14.8 %copy-start.11 = (f32[4,16,2048]{2,1,0:T(8,128)S(1)}, f32[4,16,2048]{2,1,0:T(8,128)}, u32[]{:S(2)}) copy-start(f32[4,16,2048]{2,1,0:T(8,128)} %get-tuple-element.48) | copy-start | bytes 1572868
  156.1 18.4 %collective-permute-start.17 = (f32[4,16,2048]{2,1,0:T(8,128)S(1)}, f32[4,16,2048]{2,1,0:T(8,128)S(1)}, u32[]{:S(2)}, u32[]{:S(2)}) collective-permute-start(f32[4,16,2048]{2,1,0:T(8,128)S(1)} %copy-done.10), channel_id=1, source_target_pairs={{0,48},{16,0},{32,16},{48,32},{1,49},{17,1},{33,17},{49,33},{2,50}... | collective-permute-start | bytes 1572872 | tf_op jit(solution)/shard_map/ppermute | solution.py:222
  158.8 15.8 %collective-permute-start.15 = (f32[4,16,2048]{2,1,0:T(8,128)S(1)}, f32[4,16,2048]{2,1,0:T(8,128)S(1)}, u32[]{:S(2)}, u32[]{:S(2)}) collective-permute-start(f32[4,16,2048]{2,1,0:T(8,128)S(1)} %copy-done.11), channel_id=1, source_target_pairs={{0,6},{2,0},{4,2},{6,4},{1,7},{3,1},{5,3},{7,5},{8,14},{10,8},{12,... | collective-permute-start | bytes 1572872 | tf_op jit(solution)/shard_map/ppermute | solution.py:222
  175.9 17.0 %copy-start.12 = (f32[1,16,2048]{2,1,0:T(8,128)S(1)}, f32[1,16,2048]{2,1,0:T(8,128)}, u32[]{:S(2)}) copy-start(f32[1,16,2048]{2,1,0:T(8,128)} %param.17) | copy-start | bytes 393220
  175.9 8.8 %collective-permute-start.18 = (f32[16,2048]{1,0:T(8,128)S(1)}, f32[16,2048]{1,0:T(8,128)S(1)}, u32[]{:S(2)}, u32[]{:S(2)}) collective-permute-start(f32[16,2048]{1,0:T(8,128)S(1)} %get-tuple-element.85), channel_id=1, source_target_pairs={{0,32},{16,48},{32,0},{48,16},{1,33},{17,49},{33,1},{49,17},{2,34}... | collective-permute-start | bytes 393224 | tf_op jit(solution)/shard_map/ppermute | solution.py:222
  177.4 7.4 %collective-permute-start.21 = (f32[16,2048]{1,0:T(8,128)S(1)}, f32[16,2048]{1,0:T(8,128)S(1)}, u32[]{:S(2)}, u32[]{:S(2)}) collective-permute-start(f32[16,2048]{1,0:T(8,128)S(1)} %get-tuple-element.88), channel_id=1, source_target_pairs={{0,4},{2,6},{4,0},{6,2},{1,5},{3,7},{5,1},{7,3},{8,12},{10,14},{12... | collective-permute-start | bytes 393224 | tf_op jit(solution)/shard_map/ppermute | solution.py:222
  180.3 7.7 %collective-permute-start.19 = (f32[16,2048]{1,0:T(8,128)S(1)}, f32[16,2048]{1,0:T(8,128)S(1)}, u32[]{:S(2)}, u32[]{:S(2)}) collective-permute-start(f32[16,2048]{1,0:T(8,128)S(1)} %get-tuple-element.83), channel_id=1, source_target_pairs={{0,16},{16,32},{32,48},{48,0},{1,17},{17,33},{33,49},{49,1},{2,18}... | collective-permute-start | bytes 393224 | tf_op jit(solution)/shard_map/ppermute | solution.py:222
  184.8 6.0 %collective-permute-start.20 = (f32[16,2048]{1,0:T(8,128)S(1)}, f32[16,2048]{1,0:T(8,128)S(1)}, u32[]{:S(2)}, u32[]{:S(2)}) collective-permute-start(f32[16,2048]{1,0:T(8,128)S(1)} %get-tuple-element.54), channel_id=1, source_target_pairs={{0,48},{16,0},{32,16},{48,32},{1,49},{17,1},{33,17},{49,33},{2,50}... | collective-permute-start | bytes 393224 | tf_op jit(solution)/shard_map/ppermute | solution.py:222
  184.8 7.3 %collective-permute-start.22 = (f32[16,2048]{1,0:T(8,128)S(1)}, f32[16,2048]{1,0:T(8,128)S(1)}, u32[]{:S(2)}, u32[]{:S(2)}) collective-permute-start(f32[16,2048]{1,0:T(8,128)S(1)} %get-tuple-element.86), channel_id=1, source_target_pairs={{0,2},{2,4},{4,6},{6,0},{1,3},{3,5},{5,7},{7,1},{8,10},{10,12},{12... | collective-permute-start | bytes 393224 | tf_op jit(solution)/shard_map/ppermute | solution.py:222
  184.8 7.3 %collective-permute-start.23 = (f32[16,2048]{1,0:T(8,128)S(1)}, f32[16,2048]{1,0:T(8,128)S(1)}, u32[]{:S(2)}, u32[]{:S(2)}) collective-permute-start(f32[16,2048]{1,0:T(8,128)S(1)} %get-tuple-element.59), channel_id=1, source_target_pairs={{0,6},{2,0},{4,2},{6,4},{1,7},{3,1},{5,3},{7,5},{8,14},{10,8},{12,... | collective-permute-start | bytes 393224 | tf_op jit(solution)/shard_map/ppermute | solution.py:222
  193.9 8.0 %collective-permute-start.24 = (f32[16,2048]{1,0:T(8,128)S(1)}, f32[16,2048]{1,0:T(8,128)S(1)}, u32[]{:S(2)}, u32[]{:S(2)}) collective-permute-start(f32[16,2048]{1,0:T(8,128)S(1)} %get-tuple-element.80), channel_id=1, source_target_pairs={{0,64},{8,72},{64,0},{72,8},{1,65},{9,73},{65,1},{73,9},{2,66},{10... | collective-permute-start | bytes 393224 | tf_op jit(solution)/shard_map/ppermute | solution.py:314
  196.9 6.5 %collective-permute-start.25 = (f32[16,2048]{1,0:T(8,128)S(1)}, f32[16,2048]{1,0:T(8,128)S(1)}, u32[]{:S(2)}, u32[]{:S(2)}) collective-permute-start(f32[16,2048]{1,0:T(8,128)S(1)} %get-tuple-element.81), channel_id=1, source_target_pairs={{0,8},{8,64},{64,72},{72,0},{1,9},{9,65},{65,73},{73,1},{2,10},{10... | collective-permute-start | bytes 393224 | tf_op jit(solution)/shard_map/ppermute | solution.py:314
  197.3 6.1 %collective-permute-start.26 = (f32[16,2048]{1,0:T(8,128)S(1)}, f32[16,2048]{1,0:T(8,128)S(1)}, u32[]{:S(2)}, u32[]{:S(2)}) collective-permute-start(f32[16,2048]{1,0:T(8,128)S(1)} %get-tuple-element.82), channel_id=1, source_target_pairs={{0,72},{8,0},{64,8},{72,64},{1,73},{9,1},{65,9},{73,65},{2,74},{10... | collective-permute-start | bytes 393224 | tf_op jit(solution)/shard_map/ppermute | solution.py:314
Sparse Core Ops, SparseCore 0:
  39.4 73.6 all-gather.1
Sparse Core Ops, SparseCore 1:
  101.6 91.2 reduce-scatter.3

commit v11 on v10

--- a/solution.py
+++ b/solution.py
@@ -280,13 +280,13 @@
 
     got1 = lax.ppermute(sent1, "party", SWAP)
     u_local = x - fa
-    u = lax.ppermute(after(u_local, got0), "party", SWAP)
 
     g_other = lax.ppermute(after(g, other), "core", SWAP)
     b_other = lax.ppermute(after(bb, other), "core", SWAP)
     rights = (g, bb, g_other, b_other)
     early = grad_parts(party_id, after(xs0, u_local, xs1, aa1), aa0, (x0_mine, x0_other, got0), rights, (), 1)
     sent = (got0, lax.ppermute(after(got0, early), "core", SWAP))
+    u = lax.ppermute(after(u_local, sent[1]), "party", SWAP)
     late = grad_parts(party_id, xs1, aa1, (got1,), rights, sent, LATE)
 
     early = lax.psum_scatter(early.reshape(16, 32, ff), ("z", "y"), scatter_dimension=0, tiled=True)

time: 213 us -> 211 us (level)
  waiting for transfers between devices: 57.6 us -> 53.6 us
  starting transfers between devices: 42.1 us -> 44.4 us
    ppermute x1, waiting for transfers between devices: 11.2 us -> 7.67 us  [body(): got1 = lax.ppermute(sent1, 'party', SWAP)]
    ppermute x1, waiting for transfers between devices: 0.01 us -> 2.9 us  [body(): sent = (got0, lax.ppermute(after(got0, early), 'core', SWAP))]
    ppermute x1, starting transfers between devices: 3.19 us -> 0.8 us  [body(): d_party = lax.ppermute(d, 'party', SWAP)]
    ppermute x12, waiting for transfers between devices: 7.93 us -> 5.79 us  [scattered_pair(): lax.ppermute(piece, axis, [(i, (i + step) % 4) for i in range(4)])]
    unnamed x41 -> x39, local copies, waits for them, and re-layouts: 7.2 us -> 6.51 us
  transfers between devices with their start and end apart: 29 -> 29, of which waited for: 10 -> 12; matrix products, arithmetic and copies ran while one was open for 12% -> 12% of each run, Pallas kernels for 29% -> 29%
where the time goes in v11:
time: 211 us
  Pallas kernels  65.4 us (31%)
  waiting for transfers between devices  53.6 us (25%)
  starting transfers between devices  44.4 us (21%)
  other arithmetic  17.6 us (8%)
  between operations  15.8 us (7%)
  local copies, waits for them, and re-layouts  13.7 us (6%)
    pallas_call x2, Pallas kernels, grad_parts(): pl.pallas_call(lambda *refs: grad_kernel(bool(sent), *refs), grid=(ff //...  35.5 us
    ppermute x1, waiting for transfers between devices, body(): x0_other = lax.ppermute(x_other[0], 'party', SWAP)  26.5 us
    pallas_call x2, Pallas kernels, forward_call(): pl.pallas_call(kernel, grid=(steps,), in_specs=[pl.BlockSpec((rows, d), l...  25.6 us
    ppermute x12, starting transfers between devices, scattered_pair(): lax.ppermute(piece, axis, [(i, (i + step) % 4) for i in range(4)])  21.1 us
    ppermute x1, waiting for transfers between devices, body(): got1 = lax.ppermute(sent1, 'party', SWAP)  7.67 us
    unnamed x39, local copies, waits for them, and re-layouts  6.51 us
    ppermute x3, starting transfers between devices, body(): lax.ppermute(give, ('party', 'xl'), [(i, (i + step) % 4) for i in range(4)])  6.28 us
    ppermute x12, waiting for transfers between devices, scattered_pair(): lax.ppermute(piece, axis, [(i, (i + step) % 4) for i in range(4)])  5.79 us
  transfers between devices with their start and end apart: 29, of which 12 were waited for; matrix products, arithmetic and copies ran while one was open for 12% of the time, Pallas kernels for 29%

profile of v11, /device:TPU:0, one launch (start us, length us, event | category | flops | bytes accessed | tf_op | source)
XLA Modules:
  0.0 210.5 jit_solution(622029481998241216)
XLA Ops:
  8.1 4.3 %shard_map.104 = (f32[4,4,2,8,512]{4,3,2,1,0:T(8,128)}, f32[4,4,2,8,512]{4,3,2,1,0:T(8,128)}, f32[4,4,2,8,512]{4,3,2,1,0:T(8,128)}, f32[4,4,2,8,512]{4,3,2,1,0:T(8,128)}, f32[2,2,4,4,2,8,512]{6,5,4,3,2,1,0:T(8,128)}) custom-call(s32[1]{0:T(128)} %bitcast.3.core_ref, f32[512,1024]{1,0:T(8,128)} %bitcast.103, f32[512,1024]{1,0:T(8,128)} %bitcast.112), custom_call_target="tpu_custom_call" | custom-call | bytes 8388608 | tf_op jit(solution)/shard_map/pallas_call | solution.py:62
  12.4 2.9 %collective-permute-start.10 = (f32[16,2048]{1,0:T(8,128)S(1)}, f32[16,2048]{1,0:T(8,128)S(1)}, u32[]{:S(2)}, u32[]{:S(2)}) collective-permute-start(f32[16,2048]{1,0:T(8,128)S(1)} %bitcast_subtract_fusion), channel_id=1, source_target_pairs={{0,72},{72,0},{8,64},{64,8},{1,73},{73,1},{9,65},{65,9},{2,74},{74... | collective-permute-start | bytes 393224 | tf_op jit(solution)/shard_map/ppermute | solution.py:270
  16.1 2.7 %collective-permute-start.2 = (f32[256,512]{1,0:T(8,128)}, f32[256,512]{1,0:T(8,128)}, u32[]{:S(2)}, u32[]{:S(2)}) collective-permute-start(f32[256,512]{1,0:T(8,128)} %bitcast.125), channel_id=1, source_target_pairs={{0,64},{64,0},{1,65},{65,1},{2,66},{66,2},{3,67},{67,3},{4,68},{68... | collective-permute-start | bytes 1572872 | tf_op jit(solution)/shard_map/ppermute | solution.py:244
  19.8 1.9 slice_dynamic-update-slice_fusion.1
  21.6 1.7 fusion.17
  23.3 1.3 slice_bitcast_fusion
  24.7 1.0 slice_bitcast_fusion.1
  25.7 0.8 slice_dynamic-update-slice_fusion
  28.6 1.5 pad_maximum_fusion
  30.1 2.6 %collective-permute-done.10 = f32[16,2048]{1,0:T(8,128)S(1)} collective-permute-done((f32[16,2048]{1,0:T(8,128)S(1)}, f32[16,2048]{1,0:T(8,128)S(1)}, u32[]{:S(2)}, u32[]{:S(2)}) %collective-permute-start.10) | collective-permute-done | bytes 131104 | tf_op jit(solution)/shard_map/ppermute | solution.py:270
  32.7 4.4 %collective-permute-done.9 = f32[16,4096]{1,0:T(8,128)} collective-permute-done((f32[16,4096]{1,0:T(8,128)}, f32[16,4096]{1,0:T(8,128)}, u32[]{:S(2)}, u32[]{:S(2)}) %collective-permute-start.9) | collective-permute-done | bytes 262176 | tf_op jit(solution)/shard_map/ppermute | solution.py:269
  37.1 1.1 multiply_add_fusion
  38.3 0.8 pad_maximum_fusion.4
  39.8 3.1 %collective-permute-start.1 = (f32[256,1024]{1,0:T(8,128)}, f32[256,1024]{1,0:T(8,128)S(1)}, u32[]{:S(2)}, u32[]{:S(2)}) collective-permute-start(f32[256,1024]{1,0:T(8,128)} %get-tuple-element.77), channel_id=1, source_target_pairs={{0,64},{64,0},{1,65},{65,1},{2,66},{66,2},{3,67},{67,3},{4,68},{68... | collective-permute-start | bytes 3145736 | tf_op jit(solution)/shard_map/ppermute | solution.py:255
  43.3 3.3 %bitcast_subtract_fusion.1 = f32[512,1024]{1,0:T(8,128)} fusion(f32[1,512,1024]{2,1,0:T(8,128)} %param.12, f32[1,512,1024]{2,1,0:T(8,128)S(1)} %copy-done), kind=kLoop, calls=%fused_computation.75 | loop fusion | flops 524288 | bytes 6291456 | tf_op jit(solution)/shard_map/sub | solution.py:282
  46.6 3.1 %collective-permute-start.11 = (f32[256,1536]{1,0:T(8,128)}, f32[256,1536]{1,0:T(8,128)}, u32[]{:S(2)}, u32[]{:S(2)}) collective-permute-start(f32[256,1536]{1,0:T(8,128)} %slice_dynamic-update-slice_fusion.2), channel_id=1, source_target_pairs={{0,64},{64,0},{1,65},{65,1},{2,66},{66,2},{3,67},{67,3},{4,68},{68... | collective-permute-start | bytes 4718600 | tf_op jit(solution)/shard_map/ppermute | solution.py:281
  49.7 1.0 pad_maximum_fusion.1.refs_1_
  50.7 1.5 pad_maximum_fusion.2
  52.2 26.5 %collective-permute-done.3.refs_4_ = f32[256,512]{1,0:T(8,128)S(1)} collective-permute-done((f32[256,512]{1,0:T(8,128)}, f32[256,512]{1,0:T(8,128)S(1)}, u32[]{:S(2)}, u32[]{:S(2)}) %collective-permute-start.3) | collective-permute-done | bytes 524320 | tf_op jit(solution)/shard_map/ppermute | solution.py:249
  78.7 1.0 copy-done.15
  79.9 1.8 copy-done.14
  81.8 17.0 %shard_map.105 = f32[16,2,16,2048]{3,2,1,0:T(8,128)} custom-call(s32[1]{0:T(128)} %bitcast.8.refs_0_, f32[256,1024]{1,0:T(8,128)} %pad_maximum_fusion.1.refs_1_, f32[256,1024]{1,0:T(8,128)} %get-tuple-element.76.refs_2_, f32[256,512]{1,0:T(8,128)} %collective-permute-done.2.refs_3_, f32[256,512]{1,0:T(8,128)} %copy-done.17, f32[256,1024]{1,0:T(8,128)} %copy-done.15, ...), custom_call_target="tpu_custom_call" | custom-call | flops 9663676416 | bytes 25165824 | tf_op jit(solution)/shard_map/pallas_call | solution.py:137
  99.0 2.9 %collective-permute-done.6.refs_9_ = f32[256,1024]{1,0:T(8,128)} collective-permute-done((f32[256,1024]{1,0:T(8,128)S(1)}, f32[256,1024]{1,0:T(8,128)}, u32[]{:S(2)}, u32[]{:S(2)}) %collective-permute-start.6) | collective-permute-done | bytes 1048608 | tf_op jit(solution)/shard_map/ppermute | solution.py:288
  101.9 3.0 %collective-permute-start.7 = (f32[512,1024]{1,0:T(8,128)S(1)}, f32[512,1024]{1,0:T(8,128)}, u32[]{:S(2)}, u32[]{:S(2)}) collective-permute-start(f32[512,1024]{1,0:T(8,128)S(1)} %copy-done.1), channel_id=1, source_target_pairs={{0,64},{64,0},{1,65},{65,1},{2,66},{66,2},{3,67},{67,3},{4,68},{68... | collective-permute-start | bytes 6291464 | tf_op jit(solution)/shard_map/ppermute | solution.py:289
  104.9 7.7 %collective-permute-done.11.refs_3_ = f32[256,1536]{1,0:T(8,128)} collective-permute-done((f32[256,1536]{1,0:T(8,128)}, f32[256,1536]{1,0:T(8,128)}, u32[]{:S(2)}, u32[]{:S(2)}) %collective-permute-start.11) | collective-permute-done | bytes 1572896 | tf_op jit(solution)/shard_map/ppermute | solution.py:281
  112.5 18.5 %shard_map.107 = (f32[16,16,2048]{2,1,0:T(8,128)}, f32[16,16,2048]{2,1,0:T(8,128)}) custom-call(s32[1]{0:T(128)} %bitcast.8.refs_0_, f32[256,1024]{1,0:T(8,128)} %get-tuple-element.91.refs_1_, f32[256,1024]{1,0:T(8,128)} %get-tuple-element.92.refs_2_, f32[256,1536]{1,0:T(8,128)} %collective-permute-done.11.refs_3_, f32[512,2048]{1,0:T(8,128)} %bitcast.129, ...), custom_call_target="tpu_custom_call" | custom-call | flops 77309411328 | bytes 197132288 | tf_op jit(solution)/shard_map/pallas_call | solution.py:137
  131.1 2.9 %dynamic-slice_bitcast_fusion = (f32[4,16,2048]{2,1,0:T(8,128)}, f32[4,16,2048]{2,1,0:T(8,128)}, f32[4,16,2048]{2,1,0:T(8,128)S(1)}, f32[4,16,2048]{2,1,0:T(8,128)}) fusion(f32[4,4,16,2048]{3,2,1,0:T(8,128)} %bitcast.114, s32[]{:T(128)S(6)} %select_n.155, s32[]{:T(128)S(6)} %select_n.153, s32[]{:T(128)S(6)} %select_n.147, s32[]{:T(128)S(6)} %select_n.145), kind=kLoop, calls=%fused_computation.21 | loop fusion | bytes 4194320 | tf_op jit(solution)/shard_map/jit(dynamic_index_in_dim)/squeeze | solution.py:219
  134.0 3.1 %collective-permute-start.13 = (f32[4,16,2048]{2,1,0:T(8,128)}, f32[4,16,2048]{2,1,0:T(8,128)}, u32[]{:S(2)}, u32[]{:S(2)}) collective-permute-start(f32[4,16,2048]{2,1,0:T(8,128)} %get-tuple-element.67), channel_id=1, source_target_pairs={{0,32},{16,48},{32,0},{48,16},{1,33},{17,49},{33,1},{49,17},{2,34}... | collective-permute-start | bytes 1572872 | tf_op jit(solution)/shard_map/ppermute | solution.py:222
  137.1 1.2 dynamic-slice_bitcast_fusion.2
  138.3 4.0 %collective-permute-start.12 = (f32[4,16,2048]{2,1,0:T(8,128)}, f32[4,16,2048]{2,1,0:T(8,128)}, u32[]{:S(2)}, u32[]{:S(2)}) collective-permute-start(f32[4,16,2048]{2,1,0:T(8,128)} %get-tuple-element.71), channel_id=1, source_target_pairs={{0,4},{2,6},{4,0},{6,2},{1,5},{3,7},{5,1},{7,3},{8,12},{10,14},{12... | collective-permute-start | bytes 1572872 | tf_op jit(solution)/shard_map/ppermute | solution.py:222
  143.0 1.0 collective-permute-start.14
  144.0 12.1 %shard_map.106.c_ref = f32[512,2048]{1,0:T(8,128)} custom-call(f32[512,1024]{1,0:T(8,128)} %bitcast.105, f32[512,8192]{1,0:T(8,128)} %all-gather.2.cloned.1.call-done.w0_ref.w1_ref, f32[512,8192]{1,0:T(8,128)} %all-gather.2.cloned.1.call-done.w0_ref.w1_ref, f32[512,2048]{1,0:T(8,128)} %bitcast.109), custom_call_target="tpu_custom_call" | custom-call | flops 6442450944 | bytes 20971520 | tf_op jit(solution)/shard_map/pallas_call | solution.py:194
  156.1 2.8 %collective-permute-start.17 = (f32[4,16,2048]{2,1,0:T(8,128)S(1)}, f32[4,16,2048]{2,1,0:T(8,128)S(1)}, u32[]{:S(2)}, u32[]{:S(2)}) collective-permute-start(f32[4,16,2048]{2,1,0:T(8,128)S(1)} %copy-done.10), channel_id=1, source_target_pairs={{0,48},{16,0},{32,16},{48,32},{1,49},{17,1},{33,17},{49,33},{2,50}... | collective-permute-start | bytes 1572872 | tf_op jit(solution)/shard_map/ppermute | solution.py:222
  158.9 2.2 %collective-permute-start.15 = (f32[4,16,2048]{2,1,0:T(8,128)S(1)}, f32[4,16,2048]{2,1,0:T(8,128)S(1)}, u32[]{:S(2)}, u32[]{:S(2)}) collective-permute-start(f32[4,16,2048]{2,1,0:T(8,128)S(1)} %copy-done.11), channel_id=1, source_target_pairs={{0,6},{2,0},{4,2},{6,4},{1,7},{3,1},{5,3},{7,5},{8,14},{10,8},{12,... | collective-permute-start | bytes 1572872 | tf_op jit(solution)/shard_map/ppermute | solution.py:222
  161.2 13.5 %shard_map.108 = f32[512,2048]{1,0:T(8,128)} custom-call(f32[512,1024]{1,0:T(8,128)} %bitcast.104, f32[512,1024]{1,0:T(8,128)} %bitcast.106, f32[512,1024]{1,0:T(8,128)} %collective-permute-done.7.got_ref, f32[512,8192]{1,0:T(8,128)} %all-gather.2.cloned.1.call-done.w0_ref.w1_ref, f32[512,8192]{1,0:T(8,128)} %all-gather.2.cloned.1.call-done.w0_ref.w1_ref, ...), custom_call_target="tpu_custom_call" | custom-call | flops 6442450944 | bytes 20971520 | tf_op jit(solution)/shard_map/pallas_call | solution.py:194
  174.7 1.4 add_add_fusion.1
  176.3 1.3 add_add_fusion
  177.6 2.6 %collective-permute-start.21 = (f32[16,2048]{1,0:T(8,128)S(1)}, f32[16,2048]{1,0:T(8,128)S(1)}, u32[]{:S(2)}, u32[]{:S(2)}) collective-permute-start(f32[16,2048]{1,0:T(8,128)S(1)} %get-tuple-element.88), channel_id=1, source_target_pairs={{0,4},{2,6},{4,0},{6,2},{1,5},{3,7},{5,1},{7,3},{8,12},{10,14},{12... | collective-permute-start | bytes 393224 | tf_op jit(solution)/shard_map/ppermute | solution.py:222
  181.0 2.7 %collective-permute-done.18 = f32[16,2048]{1,0:T(8,128)S(1)} collective-permute-done((f32[16,2048]{1,0:T(8,128)S(1)}, f32[16,2048]{1,0:T(8,128)S(1)}, u32[]{:S(2)}, u32[]{:S(2)}) %collective-permute-start.18) | collective-permute-done | bytes 131104 | tf_op jit(solution)/shard_map/ppermute | solution.py:222
  184.7 3.0 %collective-permute-start.23 = (f32[16,2048]{1,0:T(8,128)S(1)}, f32[16,2048]{1,0:T(8,128)S(1)}, u32[]{:S(2)}, u32[]{:S(2)}) collective-permute-start(f32[16,2048]{1,0:T(8,128)S(1)} %get-tuple-element.59), channel_id=1, source_target_pairs={{0,6},{2,0},{4,2},{6,4},{1,7},{3,1},{5,3},{7,5},{8,14},{10,8},{12,... | collective-permute-start | bytes 393224 | tf_op jit(solution)/shard_map/ppermute | solution.py:222
  187.8 1.8 collective-permute-done.20
  189.6 1.0 collective-permute-done.22
  191.0 0.9 fusion.13
  191.9 3.0 %collective-permute-start.24 = (f32[16,2048]{1,0:T(8,128)S(1)}, f32[16,2048]{1,0:T(8,128)S(1)}, u32[]{:S(2)}, u32[]{:S(2)}) collective-permute-start(f32[16,2048]{1,0:T(8,128)S(1)} %get-tuple-element.80), channel_id=1, source_target_pairs={{0,64},{8,72},{64,0},{72,8},{1,65},{9,73},{65,1},{73,9},{2,66},{10... | collective-permute-start | bytes 393224 | tf_op jit(solution)/shard_map/ppermute | solution.py:314
  195.5 2.7 %collective-permute-start.26 = (f32[16,2048]{1,0:T(8,128)S(1)}, f32[16,2048]{1,0:T(8,128)S(1)}, u32[]{:S(2)}, u32[]{:S(2)}) collective-permute-start(f32[16,2048]{1,0:T(8,128)S(1)} %get-tuple-element.82), channel_id=1, source_target_pairs={{0,72},{8,0},{64,8},{72,64},{1,73},{9,1},{65,9},{73,65},{2,74},{10... | collective-permute-start | bytes 393224 | tf_op jit(solution)/shard_map/ppermute | solution.py:314
  198.2 1.8 collective-permute-done.24
  199.9 1.6 collective-permute-done.25
  201.5 1.5 fusion.10
  (82 shorter events, 9.1 us)
Async XLA Ops:
  8.0 136.0 %all-gather.2.cloned.1.call-start = ((), (), s32[]{:S(2)}) async-start(), calls=%async_computation.1 | async-start | bytes 17301504 | tf_op jit(solution)/shard_map/all_gather | solution.py:279
  8.0 4.3 %copy-start.7 = (f32[1,16,2048]{2,1,0:T(8,128)S(1)}, f32[1,16,2048]{2,1,0:T(8,128)}, u32[]{:S(2)}) copy-start(f32[1,16,2048]{2,1,0:T(8,128)} %param.13) | copy-start | bytes 393220
  8.1 4.3 %copy-start.13 = (f32[1,16,2048]{2,1,0:T(8,128)S(1)}, f32[1,16,2048]{2,1,0:T(8,128)}, u32[]{:S(2)}) copy-start(f32[1,16,2048]{2,1,0:T(8,128)} %param.10) | copy-start | bytes 393220
  12.3 12.4 %collective-permute-start = (f32[2,2,256,512]{3,2,1,0:T(8,128)}, f32[2,2,256,512]{3,2,1,0:T(8,128)S(1)}, u32[]{:S(2)}, u32[]{:S(2)}) collective-permute-start(f32[2,2,256,512]{3,2,1,0:T(8,128)} %bitcast.133), channel_id=1, source_target_pairs={{0,1},{1,0},{2,3},{3,2},{4,5},{5,4},{6,7},{7,6},{8,9},{9,8},{10,11... | collective-permute-start | bytes 6291464 | tf_op jit(solution)/shard_map/ppermute | solution.py:245
  12.4 20.4 %collective-permute-start.10 = (f32[16,2048]{1,0:T(8,128)S(1)}, f32[16,2048]{1,0:T(8,128)S(1)}, u32[]{:S(2)}, u32[]{:S(2)}) collective-permute-start(f32[16,2048]{1,0:T(8,128)S(1)} %bitcast_subtract_fusion), channel_id=1, source_target_pairs={{0,72},{72,0},{8,64},{64,8},{1,73},{73,1},{9,65},{65,9},{2,74},{74... | collective-permute-start | bytes 393224 | tf_op jit(solution)/shard_map/ppermute | solution.py:270
  15.3 17.5 %collective-permute-start.8 = (f32[16,2048]{1,0:T(8,128)S(1)}, f32[16,2048]{1,0:T(8,128)}, u32[]{:S(2)}, u32[]{:S(2)}) collective-permute-start(f32[16,2048]{1,0:T(8,128)S(1)} %bitcast_subtract_fusion), channel_id=1, source_target_pairs={{0,64},{64,0},{1,65},{65,1},{2,66},{66,2},{3,67},{67,3},{4,68},{68... | collective-permute-start | bytes 393224 | tf_op jit(solution)/shard_map/ppermute | solution.py:268
  16.1 23.0 %collective-permute-start.2 = (f32[256,512]{1,0:T(8,128)}, f32[256,512]{1,0:T(8,128)}, u32[]{:S(2)}, u32[]{:S(2)}) collective-permute-start(f32[256,512]{1,0:T(8,128)} %bitcast.125), channel_id=1, source_target_pairs={{0,64},{64,0},{1,65},{65,1},{2,66},{66,2},{3,67},{67,3},{4,68},{68... | collective-permute-start | bytes 1572872 | tf_op jit(solution)/shard_map/ppermute | solution.py:244
  19.5 17.6 %collective-permute-start.9 = (f32[16,4096]{1,0:T(8,128)}, f32[16,4096]{1,0:T(8,128)}, u32[]{:S(2)}, u32[]{:S(2)}) collective-permute-start(f32[16,4096]{1,0:T(8,128)} %pad_maximum_fusion.5), channel_id=1, source_target_pairs={{0,8},{8,0},{1,9},{9,1},{2,10},{10,2},{3,11},{11,3},{4,12},{12,4},... | collective-permute-start | bytes 786440 | tf_op jit(solution)/shard_map/ppermute | solution.py:269
  24.7 2.5 %copy-start.5 = (f32[4,4,2,8,512]{4,3,2,1,0:T(8,128)S(1)}, f32[4,4,2,8,512]{4,3,2,1,0:T(8,128)}, u32[]{:S(2)}) copy-start(f32[4,4,2,8,512]{4,3,2,1,0:T(8,128)} %get-tuple-element.35) | copy-start | bytes 1572868
  25.6 3.0 %copy-start.8 = (f32[4,4,2,8,512]{4,3,2,1,0:T(8,128)S(1)}, f32[4,4,2,8,512]{4,3,2,1,0:T(8,128)}, u32[]{:S(2)}) copy-start(f32[4,4,2,8,512]{4,3,2,1,0:T(8,128)} %get-tuple-element.31) | copy-start | bytes 1572868
  30.1 13.2 %copy-start = (f32[1,512,1024]{2,1,0:T(8,128)S(1)}, f32[1,512,1024]{2,1,0:T(8,128)}, u32[]{:S(2)}) copy-start(f32[1,512,1024]{2,1,0:T(8,128)} %param.9) | copy-start | bytes 6291460
  39.1 151.8 %reduce-scatter.4.cloned.1.call-start = ((), (), s32[]{:S(2)}) async-start(), calls=%async_computation.2 | async-start | bytes 4456448
  39.2 39.6 %collective-permute-start.4 = (f32[512,2048]{1,0:T(8,128)}, f32[512,2048]{1,0:T(8,128)S(1)}, u32[]{:S(2)}, u32[]{:S(2)}) collective-permute-start(f32[512,2048]{1,0:T(8,128)} %bitcast.127), channel_id=1, source_target_pairs={{0,1},{1,0},{2,3},{3,2},{4,5},{5,4},{6,7},{7,6},{8,9},{9,8},{10,11... | collective-permute-start | bytes 12582920 | tf_op jit(solution)/shard_map/ppermute | solution.py:284
  39.3 40.5 %collective-permute-start.5 = (f32[512,2048]{1,0:T(8,128)}, f32[512,2048]{1,0:T(8,128)}, u32[]{:S(2)}, u32[]{:S(2)}) collective-permute-start(f32[512,2048]{1,0:T(8,128)} %bitcast.130), channel_id=1, source_target_pairs={{0,1},{1,0},{2,3},{3,2},{4,5},{5,4},{6,7},{7,6},{8,9},{9,8},{10,11... | collective-permute-start | bytes 12582920 | tf_op jit(solution)/shard_map/ppermute | solution.py:285
  39.8 39.0 %collective-permute-start.1 = (f32[256,1024]{1,0:T(8,128)}, f32[256,1024]{1,0:T(8,128)S(1)}, u32[]{:S(2)}, u32[]{:S(2)}) collective-permute-start(f32[256,1024]{1,0:T(8,128)} %get-tuple-element.77), channel_id=1, source_target_pairs={{0,64},{64,0},{1,65},{65,1},{2,66},{66,2},{3,67},{67,3},{4,68},{68... | collective-permute-start | bytes 3145736 | tf_op jit(solution)/shard_map/ppermute | solution.py:255
  42.9 6.8 %copy-start.4 = (f32[256,512]{1,0:T(8,128)S(1)}, f32[256,512]{1,0:T(8,128)}, u32[]{:S(2)}) copy-start(f32[256,512]{1,0:T(8,128)} %get-tuple-element.74) | copy-start | bytes 1572868
  42.9 6.8 %copy-start.9 = (f32[4,4,2,8,512]{4,3,2,1,0:T(8,128)S(1)}, f32[4,4,2,8,512]{4,3,2,1,0:T(8,128)}, u32[]{:S(2)}) copy-start(f32[4,4,2,8,512]{4,3,2,1,0:T(8,128)} %get-tuple-element.33) | copy-start | bytes 1572868
  42.9 35.9 %collective-permute-start.3 = (f32[256,512]{1,0:T(8,128)}, f32[256,512]{1,0:T(8,128)S(1)}, u32[]{:S(2)}, u32[]{:S(2)}) collective-permute-start(f32[256,512]{1,0:T(8,128)} %get-tuple-element.74), channel_id=1, source_target_pairs={{0,64},{64,0},{1,65},{65,1},{2,66},{66,2},{3,67},{67,3},{4,68},{68... | collective-permute-start | bytes 1572872 | tf_op jit(solution)/shard_map/ppermute | solution.py:249
  46.6 4.2 %copy-start.3 = (f32[4,4,2,8,512]{4,3,2,1,0:T(8,128)S(1)}, f32[4,4,2,8,512]{4,3,2,1,0:T(8,128)}, u32[]{:S(2)}) copy-start(f32[4,4,2,8,512]{4,3,2,1,0:T(8,128)} %get-tuple-element.34) | copy-start | bytes 1572868
  46.6 4.2 %copy-start.6 = (f32[4,4,2,8,512]{4,3,2,1,0:T(8,128)S(1)}, f32[4,4,2,8,512]{4,3,2,1,0:T(8,128)}, u32[]{:S(2)}) copy-start(f32[4,4,2,8,512]{4,3,2,1,0:T(8,128)} %get-tuple-element.35) | copy-start | bytes 1572868
  46.6 65.9 %collective-permute-start.11 = (f32[256,1536]{1,0:T(8,128)}, f32[256,1536]{1,0:T(8,128)}, u32[]{:S(2)}, u32[]{:S(2)}) collective-permute-start(f32[256,1536]{1,0:T(8,128)} %slice_dynamic-update-slice_fusion.2), channel_id=1, source_target_pairs={{0,64},{64,0},{1,65},{65,1},{2,66},{66,2},{3,67},{67,3},{4,68},{68... | collective-permute-start | bytes 4718600 | tf_op jit(solution)/shard_map/ppermute | solution.py:281
  78.7 1.2 copy-start.17
  78.7 1.0 copy-start.15
  79.7 2.0 copy-start.14
  81.8 17.0 %copy-start.16 = (f32[256,1024]{1,0:T(8,128)S(1)}, f32[256,1024]{1,0:T(8,128)}, u32[]{:S(2)}) copy-start(f32[256,1024]{1,0:T(8,128)} %copy-done.15) | copy-start | bytes 3145732
  98.8 3.1 %collective-permute-start.6 = (f32[256,1024]{1,0:T(8,128)S(1)}, f32[256,1024]{1,0:T(8,128)}, u32[]{:S(2)}, u32[]{:S(2)}) collective-permute-start(f32[256,1024]{1,0:T(8,128)S(1)} %copy-done.16), channel_id=1, source_target_pairs={{0,1},{1,0},{2,3},{3,2},{4,5},{5,4},{6,7},{7,6},{8,9},{9,8},{10,11... | collective-permute-start | bytes 3145736 | tf_op jit(solution)/shard_map/ppermute | solution.py:288
  98.9 2.9 %copy-start.1 = (f32[512,1024]{1,0:T(8,128)S(1)}, f32[512,1024]{1,0:T(8,128)}, u32[]{:S(2)}) copy-start(f32[512,1024]{1,0:T(8,128)} %bitcast_subtract_fusion.1) | copy-start | bytes 6291460
  101.9 59.3 %collective-permute-start.7 = (f32[512,1024]{1,0:T(8,128)S(1)}, f32[512,1024]{1,0:T(8,128)}, u32[]{:S(2)}, u32[]{:S(2)}) collective-permute-start(f32[512,1024]{1,0:T(8,128)S(1)} %copy-done.1), channel_id=1, source_target_pairs={{0,64},{64,0},{1,65},{65,1},{2,66},{66,2},{3,67},{67,3},{4,68},{68... | collective-permute-start | bytes 6291464 | tf_op jit(solution)/shard_map/ppermute | solution.py:289
  131.1 6.0 %copy-start.2 = (f32[16,16,2048]{2,1,0:T(8,128)S(1)}, f32[16,16,2048]{2,1,0:T(8,128)}, u32[]{:S(2)}) copy-start(f32[16,16,2048]{2,1,0:T(8,128)} %get-tuple-element.45) | copy-start | bytes 6291460
  134.0 22.1 %collective-permute-start.13 = (f32[4,16,2048]{2,1,0:T(8,128)}, f32[4,16,2048]{2,1,0:T(8,128)}, u32[]{:S(2)}, u32[]{:S(2)}) collective-permute-start(f32[4,16,2048]{2,1,0:T(8,128)} %get-tuple-element.67), channel_id=1, source_target_pairs={{0,32},{16,48},{32,0},{48,16},{1,33},{17,49},{33,1},{49,17},{2,34}... | collective-permute-start | bytes 1572872 | tf_op jit(solution)/shard_map/ppermute | solution.py:222
  138.3 20.6 %collective-permute-start.12 = (f32[4,16,2048]{2,1,0:T(8,128)}, f32[4,16,2048]{2,1,0:T(8,128)}, u32[]{:S(2)}, u32[]{:S(2)}) collective-permute-start(f32[4,16,2048]{2,1,0:T(8,128)} %get-tuple-element.71), channel_id=1, source_target_pairs={{0,4},{2,6},{4,0},{6,2},{1,5},{3,7},{5,1},{7,3},{8,12},{10,14},{12... | collective-permute-start | bytes 1572872 | tf_op jit(solution)/shard_map/ppermute | solution.py:222
  142.4 32.3 %collective-permute-start.16 = (f32[4,16,2048]{2,1,0:T(8,128)}, f32[4,16,2048]{2,1,0:T(8,128)}, u32[]{:S(2)}, u32[]{:S(2)}) collective-permute-start(f32[4,16,2048]{2,1,0:T(8,128)} %get-tuple-element.65), channel_id=1, source_target_pairs={{0,16},{16,32},{32,48},{48,0},{1,17},{17,33},{33,49},{49,1},{2,18}... | collective-permute-start | bytes 1572872 | tf_op jit(solution)/shard_map/ppermute | solution.py:222
  143.0 31.6 %collective-permute-start.14 = (f32[4,16,2048]{2,1,0:T(8,128)}, f32[4,16,2048]{2,1,0:T(8,128)}, u32[]{:S(2)}, u32[]{:S(2)}) collective-permute-start(f32[4,16,2048]{2,1,0:T(8,128)} %get-tuple-element.69), channel_id=1, source_target_pairs={{0,2},{2,4},{4,6},{6,0},{1,3},{3,5},{5,7},{7,1},{8,10},{10,12},{12... | collective-permute-start | bytes 1572872 | tf_op jit(solution)/shard_map/ppermute | solution.py:222
  144.0 12.1 %copy-start.10 = (f32[4,16,2048]{2,1,0:T(8,128)S(1)}, f32[4,16,2048]{2,1,0:T(8,128)}, u32[]{:S(2)}) copy-start(f32[4,16,2048]{2,1,0:T(8,128)} %get-tuple-element.49) | copy-start | bytes 1572868
  144.0 14.9 %copy-start.11 = (f32[4,16,2048]{2,1,0:T(8,128)S(1)}, f32[4,16,2048]{2,1,0:T(8,128)}, u32[]{:S(2)}) copy-start(f32[4,16,2048]{2,1,0:T(8,128)} %get-tuple-element.48) | copy-start | bytes 1572868
  156.1 18.6 %collective-permute-start.17 = (f32[4,16,2048]{2,1,0:T(8,128)S(1)}, f32[4,16,2048]{2,1,0:T(8,128)S(1)}, u32[]{:S(2)}, u32[]{:S(2)}) collective-permute-start(f32[4,16,2048]{2,1,0:T(8,128)S(1)} %copy-done.10), channel_id=1, source_target_pairs={{0,48},{16,0},{32,16},{48,32},{1,49},{17,1},{33,17},{49,33},{2,50}... | collective-permute-start | bytes 1572872 | tf_op jit(solution)/shard_map/ppermute | solution.py:222
  158.9 15.7 %collective-permute-start.15 = (f32[4,16,2048]{2,1,0:T(8,128)S(1)}, f32[4,16,2048]{2,1,0:T(8,128)S(1)}, u32[]{:S(2)}, u32[]{:S(2)}) collective-permute-start(f32[4,16,2048]{2,1,0:T(8,128)S(1)} %copy-done.11), channel_id=1, source_target_pairs={{0,6},{2,0},{4,2},{6,4},{1,7},{3,1},{5,3},{7,5},{8,14},{10,8},{12,... | collective-permute-start | bytes 1572872 | tf_op jit(solution)/shard_map/ppermute | solution.py:222
  176.2 14.8 %copy-start.12 = (f32[1,16,2048]{2,1,0:T(8,128)S(1)}, f32[1,16,2048]{2,1,0:T(8,128)}, u32[]{:S(2)}) copy-start(f32[1,16,2048]{2,1,0:T(8,128)} %param.17) | copy-start | bytes 393220
  176.2 7.5 %collective-permute-start.18 = (f32[16,2048]{1,0:T(8,128)S(1)}, f32[16,2048]{1,0:T(8,128)S(1)}, u32[]{:S(2)}, u32[]{:S(2)}) collective-permute-start(f32[16,2048]{1,0:T(8,128)S(1)} %get-tuple-element.85), channel_id=1, source_target_pairs={{0,32},{16,48},{32,0},{48,16},{1,33},{17,49},{33,1},{49,17},{2,34}... | collective-permute-start | bytes 393224 | tf_op jit(solution)/shard_map/ppermute | solution.py:222
  177.6 7.1 %collective-permute-start.21 = (f32[16,2048]{1,0:T(8,128)S(1)}, f32[16,2048]{1,0:T(8,128)S(1)}, u32[]{:S(2)}, u32[]{:S(2)}) collective-permute-start(f32[16,2048]{1,0:T(8,128)S(1)} %get-tuple-element.88), channel_id=1, source_target_pairs={{0,4},{2,6},{4,0},{6,2},{1,5},{3,7},{5,1},{7,3},{8,12},{10,14},{12... | collective-permute-start | bytes 393224 | tf_op jit(solution)/shard_map/ppermute | solution.py:222
  180.2 7.6 %collective-permute-start.19 = (f32[16,2048]{1,0:T(8,128)S(1)}, f32[16,2048]{1,0:T(8,128)S(1)}, u32[]{:S(2)}, u32[]{:S(2)}) collective-permute-start(f32[16,2048]{1,0:T(8,128)S(1)} %get-tuple-element.83), channel_id=1, source_target_pairs={{0,16},{16,32},{32,48},{48,0},{1,17},{17,33},{33,49},{49,1},{2,18}... | collective-permute-start | bytes 393224 | tf_op jit(solution)/shard_map/ppermute | solution.py:222
  183.7 5.8 %collective-permute-start.20 = (f32[16,2048]{1,0:T(8,128)S(1)}, f32[16,2048]{1,0:T(8,128)S(1)}, u32[]{:S(2)}, u32[]{:S(2)}) collective-permute-start(f32[16,2048]{1,0:T(8,128)S(1)} %get-tuple-element.54), channel_id=1, source_target_pairs={{0,48},{16,0},{32,16},{48,32},{1,49},{17,1},{33,17},{49,33},{2,50}... | collective-permute-start | bytes 393224 | tf_op jit(solution)/shard_map/ppermute | solution.py:222
  183.7 6.9 %collective-permute-start.22 = (f32[16,2048]{1,0:T(8,128)S(1)}, f32[16,2048]{1,0:T(8,128)S(1)}, u32[]{:S(2)}, u32[]{:S(2)}) collective-permute-start(f32[16,2048]{1,0:T(8,128)S(1)} %get-tuple-element.86), channel_id=1, source_target_pairs={{0,2},{2,4},{4,6},{6,0},{1,3},{3,5},{5,7},{7,1},{8,10},{10,12},{12... | collective-permute-start | bytes 393224 | tf_op jit(solution)/shard_map/ppermute | solution.py:222
  184.7 5.9 %collective-permute-start.23 = (f32[16,2048]{1,0:T(8,128)S(1)}, f32[16,2048]{1,0:T(8,128)S(1)}, u32[]{:S(2)}, u32[]{:S(2)}) collective-permute-start(f32[16,2048]{1,0:T(8,128)S(1)} %get-tuple-element.59), channel_id=1, source_target_pairs={{0,6},{2,0},{4,2},{6,4},{1,7},{3,1},{5,3},{7,5},{8,14},{10,8},{12,... | collective-permute-start | bytes 393224 | tf_op jit(solution)/shard_map/ppermute | solution.py:222
  191.9 8.0 %collective-permute-start.24 = (f32[16,2048]{1,0:T(8,128)S(1)}, f32[16,2048]{1,0:T(8,128)S(1)}, u32[]{:S(2)}, u32[]{:S(2)}) collective-permute-start(f32[16,2048]{1,0:T(8,128)S(1)} %get-tuple-element.80), channel_id=1, source_target_pairs={{0,64},{8,72},{64,0},{72,8},{1,65},{9,73},{65,1},{73,9},{2,66},{10... | collective-permute-start | bytes 393224 | tf_op jit(solution)/shard_map/ppermute | solution.py:314
  194.9 6.6 %collective-permute-start.25 = (f32[16,2048]{1,0:T(8,128)S(1)}, f32[16,2048]{1,0:T(8,128)S(1)}, u32[]{:S(2)}, u32[]{:S(2)}) collective-permute-start(f32[16,2048]{1,0:T(8,128)S(1)} %get-tuple-element.81), channel_id=1, source_target_pairs={{0,8},{8,64},{64,72},{72,0},{1,9},{9,65},{65,73},{73,1},{2,10},{10... | collective-permute-start | bytes 393224 | tf_op jit(solution)/shard_map/ppermute | solution.py:314
  195.5 6.0 %collective-permute-start.26 = (f32[16,2048]{1,0:T(8,128)S(1)}, f32[16,2048]{1,0:T(8,128)S(1)}, u32[]{:S(2)}, u32[]{:S(2)}) collective-permute-start(f32[16,2048]{1,0:T(8,128)S(1)} %get-tuple-element.82), channel_id=1, source_target_pairs={{0,72},{8,0},{64,8},{72,64},{1,73},{9,1},{65,9},{73,65},{2,74},{10... | collective-permute-start | bytes 393224 | tf_op jit(solution)/shard_map/ppermute | solution.py:314
Sparse Core Ops, SparseCore 0:
  39.2 75.0 all-gather.1
Sparse Core Ops, SparseCore 1:
  99.1 91.8 reduce-scatter.3
